TPU v7x, 32 devices: a whole 2x2x4 slice. The times are simulated.
32 devices in a mesh: dp: 8 (over y, x, core), tensor: 4 (over z).
Axes of the slice: x: 2, y: 2, z: 4, core: 2. Of those that a mesh axis runs over, the one named last changes fastest.
Arguments:
- patches: float32 [64, 256, 16], P('dp'), may hold values from -5 to 5
- noise_draw: float32 [64, 256, 16], P('dp'), may hold values from -5 to 5
- timesteps: int32 [64], P('dp'), may hold values from 0 to 999
- labels: int32 [64], P('dp'), may hold values from 0 to 999
- w_attn: float32 [2, 4, 768, 768], P(None, None, 'dp', 'tensor'), may hold values from -0.3125 to 0.3125
- w_mlp: float32 [2, 2, 768, 3072], P(None, None, 'dp', 'tensor'), may hold values from -0.21875 to 0.21875
- w_mod: float32 [2, 768, 4608], P(None, 'dp', 'tensor'), may hold values from -0.21875 to 0.21875
- w_embed: float32 [3592, 768], P(None, 'dp'), as said below
- biases: float32 [33, 768], replicated, may hold values from -0.4375 to 0.4375
- momentum_attn: float32 [2, 4, 768, 768], P(None, None, 'dp', 'tensor'), may hold values from -0.15625 to 0.15625
- momentum_mlp: float32 [2, 2, 768, 3072], P(None, None, 'dp', 'tensor'), may hold values from -0.15625 to 0.15625
- momentum_mod: float32 [2, 768, 4608], P(None, 'dp', 'tensor'), may hold values from -0.15625 to 0.15625
- momentum_embed: float32 [3592, 768], P(None, 'dp'), may hold values from -0.15625 to 0.15625
- momentum_bias: float32 [33, 768], replicated, may hold values from -0.15625 to 0.15625
- first_attn: float32 [2, 4, 3072, 768], P(None, None, 'dp', 'tensor'), as said below
- second_attn: float32 [2, 4, 3072, 768], P(None, None, 'dp', 'tensor'), as said below
- first_mlp: float32 [2, 2, 3072, 3072], P(None, None, 'dp', 'tensor'), as said below
- second_mlp: float32 [2, 2, 3072, 3072], P(None, None, 'dp', 'tensor'), as said below
- first_mod: float32 [2, 3072, 4608], P(None, 'dp', 'tensor'), as said below
- second_mod: float32 [2, 3072, 4608], P(None, 'dp', 'tensor'), as said below
- first_embed: float32 [3592, 3072], P(None, 'dp'), as said below
- second_embed: float32 [3592, 3072], P(None, 'dp'), as said below
- first_bias: float32 [4, 33, 768], replicated, as said below
- second_bias: float32 [4, 33, 768], replicated, as said below
Outputs:
- loss: float32 [], replicated
- group_norms: float32 [4], replicated
- bias_grads: float32 [4, 33, 768], replicated
- new_attn: float32 [2, 4, 768, 768], P(None, None, 'dp', 'tensor')
- new_mlp: float32 [2, 2, 768, 3072], P(None, None, 'dp', 'tensor')
- new_mod: float32 [2, 768, 4608], P(None, 'dp', 'tensor')
- new_embed: float32 [3592, 768], P(None, 'dp')
- new_bias: float32 [33, 768], replicated
- new_momentum_attn: float32 [2, 4, 768, 768], P(None, None, 'dp', 'tensor')
- new_momentum_mlp: float32 [2, 2, 768, 3072], P(None, None, 'dp', 'tensor')
- new_momentum_mod: float32 [2, 768, 4608], P(None, 'dp', 'tensor')
- new_momentum_embed: float32 [3592, 768], P(None, 'dp')
- new_momentum_bias: float32 [33, 768], replicated
- new_first_attn: float32 [2, 4, 3072, 768], P(None, None, 'dp', 'tensor')
- new_second_attn: float32 [2, 4, 3072, 768], P(None, None, 'dp', 'tensor')
- new_first_mlp: float32 [2, 2, 3072, 3072], P(None, None, 'dp', 'tensor')
- new_second_mlp: float32 [2, 2, 3072, 3072], P(None, None, 'dp', 'tensor')
- new_first_mod: float32 [2, 3072, 4608], P(None, 'dp', 'tensor')
- new_second_mod: float32 [2, 3072, 4608], P(None, 'dp', 'tensor')
- new_first_embed: float32 [3592, 3072], P(None, 'dp')
- new_second_embed: float32 [3592, 3072], P(None, 'dp')
- new_first_bias: float32 [4, 33, 768], replicated
- new_second_bias: float32 [4, 33, 768], replicated
Inputs may be any that keep to these rules, and one draw needn't show every extreme that they name: `w_embed`: rows scaled by block: class table 0.05, first timestep map 256^-0.5, patch map 16^-0.5, the rest 768^-0.5, truncated at 4 scales. `first_attn`: spread 0.11 g with g = 0.02 / sqrt(24017664), both signs. `second_attn`: between 1 and 4 times 0.0526 g^2, even in the logarithm. `first_mlp`: as first_attn. `second_mlp`: as second_attn. `first_mod`: as first_attn with 3 g in place of g. `second_mod`: as second_attn with 3 g in place of g. `first_embed`: as first_attn with 2 g in place of g. `second_embed`: as second_attn with 2 g in place of g. `first_bias`: as first_attn with 4 g in place of g. `second_bias`: as second_attn with 4 g in place of g.
All inputs are finite; a program needn't handle non-finite values.
Results may differ from a plain program's by a relative error of at most 0.019.
Values may be sent and summed in bfloat16 or wider, within the bound.
A program may use at most 384 MiB of HBM per device.

v0:
```python
import jax
import jax.numpy as jnp
from jax import lax
from jax.sharding import PartitionSpec as P

D = 768
HD = 64
FF = 3072
NCLS = 1000
FREQ = 256
PATCH_IN = 16
SIDE = 16
L = 2
GROUPS = 4
STEP_COUNT = 10
NSTEPS = 1000
S = 256
LB = 14


LOW_TYPE = jnp.bfloat16
LEARN_RATE = 0.03
WEIGHT_DECAY = 0.1
BETA_FIRST = 0.9
BETA_SECOND = 0.95
ADAM_EPSILON = 1e-08
CLIP_NORM = 0.02
OUTER_RATE = 0.7
OUTER_MOMENTUM = 0.9


def shortened(shard):
    return jax.tree.map(lambda a: a.astype(jnp.bfloat16) if a.dtype == jnp.float32 else a, shard)


def swapped(value, axis, bit):
    mask = 2**bit
    pairs = [(source, source ^ mask) for source in range(lax.axis_size(axis))]
    return lax.ppermute(value, axis, pairs)


def product(left, right):
    return jnp.dot(left, right, preferred_element_type=jnp.float32)


def product_t(left, right):
    return lax.dot_general(
        left, right, (((left.ndim - 1,), (1,)), ((), ())), preferred_element_type=jnp.float32
    )


def weight_grad(inputs, grads_out):
    leading = tuple(range(inputs.ndim - 1))
    return lax.dot_general(
        inputs, grads_out, ((leading, leading), ((), ())), preferred_element_type=jnp.float32
    )


def normalize(values):
    centred = values - jnp.mean(values, -1, keepdims=True)
    inverse = lax.rsqrt(jnp.mean(centred * centred, -1, keepdims=True) + 1e-06)
    return (centred * inverse, inverse)


def normalize_back(grad_in, normed, inverse):
    return inverse * (
        grad_in
        - jnp.mean(grad_in, -1, keepdims=True)
        - normed * jnp.mean(grad_in * normed, -1, keepdims=True)
    )


def gelu_tanh(values):
    return jax.nn.gelu(values, approximate=True)


def positions():
    quarter = D // 4
    omegas = 1.0 / 10000.0 ** (jnp.arange(quarter, dtype=jnp.float32) / quarter)
    places = jnp.arange(S, dtype=jnp.int32)
    across = (places % SIDE).astype(jnp.float32)[:, None] * omegas[None, :]
    downward = (places // SIDE).astype(jnp.float32)[:, None] * omegas[None, :]
    return jnp.concatenate(
        [jnp.sin(across), jnp.cos(across), jnp.sin(downward), jnp.cos(downward)], axis=1
    )


def frequencies(stamps):
    half_width = FREQ // 2
    freq_rates = jnp.exp(-jnp.log(10000.0) * jnp.arange(half_width, dtype=jnp.float32) / half_width)
    angles = stamps.astype(jnp.float32)[:, None] * freq_rates[None, :]
    return jnp.concatenate([jnp.cos(angles), jnp.sin(angles)], axis=1)


def signal_levels(stamps):
    noise_rates = jnp.linspace(0.0001, 0.02, NSTEPS, dtype=jnp.float32)
    kept_share = jnp.cumprod(1.0 - noise_rates)
    matches = stamps[:, None] == jnp.arange(NSTEPS, dtype=jnp.int32)[None, :]
    return jnp.sum(jnp.where(matches, kept_share[None, :], 0.0), axis=1)


def embed_parts(matrix):
    bounds = [
        NCLS,
        NCLS + FREQ,
        NCLS + FREQ + D,
        NCLS + FREQ + D + PATCH_IN,
        NCLS + FREQ + 3 * D + PATCH_IN,
    ]
    return (
        matrix[: bounds[0]],
        matrix[bounds[0] : bounds[1]],
        matrix[bounds[1] : bounds[2]],
        matrix[bounds[2] : bounds[3]],
        matrix[bounds[3] : bounds[4]],
        matrix[bounds[4] :],
    )


def split_heads(array_in):
    return array_in.reshape(array_in.shape[:2] + (array_in.shape[2] // HD, HD))


def head_scores(queries, key_rows):
    return jnp.einsum(
        "nqhd,nkhd->nhqk",
        split_heads(queries),
        split_heads(key_rows),
        preferred_element_type=jnp.float32,
    ) * HD ** (-0.5)


def attend(queries, key_rows, values):
    scores = head_scores(queries, key_rows)
    highest = jnp.max(scores, -1, keepdims=True)
    log_total = highest + jnp.log(jnp.sum(jnp.exp(scores - highest), -1, keepdims=True))
    weights = jnp.exp(scores - log_total).astype(LOW_TYPE)
    output = jnp.einsum(
        "nhqk,nkhd->nqhd", weights, split_heads(values), preferred_element_type=jnp.float32
    )
    return (output.reshape(queries.shape), log_total)


def attend_back(queries, key_rows, values, log_total, grad_out):
    weights = jnp.exp(head_scores(queries, key_rows) - log_total)
    grad_heads = split_heads(grad_out)
    grad_values = jnp.einsum(
        "nhqk,nqhd->nkhd", weights.astype(LOW_TYPE), grad_heads, preferred_element_type=jnp.float32
    )
    grad_weights = jnp.einsum(
        "nqhd,nkhd->nhqk", grad_heads, split_heads(values), preferred_element_type=jnp.float32
    )
    grad_scores = (
        weights * (grad_weights - jnp.sum(weights * grad_weights, -1, keepdims=True))
    ).astype(LOW_TYPE)
    grad_queries = jnp.einsum(
        "nhqk,nkhd->nqhd", grad_scores, split_heads(key_rows), preferred_element_type=jnp.float32
    ) * HD ** (-0.5)
    grad_keys = jnp.einsum(
        "nhqk,nqhd->nkhd", grad_scores, split_heads(queries), preferred_element_type=jnp.float32
    ) * HD ** (-0.5)
    return (
        grad_queries.reshape(queries.shape).astype(LOW_TYPE),
        grad_keys.reshape(queries.shape).astype(LOW_TYPE),
        grad_values.reshape(queries.shape).astype(LOW_TYPE),
    )


def tensor_forward(partial_out):
    return lax.psum(partial_out.astype(jnp.bfloat16), "tensor").astype(jnp.float32)


def tensor_backward(partial_in):
    return lax.psum(partial_in.astype(jnp.bfloat16), "tensor").astype(jnp.float32)


def place(vector_all, piece_in, offset):
    return lax.dynamic_update_slice_in_dim(vector_all, piece_in, offset, 0)


def layer_forward(stream, modulation, attn_now, mlp_now, bias_layer, shard_at):
    width_all = stream.shape[-1]
    col_width = attn_now.shape[2]
    unit_width = mlp_now.shape[2]
    mod_parts = [
        modulation[:, None, part_at * width_all : (part_at + 1) * width_all] for part_at in range(6)
    ]
    normed_one, inverse_one = normalize(stream)
    hidden_one = (normed_one * (1.0 + mod_parts[1]) + mod_parts[0]).astype(LOW_TYPE)
    queries = (
        product(hidden_one, attn_now[0])
        + lax.dynamic_slice_in_dim(bias_layer, shard_at * col_width, col_width)
    ).astype(LOW_TYPE)
    key_rows = product(hidden_one, attn_now[1]).astype(LOW_TYPE)
    values = (
        product(hidden_one, attn_now[2])
        + lax.dynamic_slice_in_dim(bias_layer, width_all + shard_at * col_width, col_width)
    ).astype(LOW_TYPE)
    attended, log_total = attend(queries, key_rows, values)
    attended = attended.astype(LOW_TYPE)
    branch_one = (
        tensor_forward(product_t(attended, attn_now[3])) + bias_layer[2 * width_all : 3 * width_all]
    )
    middle = stream + mod_parts[2] * branch_one
    normed_two, inverse_two = normalize(middle)
    hidden_two = (normed_two * (1.0 + mod_parts[4]) + mod_parts[3]).astype(LOW_TYPE)
    before = product(hidden_two, mlp_now[0]) + lax.dynamic_slice_in_dim(
        bias_layer, 3 * width_all + shard_at * unit_width, unit_width
    )
    activated = gelu_tanh(before).astype(LOW_TYPE)
    branch_two = (
        tensor_forward(product_t(activated, mlp_now[1]))
        + bias_layer[3 * width_all + FF : 4 * width_all + FF]
    )
    result = middle + mod_parts[5] * branch_two
    kept_state = (
        normed_one,
        inverse_one,
        hidden_one,
        queries,
        key_rows,
        values,
        log_total,
        attended,
        branch_one,
        normed_two,
        inverse_two,
        hidden_two,
        before,
        activated,
        branch_two,
    )
    return (result, kept_state)


def layer_backward(grad_out, modulation, attn_now, mlp_now, shard_at, kept_state):
    (
        normed_one,
        inverse_one,
        hidden_one,
        queries,
        key_rows,
        values,
        log_total,
        attended,
        branch_one,
        normed_two,
        inverse_two,
        hidden_two,
        saved_pre,
        activated,
        branch_two,
    ) = kept_state
    width_all = grad_out.shape[-1]
    col_width = attn_now.shape[2]
    unit_width = mlp_now.shape[2]
    shards = lax.axis_size("tensor")
    mod_parts = [
        modulation[:, None, part_at * width_all : (part_at + 1) * width_all] for part_at in range(6)
    ]
    grad_gate_two = jnp.sum(grad_out * branch_two, 1)
    downward = grad_out * mod_parts[5]
    down_low = downward.astype(LOW_TYPE)
    grad_down = weight_grad(down_low, activated)
    grad_act = product(down_low, mlp_now[1])
    grad_pre = jax.vjp(gelu_tanh, saved_pre)[1](grad_act)[0].astype(LOW_TYPE)
    grad_up = weight_grad(hidden_two, grad_pre)
    grad_hidden_two = tensor_backward(product_t(grad_pre, mlp_now[0]))
    grad_middle = grad_out + normalize_back(
        grad_hidden_two * (1.0 + mod_parts[4]), normed_two, inverse_two
    )
    grad_gate_one = jnp.sum(grad_middle * branch_one, 1)
    upward = grad_middle * mod_parts[2]
    up_low = upward.astype(LOW_TYPE)
    grad_out_map = weight_grad(up_low, attended)
    grad_attended = product(up_low, attn_now[3]).astype(LOW_TYPE)
    grad_queries, grad_keys, grad_values = attend_back(
        queries, key_rows, values, log_total, grad_attended
    )
    grad_query_map = weight_grad(hidden_one, grad_queries)
    grad_key_map = weight_grad(hidden_one, grad_keys)
    grad_value_map = weight_grad(hidden_one, grad_values)
    grad_hidden_one = tensor_backward(
        product_t(grad_queries, attn_now[0])
        + product_t(grad_keys, attn_now[1])
        + product_t(grad_values, attn_now[2])
    )
    grad_stream = grad_middle + normalize_back(
        grad_hidden_one * (1.0 + mod_parts[1]), normed_one, inverse_one
    )
    grad_modulation = jnp.concatenate(
        [
            jnp.sum(grad_hidden_one, 1),
            jnp.sum(grad_hidden_one * normed_one, 1),
            grad_gate_one,
            jnp.sum(grad_hidden_two, 1),
            jnp.sum(grad_hidden_two * normed_two, 1),
            grad_gate_two,
        ],
        axis=1,
    )
    bias_grad = jnp.zeros((LB * width_all,), jnp.float32)
    bias_grad = place(
        bias_grad, jnp.sum(grad_queries.astype(jnp.float32), (0, 1)), shard_at * col_width
    )
    bias_grad = place(
        bias_grad,
        jnp.sum(grad_values.astype(jnp.float32), (0, 1)),
        width_all + shard_at * col_width,
    )
    bias_grad = place(bias_grad, jnp.sum(upward, (0, 1)) / shards, 2 * width_all)
    bias_grad = place(
        bias_grad,
        jnp.sum(grad_pre.astype(jnp.float32), (0, 1)),
        3 * width_all + shard_at * unit_width,
    )
    bias_grad = place(bias_grad, jnp.sum(downward, (0, 1)) / shards, 3 * width_all + FF)
    return (
        grad_stream,
        jnp.stack([grad_query_map, grad_key_map, grad_value_map, grad_out_map]),
        jnp.stack([grad_up, grad_down]),
        grad_modulation,
        bias_grad,
    )


def split_bits(array_in, axis_at, count_bits):
    dims_in = array_in.shape
    return array_in.reshape(
        dims_in[:axis_at]
        + (2,) * count_bits
        + (dims_in[axis_at] >> count_bits,)
        + dims_in[axis_at + 1 :]
    )


def reduce_pieces(arrays, axes_at, shift_bits, count_bits, bit_order, across):
    dp_at = lax.axis_index("dp")
    blocks = [
        split_bits(array_in, axis_at, count_bits) for array_in, axis_at in zip(arrays, axes_at)
    ]
    for bit_at in bit_order:
        own_bit = dp_at >> shift_bits + bit_at & 1
        kept_half = [
            lax.dynamic_slice_in_dim(block_in, own_bit, 1, axis_at + count_bits - 1 - bit_at)
            for block_in, axis_at in zip(blocks, axes_at)
        ]
        sent_half = [
            lax.dynamic_slice_in_dim(block_in, 1 - own_bit, 1, axis_at + count_bits - 1 - bit_at)
            for block_in, axis_at in zip(blocks, axes_at)
        ]
        if across:
            received = swapped(
                (
                    shortened(sent_half[0]),
                    shortened(sent_half[1]),
                    shortened(sent_half[2]),
                    shortened(sent_half[3]),
                ),
                "dp",
                shift_bits + bit_at,
            )
        else:
            received = swapped(
                (
                    shortened(sent_half[0]),
                    shortened(sent_half[1]),
                    shortened(sent_half[2]),
                    shortened(sent_half[3]),
                ),
                "dp",
                shift_bits + bit_at,
            )
        blocks = [own_part + other_part for own_part, other_part in zip(kept_half, received)]
    return [
        block_in.reshape(
            array_in.shape[:axis_at]
            + (array_in.shape[axis_at] >> count_bits,)
            + array_in.shape[axis_at + 1 :]
        )
        for block_in, array_in, axis_at in zip(blocks, arrays, axes_at)
    ]


def adam_update(gradient, first_old, second_old):
    first_new = BETA_FIRST * first_old + (1.0 - BETA_FIRST) * gradient
    second_new = BETA_SECOND * second_old + (1.0 - BETA_SECOND) * gradient * gradient
    update = (
        first_new
        / (1.0 - BETA_FIRST**STEP_COUNT)
        / (jnp.sqrt(second_new / (1.0 - BETA_SECOND**STEP_COUNT)) + ADAM_EPSILON)
    )
    return (update, first_new, second_new)


def per_device(
    patches,
    noise_draw,
    timesteps,
    labels,
    w_attn,
    w_mlp,
    w_mod,
    w_embed,
    biases,
    momentum_attn,
    momentum_mlp,
    momentum_mod,
    momentum_embed,
    momentum_bias,
    first_attn,
    second_attn,
    first_mlp,
    second_mlp,
    first_mod,
    second_mod,
    first_embed,
    second_embed,
    first_bias,
    second_bias,
):
    shards = lax.axis_size("tensor")
    shard_at = lax.axis_index("tensor")
    dp_count = lax.axis_size("dp")
    group_at = lax.axis_index("dp") % GROUPS
    layer_span = LB * D
    attn_all, mlp_all, mod_all, embed_all = (
        lax.all_gather(w_attn.astype(LOW_TYPE), "dp", axis=2, tiled=True),
        lax.all_gather(w_mlp.astype(LOW_TYPE), "dp", axis=2, tiled=True),
        lax.all_gather(w_mod.astype(LOW_TYPE), "dp", axis=1, tiled=True),
        lax.all_gather(w_embed.astype(LOW_TYPE), "dp", axis=1, tiled=True),
    )
    class_table, first_time, second_time, patch_map, final_map, head_map = embed_parts(embed_all)
    bias_flat = biases.reshape(-1)
    bias_tail = bias_flat[L * layer_span :]
    batch_here = patches.shape[0]
    signal = signal_levels(timesteps)[:, None, None]
    noised = (jnp.sqrt(signal) * patches + jnp.sqrt(1.0 - signal) * noise_draw).astype(LOW_TYPE)
    stream = product(noised, patch_map) + bias_tail[:D] + positions()
    freq_low = frequencies(timesteps).astype(LOW_TYPE)
    hidden_time = product(freq_low, first_time) + bias_tail[D : 2 * D]
    smooth_time = jax.nn.silu(hidden_time).astype(LOW_TYPE)
    class_picks = (labels[:, None] == jnp.arange(NCLS, dtype=jnp.int32)[None, :]).astype(LOW_TYPE)
    condition = (
        product(smooth_time, second_time)
        + bias_tail[2 * D : 3 * D]
        + product(class_picks, class_table)
    )
    cond_act = jax.nn.silu(condition).astype(LOW_TYPE)
    mod_width = mod_all.shape[2]
    ada_bias = jnp.stack(
        [
            lax.dynamic_slice_in_dim(
                bias_flat, layer_at * layer_span + 4 * D + FF + shard_at * mod_width, mod_width
            )
            for layer_at in range(L)
        ]
    )
    mod_cols = (
        jnp.einsum("nd,ldm->lnm", cond_act, mod_all, preferred_element_type=jnp.float32)
        + ada_bias[:, None, :]
    )
    modulations = lax.all_gather(
        mod_cols.astype(jnp.bfloat16), "tensor", axis=2, tiled=True
    ).astype(mod_cols.dtype)
    saved_states = []
    for layer_at in range(L):
        stream, kept_state = layer_forward(
            stream,
            modulations[layer_at],
            attn_all[layer_at],
            mlp_all[layer_at],
            bias_flat[layer_at * layer_span : (layer_at + 1) * layer_span],
            shard_at,
        )
        saved_states.append(kept_state)
    final_mod = product_t(cond_act, final_map) + bias_tail[3 * D : 5 * D]
    normed_last, inverse_last = normalize(stream)
    hidden_last = (normed_last * (1.0 + final_mod[:, None, D:]) + final_mod[:, None, :D]).astype(
        LOW_TYPE
    )
    predicted = product_t(hidden_last, head_map)
    errors = predicted - noise_draw
    elements = dp_count // GROUPS * batch_here * S * PATCH_IN
    loss_here = jnp.sum(errors * errors) / elements
    grad_pred = (2.0 * errors / elements).astype(LOW_TYPE)
    grad_head = weight_grad(grad_pred, hidden_last)
    grad_hidden = product(grad_pred, head_map)
    grad_final = jnp.concatenate(
        [jnp.sum(grad_hidden, 1), jnp.sum(grad_hidden * normed_last, 1)], axis=1
    ).astype(LOW_TYPE)
    grad_stream = normalize_back(
        grad_hidden * (1.0 + final_mod[:, None, D:]), normed_last, inverse_last
    )
    grad_final_map = weight_grad(grad_final, cond_act)
    grad_cond_local = product(grad_final, final_map)
    attn_list, mlp_list, mod_list, bias_list = ([None] * L, [None] * L, [None] * L, [None] * L)
    for layer_at in range(L - 1, -1, -1):
        (
            grad_stream,
            attn_list[layer_at],
            mlp_list[layer_at],
            mod_list[layer_at],
            bias_list[layer_at],
        ) = layer_backward(
            grad_stream,
            modulations[layer_at],
            attn_all[layer_at],
            mlp_all[layer_at],
            shard_at,
            saved_states[layer_at],
        )
    grad_mods = jnp.stack(mod_list).astype(LOW_TYPE)
    own_mods = lax.dynamic_slice_in_dim(grad_mods, shard_at * mod_width, mod_width, 2)
    grad_mod_map = jnp.einsum("nd,lnm->ldm", cond_act, own_mods, preferred_element_type=jnp.float32)
    grad_ada = jnp.sum(own_mods.astype(jnp.float32), 1)
    grad_cond_parts = jnp.einsum(
        "lnm,ldm->nd", own_mods, mod_all, preferred_element_type=jnp.float32
    )
    grad_cond_act = (
        lax.psum(grad_cond_parts.astype(jnp.bfloat16), "tensor").astype(jnp.float32)
        + grad_cond_local
    )
    grad_condition = jax.vjp(jax.nn.silu, condition)[1](grad_cond_act)[0].astype(LOW_TYPE)
    grad_table = weight_grad(class_picks, grad_condition)
    grad_second = weight_grad(smooth_time, grad_condition)
    grad_smooth = product_t(grad_condition, second_time)
    grad_hidden_time = jax.vjp(jax.nn.silu, hidden_time)[1](grad_smooth)[0].astype(LOW_TYPE)
    grad_first = weight_grad(freq_low, grad_hidden_time)
    grad_patch = weight_grad(noised, grad_stream.astype(LOW_TYPE))
    grad_embed = jnp.concatenate(
        [grad_table, grad_first, grad_second, grad_patch, grad_final_map, grad_head], 0
    )
    layer_biases = [
        place(bias_list[layer_at], grad_ada[layer_at], 4 * D + FF + shard_at * mod_width)
        for layer_at in range(L)
    ]
    tail_grad = (
        jnp.concatenate(
            [
                jnp.sum(grad_stream, (0, 1)),
                jnp.sum(grad_hidden_time.astype(jnp.float32), 0),
                jnp.sum(grad_condition.astype(jnp.float32), 0),
                jnp.sum(grad_final.astype(jnp.float32), 0),
            ]
        )
        / shards
    )
    bias_grad_all = jnp.concatenate(layer_biases + [tail_grad])
    shift_group = GROUPS.bit_length() - 1
    group_bits = dp_count.bit_length() - 1 - shift_group
    bit_order = list(reversed(range(group_bits)))
    reduced = reduce_pieces(
        [jnp.stack(attn_list), jnp.stack(mlp_list), grad_mod_map, grad_embed],
        (2, 2, 1, 1),
        shift_group,
        group_bits,
        bit_order,
        False,
    )
    squares = (
        jnp.sum(reduced[0] * reduced[0])
        + jnp.sum(reduced[1] * reduced[1])
        + jnp.sum(reduced[2] * reduced[2])
        + jnp.sum(reduced[3] * reduced[3]) / shards
    )
    picked = (jnp.arange(GROUPS, dtype=jnp.int32) == group_at).astype(jnp.float32)
    bias_groups, square_groups, loss_total = lax.psum(
        (
            picked[:, None] * bias_grad_all[None, :],
            picked * squares,
            jnp.reshape(loss_here / shards, (1,)),
        ),
        ("dp", "tensor"),
    )
    group_norms = jnp.sqrt(square_groups + jnp.sum(bias_groups * bias_groups, 1))
    clip_scale = CLIP_NORM / (group_norms + 1e-06)
    own_scale = jnp.sum(picked * clip_scale)
    weights_in = (w_attn, w_mlp, w_mod, w_embed)
    momenta_in = (momentum_attn, momentum_mlp, momentum_mod, momentum_embed)
    firsts_in = (first_attn, first_mlp, first_mod, first_embed)
    seconds_in = (second_attn, second_mlp, second_mod, second_embed)
    updates, new_firsts, new_seconds = ([], [], [])
    for index_at in range(4):
        update, first_new, second_new = adam_update(
            reduced[index_at] * own_scale, firsts_in[index_at], seconds_in[index_at]
        )
        updates.append(update)
        new_firsts.append(first_new)
        new_seconds.append(second_new)
    summed = reduce_pieces(updates, (2, 2, 1, 1), 0, shift_group, list(range(shift_group)), True)
    new_weights, new_momenta = ([], [])
    for index_at in range(4):
        outer_grad = LEARN_RATE * (summed[index_at] / GROUPS + WEIGHT_DECAY * weights_in[index_at])
        momentum_new = OUTER_MOMENTUM * momenta_in[index_at] + outer_grad
        new_weights.append(
            weights_in[index_at] - OUTER_RATE * (outer_grad + OUTER_MOMENTUM * momentum_new)
        )
        new_momenta.append(momentum_new)
    clipped_bias = bias_groups * clip_scale[:, None]
    bias_updates, bias_first, bias_second = adam_update(
        clipped_bias, first_bias.reshape(GROUPS, -1), second_bias.reshape(GROUPS, -1)
    )
    outer_bias = LEARN_RATE * (jnp.mean(bias_updates, 0) + WEIGHT_DECAY * bias_flat)
    bias_momentum = OUTER_MOMENTUM * momentum_bias.reshape(-1) + outer_bias
    bias_new = bias_flat - OUTER_RATE * (outer_bias + OUTER_MOMENTUM * bias_momentum)
    return (
        loss_total[0] / GROUPS,
        group_norms,
        clipped_bias.reshape(first_bias.shape),
        new_weights[0],
        new_weights[1],
        new_weights[2],
        new_weights[3],
        bias_new.reshape(biases.shape),
        new_momenta[0],
        new_momenta[1],
        new_momenta[2],
        new_momenta[3],
        bias_momentum.reshape(biases.shape),
        new_firsts[0],
        new_seconds[0],
        new_firsts[1],
        new_seconds[1],
        new_firsts[2],
        new_seconds[2],
        new_firsts[3],
        new_seconds[3],
        bias_first.reshape(first_bias.shape),
        bias_second.reshape(second_bias.shape),
    )


def solution(mesh):
    placed = (
        P("dp", None, None),
        P("dp", None, None),
        P("dp"),
        P("dp"),
        P(None, None, "dp", "tensor"),
        P(None, None, "dp", "tensor"),
        P(None, "dp", "tensor"),
        P(None, "dp"),
        P(),
        P(None, None, "dp", "tensor"),
        P(None, None, "dp", "tensor"),
        P(None, "dp", "tensor"),
        P(None, "dp"),
        P(),
        P(None, None, "dp", "tensor"),
        P(None, None, "dp", "tensor"),
        P(None, None, "dp", "tensor"),
        P(None, None, "dp", "tensor"),
        P(None, "dp", "tensor"),
        P(None, "dp", "tensor"),
        P(None, "dp"),
        P(None, "dp"),
        P(),
        P(),
    )
    return jax.shard_map(
        per_device,
        mesh=mesh,
        in_specs=placed,
        out_specs=(
            P(),
            P(),
            P(),
            P(None, None, "dp", "tensor"),
            P(None, None, "dp", "tensor"),
            P(None, "dp", "tensor"),
            P(None, "dp"),
            P(),
            P(None, None, "dp", "tensor"),
            P(None, None, "dp", "tensor"),
            P(None, "dp", "tensor"),
            P(None, "dp"),
            P(),
            P(None, None, "dp", "tensor"),
            P(None, None, "dp", "tensor"),
            P(None, None, "dp", "tensor"),
            P(None, None, "dp", "tensor"),
            P(None, "dp", "tensor"),
            P(None, "dp", "tensor"),
            P(None, "dp"),
            P(None, "dp"),
            P(),
            P(),
        ),
        check_vma=False,
    )
```

profile of v0, /device:TPU:0, one launch (start us, length us, event | category | flops | bytes accessed | tf_op | source)
XLA Modules:
  0.0 1758.7 jit_solution(14712788562048514865)
XLA Ops:
  21.3 24.2 %all-gather.9.cloned.1.call-done = bf16[2,4,768,192]{3,1,0,2:T(4,128)(2,1)} async-done(((bf16[2,4,96,192]{3,1,0,2:T(4,128)(2,1)}), bf16[2,4,768,192]{3,1,0,2:T(4,128)(2,1)}) %all-gather.9.cloned.1.call-update) | async-done | bytes 2359312 | tf_op jit(solution)/shard_map/all_gather | solution.py:428
  45.4 10.1 fusion.195
  65.1 25.7 %all-gather.5.cloned.1.call-done = bf16[3592,768]{0,1:T(8,128)(2,1)} async-done(((bf16[3592,96]{0,1:T(8,128)(2,1)}), bf16[3592,768]{0,1:T(8,128)(2,1)}) %all-gather.5.cloned.1.call-update) | async-done | bytes 5517328 | tf_op jit(solution)/shard_map/all_gather | solution.py:431
  97.3 29.9 %all-gather.7.cloned.1.call-done = bf16[2,768,1152]{2,1,0:T(8,128)(2,1)} async-done(((bf16[2,96,1152]{2,1,0:T(8,128)(2,1)}), bf16[2,768,1152]{2,1,0:T(8,128)(2,1)}) %all-gather.7.cloned.1.call-update) | async-done | bytes 3538960 | tf_op jit(solution)/shard_map/all_gather | solution.py:430
  129.8 13.7 all_gather.17
  163.2 119.3 %all-reduce.12.cloned.1.call-done = bf16[8,256,768]{2,1,0:T(8,128)(2,1)} async-done(((bf16[8,256,768]{2,1,0:T(8,128)(2,1)}), bf16[8,256,768]{2,1,0:T(8,128)(2,1)}) %all-reduce.12.cloned.1.call-update) | async-done | bytes 3145744 | tf_op jit(solution)/shard_map/psum | solution.py:170
  282.5 5.3 fusion.194
  291.3 31.4 %all-gather.11.cloned.1.call-done = bf16[2,2,768,768]{3,2,1,0:T(8,128)(2,1)} async-done(((bf16[2,2,96,768]{3,2,1,0:T(8,128)(2,1)}), bf16[2,2,768,768]{3,2,1,0:T(8,128)(2,1)}) %all-gather.11.cloned.1.call-update) | async-done | bytes 4718608 | tf_op jit(solution)/shard_map/all_gather | solution.py:429
  322.7 5.5 fusion.101
  330.8 6.7 convolution_convert_fusion.5
  343.3 115.5 %all-reduce.14.cloned.1.call-done = bf16[8,256,768]{2,1,0:T(8,128)(2,1)} async-done(((bf16[8,256,768]{2,1,0:T(8,128)(2,1)}), bf16[8,256,768]{2,1,0:T(8,128)(2,1)}) %all-reduce.14.cloned.1.call-update) | async-done | bytes 3145744 | tf_op jit(solution)/shard_map/psum | solution.py:170
  458.8 4.8 fusion.193
  479.2 118.9 %all-reduce.16.cloned.1.call-done = bf16[8,256,768]{2,1,0:T(8,128)(2,1)} async-done(((bf16[8,256,768]{2,1,0:T(8,128)(2,1)}), bf16[8,256,768]{2,1,0:T(8,128)(2,1)}) %all-reduce.16.cloned.1.call-update) | async-done | bytes 3145744 | tf_op jit(solution)/shard_map/psum | solution.py:170
  598.1 5.0 fusion.192
  609.9 5.4 convolution_convert_fusion.4
  619.0 116.6 %all-reduce.18.cloned.1.call-done = bf16[8,256,768]{2,1,0:T(8,128)(2,1)} async-done(((bf16[8,256,768]{2,1,0:T(8,128)(2,1)}), bf16[8,256,768]{2,1,0:T(8,128)(2,1)}) %all-reduce.18.cloned.1.call-update) | async-done | bytes 3145744 | tf_op jit(solution)/shard_map/psum | solution.py:170
  735.5 4.8 fusion.191
  744.9 5.0 multiply_reduce_fusion
  754.2 10.4 convert_reduce_fusion
  770.6 6.5 copy.221
  777.2 6.5 copy.222
  785.9 5.0 fusion.50
  790.9 5.8 reshape.540
  796.7 6.7 copy.192
  803.4 87.1 %all-reduce.20.cloned.1.call-done = bf16[8,256,768]{2,1,0:T(8,128)(2,1)} async-done(((bf16[8,256,768]{2,1,0:T(8,128)(2,1)}), bf16[8,256,768]{2,1,0:T(8,128)(2,1)}) %all-reduce.20.cloned.1.call-update) | async-done | bytes 3145744 | tf_op jit(solution)/shard_map/psum | solution.py:174
  890.6 6.2 fusion.16
  896.8 8.6 multiply_reduce_fusion.15
  930.2 7.1 reshape.544
  937.3 8.6 copy.198
  947.2 8.3 fusion.138
  955.5 9.2 fusion.84
  974.5 71.0 %all-reduce.22.cloned.1.call-done = bf16[8,256,768]{2,1,0:T(8,128)(2,1)} async-done(((bf16[8,256,768]{2,1,0:T(8,128)(2,1)}), bf16[8,256,768]{2,1,0:T(8,128)(2,1)}) %all-reduce.22.cloned.1.call-update) | async-done | bytes 3145744 | tf_op jit(solution)/shard_map/psum | solution.py:174
  1045.5 5.8 fusion.21
  1051.4 7.0 multiply_reduce_fusion.14
  1058.5 6.2 convert_reduce_fusion.1
  1093.7 96.9 %all-reduce.24.cloned.1.call-done = bf16[8,256,768]{2,1,0:T(8,128)(2,1)} async-done(((bf16[8,256,768]{2,1,0:T(8,128)(2,1)}), bf16[8,256,768]{2,1,0:T(8,128)(2,1)}) %all-reduce.24.cloned.1.call-update) | async-done | bytes 3145744 | tf_op jit(solution)/shard_map/psum | solution.py:174
  1190.6 5.6 fusion.26
  1196.4 8.1 multiply_convert_fusion.4
  1233.5 4.9 multiply_reduce_fusion.21
  1241.4 17.7 %collective-permute-done = bf16[2,4,1,384,192]{3,4,2,1,0:T(8,128)(2,1)} collective-permute-done((bf16[2,4,1,384,192]{3,4,2,1,0:T(8,128)(2,1)}, bf16[2,4,1,384,192]{3,4,2,1,0:T(8,128)(2,1)}, u32[]{:S(2)}, u32[]{:S(2)}) %collective-permute-start) | collective-permute-done | bytes 1179680 | tf_op jit(solution)/shard_map/ppermute | solution.py:39
  1263.6 75.3 %all-reduce.26.cloned.1.call-done = bf16[8,256,768]{2,1,0:T(8,128)(2,1)} async-done(((bf16[8,256,768]{2,1,0:T(8,128)(2,1)}), bf16[8,256,768]{2,1,0:T(8,128)(2,1)}) %all-reduce.26.cloned.1.call-update) | async-done | bytes 3145744 | tf_op jit(solution)/shard_map/psum | solution.py:174
  1341.4 5.2 fusion.2
  1347.2 7.2 fusion.176
  1362.4 17.2 psum.93
  1390.7 6.2 fusion.90
  1401.9 14.1 reshape.547
  1415.9 7.5 constant_dynamic-slice_fusion.6
  1426.3 8.8 constant_dynamic-slice_fusion.7
  1435.1 12.9 copy.257
  1448.0 103.9 %all-reduce.28.cloned.1.call-done = f32[4,25344]{1,0:T(4,128)} async-done(((f32[4,25344]{1,0:T(4,128)}), f32[4,25344]{1,0:T(4,128)}) %all-reduce.28.cloned.1.call-update) | async-done | bytes 405520 | tf_op jit(solution)/shard_map/psum | solution.py:568
  1561.4 5.7 multiply_reduce_fusion.17
  1567.8 42.1 %all-reduce.1 = (f32[1]{0:T(128)}, f32[4]{0:T(128)S(1)}) all-reduce(f32[1]{0:T(128)} %bitcast.42, f32[4]{0:T(128)S(1)} %fusion.164), channel_id=1, replica_groups=mesh['dp'=8,'tensor'=4] {'dp','tensor'}, use_global_device_ids=true, to_apply=%region_22.23 | all-reduce | flops 5 | bytes 40 | tf_op jit(solution)/shard_map/psum | solution.py:568
  1611.0 8.0 add_divide_fusion.3
  1619.0 4.9 reshape.549
  1626.7 5.8 copy.259
  1635.0 5.8 copy.260
  1640.8 10.6 add_divide_fusion.1
  1655.5 7.6 add_divide_fusion.2
  1665.4 10.4 add_divide_fusion
  1682.1 6.3 copy.223
  1688.4 6.5 copy.224
  1703.4 8.3 collective-permute-done.5
  1722.7 11.1 collective-permute-done.7
  1735.7 13.0 collective-permute-done.11
  (719 shorter events, 284.9 us)
Async XLA Ops:
  7.2 38.2 %all-gather.9.cloned.1.call-start = ((), (), s32[]{:S(2)}) async-start(), calls=%async_computation.2 | async-start | bytes 3538944 | tf_op jit(solution)/shard_map/all_gather | solution.py:428
  9.8 81.0 %all-gather.5.cloned.1.call-start = ((), (), s32[]{:S(2)}) async-start(), calls=%async_computation | async-start | bytes 6414336 | tf_op jit(solution)/shard_map/all_gather | solution.py:431
  12.2 115.1 %all-gather.7.cloned.1.call-start = ((), (), s32[]{:S(2)}) async-start(), calls=%async_computation.1 | async-start | bytes 3981312 | tf_op jit(solution)/shard_map/all_gather | solution.py:430
  14.2 268.3 %all-reduce.12.cloned.1.call-start = ((), (), s32[]{:S(2)}) async-start(), calls=%async_computation.3 | async-start | bytes 6291456 | tf_op jit(solution)/shard_map/psum | solution.py:170
  18.1 767.7 %copy-start.104 = (f32[768]{0:T(1024)}, f32[768]{0:T(1024)S(1)}, u32[]{:S(2)}) copy-start(f32[768]{0:T(1024)S(1)} %get-tuple-element.123) | copy-start | bytes 9220
  20.3 765.6 %copy-start.8 = (f32[256,768]{1,0:T(8,128)}, f32[256,768]{1,0:T(8,128)S(1)}, u32[]{:S(2)}) copy-start(f32[256,768]{1,0:T(8,128)S(1)} %pad_maximum_fusion) | copy-start | bytes 2359300
  20.4 70.4 %copy-start.163 = (bf16[8,128]{1,0:T(8,128)(2,1)}, bf16[8,128]{1,0:T(8,128)(2,1)S(1)}, u32[]{:S(2)}) copy-start(bf16[8,128]{1,0:T(8,128)(2,1)S(1)} %get-tuple-element.212) | copy-start | bytes 6148
  20.4 70.4 %copy-start.165 = (bf16[8,128]{1,0:T(8,128)(2,1)}, bf16[8,128]{1,0:T(8,128)(2,1)S(1)}, u32[]{:S(2)}) copy-start(bf16[8,128]{1,0:T(8,128)(2,1)S(1)} %get-tuple-element.213) | copy-start | bytes 6148
  21.3 123.6 %copy-start.102 = (bf16[8,256,16]{1,2,0:T(8,128)(2,1)}, bf16[8,256,16]{1,2,0:T(8,128)(2,1)S(1)}, u32[]{:S(2)}) copy-start(bf16[8,256,16]{1,2,0:T(8,128)(2,1)S(1)} %add_convert_fusion.11) | copy-start | bytes 196612
  21.3 71.6 %copy-start.169 = (f32[768]{0:T(1024)S(1)}, f32[768]{0:T(1024)}, u32[]{:S(2)}) copy-start(f32[768]{0:T(1024)} %get-tuple-element.121) | copy-start | bytes 9220
  60.5 91.1 %copy-start.66 = (bf16[1,1,768,192]{2,3,1,0:T(8,128)(2,1)}, bf16[1,1,768,192]{2,3,1,0:T(8,128)(2,1)S(1)}, u32[]{:S(2)}) copy-start(bf16[1,1,768,192]{2,3,1,0:T(8,128)(2,1)S(1)} %copy.247) | copy-start | bytes 884740
  97.3 46.9 %copy-start.126 = (bf16[8,768]{1,0:T(8,128)(2,1)}, bf16[8,768]{1,0:T(8,128)(2,1)S(1)}, u32[]{:S(2)}) copy-start(bf16[8,768]{1,0:T(8,128)(2,1)S(1)} %get-tuple-element.216) | copy-start | bytes 36868
  147.0 638.9 %copy-start.100 = (f32[8,256]{1,0:T(8,128)}, f32[8,256]{1,0:T(8,128)S(1)}, u32[]{:S(2)}) copy-start(f32[8,256]{1,0:T(8,128)S(1)} %broadcast_multiply_fusion.19) | copy-start | bytes 24580
  161.2 161.4 %all-gather.11.cloned.1.call-start = ((), (), s32[]{:S(2)}) async-start(), calls=%async_computation.4 | async-start | bytes 5308416 | tf_op jit(solution)/shard_map/all_gather | solution.py:429
  162.2 296.6 %all-reduce.14.cloned.1.call-start = ((), (), s32[]{:S(2)}) async-start(), calls=%async_computation.5 | async-start | bytes 6291456 | tf_op jit(solution)/shard_map/psum | solution.py:170
  163.2 165.0 %copy-start.170 = (f32[768]{0:T(1024)}, f32[768]{0:T(1024)S(1)}, u32[]{:S(2)}) copy-start(f32[768]{0:T(1024)S(1)} %dynamic_slice.103) | copy-start | bytes 9220
  287.8 34.9 %copy-start.116 = (f32[8,768]{1,0:T(8,128)S(1)}, f32[8,768]{1,0:T(8,128)}, u32[]{:S(2)}) copy-start(f32[8,768]{1,0:T(8,128)} %get-tuple-element.185) | copy-start | bytes 73732
  287.8 34.8 %copy-start.161 = (f32[8,768]{1,0:T(8,128)S(1)}, f32[8,768]{1,0:T(8,128)}, u32[]{:S(2)}) copy-start(f32[8,768]{1,0:T(8,128)} %get-tuple-element.184) | copy-start | bytes 73732
  287.9 34.8 %copy-start.132 = (f32[8,256]{1,0:T(8,128)}, f32[8,256]{1,0:T(8,128)S(1)}, u32[]{:S(2)}) copy-start(f32[8,256]{1,0:T(8,128)S(1)} %broadcast_multiply_fusion.18) | copy-start | bytes 24580
  291.3 31.4 %copy-start.141 = (f32[8,256]{1,0:T(8,128)}, f32[8,256]{1,0:T(8,128)S(1)}, u32[]{:S(2)}) copy-start(f32[8,256]{1,0:T(8,128)S(1)} %add_rsqrt_fusion.3) | copy-start | bytes 24580
  337.6 121.2 %copy-start.112 = (f32[8,768]{1,0:T(8,128)S(1)}, f32[8,768]{1,0:T(8,128)}, u32[]{:S(2)}) copy-start(f32[8,768]{1,0:T(8,128)} %get-tuple-element.186) | copy-start | bytes 73732
  337.6 121.2 %copy-start.154 = (f32[768]{0:T(1024)S(1)}, f32[768]{0:T(1024)}, u32[]{:S(2)}) copy-start(f32[768]{0:T(1024)} %get-tuple-element.119) | copy-start | bytes 9220
  337.6 260.5 %all-reduce.16.cloned.1.call-start = ((), (), s32[]{:S(2)}) async-start(), calls=%async_computation.6 | async-start | bytes 6291456 | tf_op jit(solution)/shard_map/psum | solution.py:170
  341.3 126.2 %copy-start.72 = (bf16[1,1,768,192]{2,3,1,0:T(8,128)(2,1)}, bf16[1,1,768,192]{2,3,1,0:T(8,128)(2,1)S(1)}, u32[]{:S(2)}) copy-start(bf16[1,1,768,192]{2,3,1,0:T(8,128)(2,1)S(1)} %copy.251) | copy-start | bytes 884740
  341.8 124.1 %copy-start.74 = (bf16[1,1,768,192]{2,3,1,0:T(8,128)(2,1)}, bf16[1,1,768,192]{2,3,1,0:T(8,128)(2,1)S(1)}, u32[]{:S(2)}) copy-start(bf16[1,1,768,192]{2,3,1,0:T(8,128)(2,1)S(1)} %copy.252) | copy-start | bytes 884740
  343.3 121.3 %copy-start.108 = (f32[8,768]{1,0:T(8,128)}, f32[8,768]{1,0:T(8,128)S(1)}, u32[]{:S(2)}) copy-start(f32[8,768]{1,0:T(8,128)S(1)} %get-tuple-element.193) | copy-start | bytes 73732
  343.3 260.7 %copy-start.114 = (f32[8,768]{1,0:T(8,128)}, f32[8,768]{1,0:T(8,128)S(1)}, u32[]{:S(2)}) copy-start(f32[8,768]{1,0:T(8,128)S(1)} %get-tuple-element.192) | copy-start | bytes 73732
  343.3 260.7 %copy-start.159 = (f32[8,768]{1,0:T(8,128)}, f32[8,768]{1,0:T(8,128)S(1)}, u32[]{:S(2)}) copy-start(f32[8,768]{1,0:T(8,128)S(1)} %get-tuple-element.191) | copy-start | bytes 73732
  343.3 410.9 %copy-start.106 = (f32[8,768]{1,0:T(8,128)}, f32[8,768]{1,0:T(8,128)S(1)}, u32[]{:S(2)}) copy-start(f32[8,768]{1,0:T(8,128)S(1)} %get-tuple-element.190) | copy-start | bytes 73732
  473.0 125.1 %copy-start.156 = (f32[768]{0:T(1024)S(1)}, f32[768]{0:T(1024)}, u32[]{:S(2)}) copy-start(f32[768]{0:T(1024)} %get-tuple-element.118) | copy-start | bytes 9220
  477.9 257.6 %all-reduce.18.cloned.1.call-start = ((), (), s32[]{:S(2)}) async-start(), calls=%async_computation.7 | async-start | bytes 6291456 | tf_op jit(solution)/shard_map/psum | solution.py:170
  479.2 275.0 %copy-start.172 = (f32[768]{0:T(1024)}, f32[768]{0:T(1024)S(1)}, u32[]{:S(2)}) copy-start(f32[768]{0:T(1024)S(1)} %dynamic_slice.106) | copy-start | bytes 9220
  615.3 275.2 %all-reduce.20.cloned.1.call-start = ((), (), s32[]{:S(2)}) async-start(), calls=%async_computation.8 | async-start | bytes 6291456 | tf_op jit(solution)/shard_map/psum | solution.py:174
  618.9 122.3 %copy-start.110 = (f32[8,768]{1,0:T(8,128)}, f32[8,768]{1,0:T(8,128)S(1)}, u32[]{:S(2)}) copy-start(f32[8,768]{1,0:T(8,128)S(1)} %get-tuple-element.201) | copy-start | bytes 73732
  618.9 131.0 %copy-start.95 = (f32[8,768]{1,0:T(8,128)}, f32[8,768]{1,0:T(8,128)S(1)}, u32[]{:S(2)}) copy-start(f32[8,768]{1,0:T(8,128)S(1)} %get-tuple-element.200) | copy-start | bytes 73732
  770.3 275.2 %all-reduce.22.cloned.1.call-start = ((), (), s32[]{:S(2)}) async-start(), calls=%async_computation.9 | async-start | bytes 6291456 | tf_op jit(solution)/shard_map/psum | solution.py:174
  790.9 99.6 %copy-start.115 = (f32[8,768]{1,0:T(8,128)S(1)}, f32[8,768]{1,0:T(8,128)}, u32[]{:S(2)}) copy-start(f32[8,768]{1,0:T(8,128)} %copy-done.114) | copy-start | bytes 73732
  925.3 265.4 %all-reduce.24.cloned.1.call-start = ((), (), s32[]{:S(2)}) async-start(), calls=%async_computation.10 | async-start | bytes 6291456 | tf_op jit(solution)/shard_map/psum | solution.py:174
  970.2 81.1 %copy-start.27 = (bf16[8,256,768]{2,1,0:T(8,128)(2,1)S(1)}, bf16[8,256,768]{2,1,0:T(8,128)(2,1)}, u32[]{:S(2)}) copy-start(bf16[8,256,768]{2,1,0:T(8,128)(2,1)} %all-reduce.14.cloned.1.call-done) | copy-start | bytes 9437188
  970.2 81.1 %copy-start.113 = (f32[8,768]{1,0:T(8,128)S(1)}, f32[8,768]{1,0:T(8,128)}, u32[]{:S(2)}) copy-start(f32[8,768]{1,0:T(8,128)} %get-tuple-element.186) | copy-start | bytes 73732
  970.2 81.1 %copy-start.155 = (f32[768]{0:T(1024)S(1)}, f32[768]{0:T(1024)}, u32[]{:S(2)}) copy-start(f32[768]{0:T(1024)} %get-tuple-element.119) | copy-start | bytes 9220
  1070.4 268.5 %all-reduce.26.cloned.1.call-start = ((), (), s32[]{:S(2)}) async-start(), calls=%async_computation.11 | async-start | bytes 6291456 | tf_op jit(solution)/shard_map/psum | solution.py:174
  1090.4 105.9 %copy-start.99 = (f32[8,768]{1,0:T(8,128)S(1)}, f32[8,768]{1,0:T(8,128)}, u32[]{:S(2)}) copy-start(f32[8,768]{1,0:T(8,128)} %get-tuple-element.189) | copy-start | bytes 73732
  1092.1 141.4 %collective-permute-start.1 = (bf16[2,2,1,384,768]{4,3,1,0,2:T(8,128)(2,1)}, bf16[2,2,1,384,768]{4,3,1,0,2:T(8,128)(2,1)}, u32[]{:S(2)}, u32[]{:S(2)}) collective-permute-start(bf16[2,2,1,384,768]{4,3,1,0,2:T(8,128)(2,1)} %dynamic-slice_convert_fusion), channel_id=1, source_target_pairs={{0,16},{4,20},{8,24},{12,28},{16,0},{20,4},{24,8},{28,12},{1,17},{... | collective-permute-start | bytes 7077896 | tf_op jit(solution)/shard_map/ppermute | solution.py:39
  1218.7 333.3 %all-reduce.28.cloned.1.call-start = ((), (), s32[]{:S(2)}) async-start(), calls=%async_computation.12 | async-start | bytes 811008 | tf_op jit(solution)/shard_map/psum | solution.py:568
  1231.7 27.4 %collective-permute-start = (bf16[2,4,1,384,192]{3,4,2,1,0:T(8,128)(2,1)}, bf16[2,4,1,384,192]{3,4,2,1,0:T(8,128)(2,1)}, u32[]{:S(2)}, u32[]{:S(2)}) collective-permute-start(bf16[2,4,1,384,192]{3,4,2,1,0:T(8,128)(2,1)} %dynamic-slice_convert_fusion.2), channel_id=1, source_target_pairs={{0,16},{4,20},{8,24},{12,28},{16,0},{20,4},{24,8},{28,12},{1,17},{... | collective-permute-start | bytes 3538952 | tf_op jit(solution)/shard_map/ppermute | solution.py:39
  1238.3 103.0 %copy-start.9 = (f32[256,768]{1,0:T(8,128)S(1)}, f32[256,768]{1,0:T(8,128)}, u32[]{:S(2)}) copy-start(f32[256,768]{1,0:T(8,128)} %copy-done.8) | copy-start | bytes 2359300
  1238.3 103.0 %copy-start.98 = (f32[8,768]{1,0:T(8,128)S(1)}, f32[8,768]{1,0:T(8,128)}, u32[]{:S(2)}) copy-start(f32[8,768]{1,0:T(8,128)} %copy-done.97) | copy-start | bytes 73732
  1238.3 103.0 %copy-start.101 = (f32[8,256]{1,0:T(8,128)S(1)}, f32[8,256]{1,0:T(8,128)}, u32[]{:S(2)}) copy-start(f32[8,256]{1,0:T(8,128)} %copy-done.100) | copy-start | bytes 24580
  1238.4 103.0 %copy-start.105 = (f32[768]{0:T(1024)S(1)}, f32[768]{0:T(1024)}, u32[]{:S(2)}) copy-start(f32[768]{0:T(1024)} %copy-done.104) | copy-start | bytes 9220
  1238.4 103.0 %copy-start.122 = (f32[8,256]{1,0:T(8,128)S(1)}, f32[8,256]{1,0:T(8,128)}, u32[]{:S(2)}) copy-start(f32[8,256]{1,0:T(8,128)} %copy-done.120) | copy-start | bytes 24580
  1263.6 83.0 %slice-start = ((s8[6291456]{0:T(1024)(128)(4,1)}), s8[2097152]{0:T(1024)(128)(4,1)S(1)}, s32[]{:S(2)}) async-start(s8[6291456]{0:T(1024)(128)(4,1)} %bitcast.438), calls=%async_computation.13 | async-start | bytes 4194304
  1263.6 83.0 %copy-start.153 = (f32[768]{0:T(1024)S(1)}, f32[768]{0:T(1024)}, u32[]{:S(2)}) copy-start(f32[768]{0:T(1024)} %get-tuple-element.120) | copy-start | bytes 9220
  1359.9 193.4 %collective-permute-start.2 = (bf16[2,1,384,1152]{3,2,0,1:T(8,128)(2,1)}, bf16[2,1,384,1152]{3,2,0,1:T(8,128)(2,1)}, u32[]{:S(2)}, u32[]{:S(2)}) collective-permute-start(bf16[2,1,384,1152]{3,2,0,1:T(8,128)(2,1)} %bitcast_convert_fusion), channel_id=1, source_target_pairs={{0,16},{4,20},{8,24},{12,28},{16,0},{20,4},{24,8},{28,12},{1,17},{... | collective-permute-start | bytes 5308424 | tf_op jit(solution)/shard_map/ppermute | solution.py:39
  1424.0 134.1 %collective-permute-start.3 = (bf16[3592,1,384]{2,0,1:T(8,128)(2,1)S(1)}, bf16[3592,1,384]{2,0,1:T(8,128)(2,1)}, u32[]{:S(2)}, u32[]{:S(2)}) collective-permute-start(bf16[3592,1,384]{2,0,1:T(8,128)(2,1)S(1)} %copy.285), channel_id=1, source_target_pairs={{0,16},{4,20},{8,24},{12,28},{16,0},{20,4},{24,8},{28,12},{1,17},{... | collective-permute-start | bytes 8275976 | tf_op jit(solution)/shard_map/ppermute | solution.py:39
  1561.4 57.6 %copy-start.18 = (bf16[3592,1,384]{0,2,1:T(8,128)(2,1)}, bf16[3592,1,384]{0,2,1:T(8,128)(2,1)S(1)}, u32[]{:S(2)}) copy-start(bf16[3592,1,384]{0,2,1:T(8,128)(2,1)S(1)} %copy.214) | copy-start | bytes 8275972
  1640.8 56.6 %collective-permute-start.4 = (bf16[2,4,2,1,96,192]{5,4,1,0,3,2:T(8,128)(2,1)}, bf16[2,4,2,1,96,192]{5,4,1,0,3,2:T(8,128)(2,1)}, u32[]{:S(2)}, u32[]{:S(2)}) collective-permute-start(bf16[2,4,2,1,96,192]{5,4,1,0,3,2:T(8,128)(2,1)} %copy.260), channel_id=1, source_target_pairs={{0,4},{4,0},{8,12},{12,8},{16,20},{20,16},{24,28},{28,24},{1,5},{5... | collective-permute-start | bytes 1769480 | tf_op jit(solution)/shard_map/ppermute | solution.py:39
  1652.7 60.5 %collective-permute-start.6 = (bf16[2,2,2,1,96,768]{5,4,1,0,3,2:T(8,128)(2,1)}, bf16[2,2,2,1,96,768]{5,4,1,0,3,2:T(8,128)(2,1)}, u32[]{:S(2)}, u32[]{:S(2)}) collective-permute-start(bf16[2,2,2,1,96,768]{5,4,1,0,3,2:T(8,128)(2,1)} %copy.286), channel_id=1, source_target_pairs={{0,4},{4,0},{8,12},{12,8},{16,20},{20,16},{24,28},{28,24},{1,5},{5... | collective-permute-start | bytes 3538952 | tf_op jit(solution)/shard_map/ppermute | solution.py:39
  1665.2 36.5 %collective-permute-start.8 = (bf16[2,2,1,96,1152]{4,3,0,2,1:T(8,128)(2,1)}, bf16[2,2,1,96,1152]{4,3,0,2,1:T(8,128)(2,1)}, u32[]{:S(2)}, u32[]{:S(2)}) collective-permute-start(bf16[2,2,1,96,1152]{4,3,0,2,1:T(8,128)(2,1)} %copy.287), channel_id=1, source_target_pairs={{0,4},{4,0},{8,12},{12,8},{16,20},{20,16},{24,28},{28,24},{1,5},{5... | collective-permute-start | bytes 2654216 | tf_op jit(solution)/shard_map/ppermute | solution.py:39
  1679.6 37.4 %collective-permute-start.10 = (bf16[3592,2,1,96]{0,3,2,1:T(8,128)(2,1)}, bf16[3592,2,1,96]{0,3,2,1:T(8,128)(2,1)}, u32[]{:S(2)}, u32[]{:S(2)}) collective-permute-start(bf16[3592,2,1,96]{0,3,2,1:T(8,128)(2,1)} %dynamic-slice_convert_fusion.1), channel_id=1, source_target_pairs={{0,4},{4,0},{8,12},{12,8},{16,20},{20,16},{24,28},{28,24},{1,5},{5... | collective-permute-start | bytes 4137992 | tf_op jit(solution)/shard_map/ppermute | solution.py:39
  1699.4 12.3 collective-permute-start.5
  1703.3 17.9 %collective-permute-start.9 = (bf16[2,1,1,96,1152]{4,3,0,2,1:T(8,128)(2,1)S(1)}, bf16[2,1,1,96,1152]{4,3,0,2,1:T(8,128)(2,1)S(1)}, u32[]{:S(2)}, u32[]{:S(2)}) collective-permute-start(bf16[2,1,1,96,1152]{4,3,0,2,1:T(8,128)(2,1)S(1)} %dynamic-slice_convert_fusion.5), channel_id=1, source_target_pairs={{0,8},{4,12},{8,0},{12,4},{16,24},{20,28},{24,16},{28,20},{1,9},{5... | collective-permute-start | bytes 1327112 | tf_op jit(solution)/shard_map/ppermute | solution.py:39
  1714.9 18.9 %collective-permute-start.7 = (bf16[2,2,1,1,96,768]{5,4,1,0,3,2:T(8,128)(2,1)S(1)}, bf16[2,2,1,1,96,768]{5,4,1,0,3,2:T(8,128)(2,1)S(1)}, u32[]{:S(2)}, u32[]{:S(2)}) collective-permute-start(bf16[2,2,1,1,96,768]{5,4,1,0,3,2:T(8,128)(2,1)S(1)} %dynamic-slice_convert_fusion.4), channel_id=1, source_target_pairs={{0,8},{4,12},{8,0},{12,4},{16,24},{20,28},{24,16},{28,20},{1,9},{5... | collective-permute-start | bytes 1769480 | tf_op jit(solution)/shard_map/ppermute | solution.py:39
  1718.8 29.9 %collective-permute-start.11 = (bf16[3592,1,1,96]{0,3,2,1:T(8,128)(2,1)S(1)}, bf16[3592,1,1,96]{0,3,2,1:T(8,128)(2,1)S(1)}, u32[]{:S(2)}, u32[]{:S(2)}) collective-permute-start(bf16[3592,1,1,96]{0,3,2,1:T(8,128)(2,1)S(1)} %dynamic-slice_convert_fusion.3), channel_id=1, source_target_pairs={{0,8},{4,12},{8,0},{12,4},{16,24},{20,28},{24,16},{28,20},{1,9},{5... | collective-permute-start | bytes 2069000 | tf_op jit(solution)/shard_map/ppermute | solution.py:39
  (179 other events, 1451.5 us)
Sparse Core Ops, SparseCore 0:
  10.5 34.9 all-gather.8
  47.9 42.8 all-gather.4
  93.3 33.8 all-gather.6
  161.4 121.1 all-reduce.11
  284.8 37.7 all-gather.10
  337.7 121.0 all-reduce.13
  478.0 120.0 all-reduce.15
  615.4 120.0 all-reduce.17
  770.4 120.0 all-reduce.19
  925.4 120.0 all-reduce.21
  1070.5 120.0 all-reduce.23
  1218.8 120.0 all-reduce.25
  1426.5 125.4 all-reduce.27
where the time goes:
time: 1770 us; the launch traced here: 1760 us
  waiting for transfers between devices  1070 us (60%)
  other arithmetic  201 us (11%)
  local copies, waits for them, and re-layouts  199 us (11%)
  matrix products  183 us (10%)
  blocking collectives  73 us (4%)
  between operations  22.4 us (1%)
    psum x4, waiting for transfers between devices, tensor_forward(): lax.psum(partial_out.astype(jnp.bfloat16), 'tensor').astype(jnp.float32)  470 us
    psum x4, waiting for transfers between devices, tensor_backward(): lax.psum(partial_in.astype(jnp.bfloat16), 'tensor').astype(jnp.float32)  330 us
    psum x1, waiting for transfers between devices, per_device(): lax.psum((picked[:, None] * bias_grad_all[None, :], picked * squares, jnp...  104 us
    unnamed x465, local copies, waits for them, and re-layouts  101 us
    dot_general x18, matrix products, weight_grad(): lax.dot_general(inputs, grads_out, ((leading, leading), ((), ())), prefer...  65.8 us
    ppermute x12, waiting for transfers between devices, swapped(): return lax.ppermute(value, axis, pairs)  52.2 us
    dot_general x18, matrix products, product(): return jnp.dot(left, right, preferred_element_type=jnp.float32)  50.5 us
    dot_general x15, matrix products, product_t(): lax.dot_general(left, right, (((left.ndim - 1,), (1,)), ((), ())), prefer...  44 us
  transfers between devices with their start and end apart: 25, of which 18 were waited for; matrix products, arithmetic and copies ran while one was open for 19% of the time, Pallas kernels for 0%

commit v1 on v0

--- a/solution.py
+++ b/solution.py
@@ -166,51 +166,45 @@
     )
 
 
-def tensor_forward(partial_out):
-    return lax.psum(partial_out.astype(jnp.bfloat16), "tensor").astype(jnp.float32)
-
-
-def tensor_backward(partial_in):
-    return lax.psum(partial_in.astype(jnp.bfloat16), "tensor").astype(jnp.float32)
-
-
 def place(vector_all, piece_in, offset):
     return lax.dynamic_update_slice_in_dim(vector_all, piece_in, offset, 0)
 
 
-def layer_forward(stream, modulation, attn_now, mlp_now, bias_layer, shard_at):
+def flipped(value, masks):
+    shards = lax.axis_size("tensor")
+    count = lax.axis_size("dp") * shards
+    pairs = [(source, source ^ masks[source // shards & 1]) for source in range(count)]
+    return lax.ppermute(value, ("dp", "tensor"), pairs)
+
+
+def picked_at(value, index_at, axis):
+    return lax.dynamic_index_in_dim(value, index_at, axis, keepdims=False)
+
+
+def layer_forward(stream, mod_parts, attn_now, mlp_now, bias_layer):
     width_all = stream.shape[-1]
-    col_width = attn_now.shape[2]
-    unit_width = mlp_now.shape[2]
-    mod_parts = [
-        modulation[:, None, part_at * width_all : (part_at + 1) * width_all] for part_at in range(6)
-    ]
     normed_one, inverse_one = normalize(stream)
     hidden_one = (normed_one * (1.0 + mod_parts[1]) + mod_parts[0]).astype(LOW_TYPE)
-    queries = (
-        product(hidden_one, attn_now[0])
-        + lax.dynamic_slice_in_dim(bias_layer, shard_at * col_width, col_width)
-    ).astype(LOW_TYPE)
+    queries = (product(hidden_one, attn_now[0]) + bias_layer[:width_all]).astype(LOW_TYPE)
     key_rows = product(hidden_one, attn_now[1]).astype(LOW_TYPE)
-    values = (
-        product(hidden_one, attn_now[2])
-        + lax.dynamic_slice_in_dim(bias_layer, width_all + shard_at * col_width, col_width)
-    ).astype(LOW_TYPE)
+    values = (product(hidden_one, attn_now[2]) + bias_layer[width_all : 2 * width_all]).astype(
+        LOW_TYPE
+    )
     attended, log_total = attend(queries, key_rows, values)
     attended = attended.astype(LOW_TYPE)
-    branch_one = (
-        tensor_forward(product_t(attended, attn_now[3])) + bias_layer[2 * width_all : 3 * width_all]
-    )
+    branch_one = product_t(attended, attn_now[3]) + bias_layer[2 * width_all : 3 * width_all]
     middle = stream + mod_parts[2] * branch_one
     normed_two, inverse_two = normalize(middle)
     hidden_two = (normed_two * (1.0 + mod_parts[4]) + mod_parts[3]).astype(LOW_TYPE)
-    before = product(hidden_two, mlp_now[0]) + lax.dynamic_slice_in_dim(
-        bias_layer, 3 * width_all + shard_at * unit_width, unit_width
-    )
-    activated = gelu_tanh(before).astype(LOW_TYPE)
-    branch_two = (
-        tensor_forward(product_t(activated, mlp_now[1]))
-        + bias_layer[3 * width_all + FF : 4 * width_all + FF]
+    unit_width = mlp_now.shape[-1]
+    before = [
+        product(hidden_two, mlp_now[0, unit_at])
+        + bias_layer[3 * width_all + unit_at * unit_width : 3 * width_all + (unit_at + 1) * unit_width]
+        for unit_at in range(mlp_now.shape[1])
+    ]
+    activated = [gelu_tanh(part).astype(LOW_TYPE) for part in before]
+    branch_two = bias_layer[3 * width_all + FF : 4 * width_all + FF] + sum(
+        product_t(part, mlp_now[1, unit_at]) for unit_at, part in enumerate(activated)
     )
     result = middle + mod_parts[5] * branch_two
     kept_state = (
@@ -233,7 +227,7 @@
     return (result, kept_state)
 
 
-def layer_backward(grad_out, modulation, attn_now, mlp_now, shard_at, kept_state):
+def layer_backward(grad_out, mod_parts, attn_now, mlp_now, kept_state):
     (
         normed_one,
         inverse_one,
@@ -251,21 +245,19 @@
         activated,
         branch_two,
     ) = kept_state
-    width_all = grad_out.shape[-1]
-    col_width = attn_now.shape[2]
-    unit_width = mlp_now.shape[2]
-    shards = lax.axis_size("tensor")
-    mod_parts = [
-        modulation[:, None, part_at * width_all : (part_at + 1) * width_all] for part_at in range(6)
-    ]
     grad_gate_two = jnp.sum(grad_out * branch_two, 1)
     downward = grad_out * mod_parts[5]
     down_low = downward.astype(LOW_TYPE)
-    grad_down = weight_grad(down_low, activated)
-    grad_act = product(down_low, mlp_now[1])
-    grad_pre = jax.vjp(gelu_tanh, saved_pre)[1](grad_act)[0].astype(LOW_TYPE)
-    grad_up = weight_grad(hidden_two, grad_pre)
-    grad_hidden_two = tensor_backward(product_t(grad_pre, mlp_now[0]))
+    grad_pre = [
+        jax.vjp(gelu_tanh, part)[1](product(down_low, mlp_now[1, unit_at]))[0].astype(LOW_TYPE)
+        for unit_at, part in enumerate(saved_pre)
+    ]
+    grad_down = [weight_grad(down_low, part).astype(LOW_TYPE) for part in activated]
+    grad_up = [weight_grad(hidden_two, part).astype(LOW_TYPE) for part in grad_pre]
+    mlp_sums = reduced_blocks(mlp_blocks(jnp.stack([jnp.stack(grad_up), jnp.stack(grad_down)])))
+    grad_hidden_two = sum(
+        product_t(part, mlp_now[0, unit_at]) for unit_at, part in enumerate(grad_pre)
+    )
     grad_middle = grad_out + normalize_back(
         grad_hidden_two * (1.0 + mod_parts[4]), normed_two, inverse_two
     )
@@ -277,10 +269,19 @@
     grad_queries, grad_keys, grad_values = attend_back(
         queries, key_rows, values, log_total, grad_attended
     )
-    grad_query_map = weight_grad(hidden_one, grad_queries)
-    grad_key_map = weight_grad(hidden_one, grad_keys)
-    grad_value_map = weight_grad(hidden_one, grad_values)
-    grad_hidden_one = tensor_backward(
+    attn_sums = reduced_blocks(
+        attn_blocks(
+            jnp.stack(
+                [
+                    weight_grad(hidden_one, grad_queries).astype(LOW_TYPE),
+                    weight_grad(hidden_one, grad_keys).astype(LOW_TYPE),
+                    weight_grad(hidden_one, grad_values).astype(LOW_TYPE),
+                    grad_out_map.astype(LOW_TYPE),
+                ]
+            )
+        )
+    )
+    grad_hidden_one = (
         product_t(grad_queries, attn_now[0])
         + product_t(grad_keys, attn_now[1])
         + product_t(grad_values, attn_now[2])
@@ -298,30 +299,90 @@
             grad_gate_two,
         ],
         axis=1,
-    )
-    bias_grad = jnp.zeros((LB * width_all,), jnp.float32)
-    bias_grad = place(
-        bias_grad, jnp.sum(grad_queries.astype(jnp.float32), (0, 1)), shard_at * col_width
-    )
-    bias_grad = place(
-        bias_grad,
-        jnp.sum(grad_values.astype(jnp.float32), (0, 1)),
-        width_all + shard_at * col_width,
-    )
-    bias_grad = place(bias_grad, jnp.sum(upward, (0, 1)) / shards, 2 * width_all)
-    bias_grad = place(
-        bias_grad,
-        jnp.sum(grad_pre.astype(jnp.float32), (0, 1)),
-        3 * width_all + shard_at * unit_width,
-    )
-    bias_grad = place(bias_grad, jnp.sum(downward, (0, 1)) / shards, 3 * width_all + FF)
-    return (
-        grad_stream,
-        jnp.stack([grad_query_map, grad_key_map, grad_value_map, grad_out_map]),
-        jnp.stack([grad_up, grad_down]),
-        grad_modulation,
-        bias_grad,
-    )
+    ).astype(LOW_TYPE)
+    bias_grad = jnp.concatenate(
+        [
+            jnp.sum(grad_queries.astype(jnp.float32), (0, 1)),
+            jnp.sum(grad_values.astype(jnp.float32), (0, 1)),
+            jnp.sum(upward, (0, 1)),
+        ]
+        + [jnp.sum(part.astype(jnp.float32), (0, 1)) for part in grad_pre]
+        + [jnp.sum(downward, (0, 1))]
+    )
+    return (grad_stream, attn_sums, mlp_sums, grad_modulation, bias_grad)
+
+
+def attn_blocks(grads):
+    stretches = lax.axis_size("dp") // GROUPS
+    shards = lax.axis_size("tensor")
+    kinds, rows_all, width_all = grads.shape
+    shaped = grads.reshape(
+        kinds, stretches, rows_all // stretches, 2, shards // 2, width_all // shards
+    )
+    return jnp.transpose(shaped, (3, 4, 1, 2, 0, 5)).reshape(
+        2, 1, shards // 2, stretches, rows_all // stretches, kinds * width_all // shards
+    )
+
+
+def mlp_blocks(grads):
+    stretches = lax.axis_size("dp") // GROUPS
+    kinds, shards, rows_all, width = grads.shape
+    shaped = grads.reshape(kinds, 2, shards // 2, stretches, rows_all // stretches, width)
+    return jnp.transpose(shaped, (1, 0, 2, 3, 4, 5))
+
+
+def summed_low(left, right):
+    return (left.astype(jnp.float32) + right.astype(jnp.float32)).astype(LOW_TYPE)
+
+
+def reduced_blocks(blocks):
+    shards = lax.axis_size("tensor")
+    dp_at, shard_at = (lax.axis_index("dp"), lax.axis_index("tensor"))
+    low_bit, stretch, shard_low = (dp_at & 1, dp_at // GROUPS, shard_at & 1)
+    kinds, columns, stretches, rows, width = blocks.shape[1:]
+    core_mask = shards
+    received = flipped(picked_at(blocks, 1 - low_bit, 0), (core_mask, core_mask))
+    total = summed_low(picked_at(blocks, low_bit, 0), received)
+    total = jnp.where(
+        low_bit == 1,
+        total.reshape(kinds, columns * stretches, rows, width),
+        jnp.swapaxes(total, 1, 2).reshape(kinds, columns * stretches, rows, width),
+    )
+    column_step = (shard_low, 1)
+    row_steps = [
+        (stretch >> bit_at & 1, shards * GROUPS << bit_at)
+        for bit_at in reversed(range(stretches.bit_length() - 1))
+    ]
+    rows_first, columns_first = (row_steps + [column_step], [column_step] + row_steps)
+    for (bit_zero, mask_zero), (bit_one, mask_one) in zip(rows_first, columns_first):
+        own_bit = jnp.where(low_bit == 1, bit_one, bit_zero)
+        halves = total.reshape(kinds, 2, total.shape[1] // 2, rows, width)
+        received = flipped(picked_at(halves, 1 - own_bit, 1), (mask_zero, mask_one))
+        total = summed_low(picked_at(halves, own_bit, 1), received)
+    count = lax.axis_size("dp") * shards
+    pairs = []
+    for source in range(count):
+        core, high = (source // shards & 1, source % shards >> 1)
+        changed = (core ^ high) * (shards + shards // 2)
+        pairs.append((source, source ^ changed))
+    return lax.ppermute(total[:, 0], ("dp", "tensor"), pairs)
+
+
+def own_latents(value):
+    shards = lax.axis_size("tensor")
+    low_bit, shard_at = (lax.axis_index("dp") & 1, lax.axis_index("tensor"))
+    count = value.shape[0] // shards
+    base = (shard_at & 1) * 2
+    mine = lax.dynamic_slice_in_dim(value, (base + low_bit) * count, count, 0)
+    theirs = lax.dynamic_slice_in_dim(value, (base + 1 - low_bit) * count, count, 0)
+    received = flipped(theirs, (shards, shards))
+    return jnp.where(shard_at >> 1 == low_bit, mine, received)
+
+
+def natural_order(gathered, stretches):
+    shaped = gathered.reshape((stretches, 2, 2, 2, 2) + gathered.shape[1:])
+    moved = jnp.moveaxis(shaped, 2, 4)
+    return moved.reshape((-1,) + gathered.shape[2:])
 
 
 def split_bits(array_in, axis_at, count_bits):
@@ -422,66 +483,100 @@
     shards = lax.axis_size("tensor")
     shard_at = lax.axis_index("tensor")
     dp_count = lax.axis_size("dp")
-    group_at = lax.axis_index("dp") % GROUPS
+    dp_at = lax.axis_index("dp")
+    group_at = dp_at % GROUPS
+    stretches = dp_count // GROUPS
+    stretch = dp_at // GROUPS
     layer_span = LB * D
-    attn_all, mlp_all, mod_all, embed_all = (
-        lax.all_gather(w_attn.astype(LOW_TYPE), "dp", axis=2, tiled=True),
-        lax.all_gather(w_mlp.astype(LOW_TYPE), "dp", axis=2, tiled=True),
-        lax.all_gather(w_mod.astype(LOW_TYPE), "dp", axis=1, tiled=True),
-        lax.all_gather(w_embed.astype(LOW_TYPE), "dp", axis=1, tiled=True),
-    )
-    class_table, first_time, second_time, patch_map, final_map, head_map = embed_parts(embed_all)
+    col_width = w_attn.shape[3]
+    row_width = w_attn.shape[2]
+    mod_width = w_mod.shape[2]
+    latents = dp_count * patches.shape[0]
+    everyone = ("tensor", "dp")
+
+    stamps, marks = lax.all_gather(jnp.stack([timesteps, labels]), "dp", axis=1, tiled=True)
+    embed_low = w_embed.astype(LOW_TYPE)
+    conditioners = NCLS + FREQ + D + PATCH_IN
+    embed_all = lax.all_gather(
+        jnp.concatenate([embed_low[:conditioners], embed_low[-PATCH_IN:]]), "dp", axis=1, tiled=True
+    )
+    class_table = embed_all[:NCLS]
+    first_time = embed_all[NCLS : NCLS + FREQ]
+    second_time = embed_all[NCLS + FREQ : NCLS + FREQ + D]
+    patch_map = embed_all[NCLS + FREQ + D : conditioners]
+    head_map = embed_all[conditioners:]
+    attn_all, mlp_all = ([], [])
+    for layer_at in range(L):
+        attn_local = jnp.transpose(w_attn[layer_at], (1, 0, 2)).reshape(row_width, 4 * col_width)
+        local = jnp.concatenate([attn_local[None], w_mlp[layer_at]]).astype(LOW_TYPE)
+        whole = lax.all_gather(local, everyone, axis=1, tiled=True)
+        whole = whole.reshape(3, shards, D, -1)
+        attn_all.append(
+            jnp.transpose(whole[0].reshape(shards, D, 4, col_width), (2, 1, 0, 3)).reshape(4, D, D)
+        )
+        mlp_all.append(whole[1:])
+
     bias_flat = biases.reshape(-1)
     bias_tail = bias_flat[L * layer_span :]
-    batch_here = patches.shape[0]
-    signal = signal_levels(timesteps)[:, None, None]
-    noised = (jnp.sqrt(signal) * patches + jnp.sqrt(1.0 - signal) * noise_draw).astype(LOW_TYPE)
-    stream = product(noised, patch_map) + bias_tail[:D] + positions()
-    freq_low = frequencies(timesteps).astype(LOW_TYPE)
+    freq_low = frequencies(stamps).astype(LOW_TYPE)
     hidden_time = product(freq_low, first_time) + bias_tail[D : 2 * D]
     smooth_time = jax.nn.silu(hidden_time).astype(LOW_TYPE)
-    class_picks = (labels[:, None] == jnp.arange(NCLS, dtype=jnp.int32)[None, :]).astype(LOW_TYPE)
+    class_picks = (marks[:, None] == jnp.arange(NCLS, dtype=jnp.int32)[None, :]).astype(LOW_TYPE)
     condition = (
         product(smooth_time, second_time)
         + bias_tail[2 * D : 3 * D]
         + product(class_picks, class_table)
     )
     cond_act = jax.nn.silu(condition).astype(LOW_TYPE)
-    mod_width = mod_all.shape[2]
-    ada_bias = jnp.stack(
-        [
-            lax.dynamic_slice_in_dim(
-                bias_flat, layer_at * layer_span + 4 * D + FF + shard_at * mod_width, mod_width
+    mod_low = w_mod.astype(LOW_TYPE)
+    final_low = embed_low[conditioners:-PATCH_IN]
+    final_width = final_low.shape[0] // shards
+    cond_rows = lax.dynamic_slice_in_dim(cond_act, dp_at * row_width, row_width, 1)
+    mod_cols = jnp.concatenate(
+        [product(cond_rows, mod_low[layer_at]) for layer_at in range(L)]
+        + [
+            product_t(
+                cond_rows, lax.dynamic_slice_in_dim(final_low, shard_at * final_width, final_width, 0)
             )
-            for layer_at in range(L)
-        ]
-    )
-    mod_cols = (
-        jnp.einsum("nd,ldm->lnm", cond_act, mod_all, preferred_element_type=jnp.float32)
-        + ada_bias[:, None, :]
-    )
-    modulations = lax.all_gather(
-        mod_cols.astype(jnp.bfloat16), "tensor", axis=2, tiled=True
-    ).astype(mod_cols.dtype)
+        ],
+        axis=1,
+    )
+    mod_cols = lax.psum_scatter(mod_cols, "dp", scatter_dimension=0, tiled=True)
+    mod_all = own_latents(
+        jnp.swapaxes(lax.all_gather(mod_cols.astype(LOW_TYPE), "tensor"), 0, 1)
+    ).astype(jnp.float32)
+    mod_parts = []
+    for layer_at in range(L):
+        modulation = (
+            mod_all[:, :, layer_at * mod_width : (layer_at + 1) * mod_width].reshape(-1, 6 * D)
+            + bias_flat[layer_at * layer_span + 4 * D + FF : (layer_at + 1) * layer_span]
+        )
+        mod_parts.append(
+            [modulation[:, None, part_at * D : (part_at + 1) * D] for part_at in range(6)]
+        )
+    final_mod = mod_all[:, :, L * mod_width :].reshape(-1, 2 * D) + bias_tail[3 * D : 5 * D]
+
+    patches_own, noise_own = (own_latents(patches), own_latents(noise_draw))
+    signal = own_latents(signal_levels(timesteps)[:, None])[:, :, None]
+    noised = (jnp.sqrt(signal) * patches_own + jnp.sqrt(1.0 - signal) * noise_own).astype(LOW_TYPE)
+    stream = product(noised, patch_map) + bias_tail[:D] + positions()
     saved_states = []
     for layer_at in range(L):
         stream, kept_state = layer_forward(
             stream,
-            modulations[layer_at],
+            mod_parts[layer_at],
             attn_all[layer_at],
             mlp_all[layer_at],
             bias_flat[layer_at * layer_span : (layer_at + 1) * layer_span],
-            shard_at,
         )
         saved_states.append(kept_state)
-    final_mod = product_t(cond_act, final_map) + bias_tail[3 * D : 5 * D]
     normed_last, inverse_last = normalize(stream)
     hidden_last = (normed_last * (1.0 + final_mod[:, None, D:]) + final_mod[:, None, :D]).astype(
         LOW_TYPE
     )
     predicted = product_t(hidden_last, head_map)
-    errors = predicted - noise_draw
-    elements = dp_count // GROUPS * batch_here * S * PATCH_IN
+    errors = predicted - noise_own
+    elements = dp_count // GROUPS * patches.shape[0] * S * PATCH_IN
     loss_here = jnp.sum(errors * errors) / elements
     grad_pred = (2.0 * errors / elements).astype(LOW_TYPE)
     grad_head = weight_grad(grad_pred, hidden_last)
@@ -492,8 +587,6 @@
     grad_stream = normalize_back(
         grad_hidden * (1.0 + final_mod[:, None, D:]), normed_last, inverse_last
     )
-    grad_final_map = weight_grad(grad_final, cond_act)
-    grad_cond_local = product(grad_final, final_map)
     attn_list, mlp_list, mod_list, bias_list = ([None] * L, [None] * L, [None] * L, [None] * L)
     for layer_at in range(L - 1, -1, -1):
         (
@@ -504,60 +597,115 @@
             bias_list[layer_at],
         ) = layer_backward(
             grad_stream,
-            modulations[layer_at],
+            mod_parts[layer_at],
             attn_all[layer_at],
             mlp_all[layer_at],
-            shard_at,
             saved_states[layer_at],
         )
-    grad_mods = jnp.stack(mod_list).astype(LOW_TYPE)
-    own_mods = lax.dynamic_slice_in_dim(grad_mods, shard_at * mod_width, mod_width, 2)
-    grad_mod_map = jnp.einsum("nd,lnm->ldm", cond_act, own_mods, preferred_element_type=jnp.float32)
-    grad_ada = jnp.sum(own_mods.astype(jnp.float32), 1)
-    grad_cond_parts = jnp.einsum(
-        "lnm,ldm->nd", own_mods, mod_all, preferred_element_type=jnp.float32
-    )
-    grad_cond_act = (
-        lax.psum(grad_cond_parts.astype(jnp.bfloat16), "tensor").astype(jnp.float32)
-        + grad_cond_local
-    )
-    grad_condition = jax.vjp(jax.nn.silu, condition)[1](grad_cond_act)[0].astype(LOW_TYPE)
-    grad_table = weight_grad(class_picks, grad_condition)
-    grad_second = weight_grad(smooth_time, grad_condition)
+    grad_patch = weight_grad(noised, grad_stream.astype(LOW_TYPE))
+    mine = patches_own.shape[0]
+    vectors = jnp.concatenate(
+        [grad_now.reshape(-1) for grad_now in mod_list]
+        + [grad_final.reshape(-1)]
+        + [grad_now.astype(LOW_TYPE) for grad_now in bias_list]
+        + [
+            jnp.sum(grad_stream, (0, 1)).astype(LOW_TYPE),
+            grad_patch.astype(LOW_TYPE).reshape(-1),
+            grad_head.astype(LOW_TYPE).reshape(-1),
+        ]
+    )
+    gathered = lax.all_gather(vectors, ("dp", "tensor"))
+    devices = dp_count * shards
+    offset = 0
+
+    def taken(width):
+        nonlocal offset
+        offset += width
+        return gathered[:, offset - width : offset]
+
+    grad_mods = [
+        natural_order(taken(mine * 6 * D).reshape(devices, mine, 6 * D), stretches)
+        for layer_at in range(L)
+    ]
+    grad_finals = natural_order(taken(mine * 2 * D).reshape(devices, mine, 2 * D), stretches)
+
+    def group_sums(part):
+        shaped = part.astype(jnp.float32).reshape(stretches, 2, 2, 2, shards // 2, -1)
+        return jnp.sum(shaped, (0, 2, 4)).reshape(GROUPS, -1)
+
+    layer_bias = 7 * D + FF - 3 * D
+    bias_sums = [group_sums(taken(layer_bias)) for layer_at in range(L)]
+    patch_bias = group_sums(taken(D))
+    patch_sums = group_sums(taken(PATCH_IN * D)).reshape(GROUPS, PATCH_IN, D)
+    head_sums = group_sums(taken(PATCH_IN * D)).reshape(GROUPS, PATCH_IN, D)
+
+    own_mods = [
+        lax.dynamic_slice_in_dim(grad_now, shard_at * mod_width, mod_width, 1)
+        for grad_now in grad_mods
+    ]
+    grad_cond_parts = sum(
+        product_t(own_mods[layer_at], mod_low[layer_at]) for layer_at in range(L)
+    )
+    grad_cond_act = lax.psum(grad_cond_parts.astype(jnp.bfloat16), "tensor").astype(
+        jnp.float32
+    ) + product(grad_finals, final_low)
+    condition_rows = lax.dynamic_slice_in_dim(condition, dp_at * row_width, row_width, 1)
+    grad_condition = lax.all_gather(
+        jax.vjp(jax.nn.silu, condition_rows)[1](grad_cond_act)[0].astype(LOW_TYPE),
+        "dp",
+        axis=1,
+        tiled=True,
+    )
     grad_smooth = product_t(grad_condition, second_time)
     grad_hidden_time = jax.vjp(jax.nn.silu, hidden_time)[1](grad_smooth)[0].astype(LOW_TYPE)
-    grad_first = weight_grad(freq_low, grad_hidden_time)
-    grad_patch = weight_grad(noised, grad_stream.astype(LOW_TYPE))
+
+    def of_group(value):
+        shaped = value.reshape((stretches, GROUPS, latents // dp_count) + value.shape[1:])
+        return picked_at(shaped, group_at, 1).reshape((-1,) + value.shape[1:])
+
+    def of_stretch(value):
+        width = value.shape[-1] // stretches
+        return lax.dynamic_slice_in_dim(value, stretch * width, width, value.ndim - 1)
+
+    def latent_sums(value):
+        shaped = value.astype(jnp.float32).reshape(stretches, GROUPS, latents // dp_count, -1)
+        return jnp.sum(shaped, (0, 2))
+
+    grad_condition_own = of_stretch(of_group(grad_condition))
+    cond_own = of_stretch(of_group(cond_act))
     grad_embed = jnp.concatenate(
-        [grad_table, grad_first, grad_second, grad_patch, grad_final_map, grad_head], 0
-    )
-    layer_biases = [
-        place(bias_list[layer_at], grad_ada[layer_at], 4 * D + FF + shard_at * mod_width)
-        for layer_at in range(L)
-    ]
-    tail_grad = (
-        jnp.concatenate(
-            [
-                jnp.sum(grad_stream, (0, 1)),
-                jnp.sum(grad_hidden_time.astype(jnp.float32), 0),
-                jnp.sum(grad_condition.astype(jnp.float32), 0),
-                jnp.sum(grad_final.astype(jnp.float32), 0),
-            ]
-        )
-        / shards
-    )
-    bias_grad_all = jnp.concatenate(layer_biases + [tail_grad])
-    shift_group = GROUPS.bit_length() - 1
-    group_bits = dp_count.bit_length() - 1 - shift_group
-    bit_order = list(reversed(range(group_bits)))
-    reduced = reduce_pieces(
-        [jnp.stack(attn_list), jnp.stack(mlp_list), grad_mod_map, grad_embed],
-        (2, 2, 1, 1),
-        shift_group,
-        group_bits,
-        bit_order,
-        False,
-    )
+        [
+            weight_grad(of_group(class_picks), grad_condition_own),
+            weight_grad(of_group(freq_low), of_stretch(of_group(grad_hidden_time))),
+            weight_grad(of_group(smooth_time), grad_condition_own),
+            of_stretch(picked_at(patch_sums, group_at, 0)),
+            weight_grad(of_group(grad_finals), cond_own),
+            of_stretch(picked_at(head_sums, group_at, 0)),
+        ],
+        0,
+    )
+    grad_mod_map = jnp.stack([weight_grad(cond_own, of_group(grad_now)) for grad_now in own_mods])
+    bias_groups = jnp.concatenate(
+        [
+            part
+            for layer_at in range(L)
+            for part in (bias_sums[layer_at], latent_sums(grad_mods[layer_at]))
+        ]
+        + [
+            patch_bias,
+            latent_sums(grad_hidden_time),
+            latent_sums(grad_condition),
+            latent_sums(grad_finals),
+        ],
+        axis=1,
+    )
+    attn_now = jnp.stack(
+        [
+            jnp.transpose(part.reshape(-1, 4, col_width), (1, 0, 2)).astype(jnp.float32)
+            for part in attn_list
+        ]
+    )
+    reduced = [attn_now, jnp.stack(mlp_list).astype(jnp.float32), grad_mod_map, grad_embed]
     squares = (
         jnp.sum(reduced[0] * reduced[0])
         + jnp.sum(reduced[1] * reduced[1])
@@ -565,17 +713,13 @@
         + jnp.sum(reduced[3] * reduced[3]) / shards
     )
     picked = (jnp.arange(GROUPS, dtype=jnp.int32) == group_at).astype(jnp.float32)
-    bias_groups, square_groups, loss_total = lax.psum(
-        (
-            picked[:, None] * bias_grad_all[None, :],
-            picked * squares,
-            jnp.reshape(loss_here / shards, (1,)),
-        ),
-        ("dp", "tensor"),
-    )
-    group_norms = jnp.sqrt(square_groups + jnp.sum(bias_groups * bias_groups, 1))
+    totals = lax.psum(
+        jnp.concatenate([picked * squares, jnp.reshape(loss_here, (1,))]), ("dp", "tensor")
+    )
+    group_norms = jnp.sqrt(totals[:GROUPS] + jnp.sum(bias_groups * bias_groups, 1))
     clip_scale = CLIP_NORM / (group_norms + 1e-06)
     own_scale = jnp.sum(picked * clip_scale)
+    shift_group = GROUPS.bit_length() - 1
     weights_in = (w_attn, w_mlp, w_mod, w_embed)
     momenta_in = (momentum_attn, momentum_mlp, momentum_mod, momentum_embed)
     firsts_in = (first_attn, first_mlp, first_mod, first_embed)
@@ -605,7 +749,7 @@
     bias_momentum = OUTER_MOMENTUM * momentum_bias.reshape(-1) + outer_bias
     bias_new = bias_flat - OUTER_RATE * (outer_bias + OUTER_MOMENTUM * bias_momentum)
     return (
-        loss_total[0] / GROUPS,
+        totals[GROUPS] / GROUPS,
         group_norms,
         clipped_bias.reshape(first_bias.shape),
         new_weights[0],

time: 1770 us -> 1060 us (0.60)
  waiting for transfers between devices: 1070 us -> 188 us
  blocking collectives: 73 us -> 233 us
  local copies, waits for them, and re-layouts: 199 us -> 273 us
  other arithmetic: 201 us -> 150 us
  matrix products: 183 us -> 162 us
    psum x9 -> x0, waiting for transfers between devices: 905 us -> none  [the longest x4 470 us: tensor_forward(): lax.psum(partial_out.astype(jnp.bfloat16), 'tensor').astype(jnp.float32)]
    ppermute x0 -> x20, waiting for transfers between devices: none -> 66.4 us  [the longest x16 66.4 us: flipped(): return lax.ppermute(value, ('dp', 'tensor'), pairs)]
    reduce_sum x18 -> x15, other arithmetic: 75.9 us -> 10.2 us  [the longest x5 3.19 us: group_sums(): return jnp.sum(shaped, (0, 2, 4)).reshape(GROUPS, -1)]
    psum x1, blocking collectives: 17.2 us -> 77.6 us  [per_device(): lax.psum(grad_cond_parts.astype(jnp.bfloat16), 'tensor').astype(jnp.float32)]
    slice x7 -> x24, local copies, waits for them, and re-layouts: 2.19 us -> 45.8 us  [the longest x4 22.9 us: per_device(): whole[0].reshape(shards, D, 4, col_width)]
    psum x1, blocking collectives: 42.1 us -> 84.9 us  [per_device(): lax.psum(jnp.concatenate([picked * squares, jnp.reshape(loss_here, (1,))]...]
    unnamed x0 -> x1, blocking collectives: none -> 36.3 us
    convert_element_type x0 -> x21, local copies, waits for them, and re-layouts: none -> 32.3 us  [the longest x2 4.74 us: layer_backward(): weight_grad(hidden_one, grad_keys).astype(LOW_TYPE)]
  transfers between devices with their start and end apart: 25 -> 32, of which waited for: 18 -> 13; matrix products, arithmetic and copies ran while one was open for 19% -> 32% of each run, Pallas kernels for 0% -> 0%
where the time goes in v1:
time: 1060 us; the launch traced here: 1050 us
  local copies, waits for them, and re-layouts  273 us (26%)
  blocking collectives  233 us (22%)
  waiting for transfers between devices  188 us (18%)
  matrix products  162 us (15%)
  other arithmetic  150 us (14%)
  between operations  23 us (2%)
  starting transfers between devices  22.5 us (2%)
    psum x1, blocking collectives, per_device(): lax.psum(jnp.concatenate([picked * squares, jnp.reshape(loss_here, (1,))]...  84.9 us
    psum x1, blocking collectives, per_device(): lax.psum(grad_cond_parts.astype(jnp.bfloat16), 'tensor').astype(jnp.float32)  77.6 us
    all_gather x2, waiting for transfers between devices, per_device(): whole = lax.all_gather(local, everyone, axis=1, tiled=True)  72.6 us
    unnamed x500, local copies, waits for them, and re-layouts  70.4 us
    ppermute x16, waiting for transfers between devices, flipped(): return lax.ppermute(value, ('dp', 'tensor'), pairs)  66.4 us
    dot_general x29, matrix products, product_t(): lax.dot_general(left, right, (((left.ndim - 1,), (1,)), ((), ())), prefer...  49.6 us
    dot_general x32, matrix products, product(): return jnp.dot(left, right, preferred_element_type=jnp.float32)  46.6 us
    unnamed x1, blocking collectives  36.3 us
  transfers between devices with their start and end apart: 32, of which 13 were waited for; matrix products, arithmetic and copies ran while one was open for 32% of the time, Pallas kernels for 0%

profile of v1, /device:TPU:0, one launch (start us, length us, event | category | flops | bytes accessed | tf_op | source)
XLA Modules:
  0.0 1050.9 jit_solution(2550484007015176649)
XLA Ops:
  15.4 10.0 all-gather.2
  30.3 15.9 %all-gather.10.cloned.1.call-done = bf16[2056,768]{0,1:T(8,128)(2,1)} async-done(((bf16[2056,96]{0,1:T(8,128)(2,1)}), bf16[2056,768]{0,1:T(8,128)(2,1)}) %all-gather.10.cloned.1.call-update) | async-done | bytes 3158032 | tf_op jit(solution)/shard_map/all_gather | solution.py:500
  50.3 2.7 multiply_convert_fusion.22
  53.9 36.3 %all-reduce.3 = bf16[64,2688]{1,0:T(8,128)(2,1)S(1)} all-reduce(f32[64,2688]{1,0:T(8,128)S(1)} %pad_maximum_fusion.8), channel_id=4, replica_groups=mesh['dp'=8,'tensor'=4] {'dp'}, use_global_device_ids=true, to_apply=%region_5.6.clone | all-reduce | flops 172032 | bytes 1032192
  90.3 14.6 %all-gather = bf16[32,2688]{1,0:T(8,128)(2,1)S(1)} all-gather(bf16[8,2688]{1,0:T(8,128)(2,1)S(1)} %dynamic-slice_convert_fusion.5), channel_id=2, replica_groups=mesh['dp'=8,'tensor'=4] {'tensor'}, dimensions={0}, use_global_device_ids=true | all-gather | bytes 215040 | tf_op jit(solution)/shard_map/all_gather | solution.py:546
  107.5 48.8 %all-gather.12.cloned.1.call-done = bf16[3,3072,768]{2,1,0:T(8,128)(2,1)} async-done(((bf16[3,96,768]{2,1,0:T(8,128)(2,1)}), bf16[3,3072,768]{2,1,0:T(8,128)(2,1)}) %all-gather.12.cloned.1.call-update) | async-done | bytes 14155792 | tf_op jit(solution)/shard_map/all_gather | solution.py:512
  156.3 4.8 slice.489
  161.1 6.7 copy.493
  167.8 9.7 reshape_squeeze.6
  177.5 4.5 fusion.206
  194.6 2.7 copy.504
  197.3 8.0 slice.498
  219.5 13.5 %fusion.109 = f32[2,256,768]{2,1,0:T(8,128)S(1)} fusion(bf16[2,4,768,768]{3,2,1,0:T(8,128)(2,1)S(1)} %bitcast.756, f32[2,256,768]{2,1,0:T(8,128)S(1)} %convolution_add_fusion.8), kind=kOutput, calls=%fused_computation.356 | convolution fusion | flops 607518720 | bytes 4325376 | tf_op jit(solution)/shard_map/dot_general | solution.py:47
  237.0 23.8 %all-gather.14.cloned.1.call-done = bf16[3,3072,768]{2,1,0:T(8,128)(2,1)} async-done(((bf16[3,96,768]{2,1,0:T(8,128)(2,1)}), bf16[3,3072,768]{2,1,0:T(8,128)(2,1)}) %all-gather.14.cloned.1.call-update) | async-done | bytes 14155792 | tf_op jit(solution)/shard_map/all_gather | solution.py:512
  260.8 4.8 slice.513
  265.6 6.6 copy.508
  272.2 9.7 reshape_squeeze.7
  282.0 4.3 fusion.205
  309.9 4.4 convolution_convert_fusion.4
  318.7 7.9 slice.521
  329.0 3.7 fusion.117
  365.1 7.6 multiply_reduce_fusion.1
  372.7 4.6 multiply_convert_fusion.1
  401.9 5.5 multiply_reduce_fusion
  455.8 2.9 fusion.10
  462.6 2.9 fusion.8
  470.6 3.6 stack.152
  476.6 3.6 stack.153
  482.5 3.6 stack.154
  488.4 3.6 stack.155
  492.0 10.5 maximum_bitcast_fusion
  509.0 3.6 stack.158
  514.9 3.6 stack.159
  520.9 3.6 stack.160
  526.8 3.6 stack.161
  530.4 10.1 maximum_bitcast_fusion.1
  553.3 3.0 fusion.14
  564.5 12.8 %collective-permute-done.5 = bf16[1,2,384,768]{2,3,1,0:T(8,128)(2,1)} collective-permute-done((bf16[1,2,384,768]{2,3,1,0:T(8,128)(2,1)}, bf16[1,2,384,768]{2,3,1,0:T(8,128)(2,1)}, u32[]{:S(2)}, u32[]{:S(2)}) %collective-permute-start.5) | collective-permute-done | bytes 1179680 | tf_op jit(solution)/shard_map/ppermute | solution.py:177
  580.7 3.8 fusion.1
  589.2 3.7 fusion
  596.9 2.7 collective-permute-done.9
  608.2 23.9 %collective-permute-done.10 = bf16[1,1,384,768]{2,3,1,0:T(8,128)(2,1)} collective-permute-done((bf16[1,1,384,768]{2,3,1,0:T(8,128)(2,1)}, bf16[1,1,384,768]{2,3,1,0:T(8,128)(2,1)}, u32[]{:S(2)}, u32[]{:S(2)}) %collective-permute-start.10) | collective-permute-done | bytes 589856 | tf_op jit(solution)/shard_map/ppermute | solution.py:177
  639.1 5.6 collective-permute-done.13
  644.7 3.1 fusion.12
  650.0 20.0 %collective-permute-done.17 = bf16[2,2,384,768]{3,2,0,1:T(8,128)(2,1)} collective-permute-done((bf16[2,2,384,768]{3,2,0,1:T(8,128)(2,1)}, bf16[2,2,384,768]{3,2,0,1:T(8,128)(2,1)}, u32[]{:S(2)}, u32[]{:S(2)}) %collective-permute-start.17) | collective-permute-done | bytes 2359328 | tf_op jit(solution)/shard_map/ppermute | solution.py:177
  675.0 3.6 copy.743
  687.5 2.7 slice_convert_fusion
  703.2 77.6 %psum.14 = bf16[64,96]{1,0:T(8,128)(2,1)S(1)} all-reduce(bf16[64,96]{1,0:T(8,128)(2,1)S(1)} %fusion.107), channel_id=1, replica_groups=mesh['dp'=8,'tensor'=4] {'tensor'}, use_global_device_ids=true, to_apply=%region_64.65 | all-reduce | flops 6144 | bytes 24576 | tf_op jit(solution)/shard_map/psum | solution.py:649
  783.3 9.6 all-gather.4
  831.0 84.9 %psum.15 = f32[5]{0:T(128)S(1)} all-reduce(f32[5]{0:T(128)S(1)} %pad_maximum_fusion.13), channel_id=1, replica_groups=mesh['dp'=8,'tensor'=4] {'dp','tensor'}, use_global_device_ids=true, to_apply=%region_69.70 | all-reduce | flops 5 | bytes 40 | tf_op jit(solution)/shard_map/psum | solution.py:716
  917.6 11.7 %add_divide_fusion = (f32[3592,384]{1,0:T(8,128)}, f32[3592,384]{1,0:T(8,128)}, f32[3592,384]{1,0:T(8,128)}) fusion(f32[3592,384]{1,0:T(8,128)} %copy-done.8, f32[]{:T(128)} %get-tuple-element.96, f32[3592,384]{1,0:T(8,128)} %param.44, f32[3592,384]{1,0:T(8,128)} %param.45), kind=kLoop, calls=%fused_computation.28 | loop fusion | flops 16551936 | bytes 33103876 | tf_op jit(solution)/shard_map/div | solution.py:450
  929.3 6.4 copy.609
  935.7 3.0 dynamic-slice_convert_fusion
  938.8 6.8 add_divide_fusion.2
  948.8 8.6 add_divide_fusion.1
  961.4 4.5 add_divide_fusion.3
  965.9 4.9 reshape.884
  970.8 2.6 constant_dynamic-slice_fusion.4
  973.5 5.8 copy.702
  979.8 2.8 constant_dynamic-slice_fusion.5
  982.6 4.5 copy.701
  997.2 7.0 collective-permute-done.21
  1015.2 11.1 %collective-permute-done.23 = bf16[2,2,1,1,96,768]{5,4,1,0,3,2:T(8,128)(2,1)S(1)} collective-permute-done((bf16[2,2,1,1,96,768]{5,4,1,0,3,2:T(8,128)(2,1)S(1)}, bf16[2,2,1,1,96,768]{5,4,1,0,3,2:T(8,128)(2,1)S(1)}, u32[]{:S(2)}, u32[]{:S(2)}) %collective-permute-start.23) | collective-permute-done | bytes 589856 | tf_op jit(solution)/shard_map/ppermute | solution.py:39
  1028.2 12.7 %collective-permute-done.27 = bf16[3592,1,1,96]{0,3,2,1:T(8,128)(2,1)S(1)} collective-permute-done((bf16[3592,1,1,96]{0,3,2,1:T(8,128)(2,1)S(1)}, bf16[3592,1,1,96]{0,3,2,1:T(8,128)(2,1)S(1)}, u32[]{:S(2)}, u32[]{:S(2)}) %collective-permute-start.27) | collective-permute-done | bytes 689696 | tf_op jit(solution)/shard_map/ppermute | solution.py:39
  (902 shorter events, 362.5 us)
Async XLA Ops:
  7.2 39.0 %all-gather.10.cloned.1.call-start = ((), (), s32[]{:S(2)}) async-start(), calls=%async_computation | async-start | bytes 3760128 | tf_op jit(solution)/shard_map/all_gather | solution.py:500
  9.7 146.6 %all-gather.12.cloned.1.call-start = ((), (), s32[]{:S(2)}) async-start(), calls=%async_computation.1 | async-start | bytes 14598144 | tf_op jit(solution)/shard_map/all_gather | solution.py:512
  12.0 248.8 %all-gather.14.cloned.1.call-start = ((), (), s32[]{:S(2)}) async-start(), calls=%async_computation.2 | async-start | bytes 14598144 | tf_op jit(solution)/shard_map/all_gather | solution.py:512
  13.2 661.8 %all-gather.16.cloned.1.call-start = ((), (), s32[]{:S(2)}) async-start(), calls=%async_computation.3 | async-start | bytes 7805952 | tf_op jit(solution)/shard_map/all_gather | solution.py:617
  14.2 15.9 %collective-permute-start = (f32[2,1]{0,1:T(1,128)S(1)}, f32[2,1]{0,1:T(1,128)S(1)}, u32[]{:S(2)}, u32[]{:S(2)}) collective-permute-start(f32[2,1]{0,1:T(1,128)S(1)} %dynamic-slice_bitcast_fusion.9), channel_id=1, source_target_pairs={{0,4},{1,5},{2,6},{3,7},{4,0},{5,1},{6,2},{7,3},{8,12},{9,13},{10,... | collective-permute-start | bytes 32 | tf_op jit(solution)/shard_map/ppermute | solution.py:177
  14.7 15.5 %collective-permute-start.2 = (f32[2,256,16]{1,2,0:T(8,128)S(1)}, f32[2,256,16]{1,2,0:T(8,128)S(1)}, u32[]{:S(2)}, u32[]{:S(2)}) collective-permute-start(f32[2,256,16]{1,2,0:T(8,128)S(1)} %constant_dynamic-slice_fusion.20), channel_id=1, source_target_pairs={{0,4},{1,5},{2,6},{3,7},{4,0},{5,1},{6,2},{7,3},{8,12},{9,13},{10,... | collective-permute-start | bytes 98312 | tf_op jit(solution)/shard_map/ppermute | solution.py:177
  14.8 15.4 %collective-permute-start.1 = (f32[2,256,16]{1,2,0:T(8,128)S(1)}, f32[2,256,16]{1,2,0:T(8,128)S(1)}, u32[]{:S(2)}, u32[]{:S(2)}) collective-permute-start(f32[2,256,16]{1,2,0:T(8,128)S(1)} %constant_dynamic-slice_fusion.21), channel_id=1, source_target_pairs={{0,4},{1,5},{2,6},{3,7},{4,0},{5,1},{6,2},{7,3},{8,12},{9,13},{10,... | collective-permute-start | bytes 98312 | tf_op jit(solution)/shard_map/ppermute | solution.py:177
  25.6 27.8 %copy-start.59 = (bf16[2,96,1152]{2,1,0:T(8,128)(2,1)}, bf16[2,96,1152]{2,1,0:T(8,128)(2,1)S(1)}, u32[]{:S(2)}) copy-start(bf16[2,96,1152]{2,1,0:T(8,128)(2,1)S(1)} %convert_element_type.687) | copy-start | bytes 1327108
  30.3 74.7 %copy-start.133 = (bf16[2,256,16]{1,2,0:T(8,128)(2,1)}, bf16[2,256,16]{1,2,0:T(8,128)(2,1)S(1)}, u32[]{:S(2)}) copy-start(bf16[2,256,16]{1,2,0:T(8,128)(2,1)S(1)} %add_convert_fusion.13) | copy-start | bytes 49156
  104.9 1.9 collective-permute-start.3
  106.5 104.9 %copy-start.2 = (f32[2,256,768]{2,1,0:T(8,128)}, f32[2,256,768]{2,1,0:T(8,128)S(1)}, u32[]{:S(2)}) copy-start(f32[2,256,768]{2,1,0:T(8,128)S(1)} %get-tuple-element.175) | copy-start | bytes 4718596
  106.8 54.3 %copy-start.155 = (f32[2,256]{1,0:T(2,128)}, f32[2,256]{1,0:T(2,128)S(1)}, u32[]{:S(2)}) copy-start(f32[2,256]{1,0:T(2,128)S(1)} %add_rsqrt_fusion.4) | copy-start | bytes 6148
  107.0 233.1 %copy-start.148 = (f32[2,768]{1,0:T(2,128)}, f32[2,768]{1,0:T(2,128)S(1)}, u32[]{:S(2)}) copy-start(f32[2,768]{1,0:T(2,128)S(1)} %get-tuple-element.156) | copy-start | bytes 18436
  107.0 238.0 %copy-start.142 = (f32[2,768]{1,0:T(2,128)}, f32[2,768]{1,0:T(2,128)S(1)}, u32[]{:S(2)}) copy-start(f32[2,768]{1,0:T(2,128)S(1)} %get-tuple-element.155) | copy-start | bytes 18436
  107.0 54.1 %copy-start.140 = (f32[2,768]{1,0:T(2,128)}, f32[2,768]{1,0:T(2,128)S(1)}, u32[]{:S(2)}) copy-start(f32[2,768]{1,0:T(2,128)S(1)} %get-tuple-element.154) | copy-start | bytes 18436
  107.4 74.7 %copy-start.99 = (bf16[2,256,768]{2,1,0:T(8,128)(2,1)}, bf16[2,256,768]{2,1,0:T(8,128)(2,1)S(1)}, u32[]{:S(2)}) copy-start(bf16[2,256,768]{2,1,0:T(8,128)(2,1)S(1)} %add_convert_fusion.10) | copy-start | bytes 2359300
  184.3 21.0 %copy-start.29 = (bf16[2,256,768]{1,2,0:T(8,128)(2,1)}, bf16[2,256,768]{1,2,0:T(8,128)(2,1)S(1)}, u32[]{:S(2)}) copy-start(bf16[2,256,768]{1,2,0:T(8,128)(2,1)S(1)} %copy.499) | copy-start | bytes 2359300
  217.6 15.4 %copy-start.195 = (f32[2,256,768]{2,1,0:T(8,128)}, f32[2,256,768]{2,1,0:T(8,128)S(1)}, u32[]{:S(2)}) copy-start(f32[2,256,768]{2,1,0:T(8,128)S(1)} %convolution_add_fusion.6) | copy-start | bytes 4718596
  218.4 15.7 %copy-start.76 = (f32[2,256,768]{2,1,0:T(8,128)}, f32[2,256,768]{2,1,0:T(8,128)S(1)}, u32[]{:S(2)}) copy-start(f32[2,256,768]{2,1,0:T(8,128)S(1)} %convolution_add_fusion.5) | copy-start | bytes 4718596
  329.0 17.5 %copy-start.198 = (f32[2,256,768]{2,1,0:T(8,128)}, f32[2,256,768]{2,1,0:T(8,128)S(1)}, u32[]{:S(2)}) copy-start(f32[2,256,768]{2,1,0:T(8,128)S(1)} %convolution_add_fusion.2) | copy-start | bytes 4718596
  333.5 15.1 %copy-start.200 = (f32[2,256,768]{2,1,0:T(8,128)}, f32[2,256,768]{2,1,0:T(8,128)S(1)}, u32[]{:S(2)}) copy-start(f32[2,256,768]{2,1,0:T(8,128)S(1)} %convolution_add_fusion.3) | copy-start | bytes 4718596
  335.8 15.0 %copy-start.202 = (f32[2,256,768]{2,1,0:T(8,128)}, f32[2,256,768]{2,1,0:T(8,128)S(1)}, u32[]{:S(2)}) copy-start(f32[2,256,768]{2,1,0:T(8,128)S(1)} %convolution_add_fusion.1) | copy-start | bytes 4718596
  337.7 15.2 %copy-start.79 = (f32[2,256,768]{2,1,0:T(8,128)}, f32[2,256,768]{2,1,0:T(8,128)S(1)}, u32[]{:S(2)}) copy-start(f32[2,256,768]{2,1,0:T(8,128)S(1)} %convolution_add_fusion) | copy-start | bytes 4718596
  461.1 119.6 %collective-permute-start.12 = (bf16[2,2,2,384,768]{4,3,0,1,2:T(8,128)(2,1)}, bf16[2,2,2,384,768]{4,3,0,1,2:T(8,128)(2,1)}, u32[]{:S(2)}, u32[]{:S(2)}) collective-permute-start(bf16[2,2,2,384,768]{4,3,0,1,2:T(8,128)(2,1)} %bitcast.715), channel_id=1, source_target_pairs={{0,4},{1,5},{2,6},{3,7},{4,0},{5,1},{6,2},{7,3},{8,12},{9,13},{10,... | collective-permute-start | bytes 14155784 | tf_op jit(solution)/shard_map/ppermute | solution.py:177
  468.0 121.2 %collective-permute-start.16 = (bf16[2,2,2,384,768]{4,3,0,1,2:T(8,128)(2,1)}, bf16[2,2,2,384,768]{4,3,0,1,2:T(8,128)(2,1)}, u32[]{:S(2)}, u32[]{:S(2)}) collective-permute-start(bf16[2,2,2,384,768]{4,3,0,1,2:T(8,128)(2,1)} %bitcast.714), channel_id=1, source_target_pairs={{0,4},{1,5},{2,6},{3,7},{4,0},{5,1},{6,2},{7,3},{8,12},{9,13},{10,... | collective-permute-start | bytes 14155784 | tf_op jit(solution)/shard_map/ppermute | solution.py:177
  506.4 46.9 %collective-permute-start.4 = (bf16[1,2,2,384,768]{3,4,2,1,0:T(8,128)(2,1)}, bf16[1,2,2,384,768]{3,4,2,1,0:T(8,128)(2,1)}, u32[]{:S(2)}, u32[]{:S(2)}) collective-permute-start(bf16[1,2,2,384,768]{3,4,2,1,0:T(8,128)(2,1)} %dynamic-slice_bitcast_fusion.2), channel_id=1, source_target_pairs={{0,4},{1,5},{2,6},{3,7},{4,0},{5,1},{6,2},{7,3},{8,12},{9,13},{10,... | collective-permute-start | bytes 7077896 | tf_op jit(solution)/shard_map/ppermute | solution.py:177
  545.0 15.6 %collective-permute-start.8 = (bf16[1,2,2,384,768]{3,4,1,2,0:T(8,128)(2,1)}, bf16[1,2,2,384,768]{3,4,1,2,0:T(8,128)(2,1)}, u32[]{:S(2)}, u32[]{:S(2)}) collective-permute-start(bf16[1,2,2,384,768]{3,4,1,2,0:T(8,128)(2,1)} %bitcast.717), channel_id=1, source_target_pairs={{0,4},{1,5},{2,6},{3,7},{4,0},{5,1},{6,2},{7,3},{8,12},{9,13},{10,... | collective-permute-start | bytes 7077896 | tf_op jit(solution)/shard_map/ppermute | solution.py:177
  559.1 18.2 %collective-permute-start.5 = (bf16[1,2,384,768]{2,3,1,0:T(8,128)(2,1)}, bf16[1,2,384,768]{2,3,1,0:T(8,128)(2,1)}, u32[]{:S(2)}, u32[]{:S(2)}) collective-permute-start(bf16[1,2,384,768]{2,3,1,0:T(8,128)(2,1)} %dynamic-slice_bitcast_fusion.4), channel_id=1, source_target_pairs={{0,16},{1,17},{2,18},{3,19},{4,5},{5,4},{6,7},{7,6},{8,24},{9,25},... | collective-permute-start | bytes 3538952 | tf_op jit(solution)/shard_map/ppermute | solution.py:177
  560.6 20.2 %slice-start.6 = ((s8[4718592]{0:T(1024)(128)(4,1)}), s8[4194304]{0:T(1024)(128)(4,1)S(1)}, s32[]{:S(2)}) async-start(s8[4718592]{0:T(1024)(128)(4,1)} %bitcast.729), calls=%async_computation.10 | async-start | bytes 8388608
  563.0 17.7 %slice-start.7 = ((s8[4718592]{0:T(1024)(128)(4,1)}), s8[524288]{0:T(1024)(128)(4,1)S(1)}, s32[]{:S(2)}) async-start(s8[4718592]{0:T(1024)(128)(4,1)} %bitcast.729), calls=%async_computation.11 | async-start | bytes 1048576
  563.3 14.0 %copy-start.26 = (bf16[1,2,2,384,768]{3,4,2,1,0:T(8,128)(2,1)S(1)}, bf16[1,2,2,384,768]{3,4,2,1,0:T(8,128)(2,1)}, u32[]{:S(2)}) copy-start(bf16[1,2,2,384,768]{3,4,2,1,0:T(8,128)(2,1)} %copy-done.25) | copy-start | bytes 7077892
  563.4 36.2 %collective-permute-start.9 = (bf16[1,2,384,768]{2,3,1,0:T(8,128)(2,1)S(1)}, bf16[1,2,384,768]{2,3,1,0:T(8,128)(2,1)}, u32[]{:S(2)}, u32[]{:S(2)}) collective-permute-start(bf16[1,2,384,768]{2,3,1,0:T(8,128)(2,1)S(1)} %dynamic-slice_bitcast_fusion.3), channel_id=1, source_target_pairs={{0,16},{1,17},{2,18},{3,19},{4,5},{5,4},{6,7},{7,6},{8,24},{9,25},... | collective-permute-start | bytes 3538952 | tf_op jit(solution)/shard_map/ppermute | solution.py:177
  579.7 24.6 %collective-permute-start.6 = (bf16[1,1,384,768]{2,3,1,0:T(8,128)(2,1)}, bf16[1,1,384,768]{2,3,1,0:T(8,128)(2,1)}, u32[]{:S(2)}, u32[]{:S(2)}) collective-permute-start(bf16[1,1,384,768]{2,3,1,0:T(8,128)(2,1)} %constant_dynamic-slice_fusion.18), channel_id=1, source_target_pairs={{0,1},{1,0},{2,3},{3,2},{4,20},{5,21},{6,22},{7,23},{8,9},{9,8},{1... | collective-permute-start | bytes 1769480 | tf_op jit(solution)/shard_map/ppermute | solution.py:177
  587.9 56.9 %collective-permute-start.13 = (bf16[2,2,384,768]{3,2,0,1:T(8,128)(2,1)}, bf16[2,2,384,768]{3,2,0,1:T(8,128)(2,1)}, u32[]{:S(2)}, u32[]{:S(2)}) collective-permute-start(bf16[2,2,384,768]{3,2,0,1:T(8,128)(2,1)} %dynamic-slice_bitcast_fusion.1), channel_id=1, source_target_pairs={{0,16},{1,17},{2,18},{3,19},{4,5},{5,4},{6,7},{7,6},{8,24},{9,25},... | collective-permute-start | bytes 7077896 | tf_op jit(solution)/shard_map/ppermute | solution.py:177
  596.2 73.8 %collective-permute-start.17 = (bf16[2,2,384,768]{3,2,0,1:T(8,128)(2,1)}, bf16[2,2,384,768]{3,2,0,1:T(8,128)(2,1)}, u32[]{:S(2)}, u32[]{:S(2)}) collective-permute-start(bf16[2,2,384,768]{3,2,0,1:T(8,128)(2,1)} %dynamic-slice_bitcast_fusion), channel_id=1, source_target_pairs={{0,16},{1,17},{2,18},{3,19},{4,5},{5,4},{6,7},{7,6},{8,24},{9,25},... | collective-permute-start | bytes 7077896 | tf_op jit(solution)/shard_map/ppermute | solution.py:177
  602.1 30.0 %collective-permute-start.10 = (bf16[1,1,384,768]{2,3,1,0:T(8,128)(2,1)}, bf16[1,1,384,768]{2,3,1,0:T(8,128)(2,1)}, u32[]{:S(2)}, u32[]{:S(2)}) collective-permute-start(bf16[1,1,384,768]{2,3,1,0:T(8,128)(2,1)} %constant_dynamic-slice_fusion.15), channel_id=1, source_target_pairs={{0,1},{1,0},{2,3},{3,2},{4,20},{5,21},{6,22},{7,23},{8,9},{9,8},{1... | collective-permute-start | bytes 1769480 | tf_op jit(solution)/shard_map/ppermute | solution.py:177
  603.0 31.2 %copy-start.169 = (s32[64]{0:T(128)S(1)}, s32[64]{0:T(128)}, u32[]{:S(2)}) copy-start(s32[64]{0:T(128)} %get-tuple-element.163) | copy-start | bytes 772
  603.0 31.3 %copy-start.164 = (s32[64,2]{0,1:T(2,128)S(1)}, s32[64,2]{0,1:T(2,128)}, u32[]{:S(2)}) copy-start(s32[64,2]{0,1:T(2,128)} %copy-done.163) | copy-start | bytes 1540
  603.0 32.0 %copy-start.168 = (f32[128]{0:T(128)S(1)}, f32[128]{0:T(128)}, u32[]{:S(2)}) copy-start(f32[128]{0:T(128)} %copy-done.167) | copy-start | bytes 1540
  606.3 31.5 %collective-permute-start.7 = (bf16[1,384,768]{1,2,0:T(8,128)(2,1)}, bf16[1,384,768]{1,2,0:T(8,128)(2,1)S(1)}, u32[]{:S(2)}, u32[]{:S(2)}) collective-permute-start(bf16[1,384,768]{1,2,0:T(8,128)(2,1)} %fusion.126), channel_id=1, source_target_pairs={{0,0},{1,1},{2,4},{3,5},{4,2},{5,3},{6,6},{7,7},{8,8},{9,9},{10,12... | collective-permute-start | bytes 1769480 | tf_op jit(solution)/shard_map/ppermute | solution.py:368
  633.3 4.5 collective-permute-start.11
  637.9 32.1 %slice-start.4 = ((s8[4718592]{0:T(1024)(128)(4,1)}), s8[4194304]{0:T(1024)(128)(4,1)S(1)}, s32[]{:S(2)}) async-start(s8[4718592]{0:T(1024)(128)(4,1)} %bitcast.727), calls=%async_computation.8 | async-start | bytes 8388608
  639.1 30.9 %slice-start.5 = ((s8[4718592]{0:T(1024)(128)(4,1)}), s8[524288]{0:T(1024)(128)(4,1)S(1)}, s32[]{:S(2)}) async-start(s8[4718592]{0:T(1024)(128)(4,1)} %bitcast.727), calls=%async_computation.9 | async-start | bytes 1048576
  647.8 24.4 %copy-start.21 = (bf16[2,2,384,768]{3,2,0,1:T(8,128)(2,1)}, bf16[2,2,384,768]{3,2,0,1:T(8,128)(2,1)S(1)}, u32[]{:S(2)}) copy-start(bf16[2,2,384,768]{3,2,0,1:T(8,128)(2,1)S(1)} %fusion.12) | copy-start | bytes 7077892
  649.0 167.2 %collective-permute-start.14 = (bf16[2,1,384,768]{3,2,0,1:T(8,128)(2,1)}, bf16[2,1,384,768]{3,2,0,1:T(8,128)(2,1)}, u32[]{:S(2)}, u32[]{:S(2)}) collective-permute-start(bf16[2,1,384,768]{3,2,0,1:T(8,128)(2,1)} %constant_dynamic-slice_fusion.14), channel_id=1, source_target_pairs={{0,1},{1,0},{2,3},{3,2},{4,20},{5,21},{6,22},{7,23},{8,9},{9,8},{1... | collective-permute-start | bytes 3538952 | tf_op jit(solution)/shard_map/ppermute | solution.py:177
  674.1 144.8 %collective-permute-start.18 = (bf16[2,1,384,768]{3,2,0,1:T(8,128)(2,1)}, bf16[2,1,384,768]{3,2,0,1:T(8,128)(2,1)}, u32[]{:S(2)}, u32[]{:S(2)}) collective-permute-start(bf16[2,1,384,768]{3,2,0,1:T(8,128)(2,1)} %constant_dynamic-slice_fusion.13), channel_id=1, source_target_pairs={{0,1},{1,0},{2,3},{3,2},{4,20},{5,21},{6,22},{7,23},{8,9},{9,8},{1... | collective-permute-start | bytes 3538952 | tf_op jit(solution)/shard_map/ppermute | solution.py:177
  703.0 90.1 %copy-start.118 = (bf16[64,1152]{1,0:T(8,128)(2,1)}, bf16[64,1152]{1,0:T(8,128)(2,1)S(1)}, u32[]{:S(2)}) copy-start(bf16[64,1152]{1,0:T(8,128)(2,1)S(1)} %constant_dynamic-slice_fusion.10) | copy-start | bytes 442372
  703.2 90.6 %copy-start.204 = (f32[64,768]{1,0:T(8,128)S(1)}, f32[64,768]{1,0:T(8,128)}, u32[]{:S(2)}) copy-start(f32[64,768]{1,0:T(8,128)} %get-tuple-element.171) | copy-start | bytes 589828
  818.0 6.4 collective-permute-start.15
  820.5 3.9 collective-permute-start.19
  938.8 70.7 %collective-permute-start.26 = (bf16[3592,2,1,96]{0,3,2,1:T(8,128)(2,1)}, bf16[3592,2,1,96]{0,3,2,1:T(8,128)(2,1)}, u32[]{:S(2)}, u32[]{:S(2)}) collective-permute-start(bf16[3592,2,1,96]{0,3,2,1:T(8,128)(2,1)} %dynamic-slice_convert_fusion), channel_id=1, source_target_pairs={{0,4},{4,0},{8,12},{12,8},{16,20},{20,16},{24,28},{28,24},{1,5},{5... | collective-permute-start | bytes 4137992 | tf_op jit(solution)/shard_map/ppermute | solution.py:39
  947.8 46.4 %collective-permute-start.24 = (bf16[2,2,1,96,1152]{4,3,0,2,1:T(8,128)(2,1)}, bf16[2,2,1,96,1152]{4,3,0,2,1:T(8,128)(2,1)}, u32[]{:S(2)}, u32[]{:S(2)}) collective-permute-start(bf16[2,2,1,96,1152]{4,3,0,2,1:T(8,128)(2,1)} %copy.740), channel_id=1, source_target_pairs={{0,4},{4,0},{8,12},{12,8},{16,20},{20,16},{24,28},{28,24},{1,5},{5... | collective-permute-start | bytes 2654216 | tf_op jit(solution)/shard_map/ppermute | solution.py:39
  960.3 45.4 %collective-permute-start.22 = (bf16[2,2,2,1,96,768]{5,4,1,0,3,2:T(8,128)(2,1)}, bf16[2,2,2,1,96,768]{5,4,1,0,3,2:T(8,128)(2,1)}, u32[]{:S(2)}, u32[]{:S(2)}) collective-permute-start(bf16[2,2,2,1,96,768]{5,4,1,0,3,2:T(8,128)(2,1)} %copy.739), channel_id=1, source_target_pairs={{0,4},{4,0},{8,12},{12,8},{16,20},{20,16},{24,28},{28,24},{1,5},{5... | collective-permute-start | bytes 3538952 | tf_op jit(solution)/shard_map/ppermute | solution.py:39
  979.3 11.1 %collective-permute-start.20 = (bf16[2,4,2,1,96,192]{5,4,1,0,3,2:T(8,128)(2,1)}, bf16[2,4,2,1,96,192]{5,4,1,0,3,2:T(8,128)(2,1)}, u32[]{:S(2)}, u32[]{:S(2)}) collective-permute-start(bf16[2,4,2,1,96,192]{5,4,1,0,3,2:T(8,128)(2,1)} %copy.702), channel_id=1, source_target_pairs={{0,4},{4,0},{8,12},{12,8},{16,20},{20,16},{24,28},{28,24},{1,5},{5... | collective-permute-start | bytes 1769480 | tf_op jit(solution)/shard_map/ppermute | solution.py:39
  990.3 15.4 %slice-start.18 = ((s8[4718592]{0:T(1024)(128)(4,1)}), s8[4194304]{0:T(1024)(128)(4,1)S(1)}, s32[]{:S(2)}) async-start(s8[4718592]{0:T(1024)(128)(4,1)} %bitcast.786), calls=%async_computation.22 | async-start | bytes 8388608
  991.9 12.3 %collective-permute-start.21 = (bf16[2,4,1,1,96,192]{5,4,1,0,3,2:T(8,128)(2,1)S(1)}, bf16[2,4,1,1,96,192]{5,4,1,0,3,2:T(8,128)(2,1)S(1)}, u32[]{:S(2)}, u32[]{:S(2)}) collective-permute-start(bf16[2,4,1,1,96,192]{5,4,1,0,3,2:T(8,128)(2,1)S(1)} %dynamic-slice_convert_fusion.4), channel_id=1, source_target_pairs={{0,8},{4,12},{8,0},{12,4},{16,24},{20,28},{24,16},{28,20},{1,9},{5... | collective-permute-start | bytes 884744 | tf_op jit(solution)/shard_map/ppermute | solution.py:39
  994.2 15.2 %slice-start.10 = ((s8[5701632]{0:T(1024)(128)(4,1)}), s8[4194304]{0:T(1024)(128)(4,1)S(1)}, s32[]{:S(2)}) async-start(s8[5701632]{0:T(1024)(128)(4,1)} %bitcast.741), calls=%async_computation.14 | async-start | bytes 8388608
  995.8 17.8 %collective-permute-start.25 = (bf16[2,1,1,96,1152]{4,3,0,2,1:T(8,128)(2,1)S(1)}, bf16[2,1,1,96,1152]{4,3,0,2,1:T(8,128)(2,1)S(1)}, u32[]{:S(2)}, u32[]{:S(2)}) collective-permute-start(bf16[2,1,1,96,1152]{4,3,0,2,1:T(8,128)(2,1)S(1)} %dynamic-slice_convert_fusion.3), channel_id=1, source_target_pairs={{0,8},{4,12},{8,0},{12,4},{16,24},{20,28},{24,16},{28,20},{1,9},{5... | collective-permute-start | bytes 1327112 | tf_op jit(solution)/shard_map/ppermute | solution.py:39
  1007.3 19.0 %collective-permute-start.23 = (bf16[2,2,1,1,96,768]{5,4,1,0,3,2:T(8,128)(2,1)S(1)}, bf16[2,2,1,1,96,768]{5,4,1,0,3,2:T(8,128)(2,1)S(1)}, u32[]{:S(2)}, u32[]{:S(2)}) collective-permute-start(bf16[2,2,1,1,96,768]{5,4,1,0,3,2:T(8,128)(2,1)S(1)} %dynamic-slice_convert_fusion.2), channel_id=1, source_target_pairs={{0,8},{4,12},{8,0},{12,4},{16,24},{20,28},{24,16},{28,20},{1,9},{5... | collective-permute-start | bytes 1769480 | tf_op jit(solution)/shard_map/ppermute | solution.py:39
  1011.3 15.0 %copy-start.54 = (f32[2,2,96,768]{3,2,1,0:T(8,128)S(1)}, f32[2,2,96,768]{3,2,1,0:T(8,128)}, u32[]{:S(2)}) copy-start(f32[2,2,96,768]{3,2,1,0:T(8,128)} %param.29) | copy-start | bytes 3538948
  1011.3 15.0 %copy-start.82 = (f32[2,2,96,768]{3,2,1,0:T(8,128)S(1)}, f32[2,2,96,768]{3,2,1,0:T(8,128)}, u32[]{:S(2)}) copy-start(f32[2,2,96,768]{3,2,1,0:T(8,128)} %param.34) | copy-start | bytes 3538948
  1011.3 29.6 %collective-permute-start.27 = (bf16[3592,1,1,96]{0,3,2,1:T(8,128)(2,1)S(1)}, bf16[3592,1,1,96]{0,3,2,1:T(8,128)(2,1)S(1)}, u32[]{:S(2)}, u32[]{:S(2)}) collective-permute-start(bf16[3592,1,1,96]{0,3,2,1:T(8,128)(2,1)S(1)} %dynamic-slice_convert_fusion.1), channel_id=1, source_target_pairs={{0,8},{4,12},{8,0},{12,4},{16,24},{20,28},{24,16},{28,20},{1,9},{5... | collective-permute-start | bytes 2069000 | tf_op jit(solution)/shard_map/ppermute | solution.py:39
  1015.2 25.7 %copy-start.43 = (f32[3592,96]{0,1:T(8,128)S(1)}, f32[3592,96]{0,1:T(8,128)}, u32[]{:S(2)}) copy-start(f32[3592,96]{0,1:T(8,128)} %param.31) | copy-start | bytes 4137988
  1015.2 25.7 %copy-start.81 = (f32[3592,96]{0,1:T(8,128)S(1)}, f32[3592,96]{0,1:T(8,128)}, u32[]{:S(2)}) copy-start(f32[3592,96]{0,1:T(8,128)} %param.36) | copy-start | bytes 4137988
  (193 other events, 627.0 us)
Sparse Core Ops, SparseCore 0:
  10.5 35.7 all-gather.9
  49.7 106.5 all-gather.11
  159.8 100.9 all-gather.13
  553.4 94.8 all-gather.15

commit v2 on v1

--- a/solution.py
+++ b/solution.py
@@ -196,15 +196,15 @@
     middle = stream + mod_parts[2] * branch_one
     normed_two, inverse_two = normalize(middle)
     hidden_two = (normed_two * (1.0 + mod_parts[4]) + mod_parts[3]).astype(LOW_TYPE)
-    unit_width = mlp_now.shape[-1]
+    unit_width = mlp_now[0][0].shape[-1]
     before = [
-        product(hidden_two, mlp_now[0, unit_at])
+        product(hidden_two, mlp_now[0][unit_at])
         + bias_layer[3 * width_all + unit_at * unit_width : 3 * width_all + (unit_at + 1) * unit_width]
-        for unit_at in range(mlp_now.shape[1])
+        for unit_at in range(len(mlp_now[0]))
     ]
     activated = [gelu_tanh(part).astype(LOW_TYPE) for part in before]
     branch_two = bias_layer[3 * width_all + FF : 4 * width_all + FF] + sum(
-        product_t(part, mlp_now[1, unit_at]) for unit_at, part in enumerate(activated)
+        product_t(part, mlp_now[1][unit_at]) for unit_at, part in enumerate(activated)
     )
     result = middle + mod_parts[5] * branch_two
     kept_state = (
@@ -227,7 +227,91 @@
     return (result, kept_state)
 
 
-def layer_backward(grad_out, mod_parts, attn_now, mlp_now, kept_state):
+def exchanged(value, mask):
+    count = lax.axis_size("dp") * lax.axis_size("tensor")
+    return lax.ppermute(value, ("dp", "tensor"), [(source, source ^ mask) for source in range(count)])
+
+
+def half_of(value, axis, bit):
+    width = value.shape[axis] // 2
+    return lax.dynamic_slice_in_dim(value, bit * width, width, axis)
+
+
+def summed_low(left, right):
+    return (left.astype(jnp.float32) + right.astype(jnp.float32)).astype(LOW_TYPE)
+
+
+def rows_halved(value):
+    stretch = lax.axis_index("dp") // GROUPS
+    stretches = lax.axis_size("dp") // GROUPS
+    for bit_at in reversed(range(stretches.bit_length() - 1)):
+        bit = stretch >> bit_at & 1
+        received = exchanged(
+            half_of(value, 0, 1 - bit), lax.axis_size("tensor") * GROUPS << bit_at
+        )
+        value = summed_low(half_of(value, 0, bit), received)
+    return value
+
+
+def columns_halved(sent, kept):
+    return summed_low(kept, exchanged(sent, 1))
+
+
+def unit_halved(first, second):
+    picked = (lax.axis_index("tensor") & 1) == 1
+    return columns_halved(jnp.where(picked, first, second), jnp.where(picked, second, first))
+
+
+def pair_halved(first, second):
+    bit = lax.axis_index("tensor") & 1
+
+    def halves(bit_now):
+        return jnp.concatenate([half_of(first, 1, bit_now), half_of(second, 1, bit_now)], 1)
+
+    return columns_halved(halves(1 - bit), halves(bit))
+
+
+def core_summed(sent, kept):
+    return [
+        summed_low(own, exchanged(other, lax.axis_size("tensor"))) for other, own in zip(sent, kept)
+    ]
+
+
+def homeward(values):
+    shards = lax.axis_size("tensor")
+    pairs = []
+    for source in range(lax.axis_size("dp") * shards):
+        core, high = (source // shards & 1, source % shards >> 1)
+        pairs.append((source, source ^ (core ^ high) * (shards + shards // 2)))
+    return [lax.ppermute(value, ("dp", "tensor"), pairs) for value in values]
+
+
+def mlp_second(totals):
+    up_zero, up_one, down_zero, down_one = totals
+    return [rows_halved(up_zero), rows_halved(up_one), unit_halved(down_zero, down_one)]
+
+
+def mlp_third(totals):
+    up_zero, up_one, down = totals
+    return [unit_halved(up_zero, up_one), rows_halved(down)]
+
+
+def attn_second(totals):
+    query_key, value_map, out_map = totals
+    return [rows_halved(query_key), pair_halved(value_map, out_map)]
+
+
+def attn_third(totals):
+    query_key, value_out = totals
+    width = query_key.shape[1] // 2
+    return [pair_halved(query_key[:, :width], query_key[:, width:]), rows_halved(value_out)]
+
+
+def tied(value, flows):
+    return lax.optimization_barrier((value, flows))
+
+
+def layer_backward(grad_out, mod_parts, attn_now, mlp_now, kept_state, flows):
     (
         normed_one,
         inverse_one,
@@ -245,42 +329,58 @@
         activated,
         branch_two,
     ) = kept_state
+    core = lax.axis_index("dp") & 1
+    pair = len(activated) // 2
+    if flows:
+        flows = [mlp_second(flows[0]), flows[1]]
+        grad_out, flows = tied(grad_out, flows)
     grad_gate_two = jnp.sum(grad_out * branch_two, 1)
     downward = grad_out * mod_parts[5]
     down_low = downward.astype(LOW_TYPE)
     grad_pre = [
-        jax.vjp(gelu_tanh, part)[1](product(down_low, mlp_now[1, unit_at]))[0].astype(LOW_TYPE)
+        jax.vjp(gelu_tanh, part)[1](product(down_low, mlp_now[1][unit_at]))[0].astype(LOW_TYPE)
         for unit_at, part in enumerate(saved_pre)
     ]
-    grad_down = [weight_grad(down_low, part).astype(LOW_TYPE) for part in activated]
-    grad_up = [weight_grad(hidden_two, part).astype(LOW_TYPE) for part in grad_pre]
-    mlp_sums = reduced_blocks(mlp_blocks(jnp.stack([jnp.stack(grad_up), jnp.stack(grad_down)])))
+
+    def unit_grads(side):
+        picked = core == side
+        up = [jnp.where(picked, grad_pre[at + pair], grad_pre[at]) for at in range(pair)]
+        down = [jnp.where(picked, activated[at + pair], activated[at]) for at in range(pair)]
+        return [weight_grad(hidden_two, part).astype(LOW_TYPE) for part in up] + [
+            weight_grad(down_low, part).astype(LOW_TYPE) for part in down
+        ]
+
+    sent = unit_grads(0)
+    if flows:
+        flows = [mlp_third(flows[0]), attn_second(flows[1])]
+        sent, flows = tied(sent, flows)
+    mlp_sums = core_summed(sent, unit_grads(1))
     grad_hidden_two = sum(
-        product_t(part, mlp_now[0, unit_at]) for unit_at, part in enumerate(grad_pre)
+        product_t(part, mlp_now[0][unit_at]) for unit_at, part in enumerate(grad_pre)
     )
     grad_middle = grad_out + normalize_back(
         grad_hidden_two * (1.0 + mod_parts[4]), normed_two, inverse_two
     )
     grad_gate_one = jnp.sum(grad_middle * branch_one, 1)
     upward = grad_middle * mod_parts[2]
-    up_low = upward.astype(LOW_TYPE)
-    grad_out_map = weight_grad(up_low, attended)
+    up_low, mlp_sums = tied(upward.astype(LOW_TYPE), mlp_sums)
     grad_attended = product(up_low, attn_now[3]).astype(LOW_TYPE)
     grad_queries, grad_keys, grad_values = attend_back(
         queries, key_rows, values, log_total, grad_attended
     )
-    attn_sums = reduced_blocks(
-        attn_blocks(
-            jnp.stack(
-                [
-                    weight_grad(hidden_one, grad_queries).astype(LOW_TYPE),
-                    weight_grad(hidden_one, grad_keys).astype(LOW_TYPE),
-                    weight_grad(hidden_one, grad_values).astype(LOW_TYPE),
-                    grad_out_map.astype(LOW_TYPE),
-                ]
-            )
-        )
-    )
+    if flows:
+        flows = [homeward(flows[0]), attn_third(flows[1])]
+        grad_queries, flows = tied(grad_queries, flows)
+
+    def map_grads(side):
+        both = jnp.concatenate([half_of(grad_queries, 2, side), half_of(grad_keys, 2, side)], 2)
+        return [
+            weight_grad(hidden_one, both).astype(LOW_TYPE),
+            weight_grad(hidden_one, half_of(grad_values, 2, side)).astype(LOW_TYPE),
+            weight_grad(up_low, half_of(attended, 2, side)).astype(LOW_TYPE),
+        ]
+
+    attn_sums = core_summed(map_grads(1 - core), map_grads(core))
     grad_hidden_one = (
         product_t(grad_queries, attn_now[0])
         + product_t(grad_keys, attn_now[1])
@@ -309,63 +409,7 @@
         + [jnp.sum(part.astype(jnp.float32), (0, 1)) for part in grad_pre]
         + [jnp.sum(downward, (0, 1))]
     )
-    return (grad_stream, attn_sums, mlp_sums, grad_modulation, bias_grad)
-
-
-def attn_blocks(grads):
-    stretches = lax.axis_size("dp") // GROUPS
-    shards = lax.axis_size("tensor")
-    kinds, rows_all, width_all = grads.shape
-    shaped = grads.reshape(
-        kinds, stretches, rows_all // stretches, 2, shards // 2, width_all // shards
-    )
-    return jnp.transpose(shaped, (3, 4, 1, 2, 0, 5)).reshape(
-        2, 1, shards // 2, stretches, rows_all // stretches, kinds * width_all // shards
-    )
-
-
-def mlp_blocks(grads):
-    stretches = lax.axis_size("dp") // GROUPS
-    kinds, shards, rows_all, width = grads.shape
-    shaped = grads.reshape(kinds, 2, shards // 2, stretches, rows_all // stretches, width)
-    return jnp.transpose(shaped, (1, 0, 2, 3, 4, 5))
-
-
-def summed_low(left, right):
-    return (left.astype(jnp.float32) + right.astype(jnp.float32)).astype(LOW_TYPE)
-
-
-def reduced_blocks(blocks):
-    shards = lax.axis_size("tensor")
-    dp_at, shard_at = (lax.axis_index("dp"), lax.axis_index("tensor"))
-    low_bit, stretch, shard_low = (dp_at & 1, dp_at // GROUPS, shard_at & 1)
-    kinds, columns, stretches, rows, width = blocks.shape[1:]
-    core_mask = shards
-    received = flipped(picked_at(blocks, 1 - low_bit, 0), (core_mask, core_mask))
-    total = summed_low(picked_at(blocks, low_bit, 0), received)
-    total = jnp.where(
-        low_bit == 1,
-        total.reshape(kinds, columns * stretches, rows, width),
-        jnp.swapaxes(total, 1, 2).reshape(kinds, columns * stretches, rows, width),
-    )
-    column_step = (shard_low, 1)
-    row_steps = [
-        (stretch >> bit_at & 1, shards * GROUPS << bit_at)
-        for bit_at in reversed(range(stretches.bit_length() - 1))
-    ]
-    rows_first, columns_first = (row_steps + [column_step], [column_step] + row_steps)
-    for (bit_zero, mask_zero), (bit_one, mask_one) in zip(rows_first, columns_first):
-        own_bit = jnp.where(low_bit == 1, bit_one, bit_zero)
-        halves = total.reshape(kinds, 2, total.shape[1] // 2, rows, width)
-        received = flipped(picked_at(halves, 1 - own_bit, 1), (mask_zero, mask_one))
-        total = summed_low(picked_at(halves, own_bit, 1), received)
-    count = lax.axis_size("dp") * shards
-    pairs = []
-    for source in range(count):
-        core, high = (source // shards & 1, source % shards >> 1)
-        changed = (core ^ high) * (shards + shards // 2)
-        pairs.append((source, source ^ changed))
-    return lax.ppermute(total[:, 0], ("dp", "tensor"), pairs)
+    return (grad_stream, [mlp_sums, attn_sums], flows, grad_modulation, bias_grad)
 
 
 def own_latents(value):
@@ -497,41 +541,65 @@
     stamps, marks = lax.all_gather(jnp.stack([timesteps, labels]), "dp", axis=1, tiled=True)
     embed_low = w_embed.astype(LOW_TYPE)
     conditioners = NCLS + FREQ + D + PATCH_IN
-    embed_all = lax.all_gather(
-        jnp.concatenate([embed_low[:conditioners], embed_low[-PATCH_IN:]]), "dp", axis=1, tiled=True
-    )
-    class_table = embed_all[:NCLS]
-    first_time = embed_all[NCLS : NCLS + FREQ]
-    second_time = embed_all[NCLS + FREQ : NCLS + FREQ + D]
-    patch_map = embed_all[NCLS + FREQ + D : conditioners]
-    head_map = embed_all[conditioners:]
-    attn_all, mlp_all = ([], [])
-    for layer_at in range(L):
-        attn_local = jnp.transpose(w_attn[layer_at], (1, 0, 2)).reshape(row_width, 4 * col_width)
-        local = jnp.concatenate([attn_local[None], w_mlp[layer_at]]).astype(LOW_TYPE)
-        whole = lax.all_gather(local, everyone, axis=1, tiled=True)
-        whole = whole.reshape(3, shards, D, -1)
-        attn_all.append(
-            jnp.transpose(whole[0].reshape(shards, D, 4, col_width), (2, 1, 0, 3)).reshape(4, D, D)
-        )
-        mlp_all.append(whole[1:])
+    first_map = embed_low[NCLS : NCLS + FREQ]
+    second_map = embed_low[NCLS + FREQ : NCLS + FREQ + D]
+
+    def attn_local(layer_at):
+        return jnp.transpose(w_attn[layer_at], (1, 0, 2)).reshape(1, row_width, 4 * col_width)
+
+    def attn_whole(gathered):
+        shaped = gathered.reshape(shards, D, 4, col_width)
+        return jnp.transpose(shaped, (2, 1, 0, 3)).reshape(4, D, D)
+
+    first_local = [attn_local(layer_at) for layer_at in range(L)] + list(w_mlp[: L - 1])
+    first_local = jnp.concatenate(
+        [part.astype(LOW_TYPE).reshape(-1, row_width, 4 * col_width) for part in first_local]
+    )
+    first_whole = lax.all_gather(first_local, everyone, axis=1, tiled=True)
+    last_whole = lax.all_gather(w_mlp[L - 1].astype(LOW_TYPE), everyone, axis=1, tiled=True)
+    attn_all = [attn_whole(first_whole[layer_at]) for layer_at in range(L)]
+    units_whole = first_whole.reshape(-1, shards, D, 4 * col_width)
+    mlp_all = [
+        [[units_whole[L + 2 * layer_at + kind, at] for at in range(shards)] for kind in range(2)]
+        for layer_at in range(L - 1)
+    ]
+    last_whole = last_whole.reshape(2, shards, D, -1)
+    mlp_all.append([[last_whole[kind, at] for at in range(shards)] for kind in range(2)])
 
     bias_flat = biases.reshape(-1)
     bias_tail = bias_flat[L * layer_span :]
     freq_low = frequencies(stamps).astype(LOW_TYPE)
-    hidden_time = product(freq_low, first_time) + bias_tail[D : 2 * D]
+
+    def own_columns(vector):
+        return lax.dynamic_slice_in_dim(vector, dp_at * row_width, row_width, 0)
+
+    hidden_cols = product(freq_low, first_map) + own_columns(bias_tail[D : 2 * D])
+    gathered_cols = lax.all_gather(
+        jnp.concatenate(
+            [
+                hidden_cols,
+                w_embed[conditioners - PATCH_IN : conditioners],
+                w_embed[-PATCH_IN:],
+            ]
+        ),
+        "dp",
+        axis=1,
+        tiled=True,
+    )
+    hidden_time = gathered_cols[:latents]
+    patch_map = gathered_cols[latents : latents + PATCH_IN].astype(LOW_TYPE)
+    head_map = gathered_cols[latents + PATCH_IN :].astype(LOW_TYPE)
     smooth_time = jax.nn.silu(hidden_time).astype(LOW_TYPE)
     class_picks = (marks[:, None] == jnp.arange(NCLS, dtype=jnp.int32)[None, :]).astype(LOW_TYPE)
-    condition = (
-        product(smooth_time, second_time)
-        + bias_tail[2 * D : 3 * D]
-        + product(class_picks, class_table)
-    )
-    cond_act = jax.nn.silu(condition).astype(LOW_TYPE)
+    condition_rows = (
+        product(smooth_time, second_map)
+        + own_columns(bias_tail[2 * D : 3 * D])
+        + product(class_picks, embed_low[:NCLS])
+    )
+    cond_rows = jax.nn.silu(condition_rows).astype(LOW_TYPE)
     mod_low = w_mod.astype(LOW_TYPE)
     final_low = embed_low[conditioners:-PATCH_IN]
     final_width = final_low.shape[0] // shards
-    cond_rows = lax.dynamic_slice_in_dim(cond_act, dp_at * row_width, row_width, 1)
     mod_cols = jnp.concatenate(
         [product(cond_rows, mod_low[layer_at]) for layer_at in range(L)]
         + [
@@ -587,21 +655,26 @@
     grad_stream = normalize_back(
         grad_hidden * (1.0 + final_mod[:, None, D:]), normed_last, inverse_last
     )
-    attn_list, mlp_list, mod_list, bias_list = ([None] * L, [None] * L, [None] * L, [None] * L)
+    mod_list, bias_list, sums_list, flows = ([None] * L, [None] * L, [None] * L, None)
+    late, grad_stream = tied(jnp.concatenate([second_map, cond_rows]), grad_stream)
+    late = lax.all_gather(late, "dp", axis=1, tiled=True)
+    second_time, cond_act = (late[:D], late[D:])
     for layer_at in range(L - 1, -1, -1):
-        (
-            grad_stream,
-            attn_list[layer_at],
-            mlp_list[layer_at],
-            mod_list[layer_at],
-            bias_list[layer_at],
-        ) = layer_backward(
+        grad_stream, fresh, flows, mod_list[layer_at], bias_list[layer_at] = layer_backward(
             grad_stream,
             mod_parts[layer_at],
             attn_all[layer_at],
             mlp_all[layer_at],
             saved_states[layer_at],
+            flows,
         )
+        if flows:
+            sums_list[layer_at + 1] = [flows[0], homeward(flows[1])]
+        flows = fresh
+    sums_list[0] = [
+        homeward(mlp_third(mlp_second(flows[0]))),
+        homeward(attn_third(attn_second(flows[1]))),
+    ]
     grad_patch = weight_grad(noised, grad_stream.astype(LOW_TYPE))
     mine = patches_own.shape[0]
     vectors = jnp.concatenate(
@@ -646,10 +719,9 @@
     grad_cond_parts = sum(
         product_t(own_mods[layer_at], mod_low[layer_at]) for layer_at in range(L)
     )
-    grad_cond_act = lax.psum(grad_cond_parts.astype(jnp.bfloat16), "tensor").astype(
-        jnp.float32
+    grad_cond_act = jnp.sum(
+        lax.all_gather(grad_cond_parts.astype(LOW_TYPE), "tensor").astype(jnp.float32), 0
     ) + product(grad_finals, final_low)
-    condition_rows = lax.dynamic_slice_in_dim(condition, dp_at * row_width, row_width, 1)
     grad_condition = lax.all_gather(
         jax.vjp(jax.nn.silu, condition_rows)[1](grad_cond_act)[0].astype(LOW_TYPE),
         "dp",
@@ -701,11 +773,14 @@
     )
     attn_now = jnp.stack(
         [
-            jnp.transpose(part.reshape(-1, 4, col_width), (1, 0, 2)).astype(jnp.float32)
-            for part in attn_list
+            jnp.stack(
+                [part[:, at * col_width : (at + 1) * col_width] for part in sums[1] for at in (0, 1)]
+            )
+            for sums in sums_list
         ]
-    )
-    reduced = [attn_now, jnp.stack(mlp_list).astype(jnp.float32), grad_mod_map, grad_embed]
+    ).astype(jnp.float32)
+    mlp_now = jnp.stack([jnp.stack(sums[0]) for sums in sums_list]).astype(jnp.float32)
+    reduced = [attn_now, mlp_now, grad_mod_map, grad_embed]
     squares = (
         jnp.sum(reduced[0] * reduced[0])
         + jnp.sum(reduced[1] * reduced[1])
@@ -713,8 +788,11 @@
         + jnp.sum(reduced[3] * reduced[3]) / shards
     )
     picked = (jnp.arange(GROUPS, dtype=jnp.int32) == group_at).astype(jnp.float32)
-    totals = lax.psum(
-        jnp.concatenate([picked * squares, jnp.reshape(loss_here, (1,))]), ("dp", "tensor")
+    totals = jnp.sum(
+        lax.all_gather(
+            jnp.concatenate([picked * squares, jnp.reshape(loss_here, (1,))]), ("dp", "tensor")
+        ),
+        0,
     )
     group_norms = jnp.sqrt(totals[:GROUPS] + jnp.sum(bias_groups * bias_groups, 1))
     clip_scale = CLIP_NORM / (group_norms + 1e-06)

time: 1060 us -> 912 us (0.86)
  local copies, waits for them, and re-layouts: 273 us -> 186 us
  blocking collectives: 233 us -> 152 us
  starting transfers between devices: 22.5 us -> 85.3 us
  other arithmetic: 150 us -> 115 us
  waiting for transfers between devices: 188 us -> 160 us
  matrix products: 162 us -> 182 us
    psum x2 -> x0, blocking collectives: 162 us -> none  [the longest x1 84.9 us: per_device(): lax.psum(jnp.concatenate([picked * squares, jnp.reshape(loss_here, (1,))]...]
    ppermute x4 -> x40, waiting for transfers between devices: 0.01 us -> 89.4 us  [the longest x32 89.3 us: exchanged(): lax.ppermute(value, ('dp', 'tensor'), [(source, source ^ mask) for source...]
    ppermute x4 -> x40, starting transfers between devices: 4.4 us -> 76.9 us  [the longest x32 64.8 us: exchanged(): lax.ppermute(value, ('dp', 'tensor'), [(source, source ^ mask) for source...]
    ppermute x16 -> x4, waiting for transfers between devices: 66.4 us -> 0.01 us  [flipped(): return lax.ppermute(value, ('dp', 'tensor'), pairs)]
    all_gather x3, waiting for transfers between devices: 88.6 us -> 36.9 us  [the longest x1 36.9 us: per_device(): first_whole = lax.all_gather(first_local, everyone, axis=1, tiled=True)]
    unnamed x1 -> x2, blocking collectives: 36.3 us -> 78.7 us
    all_gather x0 -> x2, blocking collectives: none -> 39.3 us  [the longest x1 29.7 us: per_device(): lax.all_gather(grad_cond_parts.astype(LOW_TYPE), 'tensor')]
    another operation x14 -> x8, local copies, waits for them, and re-layouts: 48.5 us -> 20.1 us  [the longest x2 19.5 us: attn_whole(): shaped = gathered.reshape(shards, D, 4, col_width)]
  transfers between devices with their start and end apart: 32 -> 56, of which waited for: 13 -> 15; matrix products, arithmetic and copies ran while one was open for 32% -> 34% of each run, Pallas kernels for 0% -> 0%
where the time goes in v2:
time: 912 us; the launch traced here: 903 us
  local copies, waits for them, and re-layouts  186 us (20%)
  matrix products  182 us (20%)
  waiting for transfers between devices  160 us (18%)
  blocking collectives  152 us (17%)
  other arithmetic  115 us (13%)
  starting transfers between devices  85.3 us (9%)
  between operations  24.5 us (3%)
    ppermute x32, waiting for transfers between devices, exchanged(): lax.ppermute(value, ('dp', 'tensor'), [(source, source ^ mask) for source...  89.3 us
    unnamed x2, blocking collectives  78.7 us
    ppermute x32, starting transfers between devices, exchanged(): lax.ppermute(value, ('dp', 'tensor'), [(source, source ^ mask) for source...  64.8 us
    unnamed x567, local copies, waits for them, and re-layouts  60.4 us
    dot_general x36, matrix products, weight_grad(): lax.dot_general(inputs, grads_out, ((leading, leading), ((), ())), prefer...  58.1 us
    dot_general x32, matrix products, product(): return jnp.dot(left, right, preferred_element_type=jnp.float32)  49.8 us
    dot_general x29, matrix products, product_t(): lax.dot_general(left, right, (((left.ndim - 1,), (1,)), ((), ())), prefer...  49.8 us
    all_gather x1, waiting for transfers between devices, per_device(): first_whole = lax.all_gather(first_local, everyone, axis=1, tiled=True)  36.9 us
  transfers between devices with their start and end apart: 56, of which 15 were waited for; matrix products, arithmetic and copies ran while one was open for 34% of the time, Pallas kernels for 0%

profile of v2, /device:TPU:0, one launch (start us, length us, event | category | flops | bytes accessed | tf_op | source)
XLA Modules:
  0.0 903.0 jit_solution(1424550812960985094)
XLA Ops:
  16.5 10.1 %all-gather.5 = s32[8,8,2]{1,2,0:T(2,128)S(1)} all-gather(s32[1,8,2]{1,2,0:T(2,128)S(1)} %add_bitcast_fusion), channel_id=1, replica_groups=mesh['dp'=8,'tensor'=4] {'dp'}, dimensions={0}, use_global_device_ids=true | all-gather | bytes 576 | tf_op jit(solution)/shard_map/all_gather | solution.py:541
  28.5 9.6 %all_gather.43 = f32[96,768]{0,1:T(8,128)S(1)} all-gather(f32[96,96]{0,1:T(8,128)S(1)} %copy.480), channel_id=1, replica_groups=mesh['dp'=8,'tensor'=4] {'dp'}, dimensions={1}, use_global_device_ids=true | all-gather | bytes 331776 | tf_op jit(solution)/shard_map/all_gather | solution.py:577
  41.4 39.0 %all-reduce.4 = bf16[64,2688]{1,0:T(8,128)(2,1)S(1)} all-reduce(f32[64,2688]{1,0:T(8,128)S(1)} %pad_maximum_fusion.4), channel_id=7, replica_groups=mesh['dp'=8,'tensor'=4] {'dp'}, use_global_device_ids=true, to_apply=%region_5.6.clone | all-reduce | flops 172032 | bytes 1032192
  80.5 14.1 %all-gather = bf16[32,2688]{1,0:T(8,128)(2,1)S(1)} all-gather(bf16[8,2688]{1,0:T(8,128)(2,1)S(1)} %dynamic-slice_convert_fusion.5), channel_id=2, replica_groups=mesh['dp'=8,'tensor'=4] {'tensor'}, dimensions={0}, use_global_device_ids=true | all-gather | bytes 215040 | tf_op jit(solution)/shard_map/all_gather | solution.py:614
  97.9 3.7 copy.582
  111.1 36.9 %all-gather.13.cloned.1.call-done = bf16[4,3072,768]{2,1,0:T(8,128)(2,1)} async-done(((bf16[4,96,768]{2,1,0:T(8,128)(2,1)}), bf16[4,3072,768]{2,1,0:T(8,128)(2,1)}) %all-gather.13.cloned.1.call-update) | async-done | bytes 18874384 | tf_op jit(solution)/shard_map/all_gather | solution.py:558
  148.0 8.1 fusion.255
  156.1 6.6 copy.485
  162.8 9.7 %reshape_squeeze.6 = bf16[4,768,4,192]{1,0,3,2:T(4,128)(2,1)} reshape(bf16[1,3072,768]{1,2,0:T(8,128)(2,1)} %copy.485) | data formatting | bytes 9437184 | tf_op jit(solution)/shard_map/reshape;squeeze | solution.py:551
  172.5 4.3 fusion.257
  195.3 6.7 copy.500
  202.0 9.8 %reshape_squeeze.7 = bf16[4,768,4,192]{1,0,3,2:T(4,128)(2,1)} reshape(bf16[1,3072,768]{1,2,0:T(8,128)(2,1)} %copy.500) | data formatting | bytes 9437184 | tf_op jit(solution)/shard_map/reshape;squeeze | solution.py:551
  211.8 4.6 fusion.256
  234.9 2.6 fusion.253
  264.2 3.7 fusion.94
  280.6 2.5 bitcast_convert_fusion.12
  283.1 2.5 bitcast_convert_fusion.14
  285.6 3.1 fusion.274
  288.7 3.0 fusion.276
  308.5 3.3 multiply_reduce_fusion.9
  311.8 2.5 multiply_reduce_fusion.27
  317.3 3.4 add_convert_fusion.10
  320.7 4.0 add_convert_fusion.8
  324.8 3.9 add_convert_fusion.9
  328.7 3.3 add_convert_fusion.11
  335.1 5.7 bitcast_reduce_fusion.1
  383.4 8.8 collective-permute-done.8
  394.4 2.5 add_convert_fusion.33
  396.9 2.5 add_convert_fusion.34
  410.9 3.4 fusion.270
  414.3 3.4 fusion.272
  417.7 3.4 fusion.269
  421.0 3.4 fusion.271
  434.9 2.8 multiply_reduce_fusion.13
  443.5 8.1 collective-permute-done.15
  452.8 2.7 collective-permute-done.17
  460.3 5.2 collective-permute-done.25
  469.8 5.9 collective-permute-start.23
  477.6 2.5 add_convert_fusion.2
  480.1 2.5 add_convert_fusion.3
  487.6 4.9 multiply_reduce_fusion
  522.5 31.5 %collective-permute-start.30 = (bf16[768,384]{1,0:T(8,128)(2,1)S(1)}, bf16[768,384]{1,0:T(8,128)(2,1)S(1)}, u32[]{:S(2)}, u32[]{:S(2)}) collective-permute-start(bf16[768,384]{1,0:T(8,128)(2,1)S(1)} %fusion.77), channel_id=1, source_target_pairs={{0,4},{1,5},{2,6},{3,7},{4,0},{5,1},{6,2},{7,3},{8,12},{9,13},{10,... | collective-permute-start | bytes 1769480 | tf_op jit(solution)/shard_map/ppermute | solution.py:232
  554.1 7.4 collective-permute-start.26
  562.0 3.3 collective-permute-start.39
  569.2 29.4 %collective-permute-done.39 = bf16[384,768]{1,0:T(8,128)(2,1)S(1)} collective-permute-done((bf16[384,768]{1,0:T(8,128)(2,1)S(1)}, bf16[384,768]{1,0:T(8,128)(2,1)S(1)}, u32[]{:S(2)}, u32[]{:S(2)}) %collective-permute-start.39) | collective-permute-done | bytes 589856 | tf_op jit(solution)/shard_map/ppermute | solution.py:232
  602.0 16.5 %collective-permute-done.32 = bf16[768,384]{1,0:T(8,128)(2,1)S(1)} collective-permute-done((bf16[768,384]{1,0:T(8,128)(2,1)S(1)}, bf16[768,384]{1,0:T(8,128)(2,1)S(1)}, u32[]{:S(2)}, u32[]{:S(2)}) %collective-permute-start.32) | collective-permute-done | bytes 589856 | tf_op jit(solution)/shard_map/ppermute | solution.py:232
  621.5 7.2 collective-permute-done.33
  630.4 10.0 %collective-permute-done.42 = bf16[384,768]{1,0:T(8,128)(2,1)S(1)} collective-permute-done((bf16[384,768]{1,0:T(8,128)(2,1)S(1)}, bf16[384,768]{1,0:T(8,128)(2,1)S(1)}, u32[]{:S(2)}, u32[]{:S(2)}) %collective-permute-start.42) | collective-permute-done | bytes 589856 | tf_op jit(solution)/shard_map/ppermute | solution.py:232
  648.9 3.6 copy.715
  661.5 29.7 %all-gather.3 = bf16[256,96]{1,0:T(8,128)(2,1)S(1)} all-gather(bf16[64,96]{1,0:T(8,128)(2,1)S(1)} %fusion.86), channel_id=5, replica_groups=mesh['dp'=8,'tensor'=4] {'tensor'}, dimensions={0}, use_global_device_ids=true | all-gather | bytes 61440 | tf_op jit(solution)/shard_map/all_gather | solution.py:723
  693.8 9.4 %all-gather.7 = bf16[8,96,64]{1,2,0:T(8,128)(2,1)S(1)} all-gather(bf16[1,96,64]{1,2,0:T(8,128)(2,1)S(1)} %fusion.201), channel_id=1, replica_groups=mesh['dp'=8,'tensor'=4] {'dp'}, dimensions={0}, use_global_device_ids=true | all-gather | bytes 110592 | tf_op jit(solution)/shard_map/all_gather | solution.py:725
  707.5 2.7 slice_convert_fusion
  738.0 39.7 %all-reduce.1 = f32[160]{0:T(256)} all-reduce(f32[160]{0:T(256)S(1)} %maximum_dynamic-update-slice_fusion), channel_id=6, replica_groups=mesh['dp'=8,'tensor'=4] {'dp','tensor'}, use_global_device_ids=true, to_apply=%add.1 | all-reduce | flops 160 | bytes 1280
  782.1 11.7 %add_divide_fusion = (f32[3592,384]{1,0:T(8,128)}, f32[3592,384]{1,0:T(8,128)}, f32[3592,384]{1,0:T(8,128)}) fusion(f32[3592,384]{1,0:T(8,128)} %copy-done.8, f32[]{:T(128)} %get-tuple-element.273, f32[3592,384]{1,0:T(8,128)} %param.44, f32[3592,384]{1,0:T(8,128)} %param.45), kind=kLoop, calls=%fused_computation.16 | loop fusion | flops 16551936 | bytes 33103876 | tf_op jit(solution)/shard_map/div | solution.py:494
  793.8 6.4 copy.590
  800.2 3.0 dynamic-slice_convert_fusion
  803.3 7.9 add_divide_fusion.2
  815.2 4.0 add_divide_fusion.3
  822.3 6.0 add_divide_fusion.1
  831.3 3.3 copy.591
  837.7 2.9 fusion.151
  849.2 7.1 collective-permute-done.45
  867.3 11.1 %collective-permute-done.47 = bf16[2,2,1,1,96,768]{5,4,1,0,3,2:T(8,128)(2,1)S(1)} collective-permute-done((bf16[2,2,1,1,96,768]{5,4,1,0,3,2:T(8,128)(2,1)S(1)}, bf16[2,2,1,1,96,768]{5,4,1,0,3,2:T(8,128)(2,1)S(1)}, u32[]{:S(2)}, u32[]{:S(2)}) %collective-permute-start.47) | collective-permute-done | bytes 589856 | tf_op jit(solution)/shard_map/ppermute | solution.py:39
  880.3 12.7 %collective-permute-done.51 = bf16[3592,1,1,96]{0,3,2,1:T(8,128)(2,1)S(1)} collective-permute-done((bf16[3592,1,1,96]{0,3,2,1:T(8,128)(2,1)S(1)}, bf16[3592,1,1,96]{0,3,2,1:T(8,128)(2,1)S(1)}, u32[]{:S(2)}, u32[]{:S(2)}) %collective-permute-start.51) | collective-permute-done | bytes 689696 | tf_op jit(solution)/shard_map/ppermute | solution.py:39
  (1031 shorter events, 343.0 us)
Async XLA Ops:
  7.2 140.8 %all-gather.13.cloned.1.call-start = ((), (), s32[]{:S(2)}) async-start(), calls=%async_computation | async-start | bytes 19464192 | tf_op jit(solution)/shard_map/all_gather | solution.py:558
  11.1 250.7 %all-gather.17.cloned.1.call-start = ((), (), s32[]{:S(2)}) async-start(), calls=%async_computation.2 | async-start | bytes 9732096 | tf_op jit(solution)/shard_map/all_gather | solution.py:559
  12.6 94.1 %collective-permute-start = (f32[2,1]{0,1:T(1,128)}, f32[2,1]{0,1:T(1,128)}, u32[]{:S(2)}, u32[]{:S(2)}) collective-permute-start(f32[2,1]{0,1:T(1,128)} %dynamic-slice_bitcast_fusion.4), channel_id=1, source_target_pairs={{0,4},{1,5},{2,6},{3,7},{4,0},{5,1},{6,2},{7,3},{8,12},{9,13},{10,... | collective-permute-start | bytes 32 | tf_op jit(solution)/shard_map/ppermute | solution.py:177
  14.5 92.4 %collective-permute-start.2 = (f32[2,256,16]{1,2,0:T(8,128)}, f32[2,256,16]{1,2,0:T(8,128)}, u32[]{:S(2)}, u32[]{:S(2)}) collective-permute-start(f32[2,256,16]{1,2,0:T(8,128)} %constant_dynamic-slice_fusion.49), channel_id=1, source_target_pairs={{0,4},{1,5},{2,6},{3,7},{4,0},{5,1},{6,2},{7,3},{8,12},{9,13},{10,... | collective-permute-start | bytes 98312 | tf_op jit(solution)/shard_map/ppermute | solution.py:177
  15.9 91.0 %collective-permute-start.1 = (f32[2,256,16]{1,2,0:T(8,128)}, f32[2,256,16]{1,2,0:T(8,128)}, u32[]{:S(2)}, u32[]{:S(2)}) collective-permute-start(f32[2,256,16]{1,2,0:T(8,128)} %constant_dynamic-slice_fusion.50), channel_id=1, source_target_pairs={{0,4},{1,5},{2,6},{3,7},{4,0},{5,1},{6,2},{7,3},{8,12},{9,13},{10,... | collective-permute-start | bytes 98312 | tf_op jit(solution)/shard_map/ppermute | solution.py:177
  16.5 79.6 %copy-start.88 = (bf16[3592,96]{0,1:T(8,128)(2,1)}, bf16[3592,96]{0,1:T(8,128)(2,1)S(1)}, u32[]{:S(2)}) copy-start(bf16[3592,96]{0,1:T(8,128)(2,1)S(1)} %convert_element_type.839) | copy-start | bytes 2068996
  38.2 57.1 %copy-start.90 = (f32[96,768]{1,0:T(8,128)}, f32[96,768]{1,0:T(8,128)S(1)}, u32[]{:S(2)}) copy-start(f32[96,768]{1,0:T(8,128)S(1)} %copy.481) | copy-start | bytes 884740
  95.3 13.5 %collective-permute-start.3 = (bf16[2,4,2688]{2,0,1:T(2,128)(2,1)}, bf16[2,4,2688]{2,0,1:T(2,128)(2,1)}, u32[]{:S(2)}, u32[]{:S(2)}) collective-permute-start(bf16[2,4,2688]{2,0,1:T(2,128)(2,1)} %dynamic-slice_bitcast_fusion), channel_id=1, source_target_pairs={{0,4},{1,5},{2,6},{3,7},{4,0},{5,1},{6,2},{7,3},{8,12},{9,13},{10,... | collective-permute-start | bytes 129032 | tf_op jit(solution)/shard_map/ppermute | solution.py:177
  95.3 304.2 %all-gather.15.cloned.1.call-start = ((), (), s32[]{:S(2)}) async-start(), calls=%async_computation.1 | async-start | bytes 1548288 | tf_op jit(solution)/shard_map/all_gather | solution.py:660
  108.4 114.9 %copy-start.4 = (f32[2,256,768]{2,1,0:T(8,128)}, f32[2,256,768]{2,1,0:T(8,128)S(1)}, u32[]{:S(2)}) copy-start(f32[2,256,768]{2,1,0:T(8,128)S(1)} %get-tuple-element.403) | copy-start | bytes 4718596
  108.7 47.4 %copy-start.170 = (f32[2,256]{1,0:T(2,128)}, f32[2,256]{1,0:T(2,128)S(1)}, u32[]{:S(2)}) copy-start(f32[2,256]{1,0:T(2,128)S(1)} %add_rsqrt_fusion.4) | copy-start | bytes 6148
  110.2 46.0 %copy-start.148 = (f32[2,768]{1,0:T(2,128)}, f32[2,768]{1,0:T(2,128)S(1)}, u32[]{:S(2)}) copy-start(f32[2,768]{1,0:T(2,128)S(1)} %get-tuple-element.384) | copy-start | bytes 18436
  111.1 76.7 %copy-start.29 = (bf16[2,256,768]{2,1,0:T(8,128)(2,1)}, bf16[2,256,768]{2,1,0:T(8,128)(2,1)S(1)}, u32[]{:S(2)}) copy-start(bf16[2,256,768]{2,1,0:T(8,128)(2,1)S(1)} %add_convert_fusion.20) | copy-start | bytes 2359300
  302.8 17.9 %collective-permute-start.7 = (bf16[768,768]{1,0:T(8,128)(2,1)}, bf16[768,768]{1,0:T(8,128)(2,1)}, u32[]{:S(2)}, u32[]{:S(2)}) collective-permute-start(bf16[768,768]{1,0:T(8,128)(2,1)} %bitcast_convert_fusion.12), channel_id=1, source_target_pairs={{0,4},{1,5},{2,6},{3,7},{4,0},{5,1},{6,2},{7,3},{8,12},{9,13},{10,... | collective-permute-start | bytes 3538952 | tf_op jit(solution)/shard_map/ppermute | solution.py:232
  303.5 21.3 %collective-permute-start.6 = (bf16[768,768]{1,0:T(8,128)(2,1)}, bf16[768,768]{1,0:T(8,128)(2,1)}, u32[]{:S(2)}, u32[]{:S(2)}) collective-permute-start(bf16[768,768]{1,0:T(8,128)(2,1)} %bitcast_convert_fusion.14), channel_id=1, source_target_pairs={{0,4},{1,5},{2,6},{3,7},{4,0},{5,1},{6,2},{7,3},{8,12},{9,13},{10,... | collective-permute-start | bytes 3538952 | tf_op jit(solution)/shard_map/ppermute | solution.py:232
  307.9 9.3 %collective-permute-start.5 = (bf16[768,768]{1,0:T(8,128)(2,1)}, bf16[768,768]{1,0:T(8,128)(2,1)}, u32[]{:S(2)}, u32[]{:S(2)}) collective-permute-start(bf16[768,768]{1,0:T(8,128)(2,1)} %bitcast_convert_fusion.16), channel_id=1, source_target_pairs={{0,4},{1,5},{2,6},{3,7},{4,0},{5,1},{6,2},{7,3},{8,12},{9,13},{10,... | collective-permute-start | bytes 3538952 | tf_op jit(solution)/shard_map/ppermute | solution.py:232
  308.4 20.3 %collective-permute-start.4 = (bf16[768,768]{1,0:T(8,128)(2,1)}, bf16[768,768]{1,0:T(8,128)(2,1)}, u32[]{:S(2)}, u32[]{:S(2)}) collective-permute-start(bf16[768,768]{1,0:T(8,128)(2,1)} %bitcast_convert_fusion.18), channel_id=1, source_target_pairs={{0,4},{1,5},{2,6},{3,7},{4,0},{5,1},{6,2},{7,3},{8,12},{9,13},{10,... | collective-permute-start | bytes 3538952 | tf_op jit(solution)/shard_map/ppermute | solution.py:232
  314.9 333.9 %all-gather.19.cloned.1.call-start = ((), (), s32[]{:S(2)}) async-start(), calls=%async_computation.3 | async-start | bytes 7805952 | tf_op jit(solution)/shard_map/all_gather | solution.py:690
  354.3 40.1 %collective-permute-start.13 = (bf16[768,384]{1,0:T(8,128)(2,1)}, bf16[768,384]{1,0:T(8,128)(2,1)}, u32[]{:S(2)}, u32[]{:S(2)}) collective-permute-start(bf16[768,384]{1,0:T(8,128)(2,1)} %fusion.74), channel_id=1, source_target_pairs={{0,4},{1,5},{2,6},{3,7},{4,0},{5,1},{6,2},{7,3},{8,12},{9,13},{10,... | collective-permute-start | bytes 1769480 | tf_op jit(solution)/shard_map/ppermute | solution.py:232
  356.2 40.8 %collective-permute-start.12 = (bf16[768,384]{1,0:T(8,128)(2,1)}, bf16[768,384]{1,0:T(8,128)(2,1)}, u32[]{:S(2)}, u32[]{:S(2)}) collective-permute-start(bf16[768,384]{1,0:T(8,128)(2,1)} %fusion.71), channel_id=1, source_target_pairs={{0,4},{1,5},{2,6},{3,7},{4,0},{5,1},{6,2},{7,3},{8,12},{9,13},{10,... | collective-permute-start | bytes 1769480 | tf_op jit(solution)/shard_map/ppermute | solution.py:232
  360.3 40.9 %collective-permute-start.10 = (bf16[768,768]{1,0:T(8,128)(2,1)}, bf16[768,768]{1,0:T(8,128)(2,1)}, u32[]{:S(2)}, u32[]{:S(2)}) collective-permute-start(bf16[768,768]{1,0:T(8,128)(2,1)} %broadcast_select_fusion.1), channel_id=1, source_target_pairs={{0,1},{1,0},{2,3},{3,2},{4,5},{5,4},{6,7},{7,6},{8,9},{9,8},{10,11... | collective-permute-start | bytes 3538952 | tf_op jit(solution)/shard_map/ppermute | solution.py:232
  364.0 17.1 %collective-permute-start.9 = (bf16[384,768]{1,0:T(8,128)(2,1)}, bf16[384,768]{1,0:T(8,128)(2,1)}, u32[]{:S(2)}, u32[]{:S(2)}) collective-permute-start(bf16[384,768]{1,0:T(8,128)(2,1)} %constant_dynamic-slice_fusion.45), channel_id=1, source_target_pairs={{0,16},{1,17},{2,18},{3,19},{4,20},{5,21},{6,22},{7,23},{8,24},{9,... | collective-permute-start | bytes 1769480 | tf_op jit(solution)/shard_map/ppermute | solution.py:232
  367.4 24.9 %collective-permute-start.8 = (bf16[384,768]{1,0:T(8,128)(2,1)}, bf16[384,768]{1,0:T(8,128)(2,1)}, u32[]{:S(2)}, u32[]{:S(2)}) collective-permute-start(bf16[384,768]{1,0:T(8,128)(2,1)} %constant_dynamic-slice_fusion.46), channel_id=1, source_target_pairs={{0,16},{1,17},{2,18},{3,19},{4,20},{5,21},{6,22},{7,23},{8,24},{9,... | collective-permute-start | bytes 1769480 | tf_op jit(solution)/shard_map/ppermute | solution.py:232
  381.1 22.4 %collective-permute-start.11 = (bf16[768,768]{1,0:T(8,128)(2,1)}, bf16[768,768]{1,0:T(8,128)(2,1)}, u32[]{:S(2)}, u32[]{:S(2)}) collective-permute-start(bf16[768,768]{1,0:T(8,128)(2,1)} %bitcast_convert_fusion.10), channel_id=1, source_target_pairs={{0,4},{1,5},{2,6},{3,7},{4,0},{5,1},{6,2},{7,3},{8,12},{9,13},{10,... | collective-permute-start | bytes 3538952 | tf_op jit(solution)/shard_map/ppermute | solution.py:232
  424.5 18.9 %collective-permute-start.16 = (bf16[384,768]{1,0:T(8,128)(2,1)S(1)}, bf16[384,768]{1,0:T(8,128)(2,1)S(1)}, u32[]{:S(2)}, u32[]{:S(2)}) collective-permute-start(bf16[384,768]{1,0:T(8,128)(2,1)S(1)} %constant_dynamic-slice_fusion.39), channel_id=1, source_target_pairs={{0,16},{1,17},{2,18},{3,19},{4,20},{5,21},{6,22},{7,23},{8,24},{9,... | collective-permute-start | bytes 1769480 | tf_op jit(solution)/shard_map/ppermute | solution.py:232
  426.1 25.6 %collective-permute-start.15 = (bf16[384,768]{1,0:T(8,128)(2,1)S(1)}, bf16[384,768]{1,0:T(8,128)(2,1)S(1)}, u32[]{:S(2)}, u32[]{:S(2)}) collective-permute-start(bf16[384,768]{1,0:T(8,128)(2,1)S(1)} %constant_dynamic-slice_fusion.40), channel_id=1, source_target_pairs={{0,16},{1,17},{2,18},{3,19},{4,20},{5,21},{6,22},{7,23},{8,24},{9,... | collective-permute-start | bytes 1769480 | tf_op jit(solution)/shard_map/ppermute | solution.py:232
  426.7 25.8 %collective-permute-start.14 = (bf16[384,768]{1,0:T(8,128)(2,1)S(1)}, bf16[384,768]{1,0:T(8,128)(2,1)S(1)}, u32[]{:S(2)}, u32[]{:S(2)}) collective-permute-start(bf16[384,768]{1,0:T(8,128)(2,1)S(1)} %broadcast_select_fusion.3), channel_id=1, source_target_pairs={{0,1},{1,0},{2,3},{3,2},{4,5},{5,4},{6,7},{7,6},{8,9},{9,8},{10,11... | collective-permute-start | bytes 1769480 | tf_op jit(solution)/shard_map/ppermute | solution.py:232
  441.7 13.8 %collective-permute-start.17 = (bf16[768,384]{1,0:T(8,128)(2,1)S(1)}, bf16[768,384]{1,0:T(8,128)(2,1)S(1)}, u32[]{:S(2)}, u32[]{:S(2)}) collective-permute-start(bf16[768,384]{1,0:T(8,128)(2,1)S(1)} %pad_maximum_fusion.6), channel_id=1, source_target_pairs={{0,1},{1,0},{2,3},{3,2},{4,5},{5,4},{6,7},{7,6},{8,9},{9,8},{10,11... | collective-permute-start | bytes 1769480 | tf_op jit(solution)/shard_map/ppermute | solution.py:232
  455.8 21.9 %collective-permute-start.21 = (bf16[768,768]{1,0:T(8,128)(2,1)S(1)}, bf16[768,768]{1,0:T(8,128)(2,1)S(1)}, u32[]{:S(2)}, u32[]{:S(2)}) collective-permute-start(bf16[768,768]{1,0:T(8,128)(2,1)S(1)} %bitcast_convert_fusion.5), channel_id=1, source_target_pairs={{0,4},{1,5},{2,6},{3,7},{4,0},{5,1},{6,2},{7,3},{8,12},{9,13},{10,... | collective-permute-start | bytes 3538952 | tf_op jit(solution)/shard_map/ppermute | solution.py:232
  455.8 14.0 %collective-permute-start.19 = (bf16[768,768]{1,0:T(8,128)(2,1)S(1)}, bf16[768,768]{1,0:T(8,128)(2,1)S(1)}, u32[]{:S(2)}, u32[]{:S(2)}) collective-permute-start(bf16[768,768]{1,0:T(8,128)(2,1)S(1)} %bitcast_convert_fusion.7), channel_id=1, source_target_pairs={{0,4},{1,5},{2,6},{3,7},{4,0},{5,1},{6,2},{7,3},{8,12},{9,13},{10,... | collective-permute-start | bytes 3538952 | tf_op jit(solution)/shard_map/ppermute | solution.py:232
  456.4 9.1 %collective-permute-start.25 = (bf16[384,384]{1,0:T(8,128)(2,1)S(1)}, bf16[384,384]{1,0:T(8,128)(2,1)S(1)}, u32[]{:S(2)}, u32[]{:S(2)}) collective-permute-start(bf16[384,384]{1,0:T(8,128)(2,1)S(1)} %constant_dynamic-slice_fusion.30), channel_id=1, source_target_pairs={{0,16},{1,17},{2,18},{3,19},{4,20},{5,21},{6,22},{7,23},{8,24},{9,... | collective-permute-start | bytes 884744 | tf_op jit(solution)/shard_map/ppermute | solution.py:232
  458.7 8.8 collective-permute-start.24
  460.2 20.0 %collective-permute-start.20 = (bf16[768,768]{1,0:T(8,128)(2,1)S(1)}, bf16[768,768]{1,0:T(8,128)(2,1)S(1)}, u32[]{:S(2)}, u32[]{:S(2)}) collective-permute-start(bf16[768,768]{1,0:T(8,128)(2,1)S(1)} %bitcast_convert_fusion.6), channel_id=1, source_target_pairs={{0,4},{1,5},{2,6},{3,7},{4,0},{5,1},{6,2},{7,3},{8,12},{9,13},{10,... | collective-permute-start | bytes 3538952 | tf_op jit(solution)/shard_map/ppermute | solution.py:232
  465.4 17.2 %collective-permute-start.18 = (bf16[768,768]{1,0:T(8,128)(2,1)S(1)}, bf16[768,768]{1,0:T(8,128)(2,1)S(1)}, u32[]{:S(2)}, u32[]{:S(2)}) collective-permute-start(bf16[768,768]{1,0:T(8,128)(2,1)S(1)} %bitcast_convert_fusion.8), channel_id=1, source_target_pairs={{0,4},{1,5},{2,6},{3,7},{4,0},{5,1},{6,2},{7,3},{8,12},{9,13},{10,... | collective-permute-start | bytes 3538952 | tf_op jit(solution)/shard_map/ppermute | solution.py:232
  467.5 33.8 %collective-permute-start.22 = (bf16[384,768]{1,0:T(8,128)(2,1)S(1)}, bf16[384,768]{1,0:T(8,128)(2,1)}, u32[]{:S(2)}, u32[]{:S(2)}) collective-permute-start(bf16[384,768]{1,0:T(8,128)(2,1)S(1)} %add_convert_fusion.32), channel_id=1, source_target_pairs={{0,0},{1,1},{2,4},{3,5},{4,2},{5,3},{6,6},{7,7},{8,8},{9,9},{10,12... | collective-permute-start | bytes 1769480 | tf_op jit(solution)/shard_map/ppermute | solution.py:286
  469.8 31.4 %collective-permute-start.23 = (bf16[384,768]{1,0:T(8,128)(2,1)}, bf16[384,768]{1,0:T(8,128)(2,1)}, u32[]{:S(2)}, u32[]{:S(2)}) collective-permute-start(bf16[384,768]{1,0:T(8,128)(2,1)} %add_convert_fusion.31), channel_id=1, source_target_pairs={{0,0},{1,1},{2,4},{3,5},{4,2},{5,3},{6,6},{7,7},{8,8},{9,9},{10,12... | collective-permute-start | bytes 1769480 | tf_op jit(solution)/shard_map/ppermute | solution.py:286
  511.7 49.9 %collective-permute-start.37 = (bf16[384,768]{1,0:T(8,128)(2,1)S(1)}, bf16[384,768]{1,0:T(8,128)(2,1)S(1)}, u32[]{:S(2)}, u32[]{:S(2)}) collective-permute-start(bf16[384,768]{1,0:T(8,128)(2,1)S(1)} %constant_dynamic-slice_fusion.15), channel_id=1, source_target_pairs={{0,16},{1,17},{2,18},{3,19},{4,20},{5,21},{6,22},{7,23},{8,24},{9,... | collective-permute-start | bytes 1769480 | tf_op jit(solution)/shard_map/ppermute | solution.py:232
  513.4 48.3 %collective-permute-start.38 = (bf16[384,768]{1,0:T(8,128)(2,1)S(1)}, bf16[384,768]{1,0:T(8,128)(2,1)S(1)}, u32[]{:S(2)}, u32[]{:S(2)}) collective-permute-start(bf16[384,768]{1,0:T(8,128)(2,1)S(1)} %constant_dynamic-slice_fusion.14), channel_id=1, source_target_pairs={{0,16},{1,17},{2,18},{3,19},{4,20},{5,21},{6,22},{7,23},{8,24},{9,... | collective-permute-start | bytes 1769480 | tf_op jit(solution)/shard_map/ppermute | solution.py:232
  515.2 105.1 %collective-permute-start.41 = (bf16[768,768]{1,0:T(8,128)(2,1)S(1)}, bf16[768,768]{1,0:T(8,128)(2,1)S(1)}, u32[]{:S(2)}, u32[]{:S(2)}) collective-permute-start(bf16[768,768]{1,0:T(8,128)(2,1)S(1)} %broadcast_select_fusion), channel_id=1, source_target_pairs={{0,1},{1,0},{2,3},{3,2},{4,5},{5,4},{6,7},{7,6},{8,9},{9,8},{10,11... | collective-permute-start | bytes 3538952 | tf_op jit(solution)/shard_map/ppermute | solution.py:232
  516.5 5.9 collective-permute-start.35
  517.2 36.9 %collective-permute-start.36 = (bf16[384,384]{1,0:T(8,128)(2,1)S(1)}, bf16[384,384]{1,0:T(8,128)(2,1)S(1)}, u32[]{:S(2)}, u32[]{:S(2)}) collective-permute-start(bf16[384,384]{1,0:T(8,128)(2,1)S(1)} %copy-done.134), channel_id=1, source_target_pairs={{0,0},{1,1},{2,4},{3,5},{4,2},{5,3},{6,6},{7,7},{8,8},{9,9},{10,12... | collective-permute-start | bytes 884744 | tf_op jit(solution)/shard_map/ppermute | solution.py:286
  522.4 120.6 %copy-start.18 = (bf16[1,2,384,768]{3,2,1,0:T(8,128)(2,1)}, bf16[1,2,384,768]{3,2,1,0:T(8,128)(2,1)S(1)}, u32[]{:S(2)}) copy-start(bf16[1,2,384,768]{3,2,1,0:T(8,128)(2,1)S(1)} %maximum_bitcast_fusion.1) | copy-start | bytes 3538948
  522.5 42.8 %collective-permute-start.30 = (bf16[768,384]{1,0:T(8,128)(2,1)S(1)}, bf16[768,384]{1,0:T(8,128)(2,1)S(1)}, u32[]{:S(2)}, u32[]{:S(2)}) collective-permute-start(bf16[768,384]{1,0:T(8,128)(2,1)S(1)} %fusion.77), channel_id=1, source_target_pairs={{0,4},{1,5},{2,6},{3,7},{4,0},{5,1},{6,2},{7,3},{8,12},{9,13},{10,... | collective-permute-start | bytes 1769480 | tf_op jit(solution)/shard_map/ppermute | solution.py:232
  554.1 45.6 %collective-permute-start.26 = (bf16[768,768]{1,0:T(8,128)(2,1)S(1)}, bf16[768,768]{1,0:T(8,128)(2,1)S(1)}, u32[]{:S(2)}, u32[]{:S(2)}) collective-permute-start(bf16[768,768]{1,0:T(8,128)(2,1)S(1)} %bitcast_convert_fusion), channel_id=1, source_target_pairs={{0,4},{1,5},{2,6},{3,7},{4,0},{5,1},{6,2},{7,3},{8,12},{9,13},{10,... | collective-permute-start | bytes 3538952 | tf_op jit(solution)/shard_map/ppermute | solution.py:232
  561.6 4.7 collective-permute-start.31
  562.0 36.6 %collective-permute-start.39 = (bf16[384,768]{1,0:T(8,128)(2,1)S(1)}, bf16[384,768]{1,0:T(8,128)(2,1)S(1)}, u32[]{:S(2)}, u32[]{:S(2)}) collective-permute-start(bf16[384,768]{1,0:T(8,128)(2,1)S(1)} %broadcast_select_fusion.2), channel_id=1, source_target_pairs={{0,1},{1,0},{2,3},{3,2},{4,5},{5,4},{6,7},{7,6},{8,9},{9,8},{10,11... | collective-permute-start | bytes 1769480 | tf_op jit(solution)/shard_map/ppermute | solution.py:232
  567.5 51.0 %collective-permute-start.32 = (bf16[768,384]{1,0:T(8,128)(2,1)S(1)}, bf16[768,384]{1,0:T(8,128)(2,1)S(1)}, u32[]{:S(2)}, u32[]{:S(2)}) collective-permute-start(bf16[768,384]{1,0:T(8,128)(2,1)S(1)} %pad_maximum_fusion.7), channel_id=1, source_target_pairs={{0,1},{1,0},{2,3},{3,2},{4,5},{5,4},{6,7},{7,6},{8,9},{9,8},{10,11... | collective-permute-start | bytes 1769480 | tf_op jit(solution)/shard_map/ppermute | solution.py:232
  599.0 43.9 %collective-permute-start.40 = (bf16[384,768]{1,0:T(8,128)(2,1)S(1)}, bf16[384,768]{1,0:T(8,128)(2,1)S(1)}, u32[]{:S(2)}, u32[]{:S(2)}) collective-permute-start(bf16[384,768]{1,0:T(8,128)(2,1)S(1)} %add_convert_fusion.22), channel_id=1, source_target_pairs={{0,0},{1,1},{2,4},{3,5},{4,2},{5,3},{6,6},{7,7},{8,8},{9,9},{10,12... | collective-permute-start | bytes 1769480 | tf_op jit(solution)/shard_map/ppermute | solution.py:286
  600.6 28.9 %collective-permute-start.27 = (bf16[384,768]{1,0:T(8,128)(2,1)S(1)}, bf16[384,768]{1,0:T(8,128)(2,1)S(1)}, u32[]{:S(2)}, u32[]{:S(2)}) collective-permute-start(bf16[384,768]{1,0:T(8,128)(2,1)S(1)} %constant_dynamic-slice_fusion.25), channel_id=1, source_target_pairs={{0,16},{1,17},{2,18},{3,19},{4,20},{5,21},{6,22},{7,23},{8,24},{9,... | collective-permute-start | bytes 1769480 | tf_op jit(solution)/shard_map/ppermute | solution.py:232
  618.8 9.9 %collective-permute-start.33 = (bf16[384,384]{1,0:T(8,128)(2,1)S(1)}, bf16[384,384]{1,0:T(8,128)(2,1)S(1)}, u32[]{:S(2)}, u32[]{:S(2)}) collective-permute-start(bf16[384,384]{1,0:T(8,128)(2,1)S(1)} %constant_dynamic-slice_fusion.16), channel_id=1, source_target_pairs={{0,16},{1,17},{2,18},{3,19},{4,20},{5,21},{6,22},{7,23},{8,24},{9,... | collective-permute-start | bytes 884744 | tf_op jit(solution)/shard_map/ppermute | solution.py:232
  620.8 19.5 %collective-permute-start.42 = (bf16[384,768]{1,0:T(8,128)(2,1)S(1)}, bf16[384,768]{1,0:T(8,128)(2,1)S(1)}, u32[]{:S(2)}, u32[]{:S(2)}) collective-permute-start(bf16[384,768]{1,0:T(8,128)(2,1)S(1)} %constant_dynamic-slice_fusion.13), channel_id=1, source_target_pairs={{0,16},{1,17},{2,18},{3,19},{4,20},{5,21},{6,22},{7,23},{8,24},{9,... | collective-permute-start | bytes 1769480 | tf_op jit(solution)/shard_map/ppermute | solution.py:232
  628.8 13.9 %collective-permute-start.34 = (bf16[384,384]{1,0:T(8,128)(2,1)S(1)}, bf16[384,384]{1,0:T(8,128)(2,1)S(1)}, u32[]{:S(2)}, u32[]{:S(2)}) collective-permute-start(bf16[384,384]{1,0:T(8,128)(2,1)S(1)} %add_convert_fusion.37), channel_id=1, source_target_pairs={{0,0},{1,1},{2,4},{3,5},{4,2},{5,3},{6,6},{7,7},{8,8},{9,9},{10,12... | collective-permute-start | bytes 884744 | tf_op jit(solution)/shard_map/ppermute | solution.py:286
  630.3 11.3 %collective-permute-start.28 = (bf16[384,384]{1,0:T(8,128)(2,1)S(1)}, bf16[384,384]{1,0:T(8,128)(2,1)S(1)}, u32[]{:S(2)}, u32[]{:S(2)}) collective-permute-start(bf16[384,384]{1,0:T(8,128)(2,1)S(1)} %pad_maximum_fusion.9), channel_id=1, source_target_pairs={{0,1},{1,0},{2,3},{3,2},{4,5},{5,4},{6,7},{7,6},{8,9},{9,8},{10,11... | collective-permute-start | bytes 884744 | tf_op jit(solution)/shard_map/ppermute | solution.py:232
  640.5 2.4 collective-permute-start.43
  641.7 3.2 collective-permute-start.29
  661.3 42.1 %copy-start.127 = (bf16[64,1152]{1,0:T(8,128)(2,1)}, bf16[64,1152]{1,0:T(8,128)(2,1)S(1)}, u32[]{:S(2)}) copy-start(bf16[64,1152]{1,0:T(8,128)(2,1)S(1)} %constant_dynamic-slice_fusion.10) | copy-start | bytes 442372
  803.3 58.2 %collective-permute-start.50 = (bf16[3592,2,1,96]{0,3,2,1:T(8,128)(2,1)}, bf16[3592,2,1,96]{0,3,2,1:T(8,128)(2,1)}, u32[]{:S(2)}, u32[]{:S(2)}) collective-permute-start(bf16[3592,2,1,96]{0,3,2,1:T(8,128)(2,1)} %dynamic-slice_convert_fusion), channel_id=1, source_target_pairs={{0,4},{4,0},{8,12},{12,8},{16,20},{20,16},{24,28},{28,24},{1,5},{5... | collective-permute-start | bytes 4137992 | tf_op jit(solution)/shard_map/ppermute | solution.py:39
  813.5 32.8 %collective-permute-start.48 = (bf16[2,2,1,96,1152]{4,3,0,2,1:T(8,128)(2,1)}, bf16[2,2,1,96,1152]{4,3,0,2,1:T(8,128)(2,1)}, u32[]{:S(2)}, u32[]{:S(2)}) collective-permute-start(bf16[2,2,1,96,1152]{4,3,0,2,1:T(8,128)(2,1)} %copy.713), channel_id=1, source_target_pairs={{0,4},{4,0},{8,12},{12,8},{16,20},{20,16},{24,28},{28,24},{1,5},{5... | collective-permute-start | bytes 2654216 | tf_op jit(solution)/shard_map/ppermute | solution.py:39
  821.2 21.1 %collective-permute-start.44 = (bf16[2,4,2,1,96,192]{5,4,1,0,3,2:T(8,128)(2,1)}, bf16[2,4,2,1,96,192]{5,4,1,0,3,2:T(8,128)(2,1)}, u32[]{:S(2)}, u32[]{:S(2)}) collective-permute-start(bf16[2,4,2,1,96,192]{5,4,1,0,3,2:T(8,128)(2,1)} %copy.714), channel_id=1, source_target_pairs={{0,4},{4,0},{8,12},{12,8},{16,20},{20,16},{24,28},{28,24},{1,5},{5... | collective-permute-start | bytes 1769480 | tf_op jit(solution)/shard_map/ppermute | solution.py:39
  830.8 27.0 %collective-permute-start.46 = (bf16[2,2,2,1,96,768]{5,4,1,0,3,2:T(8,128)(2,1)}, bf16[2,2,2,1,96,768]{5,4,1,0,3,2:T(8,128)(2,1)}, u32[]{:S(2)}, u32[]{:S(2)}) collective-permute-start(bf16[2,2,2,1,96,768]{5,4,1,0,3,2:T(8,128)(2,1)} %copy.712), channel_id=1, source_target_pairs={{0,4},{4,0},{8,12},{12,8},{16,20},{20,16},{24,28},{28,24},{1,5},{5... | collective-permute-start | bytes 3538952 | tf_op jit(solution)/shard_map/ppermute | solution.py:39
  844.0 12.3 %collective-permute-start.45 = (bf16[2,4,1,1,96,192]{5,4,1,0,3,2:T(8,128)(2,1)S(1)}, bf16[2,4,1,1,96,192]{5,4,1,0,3,2:T(8,128)(2,1)S(1)}, u32[]{:S(2)}, u32[]{:S(2)}) collective-permute-start(bf16[2,4,1,1,96,192]{5,4,1,0,3,2:T(8,128)(2,1)S(1)} %dynamic-slice_convert_fusion.4), channel_id=1, source_target_pairs={{0,8},{4,12},{8,0},{12,4},{16,24},{20,28},{24,16},{28,20},{1,9},{5... | collective-permute-start | bytes 884744 | tf_op jit(solution)/shard_map/ppermute | solution.py:39
  847.9 17.8 %collective-permute-start.49 = (bf16[2,1,1,96,1152]{4,3,0,2,1:T(8,128)(2,1)S(1)}, bf16[2,1,1,96,1152]{4,3,0,2,1:T(8,128)(2,1)S(1)}, u32[]{:S(2)}, u32[]{:S(2)}) collective-permute-start(bf16[2,1,1,96,1152]{4,3,0,2,1:T(8,128)(2,1)S(1)} %dynamic-slice_convert_fusion.3), channel_id=1, source_target_pairs={{0,8},{4,12},{8,0},{12,4},{16,24},{20,28},{24,16},{28,20},{1,9},{5... | collective-permute-start | bytes 1327112 | tf_op jit(solution)/shard_map/ppermute | solution.py:39
  859.4 19.0 %collective-permute-start.47 = (bf16[2,2,1,1,96,768]{5,4,1,0,3,2:T(8,128)(2,1)S(1)}, bf16[2,2,1,1,96,768]{5,4,1,0,3,2:T(8,128)(2,1)S(1)}, u32[]{:S(2)}, u32[]{:S(2)}) collective-permute-start(bf16[2,2,1,1,96,768]{5,4,1,0,3,2:T(8,128)(2,1)S(1)} %dynamic-slice_convert_fusion.2), channel_id=1, source_target_pairs={{0,8},{4,12},{8,0},{12,4},{16,24},{20,28},{24,16},{28,20},{1,9},{5... | collective-permute-start | bytes 1769480 | tf_op jit(solution)/shard_map/ppermute | solution.py:39
  863.4 29.6 %collective-permute-start.51 = (bf16[3592,1,1,96]{0,3,2,1:T(8,128)(2,1)S(1)}, bf16[3592,1,1,96]{0,3,2,1:T(8,128)(2,1)S(1)}, u32[]{:S(2)}, u32[]{:S(2)}) collective-permute-start(bf16[3592,1,1,96]{0,3,2,1:T(8,128)(2,1)S(1)} %dynamic-slice_convert_fusion.1), channel_id=1, source_target_pairs={{0,8},{4,12},{8,0},{12,4},{16,24},{20,28},{24,16},{28,20},{1,9},{5... | collective-permute-start | bytes 2069000 | tf_op jit(solution)/shard_map/ppermute | solution.py:39
  (246 other events, 1357.5 us)
Sparse Core Ops, SparseCore 0:
  11.5 136.4 all-gather.12
  151.5 79.7 all-gather.16
  315.1 22.9 all-gather.14
  510.7 96.1 all-gather.18

commit v3 on v2

--- a/solution.py
+++ b/solution.py
@@ -1,6 +1,7 @@
 import jax
 import jax.numpy as jnp
 from jax import lax
+from jax.experimental import pallas as pl
 from jax.sharding import PartitionSpec as P
 
 D = 768
@@ -305,6 +306,32 @@
     query_key, value_out = totals
     width = query_key.shape[1] // 2
     return [pair_halved(query_key[:, :width], query_key[:, width:]), rows_halved(value_out)]
+
+
+def attn_maps(gathered, layer_at):
+    shards, rows_all, width_all = gathered.shape[1:]
+    width, rows = (width_all // 4, rows_all // 4)
+
+    def kernel(gathered_ref, maps_ref):
+        for kind in range(4):
+            maps_ref[kind] = jnp.concatenate(
+                [
+                    gathered_ref[0, shard][:, kind * width : (kind + 1) * width]
+                    for shard in range(shards)
+                ],
+                axis=1,
+            )
+
+    return pl.pallas_call(
+        kernel,
+        grid=(4,),
+        in_specs=[
+            pl.BlockSpec((1, shards, rows, width_all), lambda at: (layer_at, 0, at, 0)),
+        ],
+        out_specs=pl.BlockSpec((4, rows, shards * width), lambda at: (0, at, 0)),
+        out_shape=jax.ShapeDtypeStruct((4, rows_all, shards * width), gathered.dtype),
+        name="attn_maps",
+    )(gathered)
 
 
 def tied(value, flows):
@@ -439,52 +466,11 @@
     )
 
 
-def reduce_pieces(arrays, axes_at, shift_bits, count_bits, bit_order, across):
-    dp_at = lax.axis_index("dp")
-    blocks = [
-        split_bits(array_in, axis_at, count_bits) for array_in, axis_at in zip(arrays, axes_at)
-    ]
-    for bit_at in bit_order:
-        own_bit = dp_at >> shift_bits + bit_at & 1
-        kept_half = [
-            lax.dynamic_slice_in_dim(block_in, own_bit, 1, axis_at + count_bits - 1 - bit_at)
-            for block_in, axis_at in zip(blocks, axes_at)
-        ]
-        sent_half = [
-            lax.dynamic_slice_in_dim(block_in, 1 - own_bit, 1, axis_at + count_bits - 1 - bit_at)
-            for block_in, axis_at in zip(blocks, axes_at)
-        ]
-        if across:
-            received = swapped(
-                (
-                    shortened(sent_half[0]),
-                    shortened(sent_half[1]),
-                    shortened(sent_half[2]),
-                    shortened(sent_half[3]),
-                ),
-                "dp",
-                shift_bits + bit_at,
-            )
-        else:
-            received = swapped(
-                (
-                    shortened(sent_half[0]),
-                    shortened(sent_half[1]),
-                    shortened(sent_half[2]),
-                    shortened(sent_half[3]),
-                ),
-                "dp",
-                shift_bits + bit_at,
-            )
-        blocks = [own_part + other_part for own_part, other_part in zip(kept_half, received)]
-    return [
-        block_in.reshape(
-            array_in.shape[:axis_at]
-            + (array_in.shape[axis_at] >> count_bits,)
-            + array_in.shape[axis_at + 1 :]
-        )
-        for block_in, array_in, axis_at in zip(blocks, arrays, axes_at)
-    ]
+def group_step(block, axis_at, count_bits, bit_at):
+    own_bit = lax.axis_index("dp") >> bit_at & 1
+    at = axis_at + count_bits - 1 - bit_at
+    sent = shortened(lax.dynamic_slice_in_dim(block, 1 - own_bit, 1, at))
+    return lax.dynamic_slice_in_dim(block, own_bit, 1, at) + swapped(sent, "dp", bit_at)
 
 
 def adam_update(gradient, first_old, second_old):
@@ -547,18 +533,14 @@
     def attn_local(layer_at):
         return jnp.transpose(w_attn[layer_at], (1, 0, 2)).reshape(1, row_width, 4 * col_width)
 
-    def attn_whole(gathered):
-        shaped = gathered.reshape(shards, D, 4, col_width)
-        return jnp.transpose(shaped, (2, 1, 0, 3)).reshape(4, D, D)
-
     first_local = [attn_local(layer_at) for layer_at in range(L)] + list(w_mlp[: L - 1])
     first_local = jnp.concatenate(
         [part.astype(LOW_TYPE).reshape(-1, row_width, 4 * col_width) for part in first_local]
     )
     first_whole = lax.all_gather(first_local, everyone, axis=1, tiled=True)
     last_whole = lax.all_gather(w_mlp[L - 1].astype(LOW_TYPE), everyone, axis=1, tiled=True)
-    attn_all = [attn_whole(first_whole[layer_at]) for layer_at in range(L)]
     units_whole = first_whole.reshape(-1, shards, D, 4 * col_width)
+    attn_all = [attn_maps(units_whole, layer_at) for layer_at in range(L)]
     mlp_all = [
         [[units_whole[L + 2 * layer_at + kind, at] for at in range(shards)] for kind in range(2)]
         for layer_at in range(L - 1)
@@ -671,46 +653,54 @@
         if flows:
             sums_list[layer_at + 1] = [flows[0], homeward(flows[1])]
         flows = fresh
-    sums_list[0] = [
-        homeward(mlp_third(mlp_second(flows[0]))),
-        homeward(attn_third(attn_second(flows[1]))),
-    ]
+    last_mlp = homeward(mlp_third(mlp_second(flows[0])))
+    last_attn = attn_third(attn_second(flows[1]))
     grad_patch = weight_grad(noised, grad_stream.astype(LOW_TYPE))
     mine = patches_own.shape[0]
-    vectors = jnp.concatenate(
-        [grad_now.reshape(-1) for grad_now in mod_list]
+    early = jnp.concatenate(
+        [grad_now.reshape(-1) for grad_now in mod_list[1:]]
         + [grad_final.reshape(-1)]
-        + [grad_now.astype(LOW_TYPE) for grad_now in bias_list]
-        + [
+        + [grad_now.astype(LOW_TYPE) for grad_now in bias_list[1:]]
+        + [grad_head.astype(LOW_TYPE).reshape(-1)]
+    )
+    late_part = jnp.concatenate(
+        [
+            mod_list[0].reshape(-1),
+            bias_list[0].astype(LOW_TYPE),
             jnp.sum(grad_stream, (0, 1)).astype(LOW_TYPE),
             grad_patch.astype(LOW_TYPE).reshape(-1),
-            grad_head.astype(LOW_TYPE).reshape(-1),
         ]
     )
-    gathered = lax.all_gather(vectors, ("dp", "tensor"))
     devices = dp_count * shards
-    offset = 0
-
-    def taken(width):
-        nonlocal offset
-        offset += width
-        return gathered[:, offset - width : offset]
-
+
+    def cutter(vectors):
+        gathered = lax.all_gather(vectors, ("dp", "tensor"))
+        offset = 0
+
+        def taken(width):
+            nonlocal offset
+            offset += width
+            return gathered[:, offset - width : offset]
+
+        return taken
+
+    take_early, take_late = (cutter(early), cutter(late_part))
+    takers = [take_late] + [take_early] * (L - 1)
     grad_mods = [
-        natural_order(taken(mine * 6 * D).reshape(devices, mine, 6 * D), stretches)
-        for layer_at in range(L)
+        natural_order(taker(mine * 6 * D).reshape(devices, mine, 6 * D), stretches)
+        for taker in takers
     ]
-    grad_finals = natural_order(taken(mine * 2 * D).reshape(devices, mine, 2 * D), stretches)
+    grad_finals = natural_order(take_early(mine * 2 * D).reshape(devices, mine, 2 * D), stretches)
 
     def group_sums(part):
         shaped = part.astype(jnp.float32).reshape(stretches, 2, 2, 2, shards // 2, -1)
         return jnp.sum(shaped, (0, 2, 4)).reshape(GROUPS, -1)
 
     layer_bias = 7 * D + FF - 3 * D
-    bias_sums = [group_sums(taken(layer_bias)) for layer_at in range(L)]
-    patch_bias = group_sums(taken(D))
-    patch_sums = group_sums(taken(PATCH_IN * D)).reshape(GROUPS, PATCH_IN, D)
-    head_sums = group_sums(taken(PATCH_IN * D)).reshape(GROUPS, PATCH_IN, D)
+    bias_sums = [group_sums(taker(layer_bias)) for taker in takers]
+    patch_bias = group_sums(take_late(D))
+    patch_sums = group_sums(take_late(PATCH_IN * D)).reshape(GROUPS, PATCH_IN, D)
+    head_sums = group_sums(take_early(PATCH_IN * D)).reshape(GROUPS, PATCH_IN, D)
 
     own_mods = [
         lax.dynamic_slice_in_dim(grad_now, shard_at * mod_width, mod_width, 1)
@@ -771,6 +761,10 @@
         ],
         axis=1,
     )
+    side_squares = jnp.sum(grad_mod_map * grad_mod_map) + jnp.sum(grad_embed * grad_embed) / shards
+    bias_squares = jnp.sum(bias_groups * bias_groups, 1)
+    last_attn, (side_squares, bias_squares) = tied(last_attn, (side_squares, bias_squares))
+    sums_list[0] = [last_mlp, homeward(last_attn)]
     attn_now = jnp.stack(
         [
             jnp.stack(
@@ -784,17 +778,19 @@
     squares = (
         jnp.sum(reduced[0] * reduced[0])
         + jnp.sum(reduced[1] * reduced[1])
-        + jnp.sum(reduced[2] * reduced[2])
-        + jnp.sum(reduced[3] * reduced[3]) / shards
+        + side_squares
     )
     picked = (jnp.arange(GROUPS, dtype=jnp.int32) == group_at).astype(jnp.float32)
+    local_totals = jnp.concatenate(
+        [picked * squares, jnp.full((GROUPS,), loss_here), jnp.zeros((128 - 2 * GROUPS,))]
+    )
     totals = jnp.sum(
         lax.all_gather(
-            jnp.concatenate([picked * squares, jnp.reshape(loss_here, (1,))]), ("dp", "tensor")
-        ),
+            jnp.broadcast_to(local_totals, (8, 128)), ("dp", "tensor"), axis=0, tiled=True
+        ).reshape(-1, 8, 128)[:, 0],
         0,
     )
-    group_norms = jnp.sqrt(totals[:GROUPS] + jnp.sum(bias_groups * bias_groups, 1))
+    group_norms = jnp.sqrt(totals[:GROUPS] + bias_squares)
     clip_scale = CLIP_NORM / (group_norms + 1e-06)
     own_scale = jnp.sum(picked * clip_scale)
     shift_group = GROUPS.bit_length() - 1
@@ -802,15 +798,25 @@
     momenta_in = (momentum_attn, momentum_mlp, momentum_mod, momentum_embed)
     firsts_in = (first_attn, first_mlp, first_mod, first_embed)
     seconds_in = (second_attn, second_mlp, second_mod, second_embed)
-    updates, new_firsts, new_seconds = ([], [], [])
+    axes_at = (2, 2, 1, 1)
+    steps, new_firsts, new_seconds = ([], [], [])
     for index_at in range(4):
+        grad_now = reduced[index_at]
+        if index_at >= 2:
+            grad_now, steps[index_at - 2] = tied(grad_now, steps[index_at - 2])
         update, first_new, second_new = adam_update(
-            reduced[index_at] * own_scale, firsts_in[index_at], seconds_in[index_at]
+            grad_now * own_scale, firsts_in[index_at], seconds_in[index_at]
         )
-        updates.append(update)
+        axis_at = axes_at[index_at]
+        steps.append(group_step(split_bits(update, axis_at, shift_group), axis_at, shift_group, 0))
         new_firsts.append(first_new)
         new_seconds.append(second_new)
-    summed = reduce_pieces(updates, (2, 2, 1, 1), 0, shift_group, list(range(shift_group)), True)
+    summed = []
+    for index_at in range(4):
+        block = steps[index_at]
+        for bit_at in range(1, shift_group):
+            block = group_step(block, axes_at[index_at], shift_group, bit_at)
+        summed.append(block.reshape(weights_in[index_at].shape))
     new_weights, new_momenta = ([], [])
     for index_at in range(4):
         outer_grad = LEARN_RATE * (summed[index_at] / GROUPS + WEIGHT_DECAY * weights_in[index_at])

time: 912 us -> 903 us (level)
  local copies, waits for them, and re-layouts: 186 us -> 153 us
  other arithmetic: 115 us -> 143 us
  starting transfers between devices: 85.3 us -> 60.4 us
  waiting for transfers between devices: 160 us -> 136 us
  blocking collectives: 152 us -> 168 us
  matrix products: 182 us -> 195 us
  Pallas kernels: 0 us -> 10.9 us
    all_gather x0 -> x1, blocking collectives: none -> 72.9 us  [per_device(): lax.all_gather(jnp.broadcast_to(local_totals, (8, 128)), ('dp', 'tensor')...]
    ppermute x32, waiting for transfers between devices: 89.3 us -> 43.9 us  [exchanged(): lax.ppermute(value, ('dp', 'tensor'), [(source, source ^ mask) for source...]
    ppermute x32, starting transfers between devices: 64.8 us -> 21.6 us  [exchanged(): lax.ppermute(value, ('dp', 'tensor'), [(source, source ^ mask) for source...]
    unnamed x2 -> x1, blocking collectives: 78.7 us -> 38.5 us
    slice x14 -> x2, local copies, waits for them, and re-layouts: 39.6 us -> 0.08 us  [the longest x3 21.5 us: per_device(): attn_all = [attn_whole(first_whole[layer_at]) for layer_at in range(L)]]
    all_gather x1, waiting for transfers between devices: 0.02 us -> 20.4 us  [per_device(): lax.all_gather(w_mlp[L - 1].astype(LOW_TYPE), everyone, axis=1, tiled=True)]
    ppermute x8, starting transfers between devices: 12.1 us -> 32.1 us  [homeward(): return [lax.ppermute(value, ('dp', 'tensor'), pairs) for value in values]]
    another operation x6 -> x4, local copies, waits for them, and re-layouts: 20.9 us -> 2.22 us  [the longest x1 1.92 us: per_device(): group_sums(take_early(PATCH_IN * D)).reshape(GROUPS, PATCH_IN, D)]
  transfers between devices with their start and end apart: 56 -> 57, of which waited for: 15 -> 12; matrix products, arithmetic and copies ran while one was open for 34% -> 47% of each run, Pallas kernels for 0% -> 1%
where the time goes in v3:
time: 903 us; the launch traced here: 890 us
  matrix products  195 us (22%)
  blocking collectives  168 us (19%)
  local copies, waits for them, and re-layouts  153 us (17%)
  other arithmetic  143 us (16%)
  waiting for transfers between devices  136 us (15%)
  starting transfers between devices  60.4 us (7%)
  between operations  23.5 us (3%)
  Pallas kernels  10.9 us (1%)
    all_gather x1, blocking collectives, per_device(): lax.all_gather(jnp.broadcast_to(local_totals, (8, 128)), ('dp', 'tensor')...  72.9 us
    unnamed x535, local copies, waits for them, and re-layouts  71.7 us
    dot_general x36, matrix products, weight_grad(): lax.dot_general(inputs, grads_out, ((leading, leading), ((), ())), prefer...  69.3 us
    dot_general x29, matrix products, product_t(): lax.dot_general(left, right, (((left.ndim - 1,), (1,)), ((), ())), prefer...  50.2 us
    dot_general x32, matrix products, product(): return jnp.dot(left, right, preferred_element_type=jnp.float32)  49.9 us
    ppermute x32, waiting for transfers between devices, exchanged(): lax.ppermute(value, ('dp', 'tensor'), [(source, source ^ mask) for source...  43.9 us
    all_gather x1, waiting for transfers between devices, per_device(): first_whole = lax.all_gather(first_local, everyone, axis=1, tiled=True)  40.2 us
    unnamed x1, blocking collectives  38.5 us
  transfers between devices with their start and end apart: 57, of which 12 were waited for; matrix products, arithmetic and copies ran while one was open for 47% of the time, Pallas kernels for 1%

profile of v3, /device:TPU:0, one launch (start us, length us, event | category | flops | bytes accessed | tf_op | source)
XLA Modules:
  0.0 890.4 jit_solution(4461857539670440946)
XLA Ops:
  16.0 10.1 %all-gather.5 = s32[8,8,2]{1,2,0:T(2,128)S(1)} all-gather(s32[1,8,2]{1,2,0:T(2,128)S(1)} %add_bitcast_fusion), channel_id=1, replica_groups=mesh['dp'=8,'tensor'=4] {'dp'}, dimensions={0}, use_global_device_ids=true | all-gather | bytes 576 | tf_op jit(solution)/shard_map/all_gather | solution.py:527
  28.0 9.6 %all_gather.46 = f32[96,768]{0,1:T(8,128)S(1)} all-gather(f32[96,96]{0,1:T(8,128)S(1)} %copy.488), channel_id=1, replica_groups=mesh['dp'=8,'tensor'=4] {'dp'}, dimensions={1}, use_global_device_ids=true | all-gather | bytes 331776 | tf_op jit(solution)/shard_map/all_gather | solution.py:559
  40.9 38.5 %all-reduce.3 = bf16[64,2688]{1,0:T(8,128)(2,1)S(1)} all-reduce(f32[64,2688]{1,0:T(8,128)S(1)} %pad_maximum_fusion.4), channel_id=7, replica_groups=mesh['dp'=8,'tensor'=4] {'dp'}, use_global_device_ids=true, to_apply=%region_5.6.clone | all-reduce | flops 172032 | bytes 1032192
  79.5 14.3 %all-gather = bf16[32,2688]{1,0:T(8,128)(2,1)S(1)} all-gather(bf16[8,2688]{1,0:T(8,128)(2,1)S(1)} %dynamic-slice_convert_fusion.5), channel_id=2, replica_groups=mesh['dp'=8,'tensor'=4] {'tensor'}, dimensions={0}, use_global_device_ids=true | all-gather | bytes 215040 | tf_op jit(solution)/shard_map/all_gather | solution.py:596
  96.3 3.6 copy.565
  108.1 40.2 %all-gather.14.cloned.1.call-done = bf16[4,3072,768]{2,1,0:T(8,128)(2,1)} async-done(((bf16[4,96,768]{2,1,0:T(8,128)(2,1)}), bf16[4,3072,768]{2,1,0:T(8,128)(2,1)}) %all-gather.14.cloned.1.call-update) | async-done | bytes 18874384 | tf_op jit(solution)/shard_map/all_gather | solution.py:540
  148.2 5.4 attn_maps.2
  153.6 5.6 attn_maps.3
  165.1 2.9 add_convert_fusion.18
  178.2 3.8 fusion.258
  207.2 3.4 fusion.256
  211.2 20.4 %all-gather.18.cloned.1.call-done = bf16[1,2,3072,768]{3,2,1,0:T(8,128)(2,1)} async-done(((bf16[1,2,96,768]{3,2,1,0:T(8,128)(2,1)}), bf16[1,2,3072,768]{3,2,1,0:T(8,128)(2,1)}) %all-gather.18.cloned.1.call-update) | async-done | bytes 9437200 | tf_op jit(solution)/shard_map/all_gather | solution.py:541
  233.8 3.7 fusion.100
  270.4 3.1 multiply_reduce_fusion.8
  274.0 4.9 multiply_reduce_fusion.27
  282.6 3.5 add_convert_fusion.10
  286.1 3.9 add_convert_fusion.8
  290.1 3.9 add_convert_fusion.9
  294.0 3.2 add_convert_fusion.11
  297.2 3.1 convolution_convert_fusion.3
  301.7 5.7 bitcast_reduce_fusion.1
  317.3 3.2 fusion.96
  332.0 4.5 multiply_reduce_fusion.10
  362.2 3.2 multiply_add_fusion.4
  373.0 2.6 add_convert_fusion.33
  375.5 2.5 add_convert_fusion.34
  385.0 3.0 add_convert_fusion.6
  389.5 4.0 bitcast_convert_fusion.5
  400.4 2.5 fusion.273
  421.5 11.9 %collective-permute-done.15 = bf16[384,768]{1,0:T(8,128)(2,1)S(1)} collective-permute-done((bf16[384,768]{1,0:T(8,128)(2,1)S(1)}, bf16[384,768]{1,0:T(8,128)(2,1)S(1)}, u32[]{:S(2)}, u32[]{:S(2)}) %collective-permute-start.15) | collective-permute-done | bytes 589856 | tf_op jit(solution)/shard_map/ppermute | solution.py:233
  441.1 6.1 collective-permute-done.25
  449.1 6.0 collective-permute-start.22
  455.9 6.2 collective-permute-start.23
  464.0 2.5 add_convert_fusion.2
  466.6 2.5 add_convert_fusion.3
  470.9 2.9 convolution_convert_fusion.1
  475.3 4.9 multiply_reduce_fusion
  492.6 2.6 fusion.88
  496.7 2.6 multiply_reduce_fusion.11
  499.3 3.8 collective-permute-start.35
  520.5 3.1 bitcast_convert_fusion
  554.8 3.0 reduce_sum.758
  565.1 2.7 add_convert_fusion.22
  567.8 6.0 collective-permute-start.40
  582.6 9.7 %collective-permute-done.27 = bf16[384,768]{1,0:T(8,128)(2,1)S(1)} collective-permute-done((bf16[384,768]{1,0:T(8,128)(2,1)S(1)}, bf16[384,768]{1,0:T(8,128)(2,1)S(1)}, u32[]{:S(2)}, u32[]{:S(2)}) %collective-permute-start.27) | collective-permute-done | bytes 589856 | tf_op jit(solution)/shard_map/ppermute | solution.py:233
  594.7 12.4 %collective-permute-done.32 = bf16[384,384]{1,0:T(8,128)(2,1)S(1)} collective-permute-done((bf16[384,384]{1,0:T(8,128)(2,1)S(1)}, bf16[384,384]{1,0:T(8,128)(2,1)S(1)}, u32[]{:S(2)}, u32[]{:S(2)}) %collective-permute-start.32) | collective-permute-done | bytes 294944 | tf_op jit(solution)/shard_map/ppermute | solution.py:233
  608.9 6.1 collective-permute-start.43
  624.3 13.1 %all-gather.4 = bf16[256,96]{1,0:T(8,128)(2,1)S(1)} all-gather(bf16[64,96]{1,0:T(8,128)(2,1)S(1)} %fusion.86), channel_id=6, replica_groups=mesh['dp'=8,'tensor'=4] {'tensor'}, dimensions={0}, use_global_device_ids=true | all-gather | bytes 61440 | tf_op jit(solution)/shard_map/all_gather | solution.py:713
  638.8 9.2 %all-gather.7 = bf16[8,96,64]{1,2,0:T(8,128)(2,1)S(1)} all-gather(bf16[1,96,64]{1,2,0:T(8,128)(2,1)S(1)} %fusion.205), channel_id=1, replica_groups=mesh['dp'=8,'tensor'=4] {'dp'}, dimensions={0}, use_global_device_ids=true | all-gather | bytes 110592 | tf_op jit(solution)/shard_map/all_gather | solution.py:715
  669.8 3.5 pad_maximum_fusion
  689.4 72.9 %all_gather.59 = f32[256,128]{1,0:T(8,128)S(1)} all-gather(f32[8,128]{1,0:T(8,128)S(1)} %broadcast_in_dim.19), channel_id=1, replica_groups=mesh['dp'=8,'tensor'=4] {'dp','tensor'}, dimensions={0}, use_global_device_ids=true | all-gather | bytes 135168 | tf_op jit(solution)/shard_map/all_gather | solution.py:788
  764.7 6.7 add_divide_fusion.3
  774.5 8.4 add_divide_fusion.1
  785.4 3.3 copy.574
  788.8 3.3 copy.575
  792.8 3.5 fusion.155
  796.3 3.1 copy_add_fusion.2
  799.5 9.6 %add_divide_fusion.2 = (f32[2,384,1152]{2,1,0:T(8,128)}, f32[2,384,1152]{2,1,0:T(8,128)}, f32[2,384,1152]{2,1,0:T(8,128)}) fusion(f32[2,384,1152]{2,1,0:T(8,128)S(1)} %get-tuple-element.101, f32[]{:T(128)} %get-tuple-element.312, f32[2,384,1152]{2,1,0:T(8,128)} %param.42, f32[2,384,1152]{2,1,0:T(8,128)} %param.43), kind=kLoop, calls=%fused_computation.32 | loop fusion | flops 10616832 | bytes 21233668 | tf_op jit(solution)/shard_map/div | solution.py:480
  815.7 10.9 %add_divide_fusion = (f32[3592,384]{1,0:T(8,128)}, f32[3592,384]{1,0:T(8,128)}, f32[3592,384]{1,0:T(8,128)}) fusion(f32[3592,384]{1,0:T(8,128)S(1)} %bitcast.651, f32[]{:T(128)} %get-tuple-element.312, f32[3592,384]{1,0:T(8,128)} %param.44, f32[3592,384]{1,0:T(8,128)} %param.45), kind=kLoop, calls=%fused_computation.16 | loop fusion | flops 16551936 | bytes 33103876 | tf_op jit(solution)/shard_map/div | solution.py:480
  826.6 6.7 copy.573
  836.4 3.2 multiply_subtract_fusion.3
  845.7 10.2 %collective-permute-done.47 = bf16[2,2,1,1,96,768]{5,4,1,0,3,2:T(8,128)(2,1)S(1)} collective-permute-done((bf16[2,2,1,1,96,768]{5,4,1,0,3,2:T(8,128)(2,1)S(1)}, bf16[2,2,1,1,96,768]{5,4,1,0,3,2:T(8,128)(2,1)S(1)}, u32[]{:S(2)}, u32[]{:S(2)}) %collective-permute-start.47) | collective-permute-done | bytes 589856 | tf_op jit(solution)/shard_map/ppermute | solution.py:40
  857.8 7.6 collective-permute-done.49
  866.9 13.2 %collective-permute-done.51 = bf16[3592,1,1,96]{0,3,2,1:T(8,128)(2,1)S(1)} collective-permute-done((bf16[3592,1,1,96]{0,3,2,1:T(8,128)(2,1)S(1)}, bf16[3592,1,1,96]{0,3,2,1:T(8,128)(2,1)S(1)}, u32[]{:S(2)}, u32[]{:S(2)}) %collective-permute-start.51) | collective-permute-done | bytes 689696 | tf_op jit(solution)/shard_map/ppermute | solution.py:40
  (999 shorter events, 364.9 us)
Async XLA Ops:
  7.2 141.0 %all-gather.14.cloned.1.call-start = ((), (), s32[]{:S(2)}) async-start(), calls=%async_computation | async-start | bytes 19464192 | tf_op jit(solution)/shard_map/all_gather | solution.py:540
  11.1 220.5 %all-gather.18.cloned.1.call-start = ((), (), s32[]{:S(2)}) async-start(), calls=%async_computation.2 | async-start | bytes 9732096 | tf_op jit(solution)/shard_map/all_gather | solution.py:541
  12.1 93.0 %collective-permute-start = (f32[2,1]{0,1:T(1,128)S(1)}, f32[2,1]{0,1:T(1,128)S(1)}, u32[]{:S(2)}, u32[]{:S(2)}) collective-permute-start(f32[2,1]{0,1:T(1,128)S(1)} %dynamic-slice_bitcast_fusion.4), channel_id=1, source_target_pairs={{0,4},{1,5},{2,6},{3,7},{4,0},{5,1},{6,2},{7,3},{8,12},{9,13},{10,... | collective-permute-start | bytes 32 | tf_op jit(solution)/shard_map/ppermute | solution.py:178
  14.0 91.2 %collective-permute-start.2 = (f32[2,256,16]{1,2,0:T(8,128)}, f32[2,256,16]{1,2,0:T(8,128)}, u32[]{:S(2)}, u32[]{:S(2)}) collective-permute-start(f32[2,256,16]{1,2,0:T(8,128)} %constant_dynamic-slice_fusion.49), channel_id=1, source_target_pairs={{0,4},{1,5},{2,6},{3,7},{4,0},{5,1},{6,2},{7,3},{8,12},{9,13},{10,... | collective-permute-start | bytes 98312 | tf_op jit(solution)/shard_map/ppermute | solution.py:178
  15.4 89.8 %collective-permute-start.1 = (f32[2,256,16]{1,2,0:T(8,128)}, f32[2,256,16]{1,2,0:T(8,128)}, u32[]{:S(2)}, u32[]{:S(2)}) collective-permute-start(f32[2,256,16]{1,2,0:T(8,128)} %constant_dynamic-slice_fusion.50), channel_id=1, source_target_pairs={{0,4},{1,5},{2,6},{3,7},{4,0},{5,1},{6,2},{7,3},{8,12},{9,13},{10,... | collective-permute-start | bytes 98312 | tf_op jit(solution)/shard_map/ppermute | solution.py:178
  16.0 78.7 %copy-start.90 = (bf16[3592,96]{0,1:T(8,128)(2,1)}, bf16[3592,96]{0,1:T(8,128)(2,1)S(1)}, u32[]{:S(2)}) copy-start(bf16[3592,96]{0,1:T(8,128)(2,1)S(1)} %convert_element_type.839) | copy-start | bytes 2068996
  37.7 56.8 %copy-start.92 = (f32[96,768]{1,0:T(8,128)}, f32[96,768]{1,0:T(8,128)S(1)}, u32[]{:S(2)}) copy-start(f32[96,768]{1,0:T(8,128)S(1)} %copy.489) | copy-start | bytes 884740
  94.4 12.6 %collective-permute-start.3 = (bf16[2,4,2688]{2,0,1:T(2,128)(2,1)}, bf16[2,4,2688]{2,0,1:T(2,128)(2,1)}, u32[]{:S(2)}, u32[]{:S(2)}) collective-permute-start(bf16[2,4,2688]{2,0,1:T(2,128)(2,1)} %dynamic-slice_bitcast_fusion), channel_id=1, source_target_pairs={{0,4},{1,5},{2,6},{3,7},{4,0},{5,1},{6,2},{7,3},{8,12},{9,13},{10,... | collective-permute-start | bytes 129032 | tf_op jit(solution)/shard_map/ppermute | solution.py:178
  94.4 283.7 %all-gather.16.cloned.1.call-start = ((), (), s32[]{:S(2)}) async-start(), calls=%async_computation.1 | async-start | bytes 1548288 | tf_op jit(solution)/shard_map/all_gather | solution.py:642
  107.0 46.7 %copy-start.162 = (f32[2,256]{1,0:T(2,128)}, f32[2,256]{1,0:T(2,128)S(1)}, u32[]{:S(2)}) copy-start(f32[2,256]{1,0:T(2,128)S(1)} %add_rsqrt_fusion.4) | copy-start | bytes 6148
  107.2 46.5 %copy-start.143 = (f32[2,768]{1,0:T(2,128)}, f32[2,768]{1,0:T(2,128)S(1)}, u32[]{:S(2)}) copy-start(f32[2,768]{1,0:T(2,128)S(1)} %get-tuple-element.409) | copy-start | bytes 18436
  107.2 70.1 %copy-start.141 = (f32[2,768]{1,0:T(2,128)}, f32[2,768]{1,0:T(2,128)S(1)}, u32[]{:S(2)}) copy-start(f32[2,768]{1,0:T(2,128)S(1)} %get-tuple-element.407) | copy-start | bytes 18436
  107.2 82.9 %copy-start.145 = (f32[2,768]{1,0:T(2,128)}, f32[2,768]{1,0:T(2,128)S(1)}, u32[]{:S(2)}) copy-start(f32[2,768]{1,0:T(2,128)S(1)} %get-tuple-element.404) | copy-start | bytes 18436
  108.1 57.0 %copy-start.30 = (bf16[2,256,768]{2,1,0:T(8,128)(2,1)}, bf16[2,256,768]{2,1,0:T(8,128)(2,1)S(1)}, u32[]{:S(2)}) copy-start(bf16[2,256,768]{2,1,0:T(8,128)(2,1)S(1)} %add_convert_fusion.20) | copy-start | bytes 2359300
  266.7 19.4 %collective-permute-start.7 = (bf16[768,768]{1,0:T(8,128)(2,1)}, bf16[768,768]{1,0:T(8,128)(2,1)}, u32[]{:S(2)}, u32[]{:S(2)}) collective-permute-start(bf16[768,768]{1,0:T(8,128)(2,1)} %bitcast_convert_fusion.12), channel_id=1, source_target_pairs={{0,4},{1,5},{2,6},{3,7},{4,0},{5,1},{6,2},{7,3},{8,12},{9,13},{10,... | collective-permute-start | bytes 3538952 | tf_op jit(solution)/shard_map/ppermute | solution.py:233
  267.0 23.1 %collective-permute-start.6 = (bf16[768,768]{1,0:T(8,128)(2,1)}, bf16[768,768]{1,0:T(8,128)(2,1)}, u32[]{:S(2)}, u32[]{:S(2)}) collective-permute-start(bf16[768,768]{1,0:T(8,128)(2,1)} %bitcast_convert_fusion.14), channel_id=1, source_target_pairs={{0,4},{1,5},{2,6},{3,7},{4,0},{5,1},{6,2},{7,3},{8,12},{9,13},{10,... | collective-permute-start | bytes 3538952 | tf_op jit(solution)/shard_map/ppermute | solution.py:233
  269.9 11.5 %collective-permute-start.5 = (bf16[768,768]{1,0:T(8,128)(2,1)}, bf16[768,768]{1,0:T(8,128)(2,1)}, u32[]{:S(2)}, u32[]{:S(2)}) collective-permute-start(bf16[768,768]{1,0:T(8,128)(2,1)} %bitcast_convert_fusion.16), channel_id=1, source_target_pairs={{0,4},{1,5},{2,6},{3,7},{4,0},{5,1},{6,2},{7,3},{8,12},{9,13},{10,... | collective-permute-start | bytes 3538952 | tf_op jit(solution)/shard_map/ppermute | solution.py:233
  270.2 23.8 %collective-permute-start.4 = (bf16[768,768]{1,0:T(8,128)(2,1)}, bf16[768,768]{1,0:T(8,128)(2,1)}, u32[]{:S(2)}, u32[]{:S(2)}) collective-permute-start(bf16[768,768]{1,0:T(8,128)(2,1)} %bitcast_convert_fusion.18), channel_id=1, source_target_pairs={{0,4},{1,5},{2,6},{3,7},{4,0},{5,1},{6,2},{7,3},{8,12},{9,13},{10,... | collective-permute-start | bytes 3538952 | tf_op jit(solution)/shard_map/ppermute | solution.py:233
  273.6 261.6 %all-gather.20.cloned.1.call-start = ((), (), s32[]{:S(2)}) async-start(), calls=%async_computation.3 | async-start | bytes 2027520 | tf_op jit(solution)/shard_map/all_gather | solution.py:677
  315.2 57.8 %collective-permute-start.13 = (bf16[768,384]{1,0:T(8,128)(2,1)}, bf16[768,384]{1,0:T(8,128)(2,1)}, u32[]{:S(2)}, u32[]{:S(2)}) collective-permute-start(bf16[768,384]{1,0:T(8,128)(2,1)} %fusion.74), channel_id=1, source_target_pairs={{0,4},{1,5},{2,6},{3,7},{4,0},{5,1},{6,2},{7,3},{8,12},{9,13},{10,... | collective-permute-start | bytes 1769480 | tf_op jit(solution)/shard_map/ppermute | solution.py:233
  317.1 58.5 %collective-permute-start.12 = (bf16[768,384]{1,0:T(8,128)(2,1)}, bf16[768,384]{1,0:T(8,128)(2,1)}, u32[]{:S(2)}, u32[]{:S(2)}) collective-permute-start(bf16[768,384]{1,0:T(8,128)(2,1)} %fusion.71), channel_id=1, source_target_pairs={{0,4},{1,5},{2,6},{3,7},{4,0},{5,1},{6,2},{7,3},{8,12},{9,13},{10,... | collective-permute-start | bytes 1769480 | tf_op jit(solution)/shard_map/ppermute | solution.py:233
  324.5 58.3 %collective-permute-start.10 = (bf16[768,768]{1,0:T(8,128)(2,1)}, bf16[768,768]{1,0:T(8,128)(2,1)}, u32[]{:S(2)}, u32[]{:S(2)}) collective-permute-start(bf16[768,768]{1,0:T(8,128)(2,1)} %broadcast_select_fusion.1), channel_id=1, source_target_pairs={{0,1},{1,0},{2,3},{3,2},{4,5},{5,4},{6,7},{7,6},{8,9},{9,8},{10,11... | collective-permute-start | bytes 3538952 | tf_op jit(solution)/shard_map/ppermute | solution.py:233
  326.7 42.5 %collective-permute-start.9 = (bf16[384,768]{1,0:T(8,128)(2,1)}, bf16[384,768]{1,0:T(8,128)(2,1)}, u32[]{:S(2)}, u32[]{:S(2)}) collective-permute-start(bf16[384,768]{1,0:T(8,128)(2,1)} %constant_dynamic-slice_fusion.45), channel_id=1, source_target_pairs={{0,16},{1,17},{2,18},{3,19},{4,20},{5,21},{6,22},{7,23},{8,24},{9,... | collective-permute-start | bytes 1769480 | tf_op jit(solution)/shard_map/ppermute | solution.py:233
  329.0 41.5 %collective-permute-start.8 = (bf16[384,768]{1,0:T(8,128)(2,1)}, bf16[384,768]{1,0:T(8,128)(2,1)}, u32[]{:S(2)}, u32[]{:S(2)}) collective-permute-start(bf16[384,768]{1,0:T(8,128)(2,1)} %constant_dynamic-slice_fusion.46), channel_id=1, source_target_pairs={{0,16},{1,17},{2,18},{3,19},{4,20},{5,21},{6,22},{7,23},{8,24},{9,... | collective-permute-start | bytes 1769480 | tf_op jit(solution)/shard_map/ppermute | solution.py:233
  361.9 254.0 %all-gather.22.cloned.1.call-start = ((), (), s32[]{:S(2)}) async-start(), calls=%async_computation.4 | async-start | bytes 3750912 | tf_op jit(solution)/shard_map/all_gather | solution.py:677
  369.2 15.8 %collective-permute-start.11 = (bf16[768,768]{1,0:T(8,128)(2,1)}, bf16[768,768]{1,0:T(8,128)(2,1)}, u32[]{:S(2)}, u32[]{:S(2)}) collective-permute-start(bf16[768,768]{1,0:T(8,128)(2,1)} %bitcast_convert_fusion.10), channel_id=1, source_target_pairs={{0,4},{1,5},{2,6},{3,7},{4,0},{5,1},{6,2},{7,3},{8,12},{9,13},{10,... | collective-permute-start | bytes 3538952 | tf_op jit(solution)/shard_map/ppermute | solution.py:233
  405.1 16.3 %collective-permute-start.16 = (bf16[384,768]{1,0:T(8,128)(2,1)S(1)}, bf16[384,768]{1,0:T(8,128)(2,1)S(1)}, u32[]{:S(2)}, u32[]{:S(2)}) collective-permute-start(bf16[384,768]{1,0:T(8,128)(2,1)S(1)} %constant_dynamic-slice_fusion.39), channel_id=1, source_target_pairs={{0,16},{1,17},{2,18},{3,19},{4,20},{5,21},{6,22},{7,23},{8,24},{9,... | collective-permute-start | bytes 1769480 | tf_op jit(solution)/shard_map/ppermute | solution.py:233
  406.7 26.7 %collective-permute-start.15 = (bf16[384,768]{1,0:T(8,128)(2,1)S(1)}, bf16[384,768]{1,0:T(8,128)(2,1)S(1)}, u32[]{:S(2)}, u32[]{:S(2)}) collective-permute-start(bf16[384,768]{1,0:T(8,128)(2,1)S(1)} %constant_dynamic-slice_fusion.40), channel_id=1, source_target_pairs={{0,16},{1,17},{2,18},{3,19},{4,20},{5,21},{6,22},{7,23},{8,24},{9,... | collective-permute-start | bytes 1769480 | tf_op jit(solution)/shard_map/ppermute | solution.py:233
  407.3 27.0 %collective-permute-start.14 = (bf16[384,768]{1,0:T(8,128)(2,1)S(1)}, bf16[384,768]{1,0:T(8,128)(2,1)S(1)}, u32[]{:S(2)}, u32[]{:S(2)}) collective-permute-start(bf16[384,768]{1,0:T(8,128)(2,1)S(1)} %broadcast_select_fusion.3), channel_id=1, source_target_pairs={{0,1},{1,0},{2,3},{3,2},{4,5},{5,4},{6,7},{7,6},{8,9},{9,8},{10,11... | collective-permute-start | bytes 1769480 | tf_op jit(solution)/shard_map/ppermute | solution.py:233
  419.3 18.0 %collective-permute-start.17 = (bf16[768,384]{1,0:T(8,128)(2,1)S(1)}, bf16[768,384]{1,0:T(8,128)(2,1)S(1)}, u32[]{:S(2)}, u32[]{:S(2)}) collective-permute-start(bf16[768,384]{1,0:T(8,128)(2,1)S(1)} %pad_maximum_fusion.6), channel_id=1, source_target_pairs={{0,1},{1,0},{2,3},{3,2},{4,5},{5,4},{6,7},{7,6},{8,9},{9,8},{10,11... | collective-permute-start | bytes 1769480 | tf_op jit(solution)/shard_map/ppermute | solution.py:233
  437.6 26.5 %collective-permute-start.21 = (bf16[768,768]{1,0:T(8,128)(2,1)S(1)}, bf16[768,768]{1,0:T(8,128)(2,1)S(1)}, u32[]{:S(2)}, u32[]{:S(2)}) collective-permute-start(bf16[768,768]{1,0:T(8,128)(2,1)S(1)} %copy-done.188), channel_id=1, source_target_pairs={{0,4},{1,5},{2,6},{3,7},{4,0},{5,1},{6,2},{7,3},{8,12},{9,13},{10,... | collective-permute-start | bytes 3538952 | tf_op jit(solution)/shard_map/ppermute | solution.py:233
  437.7 18.3 %collective-permute-start.19 = (bf16[768,768]{1,0:T(8,128)(2,1)S(1)}, bf16[768,768]{1,0:T(8,128)(2,1)S(1)}, u32[]{:S(2)}, u32[]{:S(2)}) collective-permute-start(bf16[768,768]{1,0:T(8,128)(2,1)S(1)} %copy-done.189), channel_id=1, source_target_pairs={{0,4},{1,5},{2,6},{3,7},{4,0},{5,1},{6,2},{7,3},{8,12},{9,13},{10,... | collective-permute-start | bytes 3538952 | tf_op jit(solution)/shard_map/ppermute | solution.py:233
  438.2 9.1 %collective-permute-start.25 = (bf16[384,384]{1,0:T(8,128)(2,1)S(1)}, bf16[384,384]{1,0:T(8,128)(2,1)S(1)}, u32[]{:S(2)}, u32[]{:S(2)}) collective-permute-start(bf16[384,384]{1,0:T(8,128)(2,1)S(1)} %constant_dynamic-slice_fusion.30), channel_id=1, source_target_pairs={{0,16},{1,17},{2,18},{3,19},{4,20},{5,21},{6,22},{7,23},{8,24},{9,... | collective-permute-start | bytes 884744 | tf_op jit(solution)/shard_map/ppermute | solution.py:233
  440.3 8.8 collective-permute-start.24
  441.0 25.6 %collective-permute-start.20 = (bf16[768,768]{1,0:T(8,128)(2,1)S(1)}, bf16[768,768]{1,0:T(8,128)(2,1)S(1)}, u32[]{:S(2)}, u32[]{:S(2)}) collective-permute-start(bf16[768,768]{1,0:T(8,128)(2,1)S(1)} %bitcast_convert_fusion.6), channel_id=1, source_target_pairs={{0,4},{1,5},{2,6},{3,7},{4,0},{5,1},{6,2},{7,3},{8,12},{9,13},{10,... | collective-permute-start | bytes 3538952 | tf_op jit(solution)/shard_map/ppermute | solution.py:233
  447.2 21.9 %collective-permute-start.18 = (bf16[768,768]{1,0:T(8,128)(2,1)S(1)}, bf16[768,768]{1,0:T(8,128)(2,1)S(1)}, u32[]{:S(2)}, u32[]{:S(2)}) collective-permute-start(bf16[768,768]{1,0:T(8,128)(2,1)S(1)} %bitcast_convert_fusion.8), channel_id=1, source_target_pairs={{0,4},{1,5},{2,6},{3,7},{4,0},{5,1},{6,2},{7,3},{8,12},{9,13},{10,... | collective-permute-start | bytes 3538952 | tf_op jit(solution)/shard_map/ppermute | solution.py:233
  449.1 46.1 %collective-permute-start.22 = (bf16[384,768]{1,0:T(8,128)(2,1)}, bf16[384,768]{1,0:T(8,128)(2,1)}, u32[]{:S(2)}, u32[]{:S(2)}) collective-permute-start(bf16[384,768]{1,0:T(8,128)(2,1)} %add_convert_fusion.32), channel_id=1, source_target_pairs={{0,0},{1,1},{2,4},{3,5},{4,2},{5,3},{6,6},{7,7},{8,8},{9,9},{10,12... | collective-permute-start | bytes 1769480 | tf_op jit(solution)/shard_map/ppermute | solution.py:287
  455.9 39.3 %collective-permute-start.23 = (bf16[384,768]{1,0:T(8,128)(2,1)}, bf16[384,768]{1,0:T(8,128)(2,1)}, u32[]{:S(2)}, u32[]{:S(2)}) collective-permute-start(bf16[384,768]{1,0:T(8,128)(2,1)} %add_convert_fusion.31), channel_id=1, source_target_pairs={{0,0},{1,1},{2,4},{3,5},{4,2},{5,3},{6,6},{7,7},{8,8},{9,9},{10,12... | collective-permute-start | bytes 1769480 | tf_op jit(solution)/shard_map/ppermute | solution.py:287
  483.3 43.6 %collective-permute-start.37 = (bf16[384,768]{1,0:T(8,128)(2,1)}, bf16[384,768]{1,0:T(8,128)(2,1)}, u32[]{:S(2)}, u32[]{:S(2)}) collective-permute-start(bf16[384,768]{1,0:T(8,128)(2,1)} %constant_dynamic-slice_fusion.8), channel_id=1, source_target_pairs={{0,16},{1,17},{2,18},{3,19},{4,20},{5,21},{6,22},{7,23},{8,24},{9,... | collective-permute-start | bytes 1769480 | tf_op jit(solution)/shard_map/ppermute | solution.py:233
  484.6 42.3 %collective-permute-start.38 = (bf16[384,768]{1,0:T(8,128)(2,1)}, bf16[384,768]{1,0:T(8,128)(2,1)}, u32[]{:S(2)}, u32[]{:S(2)}) collective-permute-start(bf16[384,768]{1,0:T(8,128)(2,1)} %constant_dynamic-slice_fusion.7), channel_id=1, source_target_pairs={{0,16},{1,17},{2,18},{3,19},{4,20},{5,21},{6,22},{7,23},{8,24},{9,... | collective-permute-start | bytes 1769480 | tf_op jit(solution)/shard_map/ppermute | solution.py:233
  487.3 89.4 %collective-permute-start.41 = (bf16[768,768]{1,0:T(8,128)(2,1)}, bf16[768,768]{1,0:T(8,128)(2,1)}, u32[]{:S(2)}, u32[]{:S(2)}) collective-permute-start(bf16[768,768]{1,0:T(8,128)(2,1)} %broadcast_select_fusion), channel_id=1, source_target_pairs={{0,1},{1,0},{2,3},{3,2},{4,5},{5,4},{6,7},{7,6},{8,9},{9,8},{10,11... | collective-permute-start | bytes 3538952 | tf_op jit(solution)/shard_map/ppermute | solution.py:233
  499.3 24.3 %collective-permute-start.35 = (bf16[384,384]{1,0:T(8,128)(2,1)}, bf16[384,384]{1,0:T(8,128)(2,1)}, u32[]{:S(2)}, u32[]{:S(2)}) collective-permute-start(bf16[384,384]{1,0:T(8,128)(2,1)} %add_convert_fusion.40), channel_id=1, source_target_pairs={{0,0},{1,1},{2,4},{3,5},{4,2},{5,3},{6,6},{7,7},{8,8},{9,9},{10,12... | collective-permute-start | bytes 884744 | tf_op jit(solution)/shard_map/ppermute | solution.py:287
  503.1 22.5 %collective-permute-start.36 = (bf16[384,384]{1,0:T(8,128)(2,1)}, bf16[384,384]{1,0:T(8,128)(2,1)S(1)}, u32[]{:S(2)}, u32[]{:S(2)}) collective-permute-start(bf16[384,384]{1,0:T(8,128)(2,1)} %add_convert_fusion.39), channel_id=1, source_target_pairs={{0,0},{1,1},{2,4},{3,5},{4,2},{5,3},{6,6},{7,7},{8,8},{9,9},{10,12... | collective-permute-start | bytes 884744 | tf_op jit(solution)/shard_map/ppermute | solution.py:287
  523.6 7.4 collective-permute-start.29
  525.6 6.4 collective-permute-start.30
  526.9 46.9 %collective-permute-start.26 = (bf16[768,768]{1,0:T(8,128)(2,1)}, bf16[768,768]{1,0:T(8,128)(2,1)}, u32[]{:S(2)}, u32[]{:S(2)}) collective-permute-start(bf16[768,768]{1,0:T(8,128)(2,1)} %bitcast_convert_fusion), channel_id=1, source_target_pairs={{0,4},{1,5},{2,6},{3,7},{4,0},{5,1},{6,2},{7,3},{8,12},{9,13},{10,... | collective-permute-start | bytes 3538952 | tf_op jit(solution)/shard_map/ppermute | solution.py:233
  529.4 35.7 %collective-permute-start.39 = (bf16[384,768]{1,0:T(8,128)(2,1)}, bf16[384,768]{1,0:T(8,128)(2,1)}, u32[]{:S(2)}, u32[]{:S(2)}) collective-permute-start(bf16[384,768]{1,0:T(8,128)(2,1)} %broadcast_select_fusion.2), channel_id=1, source_target_pairs={{0,1},{1,0},{2,3},{3,2},{4,5},{5,4},{6,7},{7,6},{8,9},{9,8},{10,11... | collective-permute-start | bytes 1769480 | tf_op jit(solution)/shard_map/ppermute | solution.py:233
  534.7 45.4 %collective-permute-start.31 = (bf16[768,384]{1,0:T(8,128)(2,1)}, bf16[768,384]{1,0:T(8,128)(2,1)}, u32[]{:S(2)}, u32[]{:S(2)}) collective-permute-start(bf16[768,384]{1,0:T(8,128)(2,1)} %pad_maximum_fusion.7), channel_id=1, source_target_pairs={{0,1},{1,0},{2,3},{3,2},{4,5},{5,4},{6,7},{7,6},{8,9},{9,8},{10,11... | collective-permute-start | bytes 1769480 | tf_op jit(solution)/shard_map/ppermute | solution.py:233
  567.8 113.0 %collective-permute-start.40 = (bf16[384,768]{1,0:T(8,128)(2,1)}, bf16[384,768]{1,0:T(8,128)(2,1)}, u32[]{:S(2)}, u32[]{:S(2)}) collective-permute-start(bf16[384,768]{1,0:T(8,128)(2,1)} %add_convert_fusion.22), channel_id=1, source_target_pairs={{0,0},{1,1},{2,4},{3,5},{4,2},{5,3},{6,6},{7,7},{8,8},{9,9},{10,12... | collective-permute-start | bytes 1769480 | tf_op jit(solution)/shard_map/ppermute | solution.py:287
  576.1 16.3 %collective-permute-start.27 = (bf16[384,768]{1,0:T(8,128)(2,1)S(1)}, bf16[384,768]{1,0:T(8,128)(2,1)S(1)}, u32[]{:S(2)}, u32[]{:S(2)}) collective-permute-start(bf16[384,768]{1,0:T(8,128)(2,1)S(1)} %constant_dynamic-slice_fusion.25), channel_id=1, source_target_pairs={{0,16},{1,17},{2,18},{3,19},{4,20},{5,21},{6,22},{7,23},{8,24},{9,... | collective-permute-start | bytes 1769480 | tf_op jit(solution)/shard_map/ppermute | solution.py:233
  579.1 28.8 %collective-permute-start.42 = (bf16[384,768]{1,0:T(8,128)(2,1)S(1)}, bf16[384,768]{1,0:T(8,128)(2,1)S(1)}, u32[]{:S(2)}, u32[]{:S(2)}) collective-permute-start(bf16[384,768]{1,0:T(8,128)(2,1)S(1)} %constant_dynamic-slice_fusion.6), channel_id=1, source_target_pairs={{0,16},{1,17},{2,18},{3,19},{4,20},{5,21},{6,22},{7,23},{8,24},{9,... | collective-permute-start | bytes 1769480 | tf_op jit(solution)/shard_map/ppermute | solution.py:233
  581.5 25.7 %collective-permute-start.32 = (bf16[384,384]{1,0:T(8,128)(2,1)S(1)}, bf16[384,384]{1,0:T(8,128)(2,1)S(1)}, u32[]{:S(2)}, u32[]{:S(2)}) collective-permute-start(bf16[384,384]{1,0:T(8,128)(2,1)S(1)} %constant_dynamic-slice_fusion.16), channel_id=1, source_target_pairs={{0,16},{1,17},{2,18},{3,19},{4,20},{5,21},{6,22},{7,23},{8,24},{9,... | collective-permute-start | bytes 884744 | tf_op jit(solution)/shard_map/ppermute | solution.py:233
  593.1 21.9 %collective-permute-start.28 = (bf16[384,384]{1,0:T(8,128)(2,1)S(1)}, bf16[384,384]{1,0:T(8,128)(2,1)S(1)}, u32[]{:S(2)}, u32[]{:S(2)}) collective-permute-start(bf16[384,384]{1,0:T(8,128)(2,1)S(1)} %pad_maximum_fusion.9), channel_id=1, source_target_pairs={{0,1},{1,0},{2,3},{3,2},{4,5},{5,4},{6,7},{7,6},{8,9},{9,8},{10,11... | collective-permute-start | bytes 884744 | tf_op jit(solution)/shard_map/ppermute | solution.py:233
  608.9 71.9 %collective-permute-start.43 = (bf16[384,768]{1,0:T(8,128)(2,1)}, bf16[384,768]{1,0:T(8,128)(2,1)}, u32[]{:S(2)}, u32[]{:S(2)}) collective-permute-start(bf16[384,768]{1,0:T(8,128)(2,1)} %add_convert_fusion.21), channel_id=1, source_target_pairs={{0,0},{1,1},{2,4},{3,5},{4,2},{5,3},{6,6},{7,7},{8,8},{9,9},{10,12... | collective-permute-start | bytes 1769480 | tf_op jit(solution)/shard_map/ppermute | solution.py:287
  677.7 7.5 collective-permute-start.33
  682.5 2.9 collective-permute-start.34
  773.4 22.9 %collective-permute-start.44 = (bf16[2,4,2,1,96,192]{5,4,1,0,3,2:T(8,128)(2,1)}, bf16[2,4,2,1,96,192]{5,4,1,0,3,2:T(8,128)(2,1)}, u32[]{:S(2)}, u32[]{:S(2)}) collective-permute-start(bf16[2,4,2,1,96,192]{5,4,1,0,3,2:T(8,128)(2,1)} %copy.660), channel_id=1, source_target_pairs={{0,4},{4,0},{8,12},{12,8},{16,20},{20,16},{24,28},{28,24},{1,5},{5... | collective-permute-start | bytes 1769480 | tf_op jit(solution)/shard_map/ppermute | solution.py:40
  785.4 28.6 %collective-permute-start.46 = (bf16[2,2,2,1,96,768]{5,4,1,0,3,2:T(8,128)(2,1)}, bf16[2,2,2,1,96,768]{5,4,1,0,3,2:T(8,128)(2,1)}, u32[]{:S(2)}, u32[]{:S(2)}) collective-permute-start(bf16[2,2,2,1,96,768]{5,4,1,0,3,2:T(8,128)(2,1)} %copy.658), channel_id=1, source_target_pairs={{0,4},{4,0},{8,12},{12,8},{16,20},{20,16},{24,28},{28,24},{1,5},{5... | collective-permute-start | bytes 3538952 | tf_op jit(solution)/shard_map/ppermute | solution.py:40
  811.6 30.1 %collective-permute-start.48 = (bf16[2,2,1,96,1152]{4,3,0,2,1:T(8,128)(2,1)}, bf16[2,2,1,96,1152]{4,3,0,2,1:T(8,128)(2,1)}, u32[]{:S(2)}, u32[]{:S(2)}) collective-permute-start(bf16[2,2,1,96,1152]{4,3,0,2,1:T(8,128)(2,1)} %copy.659), channel_id=1, source_target_pairs={{0,4},{4,0},{8,12},{12,8},{16,20},{20,16},{24,28},{28,24},{1,5},{5... | collective-permute-start | bytes 2654216 | tf_op jit(solution)/shard_map/ppermute | solution.py:40
  814.1 22.3 %collective-permute-start.45 = (bf16[2,4,1,1,96,192]{5,4,1,0,3,2:T(8,128)(2,1)}, bf16[2,4,1,1,96,192]{5,4,1,0,3,2:T(8,128)(2,1)S(1)}, u32[]{:S(2)}, u32[]{:S(2)}) collective-permute-start(bf16[2,4,1,1,96,192]{5,4,1,0,3,2:T(8,128)(2,1)} %dynamic-slice_convert_fusion.4), channel_id=1, source_target_pairs={{0,8},{4,12},{8,0},{12,4},{16,24},{20,28},{24,16},{28,20},{1,9},{5... | collective-permute-start | bytes 884744 | tf_op jit(solution)/shard_map/ppermute | solution.py:40
  835.5 7.7 collective-permute-start.50
  839.6 16.3 %collective-permute-start.47 = (bf16[2,2,1,1,96,768]{5,4,1,0,3,2:T(8,128)(2,1)S(1)}, bf16[2,2,1,1,96,768]{5,4,1,0,3,2:T(8,128)(2,1)S(1)}, u32[]{:S(2)}, u32[]{:S(2)}) collective-permute-start(bf16[2,2,1,1,96,768]{5,4,1,0,3,2:T(8,128)(2,1)S(1)} %dynamic-slice_convert_fusion.2), channel_id=1, source_target_pairs={{0,8},{4,12},{8,0},{12,4},{16,24},{20,28},{24,16},{28,20},{1,9},{5... | collective-permute-start | bytes 1769480 | tf_op jit(solution)/shard_map/ppermute | solution.py:40
  843.2 22.2 %collective-permute-start.49 = (bf16[2,1,1,96,1152]{4,3,0,2,1:T(8,128)(2,1)S(1)}, bf16[2,1,1,96,1152]{4,3,0,2,1:T(8,128)(2,1)S(1)}, u32[]{:S(2)}, u32[]{:S(2)}) collective-permute-start(bf16[2,1,1,96,1152]{4,3,0,2,1:T(8,128)(2,1)S(1)} %dynamic-slice_convert_fusion.3), channel_id=1, source_target_pairs={{0,8},{4,12},{8,0},{12,4},{16,24},{20,28},{24,16},{28,20},{1,9},{5... | collective-permute-start | bytes 1327112 | tf_op jit(solution)/shard_map/ppermute | solution.py:40
  843.7 36.5 %collective-permute-start.51 = (bf16[3592,1,1,96]{0,3,2,1:T(8,128)(2,1)S(1)}, bf16[3592,1,1,96]{0,3,2,1:T(8,128)(2,1)S(1)}, u32[]{:S(2)}, u32[]{:S(2)}) collective-permute-start(bf16[3592,1,1,96]{0,3,2,1:T(8,128)(2,1)S(1)} %dynamic-slice_convert_fusion.1), channel_id=1, source_target_pairs={{0,8},{4,12},{8,0},{12,4},{16,24},{20,28},{24,16},{28,20},{1,9},{5... | collective-permute-start | bytes 2069000 | tf_op jit(solution)/shard_map/ppermute | solution.py:40
  (233 other events, 1287.3 us)
Sparse Core Ops, SparseCore 0:
  11.5 136.6 all-gather.13
  151.8 79.7 all-gather.17
  273.7 23.2 all-gather.15
  362.0 55.0 all-gather.19
  520.6 67.0 all-gather.21

commit v4 on v3

--- a/solution.py
+++ b/solution.py
@@ -285,6 +285,10 @@
         core, high = (source // shards & 1, source % shards >> 1)
         pairs.append((source, source ^ (core ^ high) * (shards + shards // 2)))
     return [lax.ppermute(value, ("dp", "tensor"), pairs) for value in values]
+
+
+def squared(values):
+    return sum(jnp.sum(jnp.square(value.astype(jnp.float32))) for value in values)
 
 
 def mlp_second(totals):
@@ -396,7 +400,7 @@
         queries, key_rows, values, log_total, grad_attended
     )
     if flows:
-        flows = [homeward(flows[0]), attn_third(flows[1])]
+        flows = [homeward(flows[0]), attn_third(flows[1]), squared(flows[0])]
         grad_queries, flows = tied(grad_queries, flows)
 
     def map_grads(side):
@@ -638,6 +642,7 @@
         grad_hidden * (1.0 + final_mod[:, None, D:]), normed_last, inverse_last
     )
     mod_list, bias_list, sums_list, flows = ([None] * L, [None] * L, [None] * L, None)
+    moved_squares = 0.0
     late, grad_stream = tied(jnp.concatenate([second_map, cond_rows]), grad_stream)
     late = lax.all_gather(late, "dp", axis=1, tiled=True)
     second_time, cond_act = (late[:D], late[D:])
@@ -652,9 +657,12 @@
         )
         if flows:
             sums_list[layer_at + 1] = [flows[0], homeward(flows[1])]
+            moved_squares = moved_squares + flows[2] + squared(flows[1])
         flows = fresh
-    last_mlp = homeward(mlp_third(mlp_second(flows[0])))
+    last_mlp = mlp_third(mlp_second(flows[0]))
     last_attn = attn_third(attn_second(flows[1]))
+    moved_squares = moved_squares + squared(last_mlp) + squared(last_attn)
+    last_mlp = homeward(last_mlp)
     grad_patch = weight_grad(noised, grad_stream.astype(LOW_TYPE))
     mine = patches_own.shape[0]
     early = jnp.concatenate(
@@ -775,21 +783,20 @@
     ).astype(jnp.float32)
     mlp_now = jnp.stack([jnp.stack(sums[0]) for sums in sums_list]).astype(jnp.float32)
     reduced = [attn_now, mlp_now, grad_mod_map, grad_embed]
-    squares = (
-        jnp.sum(reduced[0] * reduced[0])
-        + jnp.sum(reduced[1] * reduced[1])
-        + side_squares
-    )
-    picked = (jnp.arange(GROUPS, dtype=jnp.int32) == group_at).astype(jnp.float32)
-    local_totals = jnp.concatenate(
-        [picked * squares, jnp.full((GROUPS,), loss_here), jnp.zeros((128 - 2 * GROUPS,))]
-    )
-    totals = jnp.sum(
-        lax.all_gather(
-            jnp.broadcast_to(local_totals, (8, 128)), ("dp", "tensor"), axis=0, tiled=True
-        ).reshape(-1, 8, 128)[:, 0],
-        0,
-    )
+    groups_here = jnp.arange(GROUPS, dtype=jnp.int32)
+    picked = (groups_here == group_at).astype(jnp.float32)
+    moved_group = (dp_at - (dp_at & 1) + (shard_at >> 1)) % GROUPS
+    moved_picked = (groups_here == moved_group).astype(jnp.float32)
+    totals = jnp.concatenate(
+        [
+            picked * side_squares + moved_picked * moved_squares,
+            jnp.full((GROUPS,), loss_here),
+            jnp.zeros((128 - 2 * GROUPS,)),
+        ]
+    )
+    for axis in ("tensor", "dp"):
+        rows_now = lax.all_gather(jnp.broadcast_to(totals, (8, 128)), axis, axis=0, tiled=True)
+        totals = jnp.sum(rows_now.reshape(-1, 8, 128)[:, 0], 0)
     group_norms = jnp.sqrt(totals[:GROUPS] + bias_squares)
     clip_scale = CLIP_NORM / (group_norms + 1e-06)
     own_scale = jnp.sum(picked * clip_scale)
@@ -799,24 +806,30 @@
     firsts_in = (first_attn, first_mlp, first_mod, first_embed)
     seconds_in = (second_attn, second_mlp, second_mod, second_embed)
     axes_at = (2, 2, 1, 1)
-    steps, new_firsts, new_seconds = ([], [], [])
-    for index_at in range(4):
+    steps, summed, new_firsts, new_seconds = ([None] * 4, [None] * 4, [None] * 4, [None] * 4)
+
+    def crossed(index_at):
+        block = steps[index_at]
+        for bit_at in range(1, shift_group):
+            block = group_step(block, axes_at[index_at], shift_group, bit_at)
+        return block.reshape(weights_in[index_at].shape)
+
+    for index_at in (1, 0, 2, 3):
         grad_now = reduced[index_at]
-        if index_at >= 2:
-            grad_now, steps[index_at - 2] = tied(grad_now, steps[index_at - 2])
-        update, first_new, second_new = adam_update(
+        if index_at == 2:
+            grad_now, steps[1] = tied(grad_now, steps[1])
+        if index_at == 3:
+            summed[1] = crossed(1)
+            grad_now, (summed[1], steps[0]) = tied(grad_now, (summed[1], steps[0]))
+        update, new_firsts[index_at], new_seconds[index_at] = adam_update(
             grad_now * own_scale, firsts_in[index_at], seconds_in[index_at]
         )
         axis_at = axes_at[index_at]
-        steps.append(group_step(split_bits(update, axis_at, shift_group), axis_at, shift_group, 0))
-        new_firsts.append(first_new)
-        new_seconds.append(second_new)
-    summed = []
-    for index_at in range(4):
-        block = steps[index_at]
-        for bit_at in range(1, shift_group):
-            block = group_step(block, axes_at[index_at], shift_group, bit_at)
-        summed.append(block.reshape(weights_in[index_at].shape))
+        steps[index_at] = group_step(
+            split_bits(update, axis_at, shift_group), axis_at, shift_group, 0
+        )
+    for index_at in (0, 2, 3):
+        summed[index_at] = crossed(index_at)
     new_weights, new_momenta = ([], [])
     for index_at in range(4):
         outer_grad = LEARN_RATE * (summed[index_at] / GROUPS + WEIGHT_DECAY * weights_in[index_at])

time: 903 us -> 881 us (0.976)
  blocking collectives: 168 us -> 116 us
  waiting for transfers between devices: 136 us -> 154 us
  local copies, waits for them, and re-layouts: 153 us -> 140 us
  matrix products: 195 us -> 206 us
    all_gather x1 -> x2, blocking collectives: 72.9 us -> 21.9 us  [per_device(): lax.all_gather(jnp.broadcast_to(totals, (8, 128)), axis, axis=0, tiled=True)]
    ppermute x32, waiting for transfers between devices: 43.9 us -> 67.8 us  [exchanged(): lax.ppermute(value, ('dp', 'tensor'), [(source, source ^ mask) for source...]
    reduce_sum x3 -> x10, other arithmetic: 3.76 us -> 13.8 us  [the longest x8 13.8 us: squared(): jnp.sum(jnp.square(value.astype(jnp.float32)))]
    unnamed x535 -> x569, local copies, waits for them, and re-layouts: 71.7 us -> 63.3 us
    convert_element_type x16 -> x12, other arithmetic: 18.5 us -> 14.7 us  [summed_low(): (left.astype(jnp.float32) + right.astype(jnp.float32)).astype(LOW_TYPE)]
  transfers between devices with their start and end apart: 57 -> 57, of which waited for: 12 -> 14; matrix products, arithmetic and copies ran while one was open for 47% -> 47% of each run, Pallas kernels for 1% -> 1%
where the time goes in v4:
time: 881 us; the launch traced here: 868 us
  matrix products  206 us (23%)
  waiting for transfers between devices  154 us (17%)
  other arithmetic  150 us (17%)
  local copies, waits for them, and re-layouts  140 us (16%)
  blocking collectives  116 us (13%)
  starting transfers between devices  63.7 us (7%)
  between operations  27.7 us (3%)
  Pallas kernels  10.9 us (1%)
    dot_general x36, matrix products, weight_grad(): lax.dot_general(inputs, grads_out, ((leading, leading), ((), ())), prefer...  76.5 us
    ppermute x32, waiting for transfers between devices, exchanged(): lax.ppermute(value, ('dp', 'tensor'), [(source, source ^ mask) for source...  67.8 us
    unnamed x569, local copies, waits for them, and re-layouts  63.3 us
    dot_general x32, matrix products, product(): return jnp.dot(left, right, preferred_element_type=jnp.float32)  49.9 us
    dot_general x29, matrix products, product_t(): lax.dot_general(left, right, (((left.ndim - 1,), (1,)), ((), ())), prefer...  49.7 us
    all_gather x1, waiting for transfers between devices, per_device(): first_whole = lax.all_gather(first_local, everyone, axis=1, tiled=True)  40.1 us
    unnamed x1, blocking collectives  38.6 us
    ppermute x8, starting transfers between devices, homeward(): return [lax.ppermute(value, ('dp', 'tensor'), pairs) for value in values]  34.1 us
  transfers between devices with their start and end apart: 57, of which 14 were waited for; matrix products, arithmetic and copies ran while one was open for 47% of the time, Pallas kernels for 1%

profile of v4, /device:TPU:0, one launch (start us, length us, event | category | flops | bytes accessed | tf_op | source)
XLA Modules:
  0.0 868.4 jit_solution(13742209803096655324)
XLA Ops:
  16.0 10.1 %all-gather.5 = s32[8,8,2]{1,2,0:T(2,128)S(1)} all-gather(s32[1,8,2]{1,2,0:T(2,128)S(1)} %add_bitcast_fusion.1), channel_id=1, replica_groups=mesh['dp'=8,'tensor'=4] {'dp'}, dimensions={0}, use_global_device_ids=true | all-gather | bytes 576 | tf_op jit(solution)/shard_map/all_gather | solution.py:531
  28.0 9.6 %all_gather.49 = f32[96,768]{0,1:T(8,128)S(1)} all-gather(f32[96,96]{0,1:T(8,128)S(1)} %copy.488), channel_id=1, replica_groups=mesh['dp'=8,'tensor'=4] {'dp'}, dimensions={1}, use_global_device_ids=true | all-gather | bytes 331776 | tf_op jit(solution)/shard_map/all_gather | solution.py:563
  40.9 38.6 %all-reduce.3 = bf16[64,2688]{1,0:T(8,128)(2,1)S(1)} all-reduce(f32[64,2688]{1,0:T(8,128)S(1)} %pad_maximum_fusion.4), channel_id=7, replica_groups=mesh['dp'=8,'tensor'=4] {'dp'}, use_global_device_ids=true, to_apply=%region_5.6.clone | all-reduce | flops 172032 | bytes 1032192
  79.5 14.2 %all-gather = bf16[32,2688]{1,0:T(8,128)(2,1)S(1)} all-gather(bf16[8,2688]{1,0:T(8,128)(2,1)S(1)} %dynamic-slice_convert_fusion.5), channel_id=2, replica_groups=mesh['dp'=8,'tensor'=4] {'tensor'}, dimensions={0}, use_global_device_ids=true | all-gather | bytes 215040 | tf_op jit(solution)/shard_map/all_gather | solution.py:600
  96.4 3.6 copy.568
  108.1 40.1 %all-gather.14.cloned.1.call-done = bf16[4,3072,768]{2,1,0:T(8,128)(2,1)} async-done(((bf16[4,96,768]{2,1,0:T(8,128)(2,1)}), bf16[4,3072,768]{2,1,0:T(8,128)(2,1)}) %all-gather.14.cloned.1.call-update) | async-done | bytes 18874384 | tf_op jit(solution)/shard_map/all_gather | solution.py:544
  148.2 5.4 attn_maps.2
  153.6 5.6 attn_maps.3
  165.0 2.9 add_convert_fusion.18
  178.1 3.8 fusion.250
  207.2 3.4 fusion.248
  211.2 20.4 %all-gather.18.cloned.1.call-done = bf16[1,2,3072,768]{3,2,1,0:T(8,128)(2,1)} async-done(((bf16[1,2,96,768]{3,2,1,0:T(8,128)(2,1)}), bf16[1,2,3072,768]{3,2,1,0:T(8,128)(2,1)}) %all-gather.18.cloned.1.call-update) | async-done | bytes 9437200 | tf_op jit(solution)/shard_map/all_gather | solution.py:545
  233.8 3.7 fusion.91
  270.3 3.1 multiply_reduce_fusion.8
  273.9 4.9 multiply_reduce_fusion.27
  282.5 3.5 add_convert_fusion.10
  286.0 3.9 add_convert_fusion.8
  290.0 3.9 add_convert_fusion.9
  293.9 3.1 add_convert_fusion.11
  297.1 3.1 convolution_convert_fusion.3
  301.6 5.7 bitcast_reduce_fusion.1
  317.1 3.2 fusion.89
  331.7 4.5 multiply_reduce_fusion.10
  361.7 3.2 multiply_add_fusion.6
  372.6 2.6 add_convert_fusion.33
  384.6 3.0 add_convert_fusion.6
  389.1 4.0 bitcast_convert_fusion.5
  421.9 6.5 collective-permute-done.16
  428.5 11.6 %collective-permute-done.15 = bf16[384,768]{1,0:T(8,128)(2,1)S(1)} collective-permute-done((bf16[384,768]{1,0:T(8,128)(2,1)S(1)}, bf16[384,768]{1,0:T(8,128)(2,1)S(1)}, u32[]{:S(2)}, u32[]{:S(2)}) %collective-permute-start.15) | collective-permute-done | bytes 589856 | tf_op jit(solution)/shard_map/ppermute | solution.py:233
  447.0 6.0 collective-permute-start.22
  459.1 6.1 collective-permute-start.23
  467.1 3.5 add_convert_fusion.4
  470.7 3.9 add_convert_fusion.2
  479.1 2.9 convolution_convert_fusion.1
  483.5 5.1 bitcast_reduce_fusion
  488.5 4.6 multiply_reduce_fusion
  547.2 14.3 %collective-permute-done.34 = bf16[384,768]{1,0:T(8,128)(2,1)S(1)} collective-permute-done((bf16[384,768]{1,0:T(8,128)(2,1)S(1)}, bf16[384,768]{1,0:T(8,128)(2,1)S(1)}, u32[]{:S(2)}, u32[]{:S(2)}) %collective-permute-start.34) | collective-permute-done | bytes 589856 | tf_op jit(solution)/shard_map/ppermute | solution.py:233
  576.2 17.7 %collective-permute-done.31 = bf16[768,384]{1,0:T(8,128)(2,1)} collective-permute-done((bf16[768,384]{1,0:T(8,128)(2,1)}, bf16[768,384]{1,0:T(8,128)(2,1)}, u32[]{:S(2)}, u32[]{:S(2)}) %collective-permute-start.31) | collective-permute-done | bytes 589856 | tf_op jit(solution)/shard_map/ppermute | solution.py:233
  603.7 2.9 collective-permute-done.35
  606.6 2.9 multiply_reduce_fusion.35
  609.5 6.0 collective-permute-start.38
  615.5 3.3 collective-permute-done.27
  621.6 9.3 %collective-permute-done.37 = bf16[384,768]{1,0:T(8,128)(2,1)S(1)} collective-permute-done((bf16[384,768]{1,0:T(8,128)(2,1)S(1)}, bf16[384,768]{1,0:T(8,128)(2,1)S(1)}, u32[]{:S(2)}, u32[]{:S(2)}) %collective-permute-start.37) | collective-permute-done | bytes 589856 | tf_op jit(solution)/shard_map/ppermute | solution.py:233
  632.6 6.1 collective-permute-start.39
  666.4 13.2 %all-gather.4 = bf16[256,96]{1,0:T(8,128)(2,1)S(1)} all-gather(bf16[64,96]{1,0:T(8,128)(2,1)S(1)} %fusion.79), channel_id=6, replica_groups=mesh['dp'=8,'tensor'=4] {'tensor'}, dimensions={0}, use_global_device_ids=true | all-gather | bytes 61440 | tf_op jit(solution)/shard_map/all_gather | solution.py:721
  681.0 8.9 %all-gather.7 = bf16[8,96,64]{1,2,0:T(8,128)(2,1)S(1)} all-gather(bf16[1,96,64]{1,2,0:T(8,128)(2,1)S(1)} %fusion.198), channel_id=1, replica_groups=mesh['dp'=8,'tensor'=4] {'dp'}, dimensions={0}, use_global_device_ids=true | all-gather | bytes 110592 | tf_op jit(solution)/shard_map/all_gather | solution.py:723
  708.0 3.5 pad_maximum_fusion
  712.2 3.8 collective-permute-start.42
  716.0 3.8 collective-permute-start.43
  719.8 13.2 %all_gather.62 = f32[32,128]{1,0:T(8,128)S(1)} all-gather(f32[8,128]{1,0:T(8,128)S(1)} %broadcast_in_dim.21), channel_id=1, replica_groups=mesh['dp'=8,'tensor'=4] {'tensor'}, dimensions={0}, use_global_device_ids=true | all-gather | bytes 20480 | tf_op jit(solution)/shard_map/all_gather | solution.py:798
  733.1 8.7 %all_gather.63 = f32[64,128]{1,0:T(8,128)S(1)} all-gather(f32[8,128]{1,0:T(8,128)S(1)} %broadcast_in_dim.23), channel_id=1, replica_groups=mesh['dp'=8,'tensor'=4] {'dp'}, dimensions={0}, use_global_device_ids=true | all-gather | bytes 36864 | tf_op jit(solution)/shard_map/all_gather | solution.py:798
  742.9 9.1 %add_divide_fusion.1 = (f32[2,2,384,768]{3,2,1,0:T(8,128)S(1)}, f32[2,2,384,768]{3,2,1,0:T(8,128)}, f32[2,2,384,768]{3,2,1,0:T(8,128)}) fusion(f32[]{:T(128)} %get-tuple-element.316, bf16[1,2,384,768]{3,2,1,0:T(8,128)(2,1)} %maximum_bitcast_fusion.1, bf16[1,2,384,768]{3,2,1,0:T(8,128)(2,1)} %maximum_bitcast_fusion, f32[2,2,384,768]{3,2,1,0:T(8,128)} %param.40, ...), kind=kLoop, calls=%fused_computation.19 | loop fusion | flops 16515072 | bytes 25952260 | tf_op jit(solution)/shard_map/div | solution.py:484
  758.3 4.5 add_divide_fusion.3
  764.9 3.5 fusion.148
  768.4 3.0 copy_add_fusion.2
  776.2 9.5 %add_divide_fusion.2 = (f32[2,384,1152]{2,1,0:T(8,128)S(1)}, f32[2,384,1152]{2,1,0:T(8,128)}, f32[2,384,1152]{2,1,0:T(8,128)}) fusion(f32[2,384,1152]{2,1,0:T(8,128)S(1)} %get-tuple-element.105, f32[]{:T(128)} %get-tuple-element.316, f32[2,384,1152]{2,1,0:T(8,128)} %param.42, f32[2,384,1152]{2,1,0:T(8,128)} %param.43), kind=kLoop, calls=%fused_computation.26 | loop fusion | flops 10616832 | bytes 21233668 | tf_op jit(solution)/shard_map/div | solution.py:484
  787.9 3.0 collective-permute-done.41
  792.0 10.9 %add_divide_fusion = (f32[3592,384]{1,0:T(8,128)}, f32[3592,384]{1,0:T(8,128)}, f32[3592,384]{1,0:T(8,128)}) fusion(f32[3592,384]{1,0:T(8,128)S(1)} %bitcast.646, f32[]{:T(128)} %get-tuple-element.316, f32[3592,384]{1,0:T(8,128)} %param.44, f32[3592,384]{1,0:T(8,128)} %param.45), kind=kLoop, calls=%fused_computation.13 | loop fusion | flops 16551936 | bytes 33103876 | tf_op jit(solution)/shard_map/div | solution.py:484
  803.0 6.4 copy.574
  809.4 3.1 dynamic-slice_convert_fusion
  814.5 3.5 copy.575
  822.8 3.8 multiply_subtract_fusion.1
  835.3 8.0 collective-permute-done.49
  844.9 13.2 %collective-permute-done.51 = bf16[3592,1,1,96]{0,3,2,1:T(8,128)(2,1)S(1)} collective-permute-done((bf16[3592,1,1,96]{0,3,2,1:T(8,128)(2,1)S(1)}, bf16[3592,1,1,96]{0,3,2,1:T(8,128)(2,1)S(1)}, u32[]{:S(2)}, u32[]{:S(2)}) %collective-permute-start.51) | collective-permute-done | bytes 689696 | tf_op jit(solution)/shard_map/ppermute | solution.py:40
  (1039 shorter events, 378.3 us)
Async XLA Ops:
  7.2 141.0 %all-gather.14.cloned.1.call-start = ((), (), s32[]{:S(2)}) async-start(), calls=%async_computation | async-start | bytes 19464192 | tf_op jit(solution)/shard_map/all_gather | solution.py:544
  11.1 220.5 %all-gather.18.cloned.1.call-start = ((), (), s32[]{:S(2)}) async-start(), calls=%async_computation.2 | async-start | bytes 9732096 | tf_op jit(solution)/shard_map/all_gather | solution.py:545
  12.1 93.0 %collective-permute-start = (f32[2,1]{0,1:T(1,128)S(1)}, f32[2,1]{0,1:T(1,128)S(1)}, u32[]{:S(2)}, u32[]{:S(2)}) collective-permute-start(f32[2,1]{0,1:T(1,128)S(1)} %dynamic-slice_bitcast_fusion.4), channel_id=1, source_target_pairs={{0,4},{1,5},{2,6},{3,7},{4,0},{5,1},{6,2},{7,3},{8,12},{9,13},{10,... | collective-permute-start | bytes 32 | tf_op jit(solution)/shard_map/ppermute | solution.py:178
  14.0 91.3 %collective-permute-start.2 = (f32[2,256,16]{1,2,0:T(8,128)}, f32[2,256,16]{1,2,0:T(8,128)}, u32[]{:S(2)}, u32[]{:S(2)}) collective-permute-start(f32[2,256,16]{1,2,0:T(8,128)} %constant_dynamic-slice_fusion.49), channel_id=1, source_target_pairs={{0,4},{1,5},{2,6},{3,7},{4,0},{5,1},{6,2},{7,3},{8,12},{9,13},{10,... | collective-permute-start | bytes 98312 | tf_op jit(solution)/shard_map/ppermute | solution.py:178
  15.4 89.8 %collective-permute-start.1 = (f32[2,256,16]{1,2,0:T(8,128)}, f32[2,256,16]{1,2,0:T(8,128)}, u32[]{:S(2)}, u32[]{:S(2)}) collective-permute-start(f32[2,256,16]{1,2,0:T(8,128)} %constant_dynamic-slice_fusion.50), channel_id=1, source_target_pairs={{0,4},{1,5},{2,6},{3,7},{4,0},{5,1},{6,2},{7,3},{8,12},{9,13},{10,... | collective-permute-start | bytes 98312 | tf_op jit(solution)/shard_map/ppermute | solution.py:178
  16.0 78.7 %copy-start.87 = (bf16[3592,96]{0,1:T(8,128)(2,1)}, bf16[3592,96]{0,1:T(8,128)(2,1)S(1)}, u32[]{:S(2)}) copy-start(bf16[3592,96]{0,1:T(8,128)(2,1)S(1)} %convert_element_type.864) | copy-start | bytes 2068996
  37.7 56.8 %copy-start.96 = (f32[96,768]{1,0:T(8,128)}, f32[96,768]{1,0:T(8,128)S(1)}, u32[]{:S(2)}) copy-start(f32[96,768]{1,0:T(8,128)S(1)} %copy.489) | copy-start | bytes 884740
  94.4 12.6 %collective-permute-start.3 = (bf16[2,4,2688]{2,0,1:T(2,128)(2,1)}, bf16[2,4,2688]{2,0,1:T(2,128)(2,1)}, u32[]{:S(2)}, u32[]{:S(2)}) collective-permute-start(bf16[2,4,2688]{2,0,1:T(2,128)(2,1)} %dynamic-slice_bitcast_fusion), channel_id=1, source_target_pairs={{0,4},{1,5},{2,6},{3,7},{4,0},{5,1},{6,2},{7,3},{8,12},{9,13},{10,... | collective-permute-start | bytes 129032 | tf_op jit(solution)/shard_map/ppermute | solution.py:178
  94.4 283.3 %all-gather.16.cloned.1.call-start = ((), (), s32[]{:S(2)}) async-start(), calls=%async_computation.1 | async-start | bytes 1548288 | tf_op jit(solution)/shard_map/all_gather | solution.py:647
  107.0 46.6 %copy-start.176 = (f32[2,256]{1,0:T(2,128)}, f32[2,256]{1,0:T(2,128)S(1)}, u32[]{:S(2)}) copy-start(f32[2,256]{1,0:T(2,128)S(1)} %add_rsqrt_fusion.4) | copy-start | bytes 6148
  107.2 70.0 %copy-start.156 = (f32[2,768]{1,0:T(2,128)}, f32[2,768]{1,0:T(2,128)S(1)}, u32[]{:S(2)}) copy-start(f32[2,768]{1,0:T(2,128)S(1)} %get-tuple-element.419) | copy-start | bytes 18436
  107.2 82.9 %copy-start.160 = (f32[2,768]{1,0:T(2,128)}, f32[2,768]{1,0:T(2,128)S(1)}, u32[]{:S(2)}) copy-start(f32[2,768]{1,0:T(2,128)S(1)} %get-tuple-element.416) | copy-start | bytes 18436
  108.1 56.9 %copy-start.29 = (bf16[2,256,768]{2,1,0:T(8,128)(2,1)}, bf16[2,256,768]{2,1,0:T(8,128)(2,1)S(1)}, u32[]{:S(2)}) copy-start(bf16[2,256,768]{2,1,0:T(8,128)(2,1)S(1)} %add_convert_fusion.20) | copy-start | bytes 2359300
  266.6 19.4 %collective-permute-start.7 = (bf16[768,768]{1,0:T(8,128)(2,1)}, bf16[768,768]{1,0:T(8,128)(2,1)}, u32[]{:S(2)}, u32[]{:S(2)}) collective-permute-start(bf16[768,768]{1,0:T(8,128)(2,1)} %bitcast_convert_fusion.12), channel_id=1, source_target_pairs={{0,4},{1,5},{2,6},{3,7},{4,0},{5,1},{6,2},{7,3},{8,12},{9,13},{10,... | collective-permute-start | bytes 3538952 | tf_op jit(solution)/shard_map/ppermute | solution.py:233
  266.9 23.1 %collective-permute-start.6 = (bf16[768,768]{1,0:T(8,128)(2,1)}, bf16[768,768]{1,0:T(8,128)(2,1)}, u32[]{:S(2)}, u32[]{:S(2)}) collective-permute-start(bf16[768,768]{1,0:T(8,128)(2,1)} %bitcast_convert_fusion.14), channel_id=1, source_target_pairs={{0,4},{1,5},{2,6},{3,7},{4,0},{5,1},{6,2},{7,3},{8,12},{9,13},{10,... | collective-permute-start | bytes 3538952 | tf_op jit(solution)/shard_map/ppermute | solution.py:233
  269.8 11.6 %collective-permute-start.5 = (bf16[768,768]{1,0:T(8,128)(2,1)}, bf16[768,768]{1,0:T(8,128)(2,1)}, u32[]{:S(2)}, u32[]{:S(2)}) collective-permute-start(bf16[768,768]{1,0:T(8,128)(2,1)} %bitcast_convert_fusion.16), channel_id=1, source_target_pairs={{0,4},{1,5},{2,6},{3,7},{4,0},{5,1},{6,2},{7,3},{8,12},{9,13},{10,... | collective-permute-start | bytes 3538952 | tf_op jit(solution)/shard_map/ppermute | solution.py:233
  270.1 23.8 %collective-permute-start.4 = (bf16[768,768]{1,0:T(8,128)(2,1)}, bf16[768,768]{1,0:T(8,128)(2,1)}, u32[]{:S(2)}, u32[]{:S(2)}) collective-permute-start(bf16[768,768]{1,0:T(8,128)(2,1)} %bitcast_convert_fusion.18), channel_id=1, source_target_pairs={{0,4},{1,5},{2,6},{3,7},{4,0},{5,1},{6,2},{7,3},{8,12},{9,13},{10,... | collective-permute-start | bytes 3538952 | tf_op jit(solution)/shard_map/ppermute | solution.py:233
  273.5 291.6 %all-gather.20.cloned.1.call-start = ((), (), s32[]{:S(2)}) async-start(), calls=%async_computation.3 | async-start | bytes 2027520 | tf_op jit(solution)/shard_map/all_gather | solution.py:685
  315.0 57.6 %collective-permute-start.13 = (bf16[768,384]{1,0:T(8,128)(2,1)}, bf16[768,384]{1,0:T(8,128)(2,1)}, u32[]{:S(2)}, u32[]{:S(2)}) collective-permute-start(bf16[768,384]{1,0:T(8,128)(2,1)} %fusion.68), channel_id=1, source_target_pairs={{0,4},{1,5},{2,6},{3,7},{4,0},{5,1},{6,2},{7,3},{8,12},{9,13},{10,... | collective-permute-start | bytes 1769480 | tf_op jit(solution)/shard_map/ppermute | solution.py:233
  316.8 58.3 %collective-permute-start.12 = (bf16[768,384]{1,0:T(8,128)(2,1)}, bf16[768,384]{1,0:T(8,128)(2,1)}, u32[]{:S(2)}, u32[]{:S(2)}) collective-permute-start(bf16[768,384]{1,0:T(8,128)(2,1)} %fusion.65), channel_id=1, source_target_pairs={{0,4},{1,5},{2,6},{3,7},{4,0},{5,1},{6,2},{7,3},{8,12},{9,13},{10,... | collective-permute-start | bytes 1769480 | tf_op jit(solution)/shard_map/ppermute | solution.py:233
  324.3 58.1 %collective-permute-start.10 = (bf16[768,768]{1,0:T(8,128)(2,1)}, bf16[768,768]{1,0:T(8,128)(2,1)}, u32[]{:S(2)}, u32[]{:S(2)}) collective-permute-start(bf16[768,768]{1,0:T(8,128)(2,1)} %broadcast_select_fusion.1), channel_id=1, source_target_pairs={{0,1},{1,0},{2,3},{3,2},{4,5},{5,4},{6,7},{7,6},{8,9},{9,8},{10,11... | collective-permute-start | bytes 3538952 | tf_op jit(solution)/shard_map/ppermute | solution.py:233
  326.5 42.3 %collective-permute-start.9 = (bf16[384,768]{1,0:T(8,128)(2,1)}, bf16[384,768]{1,0:T(8,128)(2,1)}, u32[]{:S(2)}, u32[]{:S(2)}) collective-permute-start(bf16[384,768]{1,0:T(8,128)(2,1)} %constant_dynamic-slice_fusion.45), channel_id=1, source_target_pairs={{0,16},{1,17},{2,18},{3,19},{4,20},{5,21},{6,22},{7,23},{8,24},{9,... | collective-permute-start | bytes 1769480 | tf_op jit(solution)/shard_map/ppermute | solution.py:233
  328.8 41.3 %collective-permute-start.8 = (bf16[384,768]{1,0:T(8,128)(2,1)}, bf16[384,768]{1,0:T(8,128)(2,1)}, u32[]{:S(2)}, u32[]{:S(2)}) collective-permute-start(bf16[384,768]{1,0:T(8,128)(2,1)} %constant_dynamic-slice_fusion.46), channel_id=1, source_target_pairs={{0,16},{1,17},{2,18},{3,19},{4,20},{5,21},{6,22},{7,23},{8,24},{9,... | collective-permute-start | bytes 1769480 | tf_op jit(solution)/shard_map/ppermute | solution.py:233
  361.4 296.6 %all-gather.22.cloned.1.call-start = ((), (), s32[]{:S(2)}) async-start(), calls=%async_computation.4 | async-start | bytes 3750912 | tf_op jit(solution)/shard_map/all_gather | solution.py:685
  368.7 15.9 %collective-permute-start.11 = (bf16[768,768]{1,0:T(8,128)(2,1)}, bf16[768,768]{1,0:T(8,128)(2,1)}, u32[]{:S(2)}, u32[]{:S(2)}) collective-permute-start(bf16[768,768]{1,0:T(8,128)(2,1)} %bitcast_convert_fusion.10), channel_id=1, source_target_pairs={{0,4},{1,5},{2,6},{3,7},{4,0},{5,1},{6,2},{7,3},{8,12},{9,13},{10,... | collective-permute-start | bytes 3538952 | tf_op jit(solution)/shard_map/ppermute | solution.py:233
  411.2 30.1 %collective-permute-start.17 = (bf16[768,384]{1,0:T(8,128)(2,1)S(1)}, bf16[768,384]{1,0:T(8,128)(2,1)S(1)}, u32[]{:S(2)}, u32[]{:S(2)}) collective-permute-start(bf16[768,384]{1,0:T(8,128)(2,1)S(1)} %pad_maximum_fusion.6), channel_id=1, source_target_pairs={{0,1},{1,0},{2,3},{3,2},{4,5},{5,4},{6,7},{7,6},{8,9},{9,8},{10,11... | collective-permute-start | bytes 1769480 | tf_op jit(solution)/shard_map/ppermute | solution.py:233
  412.1 16.3 %collective-permute-start.16 = (bf16[384,768]{1,0:T(8,128)(2,1)S(1)}, bf16[384,768]{1,0:T(8,128)(2,1)S(1)}, u32[]{:S(2)}, u32[]{:S(2)}) collective-permute-start(bf16[384,768]{1,0:T(8,128)(2,1)S(1)} %constant_dynamic-slice_fusion.39), channel_id=1, source_target_pairs={{0,16},{1,17},{2,18},{3,19},{4,20},{5,21},{6,22},{7,23},{8,24},{9,... | collective-permute-start | bytes 1769480 | tf_op jit(solution)/shard_map/ppermute | solution.py:233
  413.7 26.4 %collective-permute-start.15 = (bf16[384,768]{1,0:T(8,128)(2,1)S(1)}, bf16[384,768]{1,0:T(8,128)(2,1)S(1)}, u32[]{:S(2)}, u32[]{:S(2)}) collective-permute-start(bf16[384,768]{1,0:T(8,128)(2,1)S(1)} %constant_dynamic-slice_fusion.40), channel_id=1, source_target_pairs={{0,16},{1,17},{2,18},{3,19},{4,20},{5,21},{6,22},{7,23},{8,24},{9,... | collective-permute-start | bytes 1769480 | tf_op jit(solution)/shard_map/ppermute | solution.py:233
  414.4 25.9 %collective-permute-start.14 = (bf16[384,768]{1,0:T(8,128)(2,1)S(1)}, bf16[384,768]{1,0:T(8,128)(2,1)S(1)}, u32[]{:S(2)}, u32[]{:S(2)}) collective-permute-start(bf16[384,768]{1,0:T(8,128)(2,1)S(1)} %broadcast_select_fusion.3), channel_id=1, source_target_pairs={{0,1},{1,0},{2,3},{3,2},{4,5},{5,4},{6,7},{7,6},{8,9},{9,8},{10,11... | collective-permute-start | bytes 1769480 | tf_op jit(solution)/shard_map/ppermute | solution.py:233
  421.8 57.2 %copy-start.34 = (bf16[2,256,768]{2,1,0:T(8,128)(2,1)}, bf16[2,256,768]{2,1,0:T(8,128)(2,1)S(1)}, u32[]{:S(2)}) copy-start(bf16[2,256,768]{2,1,0:T(8,128)(2,1)S(1)} %multiply_convert_fusion.14) | copy-start | bytes 2359300
  441.6 29.1 %collective-permute-start.21 = (bf16[768,768]{1,0:T(8,128)(2,1)}, bf16[768,768]{1,0:T(8,128)(2,1)}, u32[]{:S(2)}, u32[]{:S(2)}) collective-permute-start(bf16[768,768]{1,0:T(8,128)(2,1)} %bitcast_convert_fusion.5), channel_id=1, source_target_pairs={{0,4},{1,5},{2,6},{3,7},{4,0},{5,1},{6,2},{7,3},{8,12},{9,13},{10,... | collective-permute-start | bytes 3538952 | tf_op jit(solution)/shard_map/ppermute | solution.py:233
  441.7 25.3 %collective-permute-start.19 = (bf16[768,768]{1,0:T(8,128)(2,1)}, bf16[768,768]{1,0:T(8,128)(2,1)}, u32[]{:S(2)}, u32[]{:S(2)}) collective-permute-start(bf16[768,768]{1,0:T(8,128)(2,1)} %bitcast_convert_fusion.7), channel_id=1, source_target_pairs={{0,4},{1,5},{2,6},{3,7},{4,0},{5,1},{6,2},{7,3},{8,12},{9,13},{10,... | collective-permute-start | bytes 3538952 | tf_op jit(solution)/shard_map/ppermute | solution.py:233
  442.9 14.2 %collective-permute-start.25 = (bf16[384,384]{1,0:T(8,128)(2,1)}, bf16[384,384]{1,0:T(8,128)(2,1)}, u32[]{:S(2)}, u32[]{:S(2)}) collective-permute-start(bf16[384,384]{1,0:T(8,128)(2,1)} %constant_dynamic-slice_fusion.30), channel_id=1, source_target_pairs={{0,16},{1,17},{2,18},{3,19},{4,20},{5,21},{6,22},{7,23},{8,24},{9,... | collective-permute-start | bytes 884744 | tf_op jit(solution)/shard_map/ppermute | solution.py:233
  445.7 13.4 %collective-permute-start.24 = (bf16[384,384]{1,0:T(8,128)(2,1)}, bf16[384,384]{1,0:T(8,128)(2,1)}, u32[]{:S(2)}, u32[]{:S(2)}) collective-permute-start(bf16[384,384]{1,0:T(8,128)(2,1)} %pad_maximum_fusion.8), channel_id=1, source_target_pairs={{0,1},{1,0},{2,3},{3,2},{4,5},{5,4},{6,7},{7,6},{8,9},{9,8},{10,11... | collective-permute-start | bytes 884744 | tf_op jit(solution)/shard_map/ppermute | solution.py:233
  447.0 56.1 %collective-permute-start.22 = (bf16[384,768]{1,0:T(8,128)(2,1)}, bf16[384,768]{1,0:T(8,128)(2,1)}, u32[]{:S(2)}, u32[]{:S(2)}) collective-permute-start(bf16[384,768]{1,0:T(8,128)(2,1)} %add_convert_fusion.32), channel_id=1, source_target_pairs={{0,0},{1,1},{2,4},{3,5},{4,2},{5,3},{6,6},{7,7},{8,8},{9,9},{10,12... | collective-permute-start | bytes 1769480 | tf_op jit(solution)/shard_map/ppermute | solution.py:287
  457.1 17.5 %collective-permute-start.20 = (bf16[768,768]{1,0:T(8,128)(2,1)}, bf16[768,768]{1,0:T(8,128)(2,1)S(1)}, u32[]{:S(2)}, u32[]{:S(2)}) collective-permute-start(bf16[768,768]{1,0:T(8,128)(2,1)} %bitcast_convert_fusion.6), channel_id=1, source_target_pairs={{0,4},{1,5},{2,6},{3,7},{4,0},{5,1},{6,2},{7,3},{8,12},{9,13},{10,... | collective-permute-start | bytes 3538952 | tf_op jit(solution)/shard_map/ppermute | solution.py:233
  459.1 44.0 %collective-permute-start.23 = (bf16[384,768]{1,0:T(8,128)(2,1)}, bf16[384,768]{1,0:T(8,128)(2,1)}, u32[]{:S(2)}, u32[]{:S(2)}) collective-permute-start(bf16[384,768]{1,0:T(8,128)(2,1)} %copy-done.88), channel_id=1, source_target_pairs={{0,0},{1,1},{2,4},{3,5},{4,2},{5,3},{6,6},{7,7},{8,8},{9,9},{10,12... | collective-permute-start | bytes 1769480 | tf_op jit(solution)/shard_map/ppermute | solution.py:287
  467.0 10.2 %collective-permute-start.18 = (bf16[768,768]{1,0:T(8,128)(2,1)}, bf16[768,768]{1,0:T(8,128)(2,1)S(1)}, u32[]{:S(2)}, u32[]{:S(2)}) collective-permute-start(bf16[768,768]{1,0:T(8,128)(2,1)} %bitcast_convert_fusion.8), channel_id=1, source_target_pairs={{0,4},{1,5},{2,6},{3,7},{4,0},{5,1},{6,2},{7,3},{8,12},{9,13},{10,... | collective-permute-start | bytes 3538952 | tf_op jit(solution)/shard_map/ppermute | solution.py:233
  514.5 21.2 %collective-permute-start.29 = (bf16[768,384]{1,0:T(8,128)(2,1)}, bf16[768,384]{1,0:T(8,128)(2,1)}, u32[]{:S(2)}, u32[]{:S(2)}) collective-permute-start(bf16[768,384]{1,0:T(8,128)(2,1)} %fusion.71), channel_id=1, source_target_pairs={{0,4},{1,5},{2,6},{3,7},{4,0},{5,1},{6,2},{7,3},{8,12},{9,13},{10,... | collective-permute-start | bytes 1769480 | tf_op jit(solution)/shard_map/ppermute | solution.py:233
  516.0 23.9 %collective-permute-start.30 = (bf16[768,384]{1,0:T(8,128)(2,1)}, bf16[768,384]{1,0:T(8,128)(2,1)}, u32[]{:S(2)}, u32[]{:S(2)}) collective-permute-start(bf16[768,384]{1,0:T(8,128)(2,1)} %fusion.74), channel_id=1, source_target_pairs={{0,4},{1,5},{2,6},{3,7},{4,0},{5,1},{6,2},{7,3},{8,12},{9,13},{10,... | collective-permute-start | bytes 1769480 | tf_op jit(solution)/shard_map/ppermute | solution.py:233
  519.9 76.6 %collective-permute-start.26 = (bf16[768,768]{1,0:T(8,128)(2,1)}, bf16[768,768]{1,0:T(8,128)(2,1)}, u32[]{:S(2)}, u32[]{:S(2)}) collective-permute-start(bf16[768,768]{1,0:T(8,128)(2,1)} %bitcast_convert_fusion), channel_id=1, source_target_pairs={{0,4},{1,5},{2,6},{3,7},{4,0},{5,1},{6,2},{7,3},{8,12},{9,13},{10,... | collective-permute-start | bytes 3538952 | tf_op jit(solution)/shard_map/ppermute | solution.py:233
  520.0 11.9 %collective-permute-start.44 = (bf16[384,384]{1,0:T(8,128)(2,1)S(1)}, bf16[384,384]{1,0:T(8,128)(2,1)}, u32[]{:S(2)}, u32[]{:S(2)}) collective-permute-start(bf16[384,384]{1,0:T(8,128)(2,1)S(1)} %copy-done.112), channel_id=1, source_target_pairs={{0,0},{1,1},{2,4},{3,5},{4,2},{5,3},{6,6},{7,7},{8,8},{9,9},{10,12... | collective-permute-start | bytes 884744 | tf_op jit(solution)/shard_map/ppermute | solution.py:287
  521.3 12.5 %collective-permute-start.45 = (bf16[384,384]{1,0:T(8,128)(2,1)S(1)}, bf16[384,384]{1,0:T(8,128)(2,1)S(1)}, u32[]{:S(2)}, u32[]{:S(2)}) collective-permute-start(bf16[384,384]{1,0:T(8,128)(2,1)S(1)} %copy-done.108), channel_id=1, source_target_pairs={{0,0},{1,1},{2,4},{3,5},{4,2},{5,3},{6,6},{7,7},{8,8},{9,9},{10,12... | collective-permute-start | bytes 884744 | tf_op jit(solution)/shard_map/ppermute | solution.py:287
  531.9 68.6 %collective-permute-start.36 = (bf16[768,768]{1,0:T(8,128)(2,1)}, bf16[768,768]{1,0:T(8,128)(2,1)}, u32[]{:S(2)}, u32[]{:S(2)}) collective-permute-start(bf16[768,768]{1,0:T(8,128)(2,1)} %broadcast_select_fusion), channel_id=1, source_target_pairs={{0,1},{1,0},{2,3},{3,2},{4,5},{5,4},{6,7},{7,6},{8,9},{9,8},{10,11... | collective-permute-start | bytes 3538952 | tf_op jit(solution)/shard_map/ppermute | solution.py:233
  533.8 13.3 %collective-permute-start.33 = (bf16[384,768]{1,0:T(8,128)(2,1)}, bf16[384,768]{1,0:T(8,128)(2,1)S(1)}, u32[]{:S(2)}, u32[]{:S(2)}) collective-permute-start(bf16[384,768]{1,0:T(8,128)(2,1)} %constant_dynamic-slice_fusion.8), channel_id=1, source_target_pairs={{0,16},{1,17},{2,18},{3,19},{4,20},{5,21},{6,22},{7,23},{8,24},{9,... | collective-permute-start | bytes 1769480 | tf_op jit(solution)/shard_map/ppermute | solution.py:233
  535.7 25.7 %collective-permute-start.34 = (bf16[384,768]{1,0:T(8,128)(2,1)S(1)}, bf16[384,768]{1,0:T(8,128)(2,1)S(1)}, u32[]{:S(2)}, u32[]{:S(2)}) collective-permute-start(bf16[384,768]{1,0:T(8,128)(2,1)S(1)} %copy-done.135), channel_id=1, source_target_pairs={{0,16},{1,17},{2,18},{3,19},{4,20},{5,21},{6,22},{7,23},{8,24},{9,... | collective-permute-start | bytes 1769480 | tf_op jit(solution)/shard_map/ppermute | solution.py:233
  543.7 50.2 %collective-permute-start.31 = (bf16[768,384]{1,0:T(8,128)(2,1)}, bf16[768,384]{1,0:T(8,128)(2,1)}, u32[]{:S(2)}, u32[]{:S(2)}) collective-permute-start(bf16[768,384]{1,0:T(8,128)(2,1)} %pad_maximum_fusion.7), channel_id=1, source_target_pairs={{0,1},{1,0},{2,3},{3,2},{4,5},{5,4},{6,7},{7,6},{8,9},{9,8},{10,11... | collective-permute-start | bytes 1769480 | tf_op jit(solution)/shard_map/ppermute | solution.py:233
  562.6 44.0 %collective-permute-start.35 = (bf16[384,768]{1,0:T(8,128)(2,1)}, bf16[384,768]{1,0:T(8,128)(2,1)}, u32[]{:S(2)}, u32[]{:S(2)}) collective-permute-start(bf16[384,768]{1,0:T(8,128)(2,1)} %broadcast_select_fusion.2), channel_id=1, source_target_pairs={{0,1},{1,0},{2,3},{3,2},{4,5},{5,4},{6,7},{7,6},{8,9},{9,8},{10,11... | collective-permute-start | bytes 1769480 | tf_op jit(solution)/shard_map/ppermute | solution.py:233
  596.1 52.1 %collective-permute-start.32 = (bf16[384,384]{1,0:T(8,128)(2,1)}, bf16[384,384]{1,0:T(8,128)(2,1)}, u32[]{:S(2)}, u32[]{:S(2)}) collective-permute-start(bf16[384,384]{1,0:T(8,128)(2,1)} %constant_dynamic-slice_fusion.16), channel_id=1, source_target_pairs={{0,16},{1,17},{2,18},{3,19},{4,20},{5,21},{6,22},{7,23},{8,24},{9,... | collective-permute-start | bytes 884744 | tf_op jit(solution)/shard_map/ppermute | solution.py:233
  598.8 20.0 %collective-permute-start.27 = (bf16[384,768]{1,0:T(8,128)(2,1)S(1)}, bf16[384,768]{1,0:T(8,128)(2,1)S(1)}, u32[]{:S(2)}, u32[]{:S(2)}) collective-permute-start(bf16[384,768]{1,0:T(8,128)(2,1)S(1)} %constant_dynamic-slice_fusion.25), channel_id=1, source_target_pairs={{0,16},{1,17},{2,18},{3,19},{4,20},{5,21},{6,22},{7,23},{8,24},{9,... | collective-permute-start | bytes 1769480 | tf_op jit(solution)/shard_map/ppermute | solution.py:233
  602.5 28.4 %collective-permute-start.37 = (bf16[384,768]{1,0:T(8,128)(2,1)S(1)}, bf16[384,768]{1,0:T(8,128)(2,1)S(1)}, u32[]{:S(2)}, u32[]{:S(2)}) collective-permute-start(bf16[384,768]{1,0:T(8,128)(2,1)S(1)} %constant_dynamic-slice_fusion.6), channel_id=1, source_target_pairs={{0,16},{1,17},{2,18},{3,19},{4,20},{5,21},{6,22},{7,23},{8,24},{9,... | collective-permute-start | bytes 1769480 | tf_op jit(solution)/shard_map/ppermute | solution.py:233
  609.5 46.1 %collective-permute-start.38 = (bf16[384,768]{1,0:T(8,128)(2,1)}, bf16[384,768]{1,0:T(8,128)(2,1)}, u32[]{:S(2)}, u32[]{:S(2)}) collective-permute-start(bf16[384,768]{1,0:T(8,128)(2,1)} %get-tuple-element.330), channel_id=1, source_target_pairs={{0,0},{1,1},{2,4},{3,5},{4,2},{5,3},{6,6},{7,7},{8,8},{9,9},{10,12... | collective-permute-start | bytes 1769480 | tf_op jit(solution)/shard_map/ppermute | solution.py:287
  621.6 30.3 %collective-permute-start.28 = (bf16[384,384]{1,0:T(8,128)(2,1)}, bf16[384,384]{1,0:T(8,128)(2,1)}, u32[]{:S(2)}, u32[]{:S(2)}) collective-permute-start(bf16[384,384]{1,0:T(8,128)(2,1)} %pad_maximum_fusion.9), channel_id=1, source_target_pairs={{0,1},{1,0},{2,3},{3,2},{4,5},{5,4},{6,7},{7,6},{8,9},{9,8},{10,11... | collective-permute-start | bytes 884744 | tf_op jit(solution)/shard_map/ppermute | solution.py:233
  632.6 23.1 %collective-permute-start.39 = (bf16[384,768]{1,0:T(8,128)(2,1)}, bf16[384,768]{1,0:T(8,128)(2,1)}, u32[]{:S(2)}, u32[]{:S(2)}) collective-permute-start(bf16[384,768]{1,0:T(8,128)(2,1)} %get-tuple-element.328), channel_id=1, source_target_pairs={{0,0},{1,1},{2,4},{3,5},{4,2},{5,3},{6,6},{7,7},{8,8},{9,9},{10,12... | collective-permute-start | bytes 1769480 | tf_op jit(solution)/shard_map/ppermute | solution.py:287
  712.2 43.1 %collective-permute-start.42 = (bf16[384,384]{1,0:T(8,128)(2,1)}, bf16[384,384]{1,0:T(8,128)(2,1)}, u32[]{:S(2)}, u32[]{:S(2)}) collective-permute-start(bf16[384,384]{1,0:T(8,128)(2,1)} %get-tuple-element.101), channel_id=1, source_target_pairs={{0,0},{1,1},{2,4},{3,5},{4,2},{5,3},{6,6},{7,7},{8,8},{9,9},{10,12... | collective-permute-start | bytes 884744 | tf_op jit(solution)/shard_map/ppermute | solution.py:287
  716.0 41.0 %collective-permute-start.43 = (bf16[384,384]{1,0:T(8,128)(2,1)}, bf16[384,384]{1,0:T(8,128)(2,1)}, u32[]{:S(2)}, u32[]{:S(2)}) collective-permute-start(bf16[384,384]{1,0:T(8,128)(2,1)} %get-tuple-element.102), channel_id=1, source_target_pairs={{0,0},{1,1},{2,4},{3,5},{4,2},{5,3},{6,6},{7,7},{8,8},{9,9},{10,12... | collective-permute-start | bytes 884744 | tf_op jit(solution)/shard_map/ppermute | solution.py:287
  755.0 16.4 %collective-permute-start.40 = (bf16[2,2,2,1,96,768]{5,4,1,0,3,2:T(8,128)(2,1)}, bf16[2,2,2,1,96,768]{5,4,1,0,3,2:T(8,128)(2,1)}, u32[]{:S(2)}, u32[]{:S(2)}) collective-permute-start(bf16[2,2,2,1,96,768]{5,4,1,0,3,2:T(8,128)(2,1)} %copy.659), channel_id=1, source_target_pairs={{0,4},{4,0},{8,12},{12,8},{16,20},{20,16},{24,28},{28,24},{1,5},{5... | collective-permute-start | bytes 3538952 | tf_op jit(solution)/shard_map/ppermute | solution.py:40
  764.8 3.6 collective-permute-start.46
  775.2 15.7 %collective-permute-start.41 = (bf16[2,2,1,1,96,768]{5,4,1,0,3,2:T(8,128)(2,1)S(1)}, bf16[2,2,1,1,96,768]{5,4,1,0,3,2:T(8,128)(2,1)S(1)}, u32[]{:S(2)}, u32[]{:S(2)}) collective-permute-start(bf16[2,2,1,1,96,768]{5,4,1,0,3,2:T(8,128)(2,1)S(1)} %dynamic-slice_convert_fusion.2), channel_id=1, source_target_pairs={{0,8},{4,12},{8,0},{12,4},{16,24},{20,28},{24,16},{28,20},{1,9},{5... | collective-permute-start | bytes 1769480 | tf_op jit(solution)/shard_map/ppermute | solution.py:40
  787.9 38.7 %collective-permute-start.48 = (bf16[2,2,1,96,1152]{4,3,0,2,1:T(8,128)(2,1)}, bf16[2,2,1,96,1152]{4,3,0,2,1:T(8,128)(2,1)}, u32[]{:S(2)}, u32[]{:S(2)}) collective-permute-start(bf16[2,2,1,96,1152]{4,3,0,2,1:T(8,128)(2,1)} %copy.660), channel_id=1, source_target_pairs={{0,4},{4,0},{8,12},{12,8},{16,20},{20,16},{24,28},{28,24},{1,5},{5... | collective-permute-start | bytes 2654216 | tf_op jit(solution)/shard_map/ppermute | solution.py:40
  812.5 17.2 %collective-permute-start.50 = (bf16[3592,2,1,96]{0,3,2,1:T(8,128)(2,1)}, bf16[3592,2,1,96]{0,3,2,1:T(8,128)(2,1)}, u32[]{:S(2)}, u32[]{:S(2)}) collective-permute-start(bf16[3592,2,1,96]{0,3,2,1:T(8,128)(2,1)} %dynamic-slice_convert_fusion), channel_id=1, source_target_pairs={{0,4},{4,0},{8,12},{12,8},{16,20},{20,16},{24,28},{28,24},{1,5},{5... | collective-permute-start | bytes 4137992 | tf_op jit(solution)/shard_map/ppermute | solution.py:40
  821.8 12.1 %collective-permute-start.47 = (bf16[2,4,1,1,96,192]{5,4,1,0,3,2:T(8,128)(2,1)S(1)}, bf16[2,4,1,1,96,192]{5,4,1,0,3,2:T(8,128)(2,1)S(1)}, u32[]{:S(2)}, u32[]{:S(2)}) collective-permute-start(bf16[2,4,1,1,96,192]{5,4,1,0,3,2:T(8,128)(2,1)S(1)} %dynamic-slice_convert_fusion.4), channel_id=1, source_target_pairs={{0,8},{4,12},{8,0},{12,4},{16,24},{20,28},{24,16},{28,20},{1,9},{5... | collective-permute-start | bytes 884744 | tf_op jit(solution)/shard_map/ppermute | solution.py:40
  828.6 14.8 %collective-permute-start.49 = (bf16[2,1,1,96,1152]{4,3,0,2,1:T(8,128)(2,1)S(1)}, bf16[2,1,1,96,1152]{4,3,0,2,1:T(8,128)(2,1)S(1)}, u32[]{:S(2)}, u32[]{:S(2)}) collective-permute-start(bf16[2,1,1,96,1152]{4,3,0,2,1:T(8,128)(2,1)S(1)} %dynamic-slice_convert_fusion.3), channel_id=1, source_target_pairs={{0,8},{4,12},{8,0},{12,4},{16,24},{20,28},{24,16},{28,20},{1,9},{5... | collective-permute-start | bytes 1327112 | tf_op jit(solution)/shard_map/ppermute | solution.py:40
  831.7 26.4 %collective-permute-start.51 = (bf16[3592,1,1,96]{0,3,2,1:T(8,128)(2,1)S(1)}, bf16[3592,1,1,96]{0,3,2,1:T(8,128)(2,1)S(1)}, u32[]{:S(2)}, u32[]{:S(2)}) collective-permute-start(bf16[3592,1,1,96]{0,3,2,1:T(8,128)(2,1)S(1)} %dynamic-slice_convert_fusion.1), channel_id=1, source_target_pairs={{0,8},{4,12},{8,0},{12,4},{16,24},{20,28},{24,16},{28,20},{1,9},{5... | collective-permute-start | bytes 2069000 | tf_op jit(solution)/shard_map/ppermute | solution.py:40
  (250 other events, 1503.0 us)
Sparse Core Ops, SparseCore 0:
  11.5 136.6 all-gather.13
  151.7 79.8 all-gather.17
  273.6 23.2 all-gather.15
  361.5 54.8 all-gather.19
  524.1 68.1 all-gather.21

commit v5 on v4

--- a/solution.py
+++ b/solution.py
@@ -382,9 +382,6 @@
         ]
 
     sent = unit_grads(0)
-    if flows:
-        flows = [mlp_third(flows[0]), attn_second(flows[1])]
-        sent, flows = tied(sent, flows)
     mlp_sums = core_summed(sent, unit_grads(1))
     grad_hidden_two = sum(
         product_t(part, mlp_now[0][unit_at]) for unit_at, part in enumerate(grad_pre)
@@ -394,7 +391,9 @@
     )
     grad_gate_one = jnp.sum(grad_middle * branch_one, 1)
     upward = grad_middle * mod_parts[2]
-    up_low, mlp_sums = tied(upward.astype(LOW_TYPE), mlp_sums)
+    if flows:
+        flows = [mlp_third(flows[0]), attn_second(flows[1])]
+    up_low, (mlp_sums, flows) = tied(upward.astype(LOW_TYPE), (mlp_sums, flows))
     grad_attended = product(up_low, attn_now[3]).astype(LOW_TYPE)
     grad_queries, grad_keys, grad_values = attend_back(
         queries, key_rows, values, log_total, grad_attended
@@ -660,9 +659,8 @@
             moved_squares = moved_squares + flows[2] + squared(flows[1])
         flows = fresh
     last_mlp = mlp_third(mlp_second(flows[0]))
-    last_attn = attn_third(attn_second(flows[1]))
-    moved_squares = moved_squares + squared(last_mlp) + squared(last_attn)
-    last_mlp = homeward(last_mlp)
+    last_attn = attn_second(flows[1])
+    moved_squares = moved_squares + squared(last_mlp)
     grad_patch = weight_grad(noised, grad_stream.astype(LOW_TYPE))
     mine = patches_own.shape[0]
     early = jnp.concatenate(
@@ -726,8 +724,13 @@
         axis=1,
         tiled=True,
     )
+    grad_condition, (last_attn, last_mlp) = tied(grad_condition, (last_attn, last_mlp))
+    last_attn = attn_third(last_attn)
+    last_mlp = homeward(last_mlp)
     grad_smooth = product_t(grad_condition, second_time)
     grad_hidden_time = jax.vjp(jax.nn.silu, hidden_time)[1](grad_smooth)[0].astype(LOW_TYPE)
+    grad_hidden_time, last_attn = tied(grad_hidden_time, last_attn)
+    moved_squares = moved_squares + squared(last_attn)
 
     def of_group(value):
         shaped = value.reshape((stretches, GROUPS, latents // dp_count) + value.shape[1:])
@@ -814,13 +817,13 @@
             block = group_step(block, axes_at[index_at], shift_group, bit_at)
         return block.reshape(weights_in[index_at].shape)
 
-    for index_at in (1, 0, 2, 3):
+    for index_at in (3, 1, 0, 2):
         grad_now = reduced[index_at]
+        if index_at == 0:
+            grad_now, steps[3] = tied(grad_now, steps[3])
         if index_at == 2:
-            grad_now, steps[1] = tied(grad_now, steps[1])
-        if index_at == 3:
-            summed[1] = crossed(1)
-            grad_now, (summed[1], steps[0]) = tied(grad_now, (summed[1], steps[0]))
+            summed[3] = crossed(3)
+            grad_now, (summed[3], steps[1]) = tied(grad_now, (summed[3], steps[1]))
         update, new_firsts[index_at], new_seconds[index_at] = adam_update(
             grad_now * own_scale, firsts_in[index_at], seconds_in[index_at]
         )
@@ -828,7 +831,7 @@
         steps[index_at] = group_step(
             split_bits(update, axis_at, shift_group), axis_at, shift_group, 0
         )
-    for index_at in (0, 2, 3):
+    for index_at in (1, 0, 2):
         summed[index_at] = crossed(index_at)
     new_weights, new_momenta = ([], [])
     for index_at in range(4):

time: 881 us -> 889 us (level)
  waiting for transfers between devices: 154 us -> 112 us
  local copies, waits for them, and re-layouts: 140 us -> 181 us
    ppermute x32, waiting for transfers between devices: 67.8 us -> 30.7 us  [exchanged(): lax.ppermute(value, ('dp', 'tensor'), [(source, source ^ mask) for source...]
    unnamed x569 -> x595, local copies, waits for them, and re-layouts: 63.3 us -> 89.1 us
    convert_element_type x12 -> x14, other arithmetic: 14.7 us -> 22.1 us  [summed_low(): (left.astype(jnp.float32) + right.astype(jnp.float32)).astype(LOW_TYPE)]
  transfers between devices with their start and end apart: 57 -> 57, of which waited for: 14 -> 9; matrix products, arithmetic and copies ran while one was open for 47% -> 54% of each run, Pallas kernels for 1% -> 1%
where the time goes in v5:
time: 889 us; the launch traced here: 875 us
  matrix products  208 us (23%)
  local copies, waits for them, and re-layouts  181 us (20%)
  other arithmetic  156 us (18%)
  blocking collectives  119 us (13%)
  waiting for transfers between devices  112 us (13%)
  starting transfers between devices  60.6 us (7%)
  between operations  27.3 us (3%)
  Pallas kernels  10.9 us (1%)
    unnamed x595, local copies, waits for them, and re-layouts  89.1 us
    dot_general x36, matrix products, weight_grad(): lax.dot_general(inputs, grads_out, ((leading, leading), ((), ())), prefer...  76.6 us
    dot_general x29, matrix products, product_t(): lax.dot_general(left, right, (((left.ndim - 1,), (1,)), ((), ())), prefer...  57 us
    dot_general x32, matrix products, product(): return jnp.dot(left, right, preferred_element_type=jnp.float32)  49.9 us
    unnamed x1, blocking collectives  39 us
    all_gather x1, waiting for transfers between devices, per_device(): first_whole = lax.all_gather(first_local, everyone, axis=1, tiled=True)  38.4 us
    div x4, other arithmetic, adam_update(): first_new / (1.0 - BETA_FIRST ** STEP_COUNT)  34.6 us
    ppermute x8, starting transfers between devices, homeward(): return [lax.ppermute(value, ('dp', 'tensor'), pairs) for value in values]  31 us
  transfers between devices with their start and end apart: 57, of which 9 were waited for; matrix products, arithmetic and copies ran while one was open for 54% of the time, Pallas kernels for 1%

profile of v5, /device:TPU:0, one launch (start us, length us, event | category | flops | bytes accessed | tf_op | source)
XLA Modules:
  0.0 875.1 jit_solution(8145181404588080571)
XLA Ops:
  15.9 10.1 %all-gather.5 = s32[8,8,2]{1,2,0:T(2,128)S(1)} all-gather(s32[1,8,2]{1,2,0:T(2,128)S(1)} %add_bitcast_fusion.1), channel_id=1, replica_groups=mesh['dp'=8,'tensor'=4] {'dp'}, dimensions={0}, use_global_device_ids=true | all-gather | bytes 576 | tf_op jit(solution)/shard_map/all_gather | solution.py:530
  28.4 9.6 %all_gather.49 = f32[96,768]{0,1:T(8,128)S(1)} all-gather(f32[96,96]{0,1:T(8,128)S(1)} %copy.503), channel_id=1, replica_groups=mesh['dp'=8,'tensor'=4] {'dp'}, dimensions={1}, use_global_device_ids=true | all-gather | bytes 331776 | tf_op jit(solution)/shard_map/all_gather | solution.py:562
  41.3 39.0 %all-reduce.3 = bf16[64,2688]{1,0:T(8,128)(2,1)S(1)} all-reduce(f32[64,2688]{1,0:T(8,128)S(1)} %pad_maximum_fusion.3), channel_id=7, replica_groups=mesh['dp'=8,'tensor'=4] {'dp'}, use_global_device_ids=true, to_apply=%region_5.6.clone | all-reduce | flops 172032 | bytes 1032192
  80.4 14.2 %all-gather = bf16[32,2688]{1,0:T(8,128)(2,1)S(1)} all-gather(bf16[8,2688]{1,0:T(8,128)(2,1)S(1)} %dynamic-slice_convert_fusion.5), channel_id=2, replica_groups=mesh['dp'=8,'tensor'=4] {'tensor'}, dimensions={0}, use_global_device_ids=true | all-gather | bytes 215040 | tf_op jit(solution)/shard_map/all_gather | solution.py:599
  97.1 3.6 copy.584
  109.6 38.4 %all-gather.14.cloned.1.call-done = bf16[4,3072,768]{2,1,0:T(8,128)(2,1)} async-done(((bf16[4,96,768]{2,1,0:T(8,128)(2,1)}), bf16[4,3072,768]{2,1,0:T(8,128)(2,1)}) %all-gather.14.cloned.1.call-update) | async-done | bytes 18874384 | tf_op jit(solution)/shard_map/all_gather | solution.py:543
  148.0 5.4 attn_maps.2
  153.4 5.6 attn_maps.3
  164.8 2.9 add_convert_fusion.18
  177.9 3.8 fusion.250
  206.9 3.4 fusion.248
  211.0 20.4 %all-gather.18.cloned.1.call-done = bf16[1,2,3072,768]{3,2,1,0:T(8,128)(2,1)} async-done(((bf16[1,2,96,768]{3,2,1,0:T(8,128)(2,1)}), bf16[1,2,3072,768]{3,2,1,0:T(8,128)(2,1)}) %all-gather.18.cloned.1.call-update) | async-done | bytes 9437200 | tf_op jit(solution)/shard_map/all_gather | solution.py:544
  233.6 3.7 fusion.91
  270.2 3.1 multiply_reduce_fusion.8
  273.8 4.9 multiply_reduce_fusion.27
  282.4 3.5 add_convert_fusion.10
  285.9 3.9 add_convert_fusion.8
  289.9 3.9 add_convert_fusion.9
  293.8 3.1 add_convert_fusion.11
  296.9 3.1 convolution_convert_fusion.3
  301.4 5.6 bitcast_reduce_fusion.1
  316.9 3.3 fusion.89
  331.6 4.5 multiply_reduce_fusion.10
  361.8 3.2 multiply_add_fusion.6
  384.6 3.0 add_convert_fusion.6
  389.1 4.0 bitcast_convert_fusion.2
  421.6 6.5 collective-permute-done.20
  429.0 10.8 %collective-permute-done.19 = bf16[384,768]{1,0:T(8,128)(2,1)S(1)} collective-permute-done((bf16[384,768]{1,0:T(8,128)(2,1)S(1)}, bf16[384,768]{1,0:T(8,128)(2,1)S(1)}, u32[]{:S(2)}, u32[]{:S(2)}) %collective-permute-start.19) | collective-permute-done | bytes 589856 | tf_op jit(solution)/shard_map/ppermute | solution.py:233
  443.6 3.2 add_convert_fusion.4
  449.4 2.7 add_convert_fusion.3
  453.9 3.1 convolution_convert_fusion.1
  459.9 5.1 bitcast_reduce_fusion
  472.6 6.0 collective-permute-start.23
  479.4 3.4 fusion.80
  484.2 3.3 fusion.81
  493.7 6.1 collective-permute-start.22
  523.4 5.2 multiply_reduce_fusion.11
  533.5 3.9 collective-permute-start.41
  539.4 2.7 fusion.246
  578.6 11.3 %collective-permute-done.33 = bf16[384,768]{1,0:T(8,128)(2,1)S(1)} collective-permute-done((bf16[384,768]{1,0:T(8,128)(2,1)}, bf16[384,768]{1,0:T(8,128)(2,1)S(1)}, u32[]{:S(2)}, u32[]{:S(2)}) %collective-permute-start.33) | collective-permute-done | bytes 589856 | tf_op jit(solution)/shard_map/ppermute | solution.py:233
  590.0 3.1 multiply_reduce_fusion.35
  610.9 2.6 reshape.749
  630.8 2.7 multiply_reduce_fusion.34
  645.7 13.1 %all-gather.4 = bf16[256,96]{1,0:T(8,128)(2,1)S(1)} all-gather(bf16[64,96]{1,0:T(8,128)(2,1)S(1)} %fusion.79), channel_id=6, replica_groups=mesh['dp'=8,'tensor'=4] {'tensor'}, dimensions={0}, use_global_device_ids=true | all-gather | bytes 61440 | tf_op jit(solution)/shard_map/all_gather | solution.py:719
  660.2 9.9 %all-gather.7 = bf16[8,96,64]{1,2,0:T(8,128)(2,1)S(1)} all-gather(bf16[1,96,64]{1,2,0:T(8,128)(2,1)S(1)} %fusion.198), channel_id=1, replica_groups=mesh['dp'=8,'tensor'=4] {'dp'}, dimensions={0}, use_global_device_ids=true | all-gather | bytes 110592 | tf_op jit(solution)/shard_map/all_gather | solution.py:721
  672.9 6.1 collective-permute-start.46
  679.0 5.9 collective-permute-start.47
  698.2 3.1 reshape.743
  701.3 3.0 reduce_sum.822
  720.4 4.6 multiply_reduce_fusion.4
  729.3 13.2 %all_gather.62 = f32[32,128]{1,0:T(8,128)S(1)} all-gather(f32[8,128]{1,0:T(8,128)S(1)} %broadcast_in_dim.21), channel_id=1, replica_groups=mesh['dp'=8,'tensor'=4] {'tensor'}, dimensions={0}, use_global_device_ids=true | all-gather | bytes 20480 | tf_op jit(solution)/shard_map/all_gather | solution.py:801
  742.5 9.7 %all_gather.63 = f32[64,128]{1,0:T(8,128)S(1)} all-gather(f32[8,128]{1,0:T(8,128)S(1)} %broadcast_in_dim.23), channel_id=1, replica_groups=mesh['dp'=8,'tensor'=4] {'dp'}, dimensions={0}, use_global_device_ids=true | all-gather | bytes 36864 | tf_op jit(solution)/shard_map/all_gather | solution.py:801
  753.3 11.7 %add_divide_fusion = (f32[3592,384]{1,0:T(8,128)}, f32[3592,384]{1,0:T(8,128)}, f32[3592,384]{1,0:T(8,128)}) fusion(f32[3592,384]{1,0:T(8,128)} %constant_dynamic-update-slice_fusion.14, f32[]{:T(128)} %get-tuple-element.324, f32[3592,384]{1,0:T(8,128)} %param.44, f32[3592,384]{1,0:T(8,128)} %param.45), kind=kLoop, calls=%fused_computation.13 | loop fusion | flops 16551936 | bytes 33103876 | tf_op jit(solution)/shard_map/div | solution.py:483
  765.1 6.4 copy.585
  776.6 2.6 fusion.148
  781.5 8.6 add_divide_fusion.1
  792.6 5.3 collective-permute-start.48
  801.6 5.4 add_divide_fusion.3
  810.6 3.3 copy.593
  814.0 3.6 copy.594
  824.1 5.5 collective-permute-done.45
  830.9 9.0 %add_divide_fusion.2 = (f32[2,384,1152]{2,1,0:T(8,128)S(1)}, f32[2,384,1152]{2,1,0:T(8,128)}, f32[2,384,1152]{2,1,0:T(8,128)}) fusion(f32[2,384,1152]{2,1,0:T(8,128)S(1)} %get-tuple-element.113, f32[]{:T(128)} %get-tuple-element.324, f32[2,384,1152]{2,1,0:T(8,128)} %param.42, f32[2,384,1152]{2,1,0:T(8,128)} %param.43), kind=kLoop, calls=%fused_computation.26 | loop fusion | flops 10616832 | bytes 21233668 | tf_op jit(solution)/shard_map/div | solution.py:483
  846.8 9.7 %collective-permute-done.49 = bf16[2,2,1,1,96,768]{5,4,1,0,3,2:T(8,128)(2,1)S(1)} collective-permute-done((bf16[2,2,1,1,96,768]{5,4,1,0,3,2:T(8,128)(2,1)S(1)}, bf16[2,2,1,1,96,768]{5,4,1,0,3,2:T(8,128)(2,1)S(1)}, u32[]{:S(2)}, u32[]{:S(2)}) %collective-permute-start.49) | collective-permute-done | bytes 589856 | tf_op jit(solution)/shard_map/ppermute | solution.py:40
  858.4 7.1 collective-permute-done.51
  (1067 shorter events, 410.1 us)
Async XLA Ops:
  7.2 140.8 %all-gather.14.cloned.1.call-start = ((), (), s32[]{:S(2)}) async-start(), calls=%async_computation | async-start | bytes 19464192 | tf_op jit(solution)/shard_map/all_gather | solution.py:543
  11.1 220.2 %all-gather.18.cloned.1.call-start = ((), (), s32[]{:S(2)}) async-start(), calls=%async_computation.2 | async-start | bytes 9732096 | tf_op jit(solution)/shard_map/all_gather | solution.py:544
  12.6 94.0 %collective-permute-start = (f32[2,1]{0,1:T(1,128)}, f32[2,1]{0,1:T(1,128)}, u32[]{:S(2)}, u32[]{:S(2)}) collective-permute-start(f32[2,1]{0,1:T(1,128)} %dynamic-slice_bitcast_fusion.4), channel_id=1, source_target_pairs={{0,4},{1,5},{2,6},{3,7},{4,0},{5,1},{6,2},{7,3},{8,12},{9,13},{10,... | collective-permute-start | bytes 32 | tf_op jit(solution)/shard_map/ppermute | solution.py:178
  13.9 92.8 %collective-permute-start.2 = (f32[2,256,16]{1,2,0:T(8,128)S(1)}, f32[2,256,16]{1,2,0:T(8,128)}, u32[]{:S(2)}, u32[]{:S(2)}) collective-permute-start(f32[2,256,16]{1,2,0:T(8,128)S(1)} %constant_dynamic-slice_fusion.49), channel_id=1, source_target_pairs={{0,4},{1,5},{2,6},{3,7},{4,0},{5,1},{6,2},{7,3},{8,12},{9,13},{10,... | collective-permute-start | bytes 98312 | tf_op jit(solution)/shard_map/ppermute | solution.py:178
  15.3 91.4 %collective-permute-start.1 = (f32[2,256,16]{1,2,0:T(8,128)}, f32[2,256,16]{1,2,0:T(8,128)}, u32[]{:S(2)}, u32[]{:S(2)}) collective-permute-start(f32[2,256,16]{1,2,0:T(8,128)} %constant_dynamic-slice_fusion.50), channel_id=1, source_target_pairs={{0,4},{1,5},{2,6},{3,7},{4,0},{5,1},{6,2},{7,3},{8,12},{9,13},{10,... | collective-permute-start | bytes 98312 | tf_op jit(solution)/shard_map/ppermute | solution.py:178
  15.9 80.2 %copy-start.95 = (bf16[3592,96]{0,1:T(8,128)(2,1)}, bf16[3592,96]{0,1:T(8,128)(2,1)S(1)}, u32[]{:S(2)}) copy-start(bf16[3592,96]{0,1:T(8,128)(2,1)S(1)} %convert_element_type.864) | copy-start | bytes 2068996
  38.1 57.2 %copy-start.101 = (f32[96,768]{1,0:T(8,128)}, f32[96,768]{1,0:T(8,128)S(1)}, u32[]{:S(2)}) copy-start(f32[96,768]{1,0:T(8,128)S(1)} %copy.504) | copy-start | bytes 884740
  40.0 56.3 %copy-start.215 = (s32[64]{0:T(128)S(1)}, s32[64]{0:T(128)}, u32[]{:S(2)}) copy-start(s32[64]{0:T(128)} %get-tuple-element.434) | copy-start | bytes 772
  95.2 13.2 %collective-permute-start.3 = (bf16[2,4,2688]{2,0,1:T(2,128)(2,1)}, bf16[2,4,2688]{2,0,1:T(2,128)(2,1)}, u32[]{:S(2)}, u32[]{:S(2)}) collective-permute-start(bf16[2,4,2688]{2,0,1:T(2,128)(2,1)} %dynamic-slice_bitcast_fusion), channel_id=1, source_target_pairs={{0,4},{1,5},{2,6},{3,7},{4,0},{5,1},{6,2},{7,3},{8,12},{9,13},{10,... | collective-permute-start | bytes 129032 | tf_op jit(solution)/shard_map/ppermute | solution.py:178
  95.3 282.4 %all-gather.16.cloned.1.call-start = ((), (), s32[]{:S(2)}) async-start(), calls=%async_computation.1 | async-start | bytes 1548288 | tf_op jit(solution)/shard_map/all_gather | solution.py:646
  108.7 68.3 %copy-start.159 = (f32[2,768]{1,0:T(2,128)}, f32[2,768]{1,0:T(2,128)S(1)}, u32[]{:S(2)}) copy-start(f32[2,768]{1,0:T(2,128)S(1)} %get-tuple-element.423) | copy-start | bytes 18436
  108.7 81.2 %copy-start.163 = (f32[2,768]{1,0:T(2,128)}, f32[2,768]{1,0:T(2,128)S(1)}, u32[]{:S(2)}) copy-start(f32[2,768]{1,0:T(2,128)S(1)} %get-tuple-element.420) | copy-start | bytes 18436
  109.6 55.2 %copy-start.31 = (bf16[2,256,768]{2,1,0:T(8,128)(2,1)}, bf16[2,256,768]{2,1,0:T(8,128)(2,1)S(1)}, u32[]{:S(2)}) copy-start(bf16[2,256,768]{2,1,0:T(8,128)(2,1)S(1)} %add_convert_fusion.20) | copy-start | bytes 2359300
  266.4 19.4 %collective-permute-start.7 = (bf16[768,768]{1,0:T(8,128)(2,1)}, bf16[768,768]{1,0:T(8,128)(2,1)}, u32[]{:S(2)}, u32[]{:S(2)}) collective-permute-start(bf16[768,768]{1,0:T(8,128)(2,1)} %bitcast_convert_fusion.12), channel_id=1, source_target_pairs={{0,4},{1,5},{2,6},{3,7},{4,0},{5,1},{6,2},{7,3},{8,12},{9,13},{10,... | collective-permute-start | bytes 3538952 | tf_op jit(solution)/shard_map/ppermute | solution.py:233
  266.8 23.1 %collective-permute-start.6 = (bf16[768,768]{1,0:T(8,128)(2,1)}, bf16[768,768]{1,0:T(8,128)(2,1)}, u32[]{:S(2)}, u32[]{:S(2)}) collective-permute-start(bf16[768,768]{1,0:T(8,128)(2,1)} %bitcast_convert_fusion.14), channel_id=1, source_target_pairs={{0,4},{1,5},{2,6},{3,7},{4,0},{5,1},{6,2},{7,3},{8,12},{9,13},{10,... | collective-permute-start | bytes 3538952 | tf_op jit(solution)/shard_map/ppermute | solution.py:233
  269.7 11.5 %collective-permute-start.5 = (bf16[768,768]{1,0:T(8,128)(2,1)}, bf16[768,768]{1,0:T(8,128)(2,1)}, u32[]{:S(2)}, u32[]{:S(2)}) collective-permute-start(bf16[768,768]{1,0:T(8,128)(2,1)} %bitcast_convert_fusion.16), channel_id=1, source_target_pairs={{0,4},{1,5},{2,6},{3,7},{4,0},{5,1},{6,2},{7,3},{8,12},{9,13},{10,... | collective-permute-start | bytes 3538952 | tf_op jit(solution)/shard_map/ppermute | solution.py:233
  269.9 23.8 %collective-permute-start.4 = (bf16[768,768]{1,0:T(8,128)(2,1)}, bf16[768,768]{1,0:T(8,128)(2,1)}, u32[]{:S(2)}, u32[]{:S(2)}) collective-permute-start(bf16[768,768]{1,0:T(8,128)(2,1)} %bitcast_convert_fusion.18), channel_id=1, source_target_pairs={{0,4},{1,5},{2,6},{3,7},{4,0},{5,1},{6,2},{7,3},{8,12},{9,13},{10,... | collective-permute-start | bytes 3538952 | tf_op jit(solution)/shard_map/ppermute | solution.py:233
  273.3 321.9 %all-gather.20.cloned.1.call-start = ((), (), s32[]{:S(2)}) async-start(), calls=%async_computation.3 | async-start | bytes 2027520 | tf_op jit(solution)/shard_map/all_gather | solution.py:683
  314.9 57.7 %collective-permute-start.13 = (bf16[768,384]{1,0:T(8,128)(2,1)}, bf16[768,384]{1,0:T(8,128)(2,1)}, u32[]{:S(2)}, u32[]{:S(2)}) collective-permute-start(bf16[768,384]{1,0:T(8,128)(2,1)} %fusion.67), channel_id=1, source_target_pairs={{0,4},{1,5},{2,6},{3,7},{4,0},{5,1},{6,2},{7,3},{8,12},{9,13},{10,... | collective-permute-start | bytes 1769480 | tf_op jit(solution)/shard_map/ppermute | solution.py:233
  316.7 58.4 %collective-permute-start.12 = (bf16[768,384]{1,0:T(8,128)(2,1)}, bf16[768,384]{1,0:T(8,128)(2,1)}, u32[]{:S(2)}, u32[]{:S(2)}) collective-permute-start(bf16[768,384]{1,0:T(8,128)(2,1)} %fusion.64), channel_id=1, source_target_pairs={{0,4},{1,5},{2,6},{3,7},{4,0},{5,1},{6,2},{7,3},{8,12},{9,13},{10,... | collective-permute-start | bytes 1769480 | tf_op jit(solution)/shard_map/ppermute | solution.py:233
  324.1 58.2 %collective-permute-start.10 = (bf16[768,768]{1,0:T(8,128)(2,1)}, bf16[768,768]{1,0:T(8,128)(2,1)}, u32[]{:S(2)}, u32[]{:S(2)}) collective-permute-start(bf16[768,768]{1,0:T(8,128)(2,1)} %broadcast_select_fusion.1), channel_id=1, source_target_pairs={{0,1},{1,0},{2,3},{3,2},{4,5},{5,4},{6,7},{7,6},{8,9},{9,8},{10,11... | collective-permute-start | bytes 3538952 | tf_op jit(solution)/shard_map/ppermute | solution.py:233
  326.3 42.5 %collective-permute-start.9 = (bf16[384,768]{1,0:T(8,128)(2,1)}, bf16[384,768]{1,0:T(8,128)(2,1)}, u32[]{:S(2)}, u32[]{:S(2)}) collective-permute-start(bf16[384,768]{1,0:T(8,128)(2,1)} %constant_dynamic-slice_fusion.45), channel_id=1, source_target_pairs={{0,16},{1,17},{2,18},{3,19},{4,20},{5,21},{6,22},{7,23},{8,24},{9,... | collective-permute-start | bytes 1769480 | tf_op jit(solution)/shard_map/ppermute | solution.py:233
  328.7 41.5 %collective-permute-start.8 = (bf16[384,768]{1,0:T(8,128)(2,1)}, bf16[384,768]{1,0:T(8,128)(2,1)}, u32[]{:S(2)}, u32[]{:S(2)}) collective-permute-start(bf16[384,768]{1,0:T(8,128)(2,1)} %constant_dynamic-slice_fusion.46), channel_id=1, source_target_pairs={{0,16},{1,17},{2,18},{3,19},{4,20},{5,21},{6,22},{7,23},{8,24},{9,... | collective-permute-start | bytes 1769480 | tf_op jit(solution)/shard_map/ppermute | solution.py:233
  361.5 277.4 %all-gather.22.cloned.1.call-start = ((), (), s32[]{:S(2)}) async-start(), calls=%async_computation.4 | async-start | bytes 3750912 | tf_op jit(solution)/shard_map/all_gather | solution.py:683
  368.8 15.8 %collective-permute-start.11 = (bf16[768,768]{1,0:T(8,128)(2,1)}, bf16[768,768]{1,0:T(8,128)(2,1)}, u32[]{:S(2)}, u32[]{:S(2)}) collective-permute-start(bf16[768,768]{1,0:T(8,128)(2,1)} %bitcast_convert_fusion.10), channel_id=1, source_target_pairs={{0,4},{1,5},{2,6},{3,7},{4,0},{5,1},{6,2},{7,3},{8,12},{9,13},{10,... | collective-permute-start | bytes 3538952 | tf_op jit(solution)/shard_map/ppermute | solution.py:233
  410.9 29.9 %collective-permute-start.21 = (bf16[768,384]{1,0:T(8,128)(2,1)S(1)}, bf16[768,384]{1,0:T(8,128)(2,1)S(1)}, u32[]{:S(2)}, u32[]{:S(2)}) collective-permute-start(bf16[768,384]{1,0:T(8,128)(2,1)S(1)} %pad_maximum_fusion.5), channel_id=1, source_target_pairs={{0,1},{1,0},{2,3},{3,2},{4,5},{5,4},{6,7},{7,6},{8,9},{9,8},{10,11... | collective-permute-start | bytes 1769480 | tf_op jit(solution)/shard_map/ppermute | solution.py:233
  411.8 16.3 %collective-permute-start.20 = (bf16[384,768]{1,0:T(8,128)(2,1)S(1)}, bf16[384,768]{1,0:T(8,128)(2,1)S(1)}, u32[]{:S(2)}, u32[]{:S(2)}) collective-permute-start(bf16[384,768]{1,0:T(8,128)(2,1)S(1)} %constant_dynamic-slice_fusion.39), channel_id=1, source_target_pairs={{0,16},{1,17},{2,18},{3,19},{4,20},{5,21},{6,22},{7,23},{8,24},{9,... | collective-permute-start | bytes 1769480 | tf_op jit(solution)/shard_map/ppermute | solution.py:233
  413.3 26.5 %collective-permute-start.19 = (bf16[384,768]{1,0:T(8,128)(2,1)S(1)}, bf16[384,768]{1,0:T(8,128)(2,1)S(1)}, u32[]{:S(2)}, u32[]{:S(2)}) collective-permute-start(bf16[384,768]{1,0:T(8,128)(2,1)S(1)} %constant_dynamic-slice_fusion.40), channel_id=1, source_target_pairs={{0,16},{1,17},{2,18},{3,19},{4,20},{5,21},{6,22},{7,23},{8,24},{9,... | collective-permute-start | bytes 1769480 | tf_op jit(solution)/shard_map/ppermute | solution.py:233
  414.1 28.4 %collective-permute-start.18 = (bf16[384,768]{1,0:T(8,128)(2,1)S(1)}, bf16[384,768]{1,0:T(8,128)(2,1)S(1)}, u32[]{:S(2)}, u32[]{:S(2)}) collective-permute-start(bf16[384,768]{1,0:T(8,128)(2,1)S(1)} %broadcast_select_fusion.3), channel_id=1, source_target_pairs={{0,1},{1,0},{2,3},{3,2},{4,5},{5,4},{6,7},{7,6},{8,9},{9,8},{10,11... | collective-permute-start | bytes 1769480 | tf_op jit(solution)/shard_map/ppermute | solution.py:233
  418.1 25.4 %collective-permute-start.15 = (bf16[768,768]{1,0:T(8,128)(2,1)}, bf16[768,768]{1,0:T(8,128)(2,1)}, u32[]{:S(2)}, u32[]{:S(2)}) collective-permute-start(bf16[768,768]{1,0:T(8,128)(2,1)} %bitcast_convert_fusion.6), channel_id=1, source_target_pairs={{0,4},{1,5},{2,6},{3,7},{4,0},{5,1},{6,2},{7,3},{8,12},{9,13},{10,... | collective-permute-start | bytes 3538952 | tf_op jit(solution)/shard_map/ppermute | solution.py:233
  428.1 18.7 %collective-permute-start.17 = (bf16[768,768]{1,0:T(8,128)(2,1)S(1)}, bf16[768,768]{1,0:T(8,128)(2,1)S(1)}, u32[]{:S(2)}, u32[]{:S(2)}) collective-permute-start(bf16[768,768]{1,0:T(8,128)(2,1)S(1)} %copy-done.223), channel_id=1, source_target_pairs={{0,4},{1,5},{2,6},{3,7},{4,0},{5,1},{6,2},{7,3},{8,12},{9,13},{10,... | collective-permute-start | bytes 3538952 | tf_op jit(solution)/shard_map/ppermute | solution.py:233
  439.8 9.5 %collective-permute-start.16 = (bf16[768,768]{1,0:T(8,128)(2,1)S(1)}, bf16[768,768]{1,0:T(8,128)(2,1)S(1)}, u32[]{:S(2)}, u32[]{:S(2)}) collective-permute-start(bf16[768,768]{1,0:T(8,128)(2,1)S(1)} %copy-done.221), channel_id=1, source_target_pairs={{0,4},{1,5},{2,6},{3,7},{4,0},{5,1},{6,2},{7,3},{8,12},{9,13},{10,... | collective-permute-start | bytes 3538952 | tf_op jit(solution)/shard_map/ppermute | solution.py:233
  440.8 11.2 %collective-permute-start.14 = (bf16[768,768]{1,0:T(8,128)(2,1)S(1)}, bf16[768,768]{1,0:T(8,128)(2,1)S(1)}, u32[]{:S(2)}, u32[]{:S(2)}) collective-permute-start(bf16[768,768]{1,0:T(8,128)(2,1)S(1)} %copy-done.222), channel_id=1, source_target_pairs={{0,4},{1,5},{2,6},{3,7},{4,0},{5,1},{6,2},{7,3},{8,12},{9,13},{10,... | collective-permute-start | bytes 3538952 | tf_op jit(solution)/shard_map/ppermute | solution.py:233
  470.4 53.0 %copy-start.17 = (bf16[2,12,64,256]{3,2,1,0:T(8,128)(2,1)}, bf16[2,12,64,256]{3,2,1,0:T(8,128)(2,1)S(1)}, u32[]{:S(2)}) copy-start(bf16[2,12,64,256]{3,2,1,0:T(8,128)(2,1)S(1)} %multiply_convert_fusion.3) | copy-start | bytes 2359300
  472.6 49.6 %collective-permute-start.23 = (bf16[384,768]{1,0:T(8,128)(2,1)}, bf16[384,768]{1,0:T(8,128)(2,1)}, u32[]{:S(2)}, u32[]{:S(2)}) collective-permute-start(bf16[384,768]{1,0:T(8,128)(2,1)} %add_convert_fusion.31), channel_id=1, source_target_pairs={{0,0},{1,1},{2,4},{3,5},{4,2},{5,3},{6,6},{7,7},{8,8},{9,9},{10,12... | collective-permute-start | bytes 1769480 | tf_op jit(solution)/shard_map/ppermute | solution.py:287
  487.5 26.4 %collective-permute-start.28 = (bf16[768,384]{1,0:T(8,128)(2,1)}, bf16[768,384]{1,0:T(8,128)(2,1)}, u32[]{:S(2)}, u32[]{:S(2)}) collective-permute-start(bf16[768,384]{1,0:T(8,128)(2,1)} %fusion.70), channel_id=1, source_target_pairs={{0,4},{1,5},{2,6},{3,7},{4,0},{5,1},{6,2},{7,3},{8,12},{9,13},{10,... | collective-permute-start | bytes 1769480 | tf_op jit(solution)/shard_map/ppermute | solution.py:233
  488.3 21.2 %collective-permute-start.25 = (bf16[384,384]{1,0:T(8,128)(2,1)}, bf16[384,384]{1,0:T(8,128)(2,1)}, u32[]{:S(2)}, u32[]{:S(2)}) collective-permute-start(bf16[384,384]{1,0:T(8,128)(2,1)} %constant_dynamic-slice_fusion.30), channel_id=1, source_target_pairs={{0,16},{1,17},{2,18},{3,19},{4,20},{5,21},{6,22},{7,23},{8,24},{9,... | collective-permute-start | bytes 884744 | tf_op jit(solution)/shard_map/ppermute | solution.py:233
  492.4 18.9 %collective-permute-start.24 = (bf16[384,384]{1,0:T(8,128)(2,1)}, bf16[384,384]{1,0:T(8,128)(2,1)}, u32[]{:S(2)}, u32[]{:S(2)}) collective-permute-start(bf16[384,384]{1,0:T(8,128)(2,1)} %pad_maximum_fusion.7), channel_id=1, source_target_pairs={{0,1},{1,0},{2,3},{3,2},{4,5},{5,4},{6,7},{7,6},{8,9},{9,8},{10,11... | collective-permute-start | bytes 884744 | tf_op jit(solution)/shard_map/ppermute | solution.py:233
  493.7 27.2 %collective-permute-start.22 = (bf16[384,768]{1,0:T(8,128)(2,1)}, bf16[384,768]{1,0:T(8,128)(2,1)}, u32[]{:S(2)}, u32[]{:S(2)}) collective-permute-start(bf16[384,768]{1,0:T(8,128)(2,1)} %add_convert_fusion.32), channel_id=1, source_target_pairs={{0,0},{1,1},{2,4},{3,5},{4,2},{5,3},{6,6},{7,7},{8,8},{9,9},{10,12... | collective-permute-start | bytes 1769480 | tf_op jit(solution)/shard_map/ppermute | solution.py:287
  509.5 7.1 collective-permute-start.29
  511.3 64.0 %collective-permute-start.34 = (bf16[768,768]{1,0:T(8,128)(2,1)}, bf16[768,768]{1,0:T(8,128)(2,1)}, u32[]{:S(2)}, u32[]{:S(2)}) collective-permute-start(bf16[768,768]{1,0:T(8,128)(2,1)} %broadcast_select_fusion), channel_id=1, source_target_pairs={{0,1},{1,0},{2,3},{3,2},{4,5},{5,4},{6,7},{7,6},{8,9},{9,8},{10,11... | collective-permute-start | bytes 3538952 | tf_op jit(solution)/shard_map/ppermute | solution.py:233
  513.9 49.7 %collective-permute-start.31 = (bf16[384,768]{1,0:T(8,128)(2,1)}, bf16[384,768]{1,0:T(8,128)(2,1)}, u32[]{:S(2)}, u32[]{:S(2)}) collective-permute-start(bf16[384,768]{1,0:T(8,128)(2,1)} %constant_dynamic-slice_fusion.18), channel_id=1, source_target_pairs={{0,16},{1,17},{2,18},{3,19},{4,20},{5,21},{6,22},{7,23},{8,24},{9,... | collective-permute-start | bytes 1769480 | tf_op jit(solution)/shard_map/ppermute | solution.py:233
  516.6 47.1 %collective-permute-start.32 = (bf16[384,768]{1,0:T(8,128)(2,1)}, bf16[384,768]{1,0:T(8,128)(2,1)}, u32[]{:S(2)}, u32[]{:S(2)}) collective-permute-start(bf16[384,768]{1,0:T(8,128)(2,1)} %constant_dynamic-slice_fusion.17), channel_id=1, source_target_pairs={{0,16},{1,17},{2,18},{3,19},{4,20},{5,21},{6,22},{7,23},{8,24},{9,... | collective-permute-start | bytes 1769480 | tf_op jit(solution)/shard_map/ppermute | solution.py:233
  520.9 72.1 %collective-permute-start.30 = (bf16[768,384]{1,0:T(8,128)(2,1)}, bf16[768,384]{1,0:T(8,128)(2,1)}, u32[]{:S(2)}, u32[]{:S(2)}) collective-permute-start(bf16[768,384]{1,0:T(8,128)(2,1)} %pad_maximum_fusion.6), channel_id=1, source_target_pairs={{0,1},{1,0},{2,3},{3,2},{4,5},{5,4},{6,7},{7,6},{8,9},{9,8},{10,11... | collective-permute-start | bytes 1769480 | tf_op jit(solution)/shard_map/ppermute | solution.py:233
  533.5 39.6 %collective-permute-start.41 = (bf16[384,384]{1,0:T(8,128)(2,1)}, bf16[384,384]{1,0:T(8,128)(2,1)}, u32[]{:S(2)}, u32[]{:S(2)}) collective-permute-start(bf16[384,384]{1,0:T(8,128)(2,1)} %add_convert_fusion.39), channel_id=1, source_target_pairs={{0,0},{1,1},{2,4},{3,5},{4,2},{5,3},{6,6},{7,7},{8,8},{9,9},{10,12... | collective-permute-start | bytes 884744 | tf_op jit(solution)/shard_map/ppermute | solution.py:287
  563.6 55.1 %collective-permute-start.26 = (bf16[768,768]{1,0:T(8,128)(2,1)}, bf16[768,768]{1,0:T(8,128)(2,1)}, u32[]{:S(2)}, u32[]{:S(2)}) collective-permute-start(bf16[768,768]{1,0:T(8,128)(2,1)} %bitcast_convert_fusion), channel_id=1, source_target_pairs={{0,4},{1,5},{2,6},{3,7},{4,0},{5,1},{6,2},{7,3},{8,12},{9,13},{10,... | collective-permute-start | bytes 3538952 | tf_op jit(solution)/shard_map/ppermute | solution.py:233
  563.7 8.5 collective-permute-start.40
  572.2 17.8 %collective-permute-start.33 = (bf16[384,768]{1,0:T(8,128)(2,1)}, bf16[384,768]{1,0:T(8,128)(2,1)S(1)}, u32[]{:S(2)}, u32[]{:S(2)}) collective-permute-start(bf16[384,768]{1,0:T(8,128)(2,1)} %broadcast_select_fusion.2), channel_id=1, source_target_pairs={{0,1},{1,0},{2,3},{3,2},{4,5},{5,4},{6,7},{7,6},{8,9},{9,8},{10,11... | collective-permute-start | bytes 1769480 | tf_op jit(solution)/shard_map/ppermute | solution.py:233
  578.1 52.7 %collective-permute-start.35 = (bf16[384,768]{1,0:T(8,128)(2,1)}, bf16[384,768]{1,0:T(8,128)(2,1)}, u32[]{:S(2)}, u32[]{:S(2)}) collective-permute-start(bf16[384,768]{1,0:T(8,128)(2,1)} %constant_dynamic-slice_fusion.16), channel_id=1, source_target_pairs={{0,16},{1,17},{2,18},{3,19},{4,20},{5,21},{6,22},{7,23},{8,24},{9,... | collective-permute-start | bytes 1769480 | tf_op jit(solution)/shard_map/ppermute | solution.py:233
  622.9 13.9 %collective-permute-start.27 = (bf16[384,768]{1,0:T(8,128)(2,1)}, bf16[384,768]{1,0:T(8,128)(2,1)}, u32[]{:S(2)}, u32[]{:S(2)}) collective-permute-start(bf16[384,768]{1,0:T(8,128)(2,1)} %constant_dynamic-slice_fusion.23), channel_id=1, source_target_pairs={{0,16},{1,17},{2,18},{3,19},{4,20},{5,21},{6,22},{7,23},{8,24},{9,... | collective-permute-start | bytes 1769480 | tf_op jit(solution)/shard_map/ppermute | solution.py:233
  672.9 107.1 %collective-permute-start.46 = (bf16[384,768]{1,0:T(8,128)(2,1)}, bf16[384,768]{1,0:T(8,128)(2,1)}, u32[]{:S(2)}, u32[]{:S(2)}) collective-permute-start(bf16[384,768]{1,0:T(8,128)(2,1)} %get-tuple-element.108), channel_id=1, source_target_pairs={{0,0},{1,1},{2,4},{3,5},{4,2},{5,3},{6,6},{7,7},{8,8},{9,9},{10,12... | collective-permute-start | bytes 1769480 | tf_op jit(solution)/shard_map/ppermute | solution.py:287
  679.0 101.0 %collective-permute-start.47 = (bf16[384,768]{1,0:T(8,128)(2,1)}, bf16[384,768]{1,0:T(8,128)(2,1)}, u32[]{:S(2)}, u32[]{:S(2)}) collective-permute-start(bf16[384,768]{1,0:T(8,128)(2,1)} %get-tuple-element.109), channel_id=1, source_target_pairs={{0,0},{1,1},{2,4},{3,5},{4,2},{5,3},{6,6},{7,7},{8,8},{9,9},{10,12... | collective-permute-start | bytes 1769480 | tf_op jit(solution)/shard_map/ppermute | solution.py:287
  687.6 18.5 %collective-permute-start.37 = (bf16[384,384]{1,0:T(8,128)(2,1)}, bf16[384,384]{1,0:T(8,128)(2,1)}, u32[]{:S(2)}, u32[]{:S(2)}) collective-permute-start(bf16[384,384]{1,0:T(8,128)(2,1)} %constant_dynamic-slice_fusion.11), channel_id=1, source_target_pairs={{0,16},{1,17},{2,18},{3,19},{4,20},{5,21},{6,22},{7,23},{8,24},{9,... | collective-permute-start | bytes 884744 | tf_op jit(solution)/shard_map/ppermute | solution.py:233
  690.4 16.9 %collective-permute-start.36 = (bf16[384,384]{1,0:T(8,128)(2,1)}, bf16[384,384]{1,0:T(8,128)(2,1)}, u32[]{:S(2)}, u32[]{:S(2)}) collective-permute-start(bf16[384,384]{1,0:T(8,128)(2,1)} %pad_maximum_fusion.8), channel_id=1, source_target_pairs={{0,1},{1,0},{2,3},{3,2},{4,5},{5,4},{6,7},{7,6},{8,9},{9,8},{10,11... | collective-permute-start | bytes 884744 | tf_op jit(solution)/shard_map/ppermute | solution.py:233
  774.2 24.5 %collective-permute-start.42 = (bf16[3592,2,1,96]{0,3,2,1:T(8,128)(2,1)S(1)}, bf16[3592,2,1,96]{0,3,2,1:T(8,128)(2,1)S(1)}, u32[]{:S(2)}, u32[]{:S(2)}) collective-permute-start(bf16[3592,2,1,96]{0,3,2,1:T(8,128)(2,1)S(1)} %dynamic-slice_convert_fusion), channel_id=1, source_target_pairs={{0,4},{4,0},{8,12},{12,8},{16,20},{20,16},{24,28},{28,24},{1,5},{5... | collective-permute-start | bytes 4137992 | tf_op jit(solution)/shard_map/ppermute | solution.py:40
  774.5 23.3 %collective-permute-start.38 = (bf16[384,384]{1,0:T(8,128)(2,1)S(1)}, bf16[384,384]{1,0:T(8,128)(2,1)S(1)}, u32[]{:S(2)}, u32[]{:S(2)}) collective-permute-start(bf16[384,384]{1,0:T(8,128)(2,1)S(1)} %copy-done.121), channel_id=1, source_target_pairs={{0,0},{1,1},{2,4},{3,5},{4,2},{5,3},{6,6},{7,7},{8,8},{9,9},{10,12... | collective-permute-start | bytes 884744 | tf_op jit(solution)/shard_map/ppermute | solution.py:287
  775.2 22.7 %collective-permute-start.39 = (bf16[384,384]{1,0:T(8,128)(2,1)S(1)}, bf16[384,384]{1,0:T(8,128)(2,1)S(1)}, u32[]{:S(2)}, u32[]{:S(2)}) collective-permute-start(bf16[384,384]{1,0:T(8,128)(2,1)S(1)} %copy-done.113), channel_id=1, source_target_pairs={{0,0},{1,1},{2,4},{3,5},{4,2},{5,3},{6,6},{7,7},{8,8},{9,9},{10,12... | collective-permute-start | bytes 884744 | tf_op jit(solution)/shard_map/ppermute | solution.py:287
  792.6 25.0 %collective-permute-start.48 = (bf16[2,2,2,1,96,768]{5,4,1,0,3,2:T(8,128)(2,1)}, bf16[2,2,2,1,96,768]{5,4,1,0,3,2:T(8,128)(2,1)}, u32[]{:S(2)}, u32[]{:S(2)}) collective-permute-start(bf16[2,2,2,1,96,768]{5,4,1,0,3,2:T(8,128)(2,1)} %copy.677), channel_id=1, source_target_pairs={{0,4},{4,0},{8,12},{12,8},{16,20},{20,16},{24,28},{28,24},{1,5},{5... | collective-permute-start | bytes 3538952 | tf_op jit(solution)/shard_map/ppermute | solution.py:40
  808.9 11.2 %collective-permute-start.43 = (bf16[2,4,2,1,96,192]{5,4,1,0,3,2:T(8,128)(2,1)}, bf16[2,4,2,1,96,192]{5,4,1,0,3,2:T(8,128)(2,1)}, u32[]{:S(2)}, u32[]{:S(2)}) collective-permute-start(bf16[2,4,2,1,96,192]{5,4,1,0,3,2:T(8,128)(2,1)} %copy.679), channel_id=1, source_target_pairs={{0,4},{4,0},{8,12},{12,8},{16,20},{20,16},{24,28},{28,24},{1,5},{5... | collective-permute-start | bytes 1769480 | tf_op jit(solution)/shard_map/ppermute | solution.py:40
  810.5 19.2 %collective-permute-start.45 = (bf16[3592,1,1,96]{0,3,2,1:T(8,128)(2,1)}, bf16[3592,1,1,96]{0,3,2,1:T(8,128)(2,1)}, u32[]{:S(2)}, u32[]{:S(2)}) collective-permute-start(bf16[3592,1,1,96]{0,3,2,1:T(8,128)(2,1)} %dynamic-slice_convert_fusion.1), channel_id=1, source_target_pairs={{0,8},{4,12},{8,0},{12,4},{16,24},{20,28},{24,16},{28,20},{1,9},{5... | collective-permute-start | bytes 2069000 | tf_op jit(solution)/shard_map/ppermute | solution.py:40
  822.2 22.7 %collective-permute-start.44 = (bf16[2,4,1,1,96,192]{5,4,1,0,3,2:T(8,128)(2,1)S(1)}, bf16[2,4,1,1,96,192]{5,4,1,0,3,2:T(8,128)(2,1)S(1)}, u32[]{:S(2)}, u32[]{:S(2)}) collective-permute-start(bf16[2,4,1,1,96,192]{5,4,1,0,3,2:T(8,128)(2,1)S(1)} %dynamic-slice_convert_fusion.4), channel_id=1, source_target_pairs={{0,8},{4,12},{8,0},{12,4},{16,24},{20,28},{24,16},{28,20},{1,9},{5... | collective-permute-start | bytes 884744 | tf_op jit(solution)/shard_map/ppermute | solution.py:40
  840.0 3.9 collective-permute-start.50
  840.2 16.3 %collective-permute-start.49 = (bf16[2,2,1,1,96,768]{5,4,1,0,3,2:T(8,128)(2,1)S(1)}, bf16[2,2,1,1,96,768]{5,4,1,0,3,2:T(8,128)(2,1)S(1)}, u32[]{:S(2)}, u32[]{:S(2)}) collective-permute-start(bf16[2,2,1,1,96,768]{5,4,1,0,3,2:T(8,128)(2,1)S(1)} %dynamic-slice_convert_fusion.2), channel_id=1, source_target_pairs={{0,8},{4,12},{8,0},{12,4},{16,24},{20,28},{24,16},{28,20},{1,9},{5... | collective-permute-start | bytes 1769480 | tf_op jit(solution)/shard_map/ppermute | solution.py:40
  844.2 21.2 %collective-permute-start.51 = (bf16[2,1,1,96,1152]{4,3,0,2,1:T(8,128)(2,1)S(1)}, bf16[2,1,1,96,1152]{4,3,0,2,1:T(8,128)(2,1)S(1)}, u32[]{:S(2)}, u32[]{:S(2)}) collective-permute-start(bf16[2,1,1,96,1152]{4,3,0,2,1:T(8,128)(2,1)S(1)} %dynamic-slice_convert_fusion.3), channel_id=1, source_target_pairs={{0,8},{4,12},{8,0},{12,4},{16,24},{20,28},{24,16},{28,20},{1,9},{5... | collective-permute-start | bytes 1327112 | tf_op jit(solution)/shard_map/ppermute | solution.py:40
  (262 other events, 1671.2 us)
Sparse Core Ops, SparseCore 0:
  11.5 136.4 all-gather.13
  151.5 79.7 all-gather.17
  273.4 23.2 all-gather.15
  361.6 54.7 all-gather.19
  563.7 58.5 all-gather.21

commit v6 on v4

--- a/solution.py
+++ b/solution.py
@@ -814,13 +814,13 @@
             block = group_step(block, axes_at[index_at], shift_group, bit_at)
         return block.reshape(weights_in[index_at].shape)
 
-    for index_at in (1, 0, 2, 3):
+    for index_at in (3, 1, 0, 2):
         grad_now = reduced[index_at]
+        if index_at == 0:
+            grad_now, steps[3] = tied(grad_now, steps[3])
         if index_at == 2:
-            grad_now, steps[1] = tied(grad_now, steps[1])
-        if index_at == 3:
-            summed[1] = crossed(1)
-            grad_now, (summed[1], steps[0]) = tied(grad_now, (summed[1], steps[0]))
+            summed[3] = crossed(3)
+            grad_now, (summed[3], steps[1]) = tied(grad_now, (summed[3], steps[1]))
         update, new_firsts[index_at], new_seconds[index_at] = adam_update(
             grad_now * own_scale, firsts_in[index_at], seconds_in[index_at]
         )
@@ -828,7 +828,7 @@
         steps[index_at] = group_step(
             split_bits(update, axis_at, shift_group), axis_at, shift_group, 0
         )
-    for index_at in (0, 2, 3):
+    for index_at in (1, 0, 2):
         summed[index_at] = crossed(index_at)
     new_weights, new_momenta = ([], [])
     for index_at in range(4):

time: 881 us -> 839 us (0.952)
  waiting for transfers between devices: 154 us -> 109 us
  matrix products: 206 us -> 197 us
    ppermute x32, waiting for transfers between devices: 67.8 us -> 30.7 us  [exchanged(): lax.ppermute(value, ('dp', 'tensor'), [(source, source ^ mask) for source...]
    ppermute x8, starting transfers between devices: 4.58 us -> 17.6 us  [swapped(): return lax.ppermute(value, axis, pairs)]
    unnamed x569 -> x557, local copies, waits for them, and re-layouts: 63.3 us -> 63 us
  transfers between devices with their start and end apart: 57 -> 57, of which waited for: 14 -> 10; matrix products, arithmetic and copies ran while one was open for 47% -> 46% of each run, Pallas kernels for 1% -> 1%
where the time goes in v6:
time: 839 us; the launch traced here: 826 us
  matrix products  197 us (23%)
  other arithmetic  148 us (18%)
  local copies, waits for them, and re-layouts  144 us (17%)
  blocking collectives  117 us (14%)
  waiting for transfers between devices  109 us (13%)
  starting transfers between devices  71.7 us (9%)
  between operations  27.8 us (3%)
  Pallas kernels  10.9 us (1%)
    dot_general x36, matrix products, weight_grad(): lax.dot_general(inputs, grads_out, ((leading, leading), ((), ())), prefer...  73.7 us
    unnamed x557, local copies, waits for them, and re-layouts  63 us
    dot_general x29, matrix products, product_t(): lax.dot_general(left, right, (((left.ndim - 1,), (1,)), ((), ())), prefer...  49.5 us
    dot_general x32, matrix products, product(): return jnp.dot(left, right, preferred_element_type=jnp.float32)  47.6 us
    unnamed x1, blocking collectives  39 us
    all_gather x1, waiting for transfers between devices, per_device(): first_whole = lax.all_gather(first_local, everyone, axis=1, tiled=True)  38.4 us
    div x4, other arithmetic, adam_update(): first_new / (1.0 - BETA_FIRST ** STEP_COUNT)  33.8 us
    ppermute x8, starting transfers between devices, homeward(): return [lax.ppermute(value, ('dp', 'tensor'), pairs) for value in values]  31.3 us
  transfers between devices with their start and end apart: 57, of which 10 were waited for; matrix products, arithmetic and copies ran while one was open for 46% of the time, Pallas kernels for 1%

profile of v6, /device:TPU:0, one launch (start us, length us, event | category | flops | bytes accessed | tf_op | source)
XLA Modules:
  0.0 825.7 jit_solution(7450219388414499443)
XLA Ops:
  15.9 10.1 %all-gather.5 = s32[8,8,2]{1,2,0:T(2,128)S(1)} all-gather(s32[1,8,2]{1,2,0:T(2,128)S(1)} %add_bitcast_fusion.1), channel_id=1, replica_groups=mesh['dp'=8,'tensor'=4] {'dp'}, dimensions={0}, use_global_device_ids=true | all-gather | bytes 576 | tf_op jit(solution)/shard_map/all_gather | solution.py:531
  28.4 9.6 %all_gather.49 = f32[96,768]{0,1:T(8,128)S(1)} all-gather(f32[96,96]{0,1:T(8,128)S(1)} %copy.488), channel_id=1, replica_groups=mesh['dp'=8,'tensor'=4] {'dp'}, dimensions={1}, use_global_device_ids=true | all-gather | bytes 331776 | tf_op jit(solution)/shard_map/all_gather | solution.py:563
  41.3 39.0 %all-reduce.3 = bf16[64,2688]{1,0:T(8,128)(2,1)S(1)} all-reduce(f32[64,2688]{1,0:T(8,128)S(1)} %pad_maximum_fusion.3), channel_id=7, replica_groups=mesh['dp'=8,'tensor'=4] {'dp'}, use_global_device_ids=true, to_apply=%region_5.6.clone | all-reduce | flops 172032 | bytes 1032192
  80.4 14.2 %all-gather = bf16[32,2688]{1,0:T(8,128)(2,1)S(1)} all-gather(bf16[8,2688]{1,0:T(8,128)(2,1)S(1)} %dynamic-slice_convert_fusion.5), channel_id=2, replica_groups=mesh['dp'=8,'tensor'=4] {'tensor'}, dimensions={0}, use_global_device_ids=true | all-gather | bytes 215040 | tf_op jit(solution)/shard_map/all_gather | solution.py:600
  97.1 3.6 copy.566
  109.6 38.4 %all-gather.14.cloned.1.call-done = bf16[4,3072,768]{2,1,0:T(8,128)(2,1)} async-done(((bf16[4,96,768]{2,1,0:T(8,128)(2,1)}), bf16[4,3072,768]{2,1,0:T(8,128)(2,1)}) %all-gather.14.cloned.1.call-update) | async-done | bytes 18874384 | tf_op jit(solution)/shard_map/all_gather | solution.py:544
  148.0 5.4 attn_maps.2
  153.4 5.6 attn_maps.3
  164.8 2.9 add_convert_fusion.18
  177.9 3.8 fusion.250
  206.9 3.4 fusion.248
  211.0 20.4 %all-gather.18.cloned.1.call-done = bf16[1,2,3072,768]{3,2,1,0:T(8,128)(2,1)} async-done(((bf16[1,2,96,768]{3,2,1,0:T(8,128)(2,1)}), bf16[1,2,3072,768]{3,2,1,0:T(8,128)(2,1)}) %all-gather.18.cloned.1.call-update) | async-done | bytes 9437200 | tf_op jit(solution)/shard_map/all_gather | solution.py:545
  233.6 3.7 fusion.91
  270.1 3.1 multiply_reduce_fusion.8
  273.7 4.8 multiply_reduce_fusion.27
  282.3 3.5 add_convert_fusion.10
  285.8 3.9 add_convert_fusion.8
  289.8 3.9 add_convert_fusion.9
  293.7 3.1 add_convert_fusion.11
  296.9 3.1 convolution_convert_fusion.3
  301.4 5.7 bitcast_reduce_fusion.1
  316.9 3.3 fusion.89
  331.6 4.5 multiply_reduce_fusion.10
  361.7 3.2 multiply_add_fusion.6
  372.5 2.6 add_convert_fusion.33
  375.1 2.5 add_convert_fusion.34
  384.5 3.0 add_convert_fusion.6
  389.2 4.0 bitcast_convert_fusion.5
  418.6 7.5 collective-permute-done.16
  426.3 11.6 %collective-permute-done.15 = bf16[384,768]{1,0:T(8,128)(2,1)S(1)} collective-permute-done((bf16[384,768]{1,0:T(8,128)(2,1)S(1)}, bf16[384,768]{1,0:T(8,128)(2,1)S(1)}, u32[]{:S(2)}, u32[]{:S(2)}) %collective-permute-start.15) | collective-permute-done | bytes 589856 | tf_op jit(solution)/shard_map/ppermute | solution.py:233
  445.5 6.0 collective-permute-start.22
  458.7 6.1 collective-permute-start.23
  465.8 3.7 add_convert_fusion.4
  469.5 3.9 add_convert_fusion.2
  473.5 2.5 add_convert_fusion.3
  477.9 2.9 convolution_convert_fusion.1
  482.3 4.9 multiply_reduce_fusion
  499.8 2.8 fusion.81
  511.6 3.7 collective-permute-start.41
  521.0 3.0 bitcast_convert_fusion
  563.0 3.5 multiply_reduce_fusion.35
  566.5 6.0 collective-permute-start.46
  575.5 2.9 collective-permute-done.31
  580.8 3.8 collective-permute-done.37
  586.2 6.1 collective-permute-start.47
  592.4 4.8 collective-permute-done.27
  628.6 13.2 %all-gather.4 = bf16[256,96]{1,0:T(8,128)(2,1)S(1)} all-gather(bf16[64,96]{1,0:T(8,128)(2,1)S(1)} %fusion.79), channel_id=6, replica_groups=mesh['dp'=8,'tensor'=4] {'tensor'}, dimensions={0}, use_global_device_ids=true | all-gather | bytes 61440 | tf_op jit(solution)/shard_map/all_gather | solution.py:721
  643.2 8.7 %all-gather.7 = bf16[8,96,64]{1,2,0:T(8,128)(2,1)S(1)} all-gather(bf16[1,96,64]{1,2,0:T(8,128)(2,1)S(1)} %fusion.198), channel_id=1, replica_groups=mesh['dp'=8,'tensor'=4] {'dp'}, dimensions={0}, use_global_device_ids=true | all-gather | bytes 110592 | tf_op jit(solution)/shard_map/all_gather | solution.py:723
  670.0 3.5 pad_maximum_fusion
  674.3 13.2 %all_gather.62 = f32[32,128]{1,0:T(8,128)S(1)} all-gather(f32[8,128]{1,0:T(8,128)S(1)} %broadcast_in_dim.21), channel_id=1, replica_groups=mesh['dp'=8,'tensor'=4] {'tensor'}, dimensions={0}, use_global_device_ids=true | all-gather | bytes 20480 | tf_op jit(solution)/shard_map/all_gather | solution.py:798
  687.6 8.8 %all_gather.63 = f32[64,128]{1,0:T(8,128)S(1)} all-gather(f32[8,128]{1,0:T(8,128)S(1)} %broadcast_in_dim.23), channel_id=1, replica_groups=mesh['dp'=8,'tensor'=4] {'dp'}, dimensions={0}, use_global_device_ids=true | all-gather | bytes 36864 | tf_op jit(solution)/shard_map/all_gather | solution.py:798
  697.5 11.7 %add_divide_fusion = (f32[3592,384]{1,0:T(8,128)}, f32[3592,384]{1,0:T(8,128)}, f32[3592,384]{1,0:T(8,128)}) fusion(f32[3592,384]{1,0:T(8,128)} %copy-done.10, f32[]{:T(128)} %get-tuple-element.316, f32[3592,384]{1,0:T(8,128)} %param.44, f32[3592,384]{1,0:T(8,128)} %param.45), kind=kLoop, calls=%fused_computation.13 | loop fusion | flops 16551936 | bytes 33103876 | tf_op jit(solution)/shard_map/div | solution.py:484
  709.3 6.4 copy.567
  718.2 8.5 %add_divide_fusion.1 = (f32[2,2,384,768]{3,2,1,0:T(8,128)S(1)}, f32[2,2,384,768]{3,2,1,0:T(8,128)}, f32[2,2,384,768]{3,2,1,0:T(8,128)}) fusion(f32[]{:T(128)} %get-tuple-element.316, bf16[1,2,384,768]{3,2,1,0:T(8,128)(2,1)S(1)} %copy-done.54, bf16[1,2,384,768]{3,2,1,0:T(8,128)(2,1)S(1)} %copy-done.55, f32[2,2,384,768]{3,2,1,0:T(8,128)} %param.40, ...), kind=kLoop, calls=%fused_computation.19 | loop fusion | flops 16515072 | bytes 25952260 | tf_op jit(solution)/shard_map/div | solution.py:484
  739.2 5.7 add_divide_fusion.3
  747.3 12.6 %collective-permute-start.43 = (bf16[2,4,2,1,96,192]{5,4,1,0,3,2:T(8,128)(2,1)}, bf16[2,4,2,1,96,192]{5,4,1,0,3,2:T(8,128)(2,1)}, u32[]{:S(2)}, u32[]{:S(2)}) collective-permute-start(bf16[2,4,2,1,96,192]{5,4,1,0,3,2:T(8,128)(2,1)} %copy.661), channel_id=1, source_target_pairs={{0,4},{4,0},{8,12},{12,8},{16,20},{20,16},{24,28},{28,24},{1,5},{5... | collective-permute-start | bytes 1769480 | tf_op jit(solution)/shard_map/ppermute | solution.py:40
  762.9 3.1 copy_add_fusion
  766.0 3.3 copy.575
  769.3 3.3 copy.576
  776.1 5.2 collective-permute-done.45
  782.6 7.9 add_divide_fusion.2
  793.0 3.5 multiply_subtract_fusion
  799.6 8.8 %collective-permute-done.49 = bf16[2,2,1,1,96,768]{5,4,1,0,3,2:T(8,128)(2,1)S(1)} collective-permute-done((bf16[2,2,1,1,96,768]{5,4,1,0,3,2:T(8,128)(2,1)S(1)}, bf16[2,2,1,1,96,768]{5,4,1,0,3,2:T(8,128)(2,1)S(1)}, u32[]{:S(2)}, u32[]{:S(2)}) %collective-permute-start.49) | collective-permute-done | bytes 589856 | tf_op jit(solution)/shard_map/ppermute | solution.py:40
  810.3 5.7 collective-permute-done.51
  (1026 shorter events, 364.6 us)
Async XLA Ops:
  7.2 140.8 %all-gather.14.cloned.1.call-start = ((), (), s32[]{:S(2)}) async-start(), calls=%async_computation | async-start | bytes 19464192 | tf_op jit(solution)/shard_map/all_gather | solution.py:544
  11.1 220.2 %all-gather.18.cloned.1.call-start = ((), (), s32[]{:S(2)}) async-start(), calls=%async_computation.2 | async-start | bytes 9732096 | tf_op jit(solution)/shard_map/all_gather | solution.py:545
  12.6 94.0 %collective-permute-start = (f32[2,1]{0,1:T(1,128)}, f32[2,1]{0,1:T(1,128)}, u32[]{:S(2)}, u32[]{:S(2)}) collective-permute-start(f32[2,1]{0,1:T(1,128)} %dynamic-slice_bitcast_fusion.4), channel_id=1, source_target_pairs={{0,4},{1,5},{2,6},{3,7},{4,0},{5,1},{6,2},{7,3},{8,12},{9,13},{10,... | collective-permute-start | bytes 32 | tf_op jit(solution)/shard_map/ppermute | solution.py:178
  13.9 92.9 %collective-permute-start.2 = (f32[2,256,16]{1,2,0:T(8,128)S(1)}, f32[2,256,16]{1,2,0:T(8,128)}, u32[]{:S(2)}, u32[]{:S(2)}) collective-permute-start(f32[2,256,16]{1,2,0:T(8,128)S(1)} %constant_dynamic-slice_fusion.49), channel_id=1, source_target_pairs={{0,4},{1,5},{2,6},{3,7},{4,0},{5,1},{6,2},{7,3},{8,12},{9,13},{10,... | collective-permute-start | bytes 98312 | tf_op jit(solution)/shard_map/ppermute | solution.py:178
  15.3 91.4 %collective-permute-start.1 = (f32[2,256,16]{1,2,0:T(8,128)}, f32[2,256,16]{1,2,0:T(8,128)}, u32[]{:S(2)}, u32[]{:S(2)}) collective-permute-start(f32[2,256,16]{1,2,0:T(8,128)} %constant_dynamic-slice_fusion.50), channel_id=1, source_target_pairs={{0,4},{1,5},{2,6},{3,7},{4,0},{5,1},{6,2},{7,3},{8,12},{9,13},{10,... | collective-permute-start | bytes 98312 | tf_op jit(solution)/shard_map/ppermute | solution.py:178
  15.9 80.2 %copy-start.86 = (bf16[3592,96]{0,1:T(8,128)(2,1)}, bf16[3592,96]{0,1:T(8,128)(2,1)S(1)}, u32[]{:S(2)}) copy-start(bf16[3592,96]{0,1:T(8,128)(2,1)S(1)} %convert_element_type.864) | copy-start | bytes 2068996
  38.1 57.2 %copy-start.90 = (f32[96,768]{1,0:T(8,128)}, f32[96,768]{1,0:T(8,128)S(1)}, u32[]{:S(2)}) copy-start(f32[96,768]{1,0:T(8,128)S(1)} %copy.489) | copy-start | bytes 884740
  40.0 56.3 %copy-start.197 = (s32[64]{0:T(128)S(1)}, s32[64]{0:T(128)}, u32[]{:S(2)}) copy-start(s32[64]{0:T(128)} %get-tuple-element.430) | copy-start | bytes 772
  95.2 13.3 %collective-permute-start.3 = (bf16[2,4,2688]{2,0,1:T(2,128)(2,1)}, bf16[2,4,2688]{2,0,1:T(2,128)(2,1)}, u32[]{:S(2)}, u32[]{:S(2)}) collective-permute-start(bf16[2,4,2688]{2,0,1:T(2,128)(2,1)} %dynamic-slice_bitcast_fusion), channel_id=1, source_target_pairs={{0,4},{1,5},{2,6},{3,7},{4,0},{5,1},{6,2},{7,3},{8,12},{9,13},{10,... | collective-permute-start | bytes 129032 | tf_op jit(solution)/shard_map/ppermute | solution.py:178
  95.3 282.3 %all-gather.16.cloned.1.call-start = ((), (), s32[]{:S(2)}) async-start(), calls=%async_computation.1 | async-start | bytes 1548288 | tf_op jit(solution)/shard_map/all_gather | solution.py:647
  108.7 68.3 %copy-start.152 = (f32[2,768]{1,0:T(2,128)}, f32[2,768]{1,0:T(2,128)S(1)}, u32[]{:S(2)}) copy-start(f32[2,768]{1,0:T(2,128)S(1)} %get-tuple-element.419) | copy-start | bytes 18436
  108.7 81.1 %copy-start.156 = (f32[2,768]{1,0:T(2,128)}, f32[2,768]{1,0:T(2,128)S(1)}, u32[]{:S(2)}) copy-start(f32[2,768]{1,0:T(2,128)S(1)} %get-tuple-element.416) | copy-start | bytes 18436
  109.6 55.2 %copy-start.24 = (bf16[2,256,768]{2,1,0:T(8,128)(2,1)}, bf16[2,256,768]{2,1,0:T(8,128)(2,1)S(1)}, u32[]{:S(2)}) copy-start(bf16[2,256,768]{2,1,0:T(8,128)(2,1)S(1)} %add_convert_fusion.20) | copy-start | bytes 2359300
  266.4 19.4 %collective-permute-start.7 = (bf16[768,768]{1,0:T(8,128)(2,1)}, bf16[768,768]{1,0:T(8,128)(2,1)}, u32[]{:S(2)}, u32[]{:S(2)}) collective-permute-start(bf16[768,768]{1,0:T(8,128)(2,1)} %bitcast_convert_fusion.12), channel_id=1, source_target_pairs={{0,4},{1,5},{2,6},{3,7},{4,0},{5,1},{6,2},{7,3},{8,12},{9,13},{10,... | collective-permute-start | bytes 3538952 | tf_op jit(solution)/shard_map/ppermute | solution.py:233
  266.7 23.1 %collective-permute-start.6 = (bf16[768,768]{1,0:T(8,128)(2,1)}, bf16[768,768]{1,0:T(8,128)(2,1)}, u32[]{:S(2)}, u32[]{:S(2)}) collective-permute-start(bf16[768,768]{1,0:T(8,128)(2,1)} %bitcast_convert_fusion.14), channel_id=1, source_target_pairs={{0,4},{1,5},{2,6},{3,7},{4,0},{5,1},{6,2},{7,3},{8,12},{9,13},{10,... | collective-permute-start | bytes 3538952 | tf_op jit(solution)/shard_map/ppermute | solution.py:233
  269.6 11.5 %collective-permute-start.5 = (bf16[768,768]{1,0:T(8,128)(2,1)}, bf16[768,768]{1,0:T(8,128)(2,1)}, u32[]{:S(2)}, u32[]{:S(2)}) collective-permute-start(bf16[768,768]{1,0:T(8,128)(2,1)} %bitcast_convert_fusion.16), channel_id=1, source_target_pairs={{0,4},{1,5},{2,6},{3,7},{4,0},{5,1},{6,2},{7,3},{8,12},{9,13},{10,... | collective-permute-start | bytes 3538952 | tf_op jit(solution)/shard_map/ppermute | solution.py:233
  269.9 23.8 %collective-permute-start.4 = (bf16[768,768]{1,0:T(8,128)(2,1)}, bf16[768,768]{1,0:T(8,128)(2,1)}, u32[]{:S(2)}, u32[]{:S(2)}) collective-permute-start(bf16[768,768]{1,0:T(8,128)(2,1)} %bitcast_convert_fusion.18), channel_id=1, source_target_pairs={{0,4},{1,5},{2,6},{3,7},{4,0},{5,1},{6,2},{7,3},{8,12},{9,13},{10,... | collective-permute-start | bytes 3538952 | tf_op jit(solution)/shard_map/ppermute | solution.py:233
  273.3 270.1 %all-gather.20.cloned.1.call-start = ((), (), s32[]{:S(2)}) async-start(), calls=%async_computation.3 | async-start | bytes 2027520 | tf_op jit(solution)/shard_map/all_gather | solution.py:685
  314.8 57.7 %collective-permute-start.13 = (bf16[768,384]{1,0:T(8,128)(2,1)}, bf16[768,384]{1,0:T(8,128)(2,1)}, u32[]{:S(2)}, u32[]{:S(2)}) collective-permute-start(bf16[768,384]{1,0:T(8,128)(2,1)} %fusion.67), channel_id=1, source_target_pairs={{0,4},{1,5},{2,6},{3,7},{4,0},{5,1},{6,2},{7,3},{8,12},{9,13},{10,... | collective-permute-start | bytes 1769480 | tf_op jit(solution)/shard_map/ppermute | solution.py:233
  316.6 58.4 %collective-permute-start.12 = (bf16[768,384]{1,0:T(8,128)(2,1)}, bf16[768,384]{1,0:T(8,128)(2,1)}, u32[]{:S(2)}, u32[]{:S(2)}) collective-permute-start(bf16[768,384]{1,0:T(8,128)(2,1)} %fusion.64), channel_id=1, source_target_pairs={{0,4},{1,5},{2,6},{3,7},{4,0},{5,1},{6,2},{7,3},{8,12},{9,13},{10,... | collective-permute-start | bytes 1769480 | tf_op jit(solution)/shard_map/ppermute | solution.py:233
  324.1 58.2 %collective-permute-start.10 = (bf16[768,768]{1,0:T(8,128)(2,1)}, bf16[768,768]{1,0:T(8,128)(2,1)}, u32[]{:S(2)}, u32[]{:S(2)}) collective-permute-start(bf16[768,768]{1,0:T(8,128)(2,1)} %broadcast_select_fusion.1), channel_id=1, source_target_pairs={{0,1},{1,0},{2,3},{3,2},{4,5},{5,4},{6,7},{7,6},{8,9},{9,8},{10,11... | collective-permute-start | bytes 3538952 | tf_op jit(solution)/shard_map/ppermute | solution.py:233
  326.3 42.4 %collective-permute-start.9 = (bf16[384,768]{1,0:T(8,128)(2,1)}, bf16[384,768]{1,0:T(8,128)(2,1)}, u32[]{:S(2)}, u32[]{:S(2)}) collective-permute-start(bf16[384,768]{1,0:T(8,128)(2,1)} %constant_dynamic-slice_fusion.45), channel_id=1, source_target_pairs={{0,16},{1,17},{2,18},{3,19},{4,20},{5,21},{6,22},{7,23},{8,24},{9,... | collective-permute-start | bytes 1769480 | tf_op jit(solution)/shard_map/ppermute | solution.py:233
  328.6 41.4 %collective-permute-start.8 = (bf16[384,768]{1,0:T(8,128)(2,1)}, bf16[384,768]{1,0:T(8,128)(2,1)}, u32[]{:S(2)}, u32[]{:S(2)}) collective-permute-start(bf16[384,768]{1,0:T(8,128)(2,1)} %constant_dynamic-slice_fusion.46), channel_id=1, source_target_pairs={{0,16},{1,17},{2,18},{3,19},{4,20},{5,21},{6,22},{7,23},{8,24},{9,... | collective-permute-start | bytes 1769480 | tf_op jit(solution)/shard_map/ppermute | solution.py:233
  361.4 258.8 %all-gather.22.cloned.1.call-start = ((), (), s32[]{:S(2)}) async-start(), calls=%async_computation.4 | async-start | bytes 3750912 | tf_op jit(solution)/shard_map/all_gather | solution.py:685
  368.7 15.8 %collective-permute-start.11 = (bf16[768,768]{1,0:T(8,128)(2,1)}, bf16[768,768]{1,0:T(8,128)(2,1)}, u32[]{:S(2)}, u32[]{:S(2)}) collective-permute-start(bf16[768,768]{1,0:T(8,128)(2,1)} %bitcast_convert_fusion.10), channel_id=1, source_target_pairs={{0,4},{1,5},{2,6},{3,7},{4,0},{5,1},{6,2},{7,3},{8,12},{9,13},{10,... | collective-permute-start | bytes 3538952 | tf_op jit(solution)/shard_map/ppermute | solution.py:233
  409.0 30.9 %collective-permute-start.17 = (bf16[768,384]{1,0:T(8,128)(2,1)S(1)}, bf16[768,384]{1,0:T(8,128)(2,1)S(1)}, u32[]{:S(2)}, u32[]{:S(2)}) collective-permute-start(bf16[768,384]{1,0:T(8,128)(2,1)S(1)} %pad_maximum_fusion.5), channel_id=1, source_target_pairs={{0,1},{1,0},{2,3},{3,2},{4,5},{5,4},{6,7},{7,6},{8,9},{9,8},{10,11... | collective-permute-start | bytes 1769480 | tf_op jit(solution)/shard_map/ppermute | solution.py:233
  409.8 16.3 %collective-permute-start.16 = (bf16[384,768]{1,0:T(8,128)(2,1)S(1)}, bf16[384,768]{1,0:T(8,128)(2,1)S(1)}, u32[]{:S(2)}, u32[]{:S(2)}) collective-permute-start(bf16[384,768]{1,0:T(8,128)(2,1)S(1)} %constant_dynamic-slice_fusion.39), channel_id=1, source_target_pairs={{0,16},{1,17},{2,18},{3,19},{4,20},{5,21},{6,22},{7,23},{8,24},{9,... | collective-permute-start | bytes 1769480 | tf_op jit(solution)/shard_map/ppermute | solution.py:233
  411.4 26.4 %collective-permute-start.15 = (bf16[384,768]{1,0:T(8,128)(2,1)S(1)}, bf16[384,768]{1,0:T(8,128)(2,1)S(1)}, u32[]{:S(2)}, u32[]{:S(2)}) collective-permute-start(bf16[384,768]{1,0:T(8,128)(2,1)S(1)} %constant_dynamic-slice_fusion.40), channel_id=1, source_target_pairs={{0,16},{1,17},{2,18},{3,19},{4,20},{5,21},{6,22},{7,23},{8,24},{9,... | collective-permute-start | bytes 1769480 | tf_op jit(solution)/shard_map/ppermute | solution.py:233
  412.1 26.7 %collective-permute-start.14 = (bf16[384,768]{1,0:T(8,128)(2,1)S(1)}, bf16[384,768]{1,0:T(8,128)(2,1)S(1)}, u32[]{:S(2)}, u32[]{:S(2)}) collective-permute-start(bf16[384,768]{1,0:T(8,128)(2,1)S(1)} %broadcast_select_fusion.3), channel_id=1, source_target_pairs={{0,1},{1,0},{2,3},{3,2},{4,5},{5,4},{6,7},{7,6},{8,9},{9,8},{10,11... | collective-permute-start | bytes 1769480 | tf_op jit(solution)/shard_map/ppermute | solution.py:233
  418.6 59.4 %copy-start.29 = (bf16[2,256,768]{2,1,0:T(8,128)(2,1)}, bf16[2,256,768]{2,1,0:T(8,128)(2,1)S(1)}, u32[]{:S(2)}) copy-start(bf16[2,256,768]{2,1,0:T(8,128)(2,1)S(1)} %multiply_convert_fusion.14) | copy-start | bytes 2359300
  440.1 29.4 %collective-permute-start.21 = (bf16[768,768]{1,0:T(8,128)(2,1)}, bf16[768,768]{1,0:T(8,128)(2,1)}, u32[]{:S(2)}, u32[]{:S(2)}) collective-permute-start(bf16[768,768]{1,0:T(8,128)(2,1)} %bitcast_convert_fusion.5), channel_id=1, source_target_pairs={{0,4},{1,5},{2,6},{3,7},{4,0},{5,1},{6,2},{7,3},{8,12},{9,13},{10,... | collective-permute-start | bytes 3538952 | tf_op jit(solution)/shard_map/ppermute | solution.py:233
  440.2 25.5 %collective-permute-start.19 = (bf16[768,768]{1,0:T(8,128)(2,1)}, bf16[768,768]{1,0:T(8,128)(2,1)}, u32[]{:S(2)}, u32[]{:S(2)}) collective-permute-start(bf16[768,768]{1,0:T(8,128)(2,1)} %bitcast_convert_fusion.7), channel_id=1, source_target_pairs={{0,4},{1,5},{2,6},{3,7},{4,0},{5,1},{6,2},{7,3},{8,12},{9,13},{10,... | collective-permute-start | bytes 3538952 | tf_op jit(solution)/shard_map/ppermute | solution.py:233
  441.4 15.3 %collective-permute-start.25 = (bf16[384,384]{1,0:T(8,128)(2,1)}, bf16[384,384]{1,0:T(8,128)(2,1)}, u32[]{:S(2)}, u32[]{:S(2)}) collective-permute-start(bf16[384,384]{1,0:T(8,128)(2,1)} %constant_dynamic-slice_fusion.30), channel_id=1, source_target_pairs={{0,16},{1,17},{2,18},{3,19},{4,20},{5,21},{6,22},{7,23},{8,24},{9,... | collective-permute-start | bytes 884744 | tf_op jit(solution)/shard_map/ppermute | solution.py:233
  444.2 14.5 %collective-permute-start.24 = (bf16[384,384]{1,0:T(8,128)(2,1)}, bf16[384,384]{1,0:T(8,128)(2,1)S(1)}, u32[]{:S(2)}, u32[]{:S(2)}) collective-permute-start(bf16[384,384]{1,0:T(8,128)(2,1)} %pad_maximum_fusion.7), channel_id=1, source_target_pairs={{0,1},{1,0},{2,3},{3,2},{4,5},{5,4},{6,7},{7,6},{8,9},{9,8},{10,11... | collective-permute-start | bytes 884744 | tf_op jit(solution)/shard_map/ppermute | solution.py:233
  445.5 57.1 %collective-permute-start.22 = (bf16[384,768]{1,0:T(8,128)(2,1)}, bf16[384,768]{1,0:T(8,128)(2,1)}, u32[]{:S(2)}, u32[]{:S(2)}) collective-permute-start(bf16[384,768]{1,0:T(8,128)(2,1)} %add_convert_fusion.32), channel_id=1, source_target_pairs={{0,0},{1,1},{2,4},{3,5},{4,2},{5,3},{6,6},{7,7},{8,8},{9,9},{10,12... | collective-permute-start | bytes 1769480 | tf_op jit(solution)/shard_map/ppermute | solution.py:287
  456.8 16.7 %collective-permute-start.20 = (bf16[768,768]{1,0:T(8,128)(2,1)}, bf16[768,768]{1,0:T(8,128)(2,1)S(1)}, u32[]{:S(2)}, u32[]{:S(2)}) collective-permute-start(bf16[768,768]{1,0:T(8,128)(2,1)} %bitcast_convert_fusion.6), channel_id=1, source_target_pairs={{0,4},{1,5},{2,6},{3,7},{4,0},{5,1},{6,2},{7,3},{8,12},{9,13},{10,... | collective-permute-start | bytes 3538952 | tf_op jit(solution)/shard_map/ppermute | solution.py:233
  458.7 43.9 %collective-permute-start.23 = (bf16[384,768]{1,0:T(8,128)(2,1)}, bf16[384,768]{1,0:T(8,128)(2,1)}, u32[]{:S(2)}, u32[]{:S(2)}) collective-permute-start(bf16[384,768]{1,0:T(8,128)(2,1)} %add_convert_fusion.31), channel_id=1, source_target_pairs={{0,0},{1,1},{2,4},{3,5},{4,2},{5,3},{6,6},{7,7},{8,8},{9,9},{10,12... | collective-permute-start | bytes 1769480 | tf_op jit(solution)/shard_map/ppermute | solution.py:287
  465.7 10.4 %collective-permute-start.18 = (bf16[768,768]{1,0:T(8,128)(2,1)S(1)}, bf16[768,768]{1,0:T(8,128)(2,1)S(1)}, u32[]{:S(2)}, u32[]{:S(2)}) collective-permute-start(bf16[768,768]{1,0:T(8,128)(2,1)S(1)} %copy-done.203), channel_id=1, source_target_pairs={{0,4},{1,5},{2,6},{3,7},{4,0},{5,1},{6,2},{7,3},{8,12},{9,13},{10,... | collective-permute-start | bytes 3538952 | tf_op jit(solution)/shard_map/ppermute | solution.py:233
  490.5 69.0 %collective-permute-start.36 = (bf16[768,768]{1,0:T(8,128)(2,1)}, bf16[768,768]{1,0:T(8,128)(2,1)}, u32[]{:S(2)}, u32[]{:S(2)}) collective-permute-start(bf16[768,768]{1,0:T(8,128)(2,1)} %broadcast_select_fusion), channel_id=1, source_target_pairs={{0,1},{1,0},{2,3},{3,2},{4,5},{5,4},{6,7},{7,6},{8,9},{9,8},{10,11... | collective-permute-start | bytes 3538952 | tf_op jit(solution)/shard_map/ppermute | solution.py:233
  492.1 42.0 %collective-permute-start.33 = (bf16[384,768]{1,0:T(8,128)(2,1)}, bf16[384,768]{1,0:T(8,128)(2,1)}, u32[]{:S(2)}, u32[]{:S(2)}) collective-permute-start(bf16[384,768]{1,0:T(8,128)(2,1)} %constant_dynamic-slice_fusion.8), channel_id=1, source_target_pairs={{0,16},{1,17},{2,18},{3,19},{4,20},{5,21},{6,22},{7,23},{8,24},{9,... | collective-permute-start | bytes 1769480 | tf_op jit(solution)/shard_map/ppermute | solution.py:233
  493.5 41.1 %collective-permute-start.34 = (bf16[384,768]{1,0:T(8,128)(2,1)}, bf16[384,768]{1,0:T(8,128)(2,1)}, u32[]{:S(2)}, u32[]{:S(2)}) collective-permute-start(bf16[384,768]{1,0:T(8,128)(2,1)} %constant_dynamic-slice_fusion.7), channel_id=1, source_target_pairs={{0,16},{1,17},{2,18},{3,19},{4,20},{5,21},{6,22},{7,23},{8,24},{9,... | collective-permute-start | bytes 1769480 | tf_op jit(solution)/shard_map/ppermute | solution.py:233
  510.0 19.4 %collective-permute-start.40 = (bf16[384,384]{1,0:T(8,128)(2,1)}, bf16[384,384]{1,0:T(8,128)(2,1)S(1)}, u32[]{:S(2)}, u32[]{:S(2)}) collective-permute-start(bf16[384,384]{1,0:T(8,128)(2,1)} %add_convert_fusion.40), channel_id=1, source_target_pairs={{0,0},{1,1},{2,4},{3,5},{4,2},{5,3},{6,6},{7,7},{8,8},{9,9},{10,12... | collective-permute-start | bytes 884744 | tf_op jit(solution)/shard_map/ppermute | solution.py:287
  511.6 20.2 %collective-permute-start.41 = (bf16[384,384]{1,0:T(8,128)(2,1)}, bf16[384,384]{1,0:T(8,128)(2,1)}, u32[]{:S(2)}, u32[]{:S(2)}) collective-permute-start(bf16[384,384]{1,0:T(8,128)(2,1)} %add_convert_fusion.39), channel_id=1, source_target_pairs={{0,0},{1,1},{2,4},{3,5},{4,2},{5,3},{6,6},{7,7},{8,8},{9,9},{10,12... | collective-permute-start | bytes 884744 | tf_op jit(solution)/shard_map/ppermute | solution.py:287
  530.1 8.1 collective-permute-start.29
  531.8 8.1 collective-permute-start.30
  534.1 38.3 %collective-permute-start.26 = (bf16[768,768]{1,0:T(8,128)(2,1)}, bf16[768,768]{1,0:T(8,128)(2,1)}, u32[]{:S(2)}, u32[]{:S(2)}) collective-permute-start(bf16[768,768]{1,0:T(8,128)(2,1)} %bitcast_convert_fusion), channel_id=1, source_target_pairs={{0,4},{1,5},{2,6},{3,7},{4,0},{5,1},{6,2},{7,3},{8,12},{9,13},{10,... | collective-permute-start | bytes 3538952 | tf_op jit(solution)/shard_map/ppermute | solution.py:233
  537.0 25.5 %collective-permute-start.35 = (bf16[384,768]{1,0:T(8,128)(2,1)}, bf16[384,768]{1,0:T(8,128)(2,1)}, u32[]{:S(2)}, u32[]{:S(2)}) collective-permute-start(bf16[384,768]{1,0:T(8,128)(2,1)} %broadcast_select_fusion.2), channel_id=1, source_target_pairs={{0,1},{1,0},{2,3},{3,2},{4,5},{5,4},{6,7},{7,6},{8,9},{9,8},{10,11... | collective-permute-start | bytes 1769480 | tf_op jit(solution)/shard_map/ppermute | solution.py:233
  542.6 35.8 %collective-permute-start.31 = (bf16[768,384]{1,0:T(8,128)(2,1)}, bf16[768,384]{1,0:T(8,128)(2,1)}, u32[]{:S(2)}, u32[]{:S(2)}) collective-permute-start(bf16[768,384]{1,0:T(8,128)(2,1)} %pad_maximum_fusion.6), channel_id=1, source_target_pairs={{0,1},{1,0},{2,3},{3,2},{4,5},{5,4},{6,7},{7,6},{8,9},{9,8},{10,11... | collective-permute-start | bytes 1769480 | tf_op jit(solution)/shard_map/ppermute | solution.py:233
  561.8 22.8 %collective-permute-start.37 = (bf16[384,768]{1,0:T(8,128)(2,1)S(1)}, bf16[384,768]{1,0:T(8,128)(2,1)S(1)}, u32[]{:S(2)}, u32[]{:S(2)}) collective-permute-start(bf16[384,768]{1,0:T(8,128)(2,1)S(1)} %constant_dynamic-slice_fusion.6), channel_id=1, source_target_pairs={{0,16},{1,17},{2,18},{3,19},{4,20},{5,21},{6,22},{7,23},{8,24},{9,... | collective-permute-start | bytes 1769480 | tf_op jit(solution)/shard_map/ppermute | solution.py:233
  566.5 51.3 %collective-permute-start.46 = (bf16[384,768]{1,0:T(8,128)(2,1)}, bf16[384,768]{1,0:T(8,128)(2,1)}, u32[]{:S(2)}, u32[]{:S(2)}) collective-permute-start(bf16[384,768]{1,0:T(8,128)(2,1)} %get-tuple-element.330), channel_id=1, source_target_pairs={{0,0},{1,1},{2,4},{3,5},{4,2},{5,3},{6,6},{7,7},{8,8},{9,9},{10,12... | collective-permute-start | bytes 1769480 | tf_op jit(solution)/shard_map/ppermute | solution.py:287
  574.7 22.5 %collective-permute-start.27 = (bf16[384,768]{1,0:T(8,128)(2,1)S(1)}, bf16[384,768]{1,0:T(8,128)(2,1)S(1)}, u32[]{:S(2)}, u32[]{:S(2)}) collective-permute-start(bf16[384,768]{1,0:T(8,128)(2,1)S(1)} %constant_dynamic-slice_fusion.25), channel_id=1, source_target_pairs={{0,16},{1,17},{2,18},{3,19},{4,20},{5,21},{6,22},{7,23},{8,24},{9,... | collective-permute-start | bytes 1769480 | tf_op jit(solution)/shard_map/ppermute | solution.py:233
  580.6 29.8 %collective-permute-start.32 = (bf16[384,384]{1,0:T(8,128)(2,1)}, bf16[384,384]{1,0:T(8,128)(2,1)}, u32[]{:S(2)}, u32[]{:S(2)}) collective-permute-start(bf16[384,384]{1,0:T(8,128)(2,1)} %constant_dynamic-slice_fusion.16), channel_id=1, source_target_pairs={{0,16},{1,17},{2,18},{3,19},{4,20},{5,21},{6,22},{7,23},{8,24},{9,... | collective-permute-start | bytes 884744 | tf_op jit(solution)/shard_map/ppermute | solution.py:233
  586.2 31.6 %collective-permute-start.47 = (bf16[384,768]{1,0:T(8,128)(2,1)}, bf16[384,768]{1,0:T(8,128)(2,1)}, u32[]{:S(2)}, u32[]{:S(2)}) collective-permute-start(bf16[384,768]{1,0:T(8,128)(2,1)} %get-tuple-element.328), channel_id=1, source_target_pairs={{0,0},{1,1},{2,4},{3,5},{4,2},{5,3},{6,6},{7,7},{8,8},{9,9},{10,12... | collective-permute-start | bytes 1769480 | tf_op jit(solution)/shard_map/ppermute | solution.py:287
  600.0 14.0 %collective-permute-start.28 = (bf16[384,384]{1,0:T(8,128)(2,1)}, bf16[384,384]{1,0:T(8,128)(2,1)}, u32[]{:S(2)}, u32[]{:S(2)}) collective-permute-start(bf16[384,384]{1,0:T(8,128)(2,1)} %pad_maximum_fusion.8), channel_id=1, source_target_pairs={{0,1},{1,0},{2,3},{3,2},{4,5},{5,4},{6,7},{7,6},{8,9},{9,8},{10,11... | collective-permute-start | bytes 884744 | tf_op jit(solution)/shard_map/ppermute | solution.py:233
  717.8 17.5 %collective-permute-start.42 = (bf16[3592,2,1,96]{0,3,2,1:T(8,128)(2,1)S(1)}, bf16[3592,2,1,96]{0,3,2,1:T(8,128)(2,1)S(1)}, u32[]{:S(2)}, u32[]{:S(2)}) collective-permute-start(bf16[3592,2,1,96]{0,3,2,1:T(8,128)(2,1)S(1)} %dynamic-slice_convert_fusion), channel_id=1, source_target_pairs={{0,4},{4,0},{8,12},{12,8},{16,20},{20,16},{24,28},{28,24},{1,5},{5... | collective-permute-start | bytes 4137992 | tf_op jit(solution)/shard_map/ppermute | solution.py:40
  728.0 34.9 %collective-permute-start.48 = (bf16[2,2,2,1,96,768]{5,4,1,0,3,2:T(8,128)(2,1)}, bf16[2,2,2,1,96,768]{5,4,1,0,3,2:T(8,128)(2,1)}, u32[]{:S(2)}, u32[]{:S(2)}) collective-permute-start(bf16[2,2,2,1,96,768]{5,4,1,0,3,2:T(8,128)(2,1)} %copy.659), channel_id=1, source_target_pairs={{0,4},{4,0},{8,12},{12,8},{16,20},{20,16},{24,28},{28,24},{1,5},{5... | collective-permute-start | bytes 3538952 | tf_op jit(solution)/shard_map/ppermute | solution.py:40
  728.3 5.4 collective-permute-start.38
  729.1 4.8 collective-permute-start.39
  747.3 25.4 %collective-permute-start.43 = (bf16[2,4,2,1,96,192]{5,4,1,0,3,2:T(8,128)(2,1)}, bf16[2,4,2,1,96,192]{5,4,1,0,3,2:T(8,128)(2,1)}, u32[]{:S(2)}, u32[]{:S(2)}) collective-permute-start(bf16[2,4,2,1,96,192]{5,4,1,0,3,2:T(8,128)(2,1)} %copy.661), channel_id=1, source_target_pairs={{0,4},{4,0},{8,12},{12,8},{16,20},{20,16},{24,28},{28,24},{1,5},{5... | collective-permute-start | bytes 1769480 | tf_op jit(solution)/shard_map/ppermute | solution.py:40
  762.1 19.2 %collective-permute-start.45 = (bf16[3592,1,1,96]{0,3,2,1:T(8,128)(2,1)}, bf16[3592,1,1,96]{0,3,2,1:T(8,128)(2,1)}, u32[]{:S(2)}, u32[]{:S(2)}) collective-permute-start(bf16[3592,1,1,96]{0,3,2,1:T(8,128)(2,1)} %dynamic-slice_convert_fusion.1), channel_id=1, source_target_pairs={{0,8},{4,12},{8,0},{12,4},{16,24},{20,28},{24,16},{28,20},{1,9},{5... | collective-permute-start | bytes 2069000 | tf_op jit(solution)/shard_map/ppermute | solution.py:40
  774.8 23.4 %collective-permute-start.44 = (bf16[2,4,1,1,96,192]{5,4,1,0,3,2:T(8,128)(2,1)S(1)}, bf16[2,4,1,1,96,192]{5,4,1,0,3,2:T(8,128)(2,1)S(1)}, u32[]{:S(2)}, u32[]{:S(2)}) collective-permute-start(bf16[2,4,1,1,96,192]{5,4,1,0,3,2:T(8,128)(2,1)S(1)} %dynamic-slice_convert_fusion.4), channel_id=1, source_target_pairs={{0,8},{4,12},{8,0},{12,4},{16,24},{20,28},{24,16},{28,20},{1,9},{5... | collective-permute-start | bytes 884744 | tf_op jit(solution)/shard_map/ppermute | solution.py:40
  790.6 5.8 collective-permute-start.50
  792.2 16.3 %collective-permute-start.49 = (bf16[2,2,1,1,96,768]{5,4,1,0,3,2:T(8,128)(2,1)S(1)}, bf16[2,2,1,1,96,768]{5,4,1,0,3,2:T(8,128)(2,1)S(1)}, u32[]{:S(2)}, u32[]{:S(2)}) collective-permute-start(bf16[2,2,1,1,96,768]{5,4,1,0,3,2:T(8,128)(2,1)S(1)} %dynamic-slice_convert_fusion.2), channel_id=1, source_target_pairs={{0,8},{4,12},{8,0},{12,4},{16,24},{20,28},{24,16},{28,20},{1,9},{5... | collective-permute-start | bytes 1769480 | tf_op jit(solution)/shard_map/ppermute | solution.py:40
  796.8 19.3 %collective-permute-start.51 = (bf16[2,1,1,96,1152]{4,3,0,2,1:T(8,128)(2,1)S(1)}, bf16[2,1,1,96,1152]{4,3,0,2,1:T(8,128)(2,1)S(1)}, u32[]{:S(2)}, u32[]{:S(2)}) collective-permute-start(bf16[2,1,1,96,1152]{4,3,0,2,1:T(8,128)(2,1)S(1)} %dynamic-slice_convert_fusion.3), channel_id=1, source_target_pairs={{0,8},{4,12},{8,0},{12,4},{16,24},{20,28},{24,16},{28,20},{1,9},{5... | collective-permute-start | bytes 1327112 | tf_op jit(solution)/shard_map/ppermute | solution.py:40
  (243 other events, 1341.8 us)
Sparse Core Ops, SparseCore 0:
  11.5 136.4 all-gather.13
  151.5 79.7 all-gather.17
  273.4 23.2 all-gather.15
  361.5 54.7 all-gather.19
  521.1 69.3 all-gather.21
